TPU v7x, 32 devices: a whole 2x2x4 slice. The times are simulated.
32 devices in a mesh: dp: 8 (over z, x), mp: 4 (over y, core).
Axes of the slice: x: 2, y: 2, z: 4, core: 2. Of those that a mesh axis runs over, the one named last changes fastest.
Arguments:
- tokens: float32 [10240, 1024], P(('dp', 'mp')), may hold values from -6 to 6
- cotangent: float32 [10240, 1024], P(('dp', 'mp')), may hold values from -6 to 6
- segments: int32 [10240], P('dp'), may hold values from 0 to 63, as said below
- attention_weights: float32 [2, 4, 1024, 1024], P(None, None, 'dp', 'mp')
- attention_first: float32 [2, 4, 1024, 1024], P(None, None, 'dp', 'mp')
- attention_second: float32 [2, 4, 1024, 1024], P(None, None, 'dp', 'mp')
- dense_weights: float32 [2, 2, 1024, 4096], P(None, None, 'dp', 'mp')
- dense_first: float32 [2, 2, 1024, 4096], P(None, None, 'dp', 'mp')
- dense_second: float32 [2, 2, 1024, 4096], P(None, None, 'dp', 'mp')
- norm_params: float32 [2, 4, 1024], replicated
- norm_first: float32 [2, 4, 1024], replicated
- norm_second: float32 [2, 4, 1024], replicated
Outputs:
- outcome: float32 [10240, 1024], P(('dp', 'mp'))
- grad_tokens: float32 [10240, 1024], P(('dp', 'mp'))
- attention_new: float32 [2, 4, 1024, 1024], P(None, None, 'dp', 'mp')
- attention_first_new: float32 [2, 4, 1024, 1024], P(None, None, 'dp', 'mp')
- attention_second_new: float32 [2, 4, 1024, 1024], P(None, None, 'dp', 'mp')
- attention_copy: bfloat16 [2, 4, 1024, 1024], P(None, None, 'dp', 'mp')
- dense_new: float32 [2, 2, 1024, 4096], P(None, None, 'dp', 'mp')
- dense_first_new: float32 [2, 2, 1024, 4096], P(None, None, 'dp', 'mp')
- dense_second_new: float32 [2, 2, 1024, 4096], P(None, None, 'dp', 'mp')
- dense_copy: bfloat16 [2, 2, 1024, 4096], P(None, None, 'dp', 'mp')
- norm_new: float32 [2, 4, 1024], replicated
- norm_first_new: float32 [2, 4, 1024], replicated
- norm_second_new: float32 [2, 4, 1024], replicated
- norms: float32 [2, 6, 2], replicated
- second_norm_grad: float32 [2, 2, 1024], replicated
Inputs may be any that keep to these rules, and one draw needn't show every extreme that they name: `segments`: in each aligned block of 1280 tokens crop numbers start at 0 and never fall; a block holds 2·8 crops of 50 tokens and 6·8 crops of 10 tokens in an order drawn from the seed.
All inputs are finite; a program needn't handle non-finite values.
Results may differ from a plain program's by a relative error of at most 0.029.
Values may be sent and summed in bfloat16 or wider, within the bound.
No kernel may reach another device: no remote copies, remote signals or barrier semaphores. Data moves between devices by JAX's collectives and lax.ppermute only.
A program may use at most 320 MiB of HBM per device.

v0:
```python
import jax
import jax.numpy as jnp
from jax import lax
from jax.sharding import PartitionSpec as P

D = 1024
HEADS = 16
HD = 64
FF = 4096
STEP = 10


EPS_NORM = 1e-06
BETA_ONE = 0.9
BETA_TWO = 0.999
ADAM_EPS = 1e-06
WEIGHT_DECAY = 0.01
LEARN_RATE = 0.5
MASKED = -1000000000.0


def layer_norm(stream, gain, shift):
    centre = stream - jnp.mean(stream, axis=-1, keepdims=True)
    spread = jnp.mean(centre * centre, axis=-1, keepdims=True)
    return centre * lax.rsqrt(spread + EPS_NORM) * gain + shift


def gelu_exact(values_in):
    return jax.nn.gelu(values_in, approximate=False)


def adam_part(gradient, weight, first, second, decay):
    first_new = BETA_ONE * first + (1.0 - BETA_ONE) * gradient
    second_new = BETA_TWO * second + (1.0 - BETA_TWO) * gradient * gradient
    step_dir = (
        first_new
        / (1.0 - BETA_ONE**STEP)
        / (jnp.sqrt(second_new / (1.0 - BETA_TWO**STEP)) + ADAM_EPS)
        + decay * weight
    )
    return (first_new, second_new, step_dir)


def masked_scores(query, keys_in, same_crop):
    scores = jnp.einsum(
        "qhe,khe->hqk", query, keys_in, preferred_element_type=jnp.float32
    ) * HD ** (-0.5)
    return jnp.where(same_crop, scores, MASKED)


def attend(query, keys_in, values_in, same_crop):
    scores = masked_scores(query, keys_in, same_crop)
    row_max = jnp.max(scores, axis=-1, keepdims=True)
    powered = jnp.exp(scores - row_max)
    row_sum = jnp.sum(powered, axis=-1, keepdims=True)
    shares = (powered / row_sum).astype(jnp.bfloat16)
    attended = jnp.einsum("hqk,khe->qhe", shares, values_in, preferred_element_type=jnp.float32)
    return (attended, row_max + jnp.log(row_sum))


def attend_back(query, keys_in, values_in, same_crop, log_total, grad_attended):
    shares = jnp.exp(masked_scores(query, keys_in, same_crop) - log_total)
    grad_shares = jnp.einsum(
        "qhe,khe->hqk", grad_attended, values_in, preferred_element_type=jnp.float32
    )
    row_inner = jnp.sum(grad_shares * shares, axis=-1, keepdims=True)
    grad_scores = (shares * (grad_shares - row_inner)).astype(jnp.bfloat16)
    score_scale = HD ** (-0.5)
    grad_query = (
        jnp.einsum("hqk,khe->qhe", grad_scores, keys_in, preferred_element_type=jnp.float32)
        * score_scale
    )
    grad_keys = (
        jnp.einsum("hqk,qhe->khe", grad_scores, query, preferred_element_type=jnp.float32)
        * score_scale
    )
    grad_values = jnp.einsum(
        "hqk,qhe->khe",
        shares.astype(jnp.bfloat16),
        grad_attended,
        preferred_element_type=jnp.float32,
    )
    return jnp.stack([grad_query, grad_keys, grad_values], axis=1)


def shards(
    tokens,
    cotangent,
    segments,
    attention_weights,
    attention_first,
    attention_second,
    dense_weights,
    dense_first,
    dense_second,
    norm_params,
    norm_first,
    norm_second,
):
    layers = attention_weights.shape[0]
    token_count = segments.shape[0]
    heads_here = attention_weights.shape[3] // HD
    same_crop = (segments[:, None] == segments[None, :])[None]
    mixer_low = attention_weights.astype(jnp.bfloat16)
    dense_low = dense_weights.astype(jnp.bfloat16)
    copies = []
    for current in range(layers):
        copies.append(
            (
                lax.all_gather(mixer_low[current], "dp", axis=1, tiled=True),
                lax.all_gather(dense_low[current], "dp", axis=1, tiled=True),
            )
        )
    saved_forward = []
    stream = tokens
    for current in range(layers):
        mixer_full, dense_full = copies[current]
        params = norm_params[current]
        normed = layer_norm(stream, params[0], params[1]).astype(jnp.bfloat16)
        gathered = lax.all_gather(normed, "mp", axis=0, tiled=True)
        projected = jnp.einsum(
            "td,sdh->tsh", gathered, mixer_full[:3], preferred_element_type=jnp.float32
        ).astype(jnp.bfloat16)
        split_heads = projected.reshape(token_count, 3, heads_here, HD)
        attended, log_total = attend(
            split_heads[:, 0], split_heads[:, 1], split_heads[:, 2], same_crop
        )
        attended = attended.reshape(token_count, heads_here * HD).astype(jnp.bfloat16)
        middle = stream + lax.psum_scatter(
            jnp.einsum(
                "th,dh->td", attended, mixer_full[3], preferred_element_type=jnp.float32
            ).astype(jnp.bfloat16),
            "mp",
            scatter_dimension=0,
            tiled=True,
        ).astype(jnp.float32)
        normed_two = layer_norm(middle, params[2], params[3]).astype(jnp.bfloat16)
        dense_wide = dense_full
        gathered_two = lax.all_gather(normed_two, "mp", axis=0, tiled=True)
        hidden = jnp.dot(gathered_two, dense_full[0], preferred_element_type=jnp.float32)
        active = gelu_exact(hidden).astype(jnp.bfloat16)
        after_dense = middle + lax.psum_scatter(
            jnp.einsum(
                "tf,df->td", active, dense_full[1], preferred_element_type=jnp.float32
            ).astype(jnp.bfloat16),
            "mp",
            scatter_dimension=0,
            tiled=True,
        ).astype(jnp.float32)
        saved_forward.append(
            (
                stream,
                gathered,
                projected,
                log_total,
                attended,
                middle,
                gathered_two,
                hidden,
                active,
                dense_wide,
            )
        )
        stream = after_dense
    stream_grad = cotangent
    states = [None] * layers
    squares_list = [None] * layers
    vector_list = [None] * layers
    summed_list = [None] * layers
    for current in reversed(range(layers)):
        (
            stream_in,
            gathered,
            projected,
            log_total,
            attended,
            middle,
            gathered_two,
            hidden,
            active,
            dense_wide,
        ) = saved_forward[current]
        mixer_full, dense_full = copies[current]
        params = norm_params[current]
        back_rows = lax.all_gather(stream_grad.astype(jnp.bfloat16), "mp", axis=0, tiled=True)
        grad_active = jnp.dot(back_rows, dense_full[1], preferred_element_type=jnp.float32)
        grad_down = jnp.einsum("td,tf->df", back_rows, active, preferred_element_type=jnp.float32)
        gelu_value, gelu_pull = jax.vjp(gelu_exact, hidden)
        grad_hidden = gelu_pull(grad_active)[0].astype(jnp.bfloat16)
        grad_up = jnp.einsum(
            "td,tf->df", gathered_two, grad_hidden, preferred_element_type=jnp.float32
        )
        grad_normed_two = lax.psum_scatter(
            jnp.einsum(
                "tf,df->td", grad_hidden, dense_full[0], preferred_element_type=jnp.float32
            ).astype(jnp.bfloat16),
            "mp",
            scatter_dimension=0,
            tiled=True,
        ).astype(jnp.float32)
        norm_value, norm_pull = jax.vjp(layer_norm, middle, params[2], params[3])
        grad_middle, grad_gain_two, grad_shift_two = norm_pull(grad_normed_two)
        stream_grad = stream_grad + grad_middle
        back_rows_two = lax.all_gather(stream_grad.astype(jnp.bfloat16), "mp", axis=0, tiled=True)
        grad_attended = jnp.dot(
            back_rows_two, mixer_full[3], preferred_element_type=jnp.float32
        ).astype(jnp.bfloat16)
        grad_output_map = jnp.einsum(
            "td,th->dh", back_rows_two, attended, preferred_element_type=jnp.float32
        )
        split_heads = projected.reshape(token_count, 3, heads_here, HD)
        grad_split = attend_back(
            split_heads[:, 0],
            split_heads[:, 1],
            split_heads[:, 2],
            same_crop,
            log_total,
            grad_attended.reshape(token_count, heads_here, HD),
        )
        grad_projected = grad_split.reshape(token_count, 3, heads_here * HD).astype(jnp.bfloat16)
        grad_inputs_map = jnp.einsum(
            "td,tsh->sdh", gathered, grad_projected, preferred_element_type=jnp.float32
        )
        grad_normed = lax.psum_scatter(
            jnp.einsum(
                "tsh,sdh->td", grad_projected, mixer_full[:3], preferred_element_type=jnp.float32
            ).astype(jnp.bfloat16),
            "mp",
            scatter_dimension=0,
            tiled=True,
        ).astype(jnp.float32)
        norm_value_one, norm_pull_one = jax.vjp(layer_norm, stream_in, params[0], params[1])
        grad_inner, grad_gain_one, grad_shift_one = norm_pull_one(grad_normed)
        stream_grad = stream_grad + grad_inner
        mixer_grad = jnp.concatenate([grad_inputs_map, grad_output_map[None]], axis=0)
        dense_grad = jnp.stack([grad_up, grad_down], axis=0)
        mixer_grad, dense_grad = (
            lax.psum_scatter(mixer_grad, "dp", scatter_dimension=1, tiled=True),
            lax.psum_scatter(dense_grad, "dp", scatter_dimension=1, tiled=True),
        )
        mixer_first, mixer_second, mixer_step = adam_part(
            mixer_grad,
            attention_weights[current],
            attention_first[current],
            attention_second[current],
            WEIGHT_DECAY,
        )
        dense_first_new, dense_second_new, dense_step = adam_part(
            dense_grad,
            dense_weights[current],
            dense_first[current],
            dense_second[current],
            WEIGHT_DECAY,
        )
        weight_squares = jnp.concatenate(
            [
                jnp.sum(attention_weights[current] * attention_weights[current], axis=(1, 2)),
                jnp.sum(dense_weights[current] * dense_weights[current], axis=(1, 2)),
            ]
        )
        step_squares = jnp.concatenate(
            [
                jnp.sum(mixer_step * mixer_step, axis=(1, 2)),
                jnp.sum(dense_step * dense_step, axis=(1, 2)),
            ]
        )
        squares = jnp.stack([weight_squares, step_squares], axis=-1)
        vector_grad = jnp.stack(
            [grad_gain_one, grad_shift_one, grad_gain_two, grad_shift_two], axis=0
        )
        states[current] = (
            mixer_first,
            mixer_second,
            mixer_step,
            dense_first_new,
            dense_second_new,
            dense_step,
        )
        squares_list[current] = squares
        vector_list[current] = vector_grad
        summed_list[current] = lax.psum((squares, vector_grad), ("dp", "mp"))
    total_squares = jnp.stack([entry[0] for entry in summed_list])
    total_vectors = jnp.stack([entry[1] for entry in summed_list])
    sizes_all = jnp.sqrt(total_squares[:, :, 0])
    moves_all = jnp.sqrt(total_squares[:, :, 1])
    trust_all = sizes_all / moves_all
    mixer_new = jnp.stack(
        [
            attention_weights[current]
            - LEARN_RATE * trust_all[current, :4, None, None] * states[current][2]
            for current in range(layers)
        ]
    )
    dense_new = jnp.stack(
        [
            dense_weights[current]
            - LEARN_RATE * trust_all[current, 4:, None, None] * states[current][5]
            for current in range(layers)
        ]
    )
    mixer_first_all = jnp.stack([states[current][0] for current in range(layers)])
    mixer_second_all = jnp.stack([states[current][1] for current in range(layers)])
    dense_first_all = jnp.stack([states[current][3] for current in range(layers)])
    dense_second_all = jnp.stack([states[current][4] for current in range(layers)])
    params_first, params_second, params_step = adam_part(
        total_vectors, norm_params, norm_first, norm_second, 0.0
    )
    params_size = jnp.sqrt(jnp.sum(norm_params * norm_params, axis=-1))
    params_move = jnp.sqrt(jnp.sum(params_step * params_step, axis=-1))
    params_new = norm_params - LEARN_RATE * (params_size / params_move)[:, :, None] * params_step
    mixer_entries = float(D * HEADS * HD) ** 0.5
    dense_entries = float(D * FF) ** 0.5
    entry_roots = jnp.array([mixer_entries] * 4 + [dense_entries] * 2, jnp.float32)
    norms = jnp.stack([sizes_all / entry_roots[None, :], moves_all / entry_roots[None, :]], axis=-1)
    second_norm_grad = total_vectors[:, 2:4]
    return (
        stream,
        stream_grad,
        mixer_new,
        mixer_first_all,
        mixer_second_all,
        mixer_new.astype(jnp.bfloat16),
        dense_new,
        dense_first_all,
        dense_second_all,
        dense_new.astype(jnp.bfloat16),
        params_new,
        params_first,
        params_second,
        norms,
        second_norm_grad,
    )


def solution(mesh):
    in_specs = (
        P(("dp", "mp"), None),
        P(("dp", "mp"), None),
        P("dp"),
        P(None, None, "dp", "mp"),
        P(None, None, "dp", "mp"),
        P(None, None, "dp", "mp"),
        P(None, None, "dp", "mp"),
        P(None, None, "dp", "mp"),
        P(None, None, "dp", "mp"),
        P(),
        P(),
        P(),
    )
    out_specs = (
        P(("dp", "mp"), None),
        P(("dp", "mp"), None),
        P(None, None, "dp", "mp"),
        P(None, None, "dp", "mp"),
        P(None, None, "dp", "mp"),
        P(None, None, "dp", "mp"),
        P(None, None, "dp", "mp"),
        P(None, None, "dp", "mp"),
        P(None, None, "dp", "mp"),
        P(None, None, "dp", "mp"),
        P(),
        P(),
        P(),
        P(),
        P(),
    )
    return jax.shard_map(shards, mesh=mesh, in_specs=in_specs, out_specs=out_specs, check_vma=False)
```

profile of v0, /device:TPU:0, one launch (start us, length us, event | category | flops | bytes accessed | tf_op | source)
XLA Modules:
  0.0 1624.6 jit_solution(6079072630626825102)
XLA Ops:
  13.5 51.0 %all-gather.33.cloned.1.call-done = bf16[1,4,1024,256]{2,3,1,0:T(8,128)(2,1)} async-done(((bf16[1,4,128,256]{2,3,1,0:T(8,128)(2,1)}), bf16[1,4,1024,256]{2,3,1,0:T(8,128)(2,1)}) %all-gather.33.cloned.1.call-update) | async-done | bytes 2097168 | tf_op jit(solution)/shard_map/all_gather | solution.py:110
  64.4 25.9 %all-gather.17.cloned.1.call-done = bf16[1280,1024]{1,0:T(8,128)(2,1)} async-done(((bf16[320,1024]{1,0:T(8,128)(2,1)}), bf16[1280,1024]{1,0:T(8,128)(2,1)}) %all-gather.17.cloned.1.call-update) | async-done | bytes 2621456 | tf_op jit(solution)/shard_map/all_gather | solution.py:120
  90.4 4.4 convolution_convert_fusion.7
  94.8 11.0 fusion.121
  105.9 10.6 fusion.2
  116.5 11.0 fusion.43
  128.3 3.6 convolution_convert_fusion.1
  133.2 33.5 %reduce-scatter.13.cloned.1.call-done = bf16[320,1024]{1,0:T(8,128)(2,1)} async-done(((bf16[1280,1024]{1,0:T(8,128)(2,1)}), bf16[320,1024]{1,0:T(8,128)(2,1)}) %reduce-scatter.13.cloned.1.call-update) | async-done | bytes 655376 | tf_op jit(solution)/shard_map/reduce_scatter | solution.py:129
  169.8 73.1 %all-gather.35.cloned.1.call-done = bf16[1,2,1024,1024]{3,2,1,0:T(8,128)(2,1)} async-done(((bf16[1,2,128,1024]{3,2,1,0:T(8,128)(2,1)}), bf16[1,2,1024,1024]{3,2,1,0:T(8,128)(2,1)}) %all-gather.35.cloned.1.call-update) | async-done | bytes 4194320 | tf_op jit(solution)/shard_map/all_gather | solution.py:111
  243.0 25.9 %all-gather.19.cloned.1.call-done = bf16[1280,1024]{1,0:T(8,128)(2,1)} async-done(((bf16[320,1024]{1,0:T(8,128)(2,1)}), bf16[1280,1024]{1,0:T(8,128)(2,1)}) %all-gather.19.cloned.1.call-update) | async-done | bytes 2621456 | tf_op jit(solution)/shard_map/all_gather | solution.py:139
  268.9 17.2 %multiply_convert_fusion.3 = (bf16[1280,1024]{1,0:T(8,128)(2,1)S(1)}, f32[1280,1024]{1,0:T(8,128)}, f32[1280,1024]{1,0:T(8,128)}) fusion(bf16[1280,1024]{1,0:T(8,128)(2,1)} %all-gather.19.cloned.1.call-done, bf16[1,2,1024,1024]{3,2,1,0:T(8,128)(2,1)} %all-gather.35.cloned.1.call-done), kind=kOutput, calls=%fused_computation.47 | convolution fusion | flops 2769551360 | bytes 17825792 | tf_op jit(solution)/shard_map/dot_general | solution.py:140
  287.7 4.2 convolution_convert_fusion.5
  292.7 34.0 %reduce-scatter.15.cloned.1.call-done = bf16[320,1024]{1,0:T(8,128)(2,1)} async-done(((bf16[1280,1024]{1,0:T(8,128)(2,1)}), bf16[320,1024]{1,0:T(8,128)(2,1)}) %reduce-scatter.15.cloned.1.call-update) | async-done | bytes 655376 | tf_op jit(solution)/shard_map/reduce_scatter | solution.py:142
  329.6 50.9 %all-gather.37.cloned.1.call-done = bf16[1,4,1024,256]{2,3,1,0:T(8,128)(2,1)} async-done(((bf16[1,4,128,256]{2,3,1,0:T(8,128)(2,1)}), bf16[1,4,1024,256]{2,3,1,0:T(8,128)(2,1)}) %all-gather.37.cloned.1.call-update) | async-done | bytes 2097168 | tf_op jit(solution)/shard_map/all_gather | solution.py:110
  380.5 25.9 %all-gather.21.cloned.1.call-done = bf16[1280,1024]{1,0:T(8,128)(2,1)} async-done(((bf16[320,1024]{1,0:T(8,128)(2,1)}), bf16[1280,1024]{1,0:T(8,128)(2,1)}) %all-gather.21.cloned.1.call-update) | async-done | bytes 2621456 | tf_op jit(solution)/shard_map/all_gather | solution.py:120
  406.4 4.4 convolution_convert_fusion.6
  410.8 11.0 fusion.122
  421.8 10.6 fusion.3
  432.4 11.0 fusion.42
  444.2 3.5 convolution_convert_fusion
  448.4 34.2 %reduce-scatter.17.cloned.1.call-done = bf16[320,1024]{1,0:T(8,128)(2,1)} async-done(((bf16[1280,1024]{1,0:T(8,128)(2,1)}), bf16[320,1024]{1,0:T(8,128)(2,1)}) %reduce-scatter.17.cloned.1.call-update) | async-done | bytes 655376 | tf_op jit(solution)/shard_map/reduce_scatter | solution.py:129
  487.6 9.1 reduce-scatter.21.cloned.1.call-start
  496.8 62.0 %all-gather.39.cloned.1.call-done = bf16[1,2,1024,1024]{3,2,1,0:T(8,128)(2,1)} async-done(((bf16[1,2,128,1024]{3,2,1,0:T(8,128)(2,1)}), bf16[1,2,1024,1024]{3,2,1,0:T(8,128)(2,1)}) %all-gather.39.cloned.1.call-update) | async-done | bytes 4194320 | tf_op jit(solution)/shard_map/all_gather | solution.py:111
  558.8 26.1 %all-gather.23.cloned.1.call-done = bf16[1280,1024]{1,0:T(8,128)(2,1)} async-done(((bf16[320,1024]{1,0:T(8,128)(2,1)}), bf16[1280,1024]{1,0:T(8,128)(2,1)}) %all-gather.23.cloned.1.call-update) | async-done | bytes 2621456 | tf_op jit(solution)/shard_map/all_gather | solution.py:139
  584.9 17.3 %multiply_convert_fusion.2 = (bf16[1280,1024]{1,0:T(8,128)(2,1)}, f32[1280,1024]{1,0:T(8,128)}, f32[1280,1024]{1,0:T(8,128)}) fusion(bf16[1280,1024]{1,0:T(8,128)(2,1)} %all-gather.23.cloned.1.call-done, bf16[1,2,1024,1024]{3,2,1,0:T(8,128)(2,1)} %all-gather.39.cloned.1.call-done), kind=kOutput, calls=%fused_computation.34 | convolution fusion | flops 2769551360 | bytes 17825792 | tf_op jit(solution)/shard_map/dot_general | solution.py:140
  602.2 10.3 all-gather.25.cloned.1.call-done
  612.5 9.8 add_convert_fusion.1
  623.9 4.3 convolution_convert_fusion.3
  628.2 6.8 convolution_convert_fusion.4
  635.0 27.9 %reduce-scatter.21.cloned.1.call-done = bf16[320,1024]{1,0:T(8,128)(2,1)} async-done(((bf16[1280,1024]{1,0:T(8,128)(2,1)}), bf16[320,1024]{1,0:T(8,128)(2,1)}) %reduce-scatter.21.cloned.1.call-update) | async-done | bytes 655376 | tf_op jit(solution)/shard_map/reduce_scatter | solution.py:193
  665.2 34.9 %reduce-scatter.19.cloned.1.call-done = bf16[320,1024]{1,0:T(8,128)(2,1)} async-done(((bf16[1280,1024]{1,0:T(8,128)(2,1)}), bf16[320,1024]{1,0:T(8,128)(2,1)}) %reduce-scatter.19.cloned.1.call-update) | async-done | bytes 655376 | tf_op jit(solution)/shard_map/reduce_scatter | solution.py:142
  705.4 25.4 %all-gather.27.cloned.1.call-done = bf16[1280,1024]{1,0:T(8,128)(2,1)} async-done(((bf16[320,1024]{1,0:T(8,128)(2,1)}), bf16[1280,1024]{1,0:T(8,128)(2,1)}) %all-gather.27.cloned.1.call-update) | async-done | bytes 2621456 | tf_op jit(solution)/shard_map/all_gather | solution.py:204
  733.6 10.8 fusion.32
  744.3 16.7 %multiply_reduce_fusion.1 = (f32[4,1280]{1,0:T(4,128)S(1)}, f32[4,1280,1280]{1,2,0:T(8,128)}) fusion(f32[4,1280,1280]{1,2,0:T(8,128)} %get-tuple-element.129, f32[4,1280]{1,0:T(4,128)S(1)} %log_add_fusion.1, bf16[1280,4,64]{0,2,1:T(8,128)(2,1)S(1)} %bitcast.336, bf16[1280,3,4,64]{0,3,2,1:T(8,128)(2,1)} %bitcast.346), kind=kOutput, calls=%fused_computation.8 | convolution fusion | flops 858516480 | bytes 53780480 | tf_op jit(solution)/shard_map/qhe,khe->hqk/dot_general | solution.py:63
  761.1 22.2 %multiply_convert_fusion.1 = bf16[4,1280,1280]{1,2,0:T(8,128)(2,1)} fusion(f32[4,1280,1280]{1,2,0:T(8,128)} %get-tuple-element.132, f32[4,1280,1280]{1,2,0:T(8,128)} %get-tuple-element.129, f32[4,1280]{1,0:T(4,128)S(1)} %get-tuple-element.131, f32[4,1280]{1,0:T(4,128)S(1)} %log_add_fusion.1), kind=kLoop, calls=%fused_computation.7 | loop fusion | flops 26214400 | bytes 65576960 | tf_op jit(solution)/shard_map/convert_element_type | solution.py:67
  783.3 8.8 fusion.39
  792.1 7.1 fusion.38
  801.6 5.5 bitcast_convert_fusion.1
  807.6 34.4 %reduce-scatter.23.cloned.1.call-done = bf16[320,1024]{1,0:T(8,128)(2,1)} async-done(((bf16[1280,1024]{1,0:T(8,128)(2,1)}), bf16[320,1024]{1,0:T(8,128)(2,1)}) %reduce-scatter.23.cloned.1.call-update) | async-done | bytes 655376 | tf_op jit(solution)/shard_map/reduce_scatter | solution.py:224
  847.4 25.7 %all-gather.29.cloned.1.call-done = bf16[1280,1024]{1,0:T(8,128)(2,1)} async-done(((bf16[320,1024]{1,0:T(8,128)(2,1)}), bf16[1280,1024]{1,0:T(8,128)(2,1)}) %all-gather.29.cloned.1.call-update) | async-done | bytes 2621456 | tf_op jit(solution)/shard_map/all_gather | solution.py:185
  873.0 9.8 add_convert_fusion
  884.4 4.3 convolution_convert_fusion.2
  888.7 34.8 %reduce-scatter.25.cloned.1.call-done = bf16[320,1024]{1,0:T(8,128)(2,1)} async-done(((bf16[1280,1024]{1,0:T(8,128)(2,1)}), bf16[320,1024]{1,0:T(8,128)(2,1)}) %reduce-scatter.25.cloned.1.call-update) | async-done | bytes 655376 | tf_op jit(solution)/shard_map/reduce_scatter | solution.py:193
  929.2 25.5 %all-gather.31.cloned.1.call-done = bf16[1280,1024]{1,0:T(8,128)(2,1)} async-done(((bf16[320,1024]{1,0:T(8,128)(2,1)}), bf16[1280,1024]{1,0:T(8,128)(2,1)}) %all-gather.31.cloned.1.call-update) | async-done | bytes 2621456 | tf_op jit(solution)/shard_map/all_gather | solution.py:204
  957.4 11.7 fusion.35
  969.1 16.6 %multiply_reduce_fusion = (f32[4,1280]{1,0:T(4,128)S(1)}, f32[4,1280,1280]{1,2,0:T(8,128)}) fusion(f32[4,1280,1280]{1,2,0:T(8,128)} %get-tuple-element.126, f32[4,1280]{1,0:T(4,128)S(1)} %log_add_fusion, bf16[1280,4,64]{0,2,1:T(8,128)(2,1)S(1)} %bitcast.338, bf16[1280,3,4,64]{0,3,2,1:T(8,128)(2,1)S(1)} %bitcast.341), kind=kOutput, calls=%fused_computation.5 | convolution fusion | flops 858516480 | bytes 53780480 | tf_op jit(solution)/shard_map/qhe,khe->hqk/dot_general | solution.py:63
  985.7 22.1 %multiply_convert_fusion = bf16[4,1280,1280]{1,2,0:T(8,128)(2,1)} fusion(f32[4,1280,1280]{1,2,0:T(8,128)} %get-tuple-element.134, f32[4,1280,1280]{1,2,0:T(8,128)} %get-tuple-element.126, f32[4,1280]{1,0:T(4,128)S(1)} %get-tuple-element.133, f32[4,1280]{1,0:T(4,128)S(1)} %log_add_fusion), kind=kLoop, calls=%fused_computation.4 | loop fusion | flops 26214400 | bytes 65576960 | tf_op jit(solution)/shard_map/convert_element_type | solution.py:67
  1007.8 8.8 fusion.41
  1016.5 7.1 fusion.40
  1025.4 5.1 bitcast_convert_fusion
  1030.9 5.8 convolution_bitcast_fusion
  1036.7 3.0 convolution_bitcast_fusion.1
  1039.7 4.1 pad_maximum_fusion.1
  1044.3 5.7 convolution_bitcast_fusion.3
  1053.0 4.1 pad_maximum_fusion
  1060.1 4.0 fusion.47
  1083.7 3.5 add_add_fusion.4
  1087.2 130.8 %reduce-scatter.35.cloned.1.call-done = f32[2,128,1024]{2,1,0:T(8,128)} async-done(((f32[2,1024,1024]{2,1,0:T(8,128)}), f32[2,128,1024]{2,1,0:T(8,128)}) %reduce-scatter.35.cloned.1.call-update) | async-done | bytes 1048592 | tf_op jit(solution)/shard_map/reduce_scatter | solution.py:239
  1218.0 152.1 %reduce-scatter.31.cloned.1.call-done = f32[2,128,1024]{2,1,0:T(8,128)} async-done(((f32[2,1024,1024]{2,1,0:T(8,128)}), f32[2,128,1024]{2,1,0:T(8,128)}) %reduce-scatter.31.cloned.1.call-update) | async-done | bytes 1048592 | tf_op jit(solution)/shard_map/reduce_scatter | solution.py:239
  1370.1 5.7 multiply_reduce_fusion.6
  1378.1 83.2 %reduce-scatter.33.cloned.1.call-done = f32[4,128,256]{1,2,0:T(8,128)} async-done(((f32[4,1024,256]{1,2,0:T(8,128)}), f32[4,128,256]{1,2,0:T(8,128)}) %reduce-scatter.33.cloned.1.call-update) | async-done | bytes 524304 | tf_op jit(solution)/shard_map/reduce_scatter | solution.py:238
  1461.2 92.2 %reduce-scatter.29.cloned.1.call-done = f32[4,128,256]{1,2,0:T(8,128)} async-done(((f32[4,1024,256]{1,2,0:T(8,128)}), f32[4,128,256]{1,2,0:T(8,128)}) %reduce-scatter.29.cloned.1.call-update) | async-done | bytes 524304 | tf_op jit(solution)/shard_map/reduce_scatter | solution.py:238
  1553.4 4.2 multiply_reduce_fusion.10
  1557.9 40.8 %all-reduce = (f32[1,6,2]{1,2,0:T(2,128)S(1)}, f32[1,6,2]{1,2,0:T(2,128)S(1)}, f32[1,4,1024]{2,1,0:T(4,128)S(1)}, f32[1,4,1024]{2,1,0:T(4,128)S(1)}) all-reduce(f32[1,6,2]{1,2,0:T(2,128)S(1)} %maximum_bitcast_fusion.2, f32[1,6,2]{1,2,0:T(2,128)S(1)} %maximum_bitcast_fusion.3, ...), channel_id=1, replica_groups=mesh['dp'=8,'mp'=4] {'dp','mp'}, use_global_device_ids=true, to_apply=%region_36.37 | all-reduce | flops 8216 | bytes 65728 | tf_op jit(solution)/shard_map/psum | solution.py:281
  (311 shorter events, 102.2 us)
Async XLA Ops:
  7.2 57.3 %all-gather.33.cloned.1.call-start = ((), (), s32[]{:S(2)}) async-start(), calls=%async_computation.32 | async-start | bytes 2359296 | tf_op jit(solution)/shard_map/all_gather | solution.py:110
  10.0 80.3 %all-gather.17.cloned.1.call-start = ((), (), s32[]{:S(2)}) async-start(), calls=%async_computation.12 | async-start | bytes 3276800 | tf_op jit(solution)/shard_map/all_gather | solution.py:120
  10.6 84.2 %copy-start.58 = (f32[320]{0:T(512)}, f32[320]{0:T(512)S(1)}, u32[]{:S(2)}) copy-start(f32[320]{0:T(512)S(1)} %fusion.93) | copy-start | bytes 3844
  11.2 157.1 %copy-start.48 = (f32[1,1,1024]{2,1,0:T(1,128)}, f32[1,1,1024]{2,1,0:T(1,128)S(1)}, u32[]{:S(2)}) copy-start(f32[1,1,1024]{2,1,0:T(1,128)S(1)} %get-tuple-element.115) | copy-start | bytes 12292
  11.2 317.2 %copy-start.38 = (f32[1,1,1024]{2,1,0:T(1,128)}, f32[1,1,1024]{2,1,0:T(1,128)S(1)}, u32[]{:S(2)}) copy-start(f32[1,1,1024]{2,1,0:T(1,128)S(1)} %get-tuple-element.113) | copy-start | bytes 12292
  12.4 154.3 %reduce-scatter.13.cloned.1.call-start = ((), (), s32[]{:S(2)}) async-start(), calls=%async_computation.13 | async-start | bytes 3276800 | tf_op jit(solution)/shard_map/reduce_scatter | solution.py:129
  13.4 81.4 %copy-start.20 = (pred[1280,1280]{0,1:T(8,128)(4,1)}, pred[1280,1280]{0,1:T(8,128)(4,1)S(1)}, u32[]{:S(2)}) copy-start(pred[1280,1280]{0,1:T(8,128)(4,1)S(1)} %broadcast_compare_fusion) | copy-start | bytes 4915204
  94.8 21.6 %copy-start.16 = (bf16[1280,3,256]{0,2,1:T(8,128)(2,1)}, bf16[1280,3,256]{0,2,1:T(8,128)(2,1)S(1)}, u32[]{:S(2)}) copy-start(bf16[1280,3,256]{0,2,1:T(8,128)(2,1)S(1)} %convolution_convert_fusion.7) | copy-start | bytes 5898244
  105.9 10.6 copy-start.40
  116.4 11.0 copy-start.42
  131.9 111.1 %all-gather.35.cloned.1.call-start = ((), (), s32[]{:S(2)}) async-start(), calls=%async_computation.33 | async-start | bytes 4718592 | tf_op jit(solution)/shard_map/all_gather | solution.py:111
  133.2 135.7 %all-gather.19.cloned.1.call-start = ((), (), s32[]{:S(2)}) async-start(), calls=%async_computation.14 | async-start | bytes 3276800 | tf_op jit(solution)/shard_map/all_gather | solution.py:139
  168.0 158.7 %copy-start.2 = (f32[320,1024]{1,0:T(8,128)}, f32[320,1024]{1,0:T(8,128)S(1)}, u32[]{:S(2)}) copy-start(f32[320,1024]{1,0:T(8,128)S(1)} %get-tuple-element.79) | copy-start | bytes 3932164
  168.0 118.1 %copy-start.51 = (f32[320]{0:T(512)}, f32[320]{0:T(512)S(1)}, u32[]{:S(2)}) copy-start(f32[320]{0:T(512)S(1)} %broadcast_multiply_fusion.2) | copy-start | bytes 3844
  168.3 117.8 %copy-start.64 = (f32[320]{0:T(512)}, f32[320]{0:T(512)S(1)}, u32[]{:S(2)}) copy-start(f32[320]{0:T(512)S(1)} %multiply_reduce_fusion.4) | copy-start | bytes 3844
  168.4 117.8 %copy-start.56 = (f32[320]{0:T(512)}, f32[320]{0:T(512)S(1)}, u32[]{:S(2)}) copy-start(f32[320]{0:T(512)S(1)} %fusion.94) | copy-start | bytes 3844
  169.5 157.2 %reduce-scatter.15.cloned.1.call-start = ((), (), s32[]{:S(2)}) async-start(), calls=%async_computation.15 | async-start | bytes 3276800 | tf_op jit(solution)/shard_map/reduce_scatter | solution.py:142
  268.9 18.8 %copy-start.72 = (bf16[1,2,1024,1024]{3,2,1,0:T(8,128)(2,1)S(1)}, bf16[1,2,1024,1024]{3,2,1,0:T(8,128)(2,1)}, u32[]{:S(2)}) copy-start(bf16[1,2,1024,1024]{3,2,1,0:T(8,128)(2,1)} %all-gather.35.cloned.1.call-done) | copy-start | bytes 12582916
  291.9 88.6 %all-gather.37.cloned.1.call-start = ((), (), s32[]{:S(2)}) async-start(), calls=%async_computation.34 | async-start | bytes 2359296 | tf_op jit(solution)/shard_map/all_gather | solution.py:110
  292.7 113.7 %all-gather.21.cloned.1.call-start = ((), (), s32[]{:S(2)}) async-start(), calls=%async_computation.16 | async-start | bytes 3276800 | tf_op jit(solution)/shard_map/all_gather | solution.py:120
  329.5 81.3 %copy-start.21 = (pred[1280,1280]{0,1:T(8,128)(4,1)S(1)}, pred[1280,1280]{0,1:T(8,128)(4,1)}, u32[]{:S(2)}) copy-start(pred[1280,1280]{0,1:T(8,128)(4,1)} %copy-done.20) | copy-start | bytes 4915204
  329.6 153.0 %reduce-scatter.17.cloned.1.call-start = ((), (), s32[]{:S(2)}) async-start(), calls=%async_computation.17 | async-start | bytes 3276800 | tf_op jit(solution)/shard_map/reduce_scatter | solution.py:129
  410.8 21.6 %copy-start.18 = (bf16[1280,3,256]{0,2,1:T(8,128)(2,1)}, bf16[1280,3,256]{0,2,1:T(8,128)(2,1)S(1)}, u32[]{:S(2)}) copy-start(bf16[1280,3,256]{0,2,1:T(8,128)(2,1)S(1)} %convolution_convert_fusion.6) | copy-start | bytes 5898244
  447.7 36.5 %copy-start.50 = (f32[1,1,1024]{2,1,0:T(1,128)S(1)}, f32[1,1,1024]{2,1,0:T(1,128)}, u32[]{:S(2)}) copy-start(f32[1,1,1024]{2,1,0:T(1,128)} %get-tuple-element.110) | copy-start | bytes 12292
  447.7 36.5 %copy-start.70 = (f32[1,1,1024]{2,1,0:T(1,128)S(1)}, f32[1,1,1024]{2,1,0:T(1,128)}, u32[]{:S(2)}) copy-start(f32[1,1,1024]{2,1,0:T(1,128)} %get-tuple-element.111) | copy-start | bytes 12292
  447.7 111.1 %all-gather.39.cloned.1.call-start = ((), (), s32[]{:S(2)}) async-start(), calls=%async_computation.35 | async-start | bytes 4718592 | tf_op jit(solution)/shard_map/all_gather | solution.py:111
  448.3 136.6 %all-gather.23.cloned.1.call-start = ((), (), s32[]{:S(2)}) async-start(), calls=%async_computation.18 | async-start | bytes 3276800 | tf_op jit(solution)/shard_map/all_gather | solution.py:139
  485.3 127.2 %all-gather.25.cloned.1.call-start = ((), (), s32[]{:S(2)}) async-start(), calls=%async_computation.20 | async-start | bytes 3276800 | tf_op jit(solution)/shard_map/all_gather | solution.py:185
  487.6 175.3 %reduce-scatter.21.cloned.1.call-start = ((), (), s32[]{:S(2)}) async-start(), calls=%async_computation.21 | async-start | bytes 3276800 | tf_op jit(solution)/shard_map/reduce_scatter | solution.py:193
  612.5 11.3 copy-start.74
  628.1 71.9 %reduce-scatter.19.cloned.1.call-start = ((), (), s32[]{:S(2)}) async-start(), calls=%async_computation.19 | async-start | bytes 3276800 | tf_op jit(solution)/shard_map/reduce_scatter | solution.py:142
  635.0 95.9 %all-gather.27.cloned.1.call-start = ((), (), s32[]{:S(2)}) async-start(), calls=%async_computation.22 | async-start | bytes 3276800 | tf_op jit(solution)/shard_map/all_gather | solution.py:204
  705.1 136.9 %reduce-scatter.23.cloned.1.call-start = ((), (), s32[]{:S(2)}) async-start(), calls=%async_computation.23 | async-start | bytes 3276800 | tf_op jit(solution)/shard_map/reduce_scatter | solution.py:224
  761.1 22.3 %copy-start.19 = (bf16[1280,3,256]{0,2,1:T(8,128)(2,1)S(1)}, bf16[1280,3,256]{0,2,1:T(8,128)(2,1)}, u32[]{:S(2)}) copy-start(bf16[1280,3,256]{0,2,1:T(8,128)(2,1)} %copy-done.18) | copy-start | bytes 5898244
  801.6 5.5 copy-start.27
  807.1 34.9 %copy-start.39 = (f32[1,1,1024]{2,1,0:T(1,128)S(1)}, f32[1,1,1024]{2,1,0:T(1,128)}, u32[]{:S(2)}) copy-start(f32[1,1,1024]{2,1,0:T(1,128)} %copy-done.38) | copy-start | bytes 12292
  807.1 34.9 %copy-start.47 = (f32[320]{0:T(512)S(1)}, f32[320]{0:T(512)}, u32[]{:S(2)}) copy-start(f32[320]{0:T(512)} %copy-done.46) | copy-start | bytes 3844
  807.1 36.4 %copy-start.67 = (f32[320]{0:T(512)S(1)}, f32[320]{0:T(512)}, u32[]{:S(2)}) copy-start(f32[320]{0:T(512)} %copy-done.66) | copy-start | bytes 3844
  807.1 36.5 %copy-start.61 = (f32[320]{0:T(512)S(1)}, f32[320]{0:T(512)}, u32[]{:S(2)}) copy-start(f32[320]{0:T(512)} %copy-done.60) | copy-start | bytes 3844
  807.2 38.2 %copy-start.10 = (f32[320,1024]{1,0:T(8,128)S(1)}, f32[320,1024]{1,0:T(8,128)}, u32[]{:S(2)}) copy-start(f32[320,1024]{1,0:T(8,128)} %param.14) | copy-start | bytes 3932164
  807.2 65.8 %all-gather.29.cloned.1.call-start = ((), (), s32[]{:S(2)}) async-start(), calls=%async_computation.24 | async-start | bytes 3276800 | tf_op jit(solution)/shard_map/all_gather | solution.py:185
  847.3 76.2 %reduce-scatter.25.cloned.1.call-start = ((), (), s32[]{:S(2)}) async-start(), calls=%async_computation.25 | async-start | bytes 3276800 | tf_op jit(solution)/shard_map/reduce_scatter | solution.py:193
  873.0 11.3 copy-start.73
  888.6 34.9 %copy-start.3 = (f32[320,1024]{1,0:T(8,128)S(1)}, f32[320,1024]{1,0:T(8,128)}, u32[]{:S(2)}) copy-start(f32[320,1024]{1,0:T(8,128)} %copy-done.2) | copy-start | bytes 3932164
  888.6 34.9 %copy-start.49 = (f32[1,1,1024]{2,1,0:T(1,128)S(1)}, f32[1,1,1024]{2,1,0:T(1,128)}, u32[]{:S(2)}) copy-start(f32[1,1,1024]{2,1,0:T(1,128)} %copy-done.48) | copy-start | bytes 12292
  888.6 34.9 %copy-start.52 = (f32[320]{0:T(512)S(1)}, f32[320]{0:T(512)}, u32[]{:S(2)}) copy-start(f32[320]{0:T(512)} %copy-done.51) | copy-start | bytes 3844
  888.6 34.9 %copy-start.57 = (f32[320]{0:T(512)S(1)}, f32[320]{0:T(512)}, u32[]{:S(2)}) copy-start(f32[320]{0:T(512)} %copy-done.56) | copy-start | bytes 3844
  888.7 36.5 %copy-start.65 = (f32[320]{0:T(512)S(1)}, f32[320]{0:T(512)}, u32[]{:S(2)}) copy-start(f32[320]{0:T(512)} %copy-done.64) | copy-start | bytes 3844
  888.7 39.1 %copy-start.11 = (f32[320,1024]{1,0:T(8,128)S(1)}, f32[320,1024]{1,0:T(8,128)}, u32[]{:S(2)}) copy-start(f32[320,1024]{1,0:T(8,128)} %get-tuple-element.67) | copy-start | bytes 3932164
  888.7 66.0 %all-gather.31.cloned.1.call-start = ((), (), s32[]{:S(2)}) async-start(), calls=%async_computation.26 | async-start | bytes 3276800 | tf_op jit(solution)/shard_map/all_gather | solution.py:204
  929.0 151.3 %reduce-scatter.27.cloned.1.call-start = ((), (), s32[]{:S(2)}) async-start(), calls=%async_computation.27 | async-start | bytes 3276800 | tf_op jit(solution)/shard_map/reduce_scatter | solution.py:224
  957.4 11.7 copy-start.17
  1025.2 5.4 copy-start.29
  1030.6 187.4 %reduce-scatter.35.cloned.1.call-start = ((), (), s32[]{:S(2)}) async-start(), calls=%async_computation.31 | async-start | bytes 9437184 | tf_op jit(solution)/shard_map/reduce_scatter | solution.py:239
  1030.9 5.8 copy-start.76
  1030.9 5.8 copy-start.81
  1043.8 326.3 %reduce-scatter.31.cloned.1.call-start = ((), (), s32[]{:S(2)}) async-start(), calls=%async_computation.29 | async-start | bytes 9437184 | tf_op jit(solution)/shard_map/reduce_scatter | solution.py:239
  1044.2 5.7 copy-start.77
  1044.3 5.7 copy-start.79
  1057.1 404.1 %reduce-scatter.33.cloned.1.call-start = ((), (), s32[]{:S(2)}) async-start(), calls=%async_computation.30 | async-start | bytes 4718592 | tf_op jit(solution)/shard_map/reduce_scatter | solution.py:238
  1066.5 487.0 %reduce-scatter.29.cloned.1.call-start = ((), (), s32[]{:S(2)}) async-start(), calls=%async_computation.28 | async-start | bytes 4718592 | tf_op jit(solution)/shard_map/reduce_scatter | solution.py:238
  1083.7 286.4 %copy-start.5 = (f32[2,2,128,1024]{3,2,1,0:T(8,128)S(1)}, f32[2,2,128,1024]{3,2,1,0:T(8,128)}, u32[]{:S(2)}) copy-start(f32[2,2,128,1024]{3,2,1,0:T(8,128)} %param.19) | copy-start | bytes 6291460
  1375.8 177.7 %copy-start.7 = (f32[2,4,128,256]{2,3,1,0:T(8,128)S(1)}, f32[2,4,128,256]{2,3,1,0:T(8,128)}, u32[]{:S(2)}) copy-start(f32[2,4,128,256]{2,3,1,0:T(8,128)} %copy-done.6) | copy-start | bytes 3145732
  1378.1 220.6 %copy-start.71 = (f32[6]{0:T(128)S(1)}, f32[6]{0:T(128)}, u32[]{:S(2)}) copy-start(f32[6]{0:T(128)} %constant.139) | copy-start | bytes 76
  (43 other events, 108.3 us)
Sparse Core Ops, SparseCore 0:
  10.6 53.7 all-gather.32
  66.6 23.7 all-gather.16
  132.0 34.6 reduce-scatter.12
  169.6 73.3 all-gather.34
  245.0 23.8 all-gather.18
  292.0 34.6 reduce-scatter.14
  329.3 51.0 all-gather.36
  382.6 23.7 all-gather.20
  447.8 34.6 reduce-scatter.16
  485.4 73.3 all-gather.38
  561.0 23.8 all-gather.22
  586.9 25.5 all-gather.24
  628.3 34.6 reduce-scatter.20
  665.4 34.6 reduce-scatter.18
  705.2 25.5 all-gather.26
  807.3 34.6 reduce-scatter.22
  847.4 25.5 all-gather.28
  888.8 34.6 reduce-scatter.24
  929.1 25.5 all-gather.30
  1030.7 34.6 reduce-scatter.26
  1069.1 148.8 reduce-scatter.34
  1222.1 147.9 reduce-scatter.30
  1373.7 87.4 reduce-scatter.32
  1465.2 88.2 reduce-scatter.28
where the time goes:
time: 1630 us; the launch traced here: 1620 us
  waiting for transfers between devices  1120 us (69%)
  matrix products  266 us (16%)
  other arithmetic  137 us (8%)
  blocking collectives  40.8 us (3%)
  local copies, waits for them, and re-layouts  31.1 us (2%)
    reduce_scatter x2, waiting for transfers between devices, shards(): lax.psum_scatter(dense_grad, 'dp', scatter_dimension=1, tiled=True)  283 us
    reduce_scatter x2, waiting for transfers between devices, shards(): lax.psum_scatter(mixer_grad, 'dp', scatter_dimension=1, tiled=True)  175 us
    all_gather x2, waiting for transfers between devices, shards(): lax.all_gather(dense_low[current], 'dp', axis=1, tiled=True)  135 us
    all_gather x2, waiting for transfers between devices, shards(): lax.all_gather(mixer_low[current], 'dp', axis=1, tiled=True)  102 us
    all_gather x4, waiting for transfers between devices, shards(): lax.all_gather(stream_grad.astype(jnp.bfloat16), 'mp', axis=0, tiled=True)  86.9 us
    reduce_scatter x2, waiting for transfers between devices, shards(): lax.psum_scatter(jnp.einsum('tf,df->td', active, dense_full[1], preferred...  68.9 us
    reduce_scatter x2, waiting for transfers between devices, shards(): lax.psum_scatter(jnp.einsum('th,dh->td', attended, mixer_full[3], preferr...  67.7 us
    reduce_scatter x2, waiting for transfers between devices, shards(): lax.psum_scatter(jnp.einsum('tf,df->td', grad_hidden, dense_full[0], pref...  62.7 us
  transfers between devices with their start and end apart: 24, of which 23 were waited for; matrix products, arithmetic and copies ran while one was open for 6% of the time, Pallas kernels for 0%

commit v1 on v0

v1 whole, which is shorter than its diff:
```python
import functools

import jax
import jax.numpy as jnp
from jax import lax
from jax.experimental import pallas as pl
from jax.experimental.pallas import tpu as pltpu
from jax.sharding import PartitionSpec as P

D = 1024
HEADS = 16
HD = 64
FF = 4096
STEP = 10


EPS_NORM = 1e-06
BETA_ONE = 0.9
BETA_TWO = 0.999
ADAM_EPS = 1e-06
WEIGHT_DECAY = 0.01
LEARN_RATE = 0.5
MASKED = -1000000000.0

QUERIES = 128
REACH = 64
WINDOW = QUERIES + 2 * REACH

NT = (((1,), (1,)), ((), ()))
TN = (((0,), (0,)), ((), ()))


def layer_norm(stream, gain, shift):
    centre = stream - jnp.mean(stream, axis=-1, keepdims=True)
    spread = jnp.mean(centre * centre, axis=-1, keepdims=True)
    return centre * lax.rsqrt(spread + EPS_NORM) * gain + shift


def adam_part(gradient, weight, first, second, decay):
    first_new = BETA_ONE * first + (1.0 - BETA_ONE) * gradient
    second_new = BETA_TWO * second + (1.0 - BETA_TWO) * gradient * gradient
    step_dir = (
        first_new
        / (1.0 - BETA_ONE**STEP)
        / (jnp.sqrt(second_new / (1.0 - BETA_TWO**STEP)) + ADAM_EPS)
        + decay * weight
    )
    return (first_new, second_new, step_dir)


def dot(left, right, dims=(((1,), (0,)), ((), ()))):
    return lax.dot_general(left, right, dims, preferred_element_type=jnp.float32)


def head_lanes(rows, width, value):
    lane_head = lax.broadcasted_iota(jnp.int32, (rows, width), 1) // HD
    return [
        jnp.where(lane_head == head, value, 0.0).astype(jnp.float32) for head in range(width // HD)
    ]


def block_shares(query_wide, keys_in, mask):
    heads_here = query_wide.shape[0] // QUERIES
    scores = dot(query_wide, keys_in, NT).reshape(heads_here, QUERIES, WINDOW)
    scores = jnp.where((mask > 0.5)[None], scores, MASKED)
    powered = jnp.exp(scores - jnp.max(scores, axis=-1, keepdims=True))
    shares = powered / jnp.sum(powered, axis=-1, keepdims=True)
    return shares.reshape(heads_here * QUERIES, WINDOW)


def fold_heads(wide, lanes):
    total = wide[:QUERIES] * lanes[0]
    for head in range(1, len(lanes)):
        total += wide[head * QUERIES : (head + 1) * QUERIES] * lanes[head]
    return total


def in_token_order(place_ref, refs, store, start):
    rows = refs[0].shape[0]
    for relative, ref in enumerate(refs):
        block = jnp.bitwise_xor(place_ref[0], relative)
        store[pl.ds(pl.multiple_of(start + block * rows, 16), rows), :] = ref[...]


def attend_kernel(pieces, place_ref, mask_ref, *refs):
    ins, outs, (all_in, all_out) = refs[:pieces], refs[pieces : 2 * pieces], refs[2 * pieces :]
    count, width = all_out.shape
    all_in[:REACH, :] = jnp.zeros((REACH, 3 * width), jnp.bfloat16)
    all_in[REACH + count :, :] = jnp.zeros((REACH, 3 * width), jnp.bfloat16)
    in_token_order(place_ref, ins, all_in, REACH)
    scaled = [lane.astype(jnp.bfloat16) for lane in head_lanes(QUERIES, width, HD ** (-0.5))]
    plain = head_lanes(QUERIES, width, 1.0)

    @pl.loop(0, count // QUERIES)
    def _(block):
        base = pl.multiple_of(block * QUERIES, QUERIES)
        query = all_in[pl.ds(base + REACH, QUERIES), :width]
        keys_in = all_in[pl.ds(base, WINDOW), width : 2 * width]
        values_in = all_in[pl.ds(base, WINDOW), 2 * width :]
        query_wide = jnp.concatenate([query * lane for lane in scaled], axis=0)
        shares = block_shares(query_wide, keys_in, mask_ref[pl.ds(base, QUERIES), :])
        wide = dot(shares.astype(jnp.bfloat16), values_in)
        all_out[pl.ds(base, QUERIES), :] = fold_heads(wide, plain).astype(jnp.bfloat16)

    rows = outs[0].shape[0]
    for relative, out in enumerate(outs):
        block = jnp.bitwise_xor(place_ref[0], relative)
        out[...] = all_out[pl.ds(pl.multiple_of(block * rows, 16), rows), :]


def attend_back_kernel(pieces, place_ref, mask_ref, *refs):
    ins, grads, outs = refs[:pieces], refs[pieces : 2 * pieces], refs[2 * pieces : 3 * pieces]
    all_in, all_grad, query_sum, key_sum, value_sum = refs[3 * pieces :]
    count, width = all_grad.shape
    all_in[:REACH, :] = jnp.zeros((REACH, 3 * width), jnp.bfloat16)
    all_in[REACH + count :, :] = jnp.zeros((REACH, 3 * width), jnp.bfloat16)
    in_token_order(place_ref, ins, all_in, REACH)
    in_token_order(place_ref, grads, all_grad, 0)
    key_sum[...] = jnp.zeros_like(key_sum)
    value_sum[...] = jnp.zeros_like(value_sum)
    scaled = [lane.astype(jnp.bfloat16) for lane in head_lanes(QUERIES, width, HD ** (-0.5))]
    plain_low = [lane.astype(jnp.bfloat16) for lane in head_lanes(QUERIES, width, 1.0)]
    scaled_wide = head_lanes(QUERIES, width, HD ** (-0.5))

    @pl.loop(0, count // QUERIES)
    def _(block):
        base = pl.multiple_of(block * QUERIES, QUERIES)
        query = all_in[pl.ds(base + REACH, QUERIES), :width]
        keys_in = all_in[pl.ds(base, WINDOW), width : 2 * width]
        values_in = all_in[pl.ds(base, WINDOW), 2 * width :]
        grad = all_grad[pl.ds(base, QUERIES), :]
        query_wide = jnp.concatenate([query * lane for lane in scaled], axis=0)
        grad_wide = jnp.concatenate([grad * lane for lane in plain_low], axis=0)
        shares = block_shares(query_wide, keys_in, mask_ref[pl.ds(base, QUERIES), :])
        grad_shares = dot(grad_wide, values_in, NT)
        inner = jnp.sum(grad_shares * shares, axis=-1, keepdims=True)
        grad_scores = (shares * (grad_shares - inner)).astype(jnp.bfloat16)
        query_sum[pl.ds(base, QUERIES), :] = fold_heads(dot(grad_scores, keys_in), scaled_wide)
        key_sum[pl.ds(base, WINDOW), :] += dot(grad_scores, query_wide, TN)
        value_sum[pl.ds(base, WINDOW), :] += dot(shares.astype(jnp.bfloat16), grad_wide, TN)

    rows = outs[0].shape[0]
    for relative, out in enumerate(outs):
        block = jnp.bitwise_xor(place_ref[0], relative)
        start = pl.multiple_of(block * rows, 16)
        out[:, :width] = query_sum[pl.ds(start, rows), :].astype(jnp.bfloat16)
        out[:, width : 2 * width] = key_sum[pl.ds(start + REACH, rows), :].astype(jnp.bfloat16)
        out[:, 2 * width :] = value_sum[pl.ds(start + REACH, rows), :].astype(jnp.bfloat16)


VMEM_SPEC = pl.BlockSpec(memory_space=pltpu.VMEM)
SMEM_SPEC = pl.BlockSpec(memory_space=pltpu.SMEM)


def attend(place, mask, projected):
    pieces = len(projected)
    rows, width = projected[0].shape[0], projected[0].shape[1] // 3
    count = rows * pieces
    return pl.pallas_call(
        functools.partial(attend_kernel, pieces),
        out_shape=[jax.ShapeDtypeStruct((rows, width), jnp.bfloat16)] * pieces,
        in_specs=[SMEM_SPEC] + [VMEM_SPEC] * (1 + pieces),
        out_specs=[VMEM_SPEC] * pieces,
        scratch_shapes=[
            pltpu.VMEM((count + 2 * REACH, 3 * width), jnp.bfloat16),
            pltpu.VMEM((count, width), jnp.bfloat16),
        ],
        compiler_params=pltpu.CompilerParams(vmem_limit_bytes=32 << 20),
        cost_estimate=pl.CostEstimate(
            flops=4 * count * WINDOW * width * width // HD,
            bytes_accessed=count * width * 8 + count * WINDOW * 4,
            transcendentals=count * WINDOW * width // HD,
        ),
        name="attend",
    )(place, mask, *projected)


def attend_back(place, mask, projected, grads):
    pieces = len(projected)
    rows, width = projected[0].shape[0], projected[0].shape[1] // 3
    count = rows * pieces
    return pl.pallas_call(
        functools.partial(attend_back_kernel, pieces),
        out_shape=[jax.ShapeDtypeStruct((rows, 3 * width), jnp.bfloat16)] * pieces,
        in_specs=[SMEM_SPEC] + [VMEM_SPEC] * (1 + 2 * pieces),
        out_specs=[VMEM_SPEC] * pieces,
        scratch_shapes=[
            pltpu.VMEM((count + 2 * REACH, 3 * width), jnp.bfloat16),
            pltpu.VMEM((count, width), jnp.bfloat16),
            pltpu.VMEM((count, width), jnp.float32),
            pltpu.VMEM((count + 2 * REACH, width), jnp.float32),
            pltpu.VMEM((count + 2 * REACH, width), jnp.float32),
        ],
        compiler_params=pltpu.CompilerParams(vmem_limit_bytes=40 << 20),
        cost_estimate=pl.CostEstimate(
            flops=10 * count * WINDOW * width * width // HD,
            bytes_accessed=count * width * 14 + count * WINDOW * 4,
            transcendentals=count * WINDOW * width // HD,
        ),
        name="attend_back",
    )(place, mask, *projected, *grads)


def crop_mask(segments):
    blocks = segments.shape[0] // QUERIES
    edge = jnp.full((REACH,), -1, segments.dtype)
    padded = jnp.concatenate([edge, segments, edge])
    keys_of = jnp.stack([padded[b * QUERIES : b * QUERIES + WINDOW] for b in range(blocks)])
    same = segments.reshape(blocks, QUERIES)[:, :, None] == keys_of[:, None, :]
    return same.astype(jnp.float32).reshape(blocks * QUERIES, WINDOW)


def move_columns(wide, order, back):
    rows, width = wide.shape
    blocks = order.shape[0]
    block = width // blocks
    if block % 128:
        if back:
            order = jnp.argsort(order)
        columns = (order[:, None] * block + jnp.arange(block)[None, :]).reshape(-1)
        return jnp.take(wide, columns, axis=1)

    def copy(order_ref, in_ref, out_ref):
        out_ref[...] = in_ref[...]

    there = lambda t, order_ref: (0, order_ref[t])
    here = lambda t, order_ref: (0, t)
    return pl.pallas_call(
        copy,
        out_shape=jax.ShapeDtypeStruct(wide.shape, wide.dtype),
        grid_spec=pltpu.PrefetchScalarGridSpec(
            num_scalar_prefetch=1,
            grid=(blocks,),
            in_specs=[pl.BlockSpec((rows, block), here if back else there)],
            out_specs=pl.BlockSpec((rows, block), there if back else here),
        ),
        cost_estimate=pl.CostEstimate(
            flops=0, bytes_accessed=2 * wide.size * wide.dtype.itemsize, transcendentals=0
        ),
        name="move_columns",
    )(order, wide)


def digits_of(size):
    sizes = []
    while size > 1:
        digit = 4 if size % 4 == 0 else (2 if size % 2 == 0 else size)
        sizes.append(digit)
        size //= digit
    return sizes


def strides_of(sizes):
    strides, stride = [], 1
    for size in reversed(sizes):
        strides.append(stride)
        stride *= size
    return strides[::-1]


def shift_pairs(total, size, stride, shift):
    pairs = []
    for source in range(total):
        digit = source // stride % size
        pairs.append((source, source + ((digit + shift) % size - digit) * stride))
    return pairs


class Rows:
    def __init__(self, total):
        self.total = total
        self.sizes = digits_of(total)
        self.strides = strides_of(self.sizes)

    def order(self):
        me = lax.axis_index("dp")
        places = jnp.zeros((1,), jnp.int32)
        for size, stride in zip(self.sizes, self.strides):
            digit = me // stride % size
            there = (digit + size - jnp.arange(size)) % size * stride
            places = (there[:, None] + places[None, :]).reshape(-1)
        return places.astype(jnp.int32)

    def gather(self, block):
        for size, stride in zip(self.sizes, self.strides):
            parts = [block] + [
                lax.ppermute(block, "dp", shift_pairs(self.total, size, stride, shift))
                for shift in range(1, size)
            ]
            block = jnp.concatenate(parts, axis=0)
        return block

    def reduce(self, parts):
        for level in reversed(range(len(self.sizes))):
            size, stride = self.sizes[level], self.strides[level]
            total = parts[0].astype(jnp.float32)
            for shift in range(1, size):
                total += lax.ppermute(
                    parts[shift], "dp", shift_pairs(self.total, size, stride, -shift)
                ).astype(jnp.float32)
            if level == 0:
                return total
            low = total.astype(jnp.bfloat16)
            inner = self.sizes[level - 1]
            step = low.shape[0] // inner
            parts = [low[s * step : (s + 1) * step] for s in range(inner)]


def core_swap(values_in):
    return lax.ppermute(values_in, "mp", [(0, 1), (1, 0), (2, 3), (3, 2)])


def chip_swap(values_in):
    return lax.ppermute(values_in, "mp", [(0, 2), (2, 0), (1, 3), (3, 1)])


def spread(mine):
    beyond = chip_swap(mine)
    return [mine, core_swap(mine), beyond, core_swap(beyond)]


def collect(parts):
    half = (parts[2].astype(jnp.float32) + core_swap(parts[3]).astype(jnp.float32)).astype(
        jnp.bfloat16
    )
    near = parts[0].astype(jnp.float32) + core_swap(parts[1]).astype(jnp.float32)
    return near + chip_swap(half).astype(jnp.float32)


def total_everywhere(value, rows_total):
    value = value + core_swap(value)
    value = value + chip_swap(value)
    stride = 1
    while stride < rows_total:
        value = value + lax.ppermute(
            value, "dp", [(source, source ^ stride) for source in range(rows_total)]
        )
        stride *= 2
    return value


def shards(
    rows_total,
    tokens,
    cotangent,
    segments,
    attention_weights,
    attention_first,
    attention_second,
    dense_weights,
    dense_first,
    dense_second,
    norm_params,
    norm_first,
    norm_second,
):
    layers = attention_weights.shape[0]
    width = attention_weights.shape[3]
    rows = Rows(rows_total)
    order = rows.order()
    place = lax.axis_index("mp").astype(jnp.int32).reshape(1)
    mask = crop_mask(segments)
    mixer_low = attention_weights.astype(jnp.bfloat16)
    dense_low = dense_weights.astype(jnp.bfloat16)
    copies = []
    for current in range(layers):
        inputs_own = jnp.concatenate([mixer_low[current, s] for s in range(3)], axis=1)
        copies.append(
            (
                rows.gather(inputs_own),
                rows.gather(mixer_low[current, 3]),
                rows.gather(dense_low[current, 0]),
                rows.gather(dense_low[current, 1]),
            )
        )
    stream = move_columns(tokens, order, False)
    stream_grad = move_columns(cotangent, order, False)
    params_here = move_columns(norm_params.reshape(layers * 4, D), order, False)
    params_here = params_here.reshape(layers, 4, D)
    saved_forward = []
    for current in range(layers):
        inputs_map, output_map, up_map, down_map = copies[current]
        params = params_here[current]
        normed = spread(layer_norm(stream, params[0], params[1]).astype(jnp.bfloat16))
        projected = [dot(piece, inputs_map).astype(jnp.bfloat16) for piece in normed]
        attended = attend(place, mask, projected)
        middle = stream + collect(
            [dot(piece, output_map, NT).astype(jnp.bfloat16) for piece in attended]
        )
        normed_two = spread(layer_norm(middle, params[2], params[3]).astype(jnp.bfloat16))
        active, slope, parts = [], [], []
        for piece in normed_two:
            hidden = dot(piece, up_map)
            below = 0.5 * (1.0 + lax.erf(hidden * (0.5**0.5)))
            density = jnp.exp(-0.5 * hidden * hidden) * 0.3989422804014327
            active.append((hidden * below).astype(jnp.bfloat16))
            slope.append((below + hidden * density).astype(jnp.bfloat16))
            parts.append(dot(active[-1], down_map, NT).astype(jnp.bfloat16))
        after_dense = middle + collect(parts)
        saved_forward.append((stream, normed, projected, attended, middle, normed_two, active, slope))
        stream = after_dense
    outcome = move_columns(stream, order, True)

    states = [None] * layers
    squares_list = [None] * layers
    vector_list = [None] * layers

    def weight_grad(left, right):
        left, right = jnp.concatenate(left, axis=0), jnp.concatenate(right, axis=0)
        groups = rows.sizes[-1]
        step = left.shape[1] // groups
        return rows.reduce(
            [
                dot(left[:, g * step : (g + 1) * step], right, TN).astype(jnp.bfloat16)
                for g in range(groups)
            ]
        )

    for current in reversed(range(layers)):
        stream_in, normed, projected, attended, middle, normed_two, active, slope = saved_forward[
            current
        ]
        inputs_map, output_map, up_map, down_map = copies[current]
        params = params_here[current]
        back_rows = spread(stream_grad.astype(jnp.bfloat16))
        grad_hidden = [
            (dot(piece, down_map) * bend.astype(jnp.float32)).astype(jnp.bfloat16)
            for piece, bend in zip(back_rows, slope)
        ]
        grad_normed_two = collect(
            [dot(piece, up_map, NT).astype(jnp.bfloat16) for piece in grad_hidden]
        )
        grad_down = weight_grad(back_rows, active)
        grad_up = weight_grad(normed_two, grad_hidden)
        _, norm_pull = jax.vjp(layer_norm, middle, params[2], params[3])
        grad_middle, grad_gain_two, grad_shift_two = norm_pull(grad_normed_two)
        stream_grad = stream_grad + grad_middle
        back_rows_two = spread(stream_grad.astype(jnp.bfloat16))
        grad_attended = [dot(piece, output_map).astype(jnp.bfloat16) for piece in back_rows_two]
        grad_projected = attend_back(place, mask, projected, grad_attended)
        grad_normed = collect(
            [dot(piece, inputs_map, NT).astype(jnp.bfloat16) for piece in grad_projected]
        )
        grad_output_map = weight_grad(back_rows_two, attended)
        grad_inputs_map = weight_grad(normed, grad_projected)
        _, norm_pull_one = jax.vjp(layer_norm, stream_in, params[0], params[1])
        grad_inner, grad_gain_one, grad_shift_one = norm_pull_one(grad_normed)
        stream_grad = stream_grad + grad_inner
        mixer_grad = jnp.stack(
            [grad_inputs_map[:, s * width : (s + 1) * width] for s in range(3)] + [grad_output_map]
        )
        dense_grad = jnp.stack([grad_up, grad_down], axis=0)
        mixer_first, mixer_second, mixer_step = adam_part(
            mixer_grad,
            attention_weights[current],
            attention_first[current],
            attention_second[current],
            WEIGHT_DECAY,
        )
        dense_first_new, dense_second_new, dense_step = adam_part(
            dense_grad,
            dense_weights[current],
            dense_first[current],
            dense_second[current],
            WEIGHT_DECAY,
        )
        weight_squares = jnp.concatenate(
            [
                jnp.sum(attention_weights[current] * attention_weights[current], axis=(1, 2)),
                jnp.sum(dense_weights[current] * dense_weights[current], axis=(1, 2)),
            ]
        )
        step_squares = jnp.concatenate(
            [
                jnp.sum(mixer_step * mixer_step, axis=(1, 2)),
                jnp.sum(dense_step * dense_step, axis=(1, 2)),
            ]
        )
        squares_list[current] = jnp.stack([weight_squares, step_squares], axis=-1)
        vector_list[current] = jnp.stack(
            [grad_gain_one, grad_shift_one, grad_gain_two, grad_shift_two], axis=0
        )
        states[current] = (
            mixer_first,
            mixer_second,
            mixer_step,
            dense_first_new,
            dense_second_new,
            dense_step,
        )
    grad_tokens = move_columns(stream_grad, order, True)
    vectors = move_columns(jnp.concatenate(vector_list, axis=0), order, True)
    total_vectors = total_everywhere(vectors, rows_total).reshape(layers, 4, D)
    total_squares = total_everywhere(jnp.stack(squares_list), rows_total)
    sizes_all = jnp.sqrt(total_squares[:, :, 0])
    moves_all = jnp.sqrt(total_squares[:, :, 1])
    trust_all = sizes_all / moves_all
    mixer_new = jnp.stack(
        [
            attention_weights[current]
            - LEARN_RATE * trust_all[current, :4, None, None] * states[current][2]
            for current in range(layers)
        ]
    )
    dense_new = jnp.stack(
        [
            dense_weights[current]
            - LEARN_RATE * trust_all[current, 4:, None, None] * states[current][5]
            for current in range(layers)
        ]
    )
    mixer_first_all = jnp.stack([states[current][0] for current in range(layers)])
    mixer_second_all = jnp.stack([states[current][1] for current in range(layers)])
    dense_first_all = jnp.stack([states[current][3] for current in range(layers)])
    dense_second_all = jnp.stack([states[current][4] for current in range(layers)])
    params_first, params_second, params_step = adam_part(
        total_vectors, norm_params, norm_first, norm_second, 0.0
    )
    params_size = jnp.sqrt(jnp.sum(norm_params * norm_params, axis=-1))
    params_move = jnp.sqrt(jnp.sum(params_step * params_step, axis=-1))
    params_new = norm_params - LEARN_RATE * (params_size / params_move)[:, :, None] * params_step
    mixer_entries = float(D * HEADS * HD) ** 0.5
    dense_entries = float(D * FF) ** 0.5
    entry_roots = jnp.array([mixer_entries] * 4 + [dense_entries] * 2, jnp.float32)
    norms = jnp.stack([sizes_all / entry_roots[None, :], moves_all / entry_roots[None, :]], axis=-1)
    second_norm_grad = total_vectors[:, 2:4]
    return (
        outcome,
        grad_tokens,
        mixer_new,
        mixer_first_all,
        mixer_second_all,
        mixer_new.astype(jnp.bfloat16),
        dense_new,
        dense_first_all,
        dense_second_all,
        dense_new.astype(jnp.bfloat16),
        params_new,
        params_first,
        params_second,
        norms,
        second_norm_grad,
    )


def solution(mesh):
    rows_spec = P(("dp", "mp"), None)
    weight_spec = P(None, None, "dp", "mp")
    in_specs = (rows_spec, rows_spec, P("dp")) + (weight_spec,) * 6 + (P(),) * 3
    out_specs = (rows_spec,) * 2 + (weight_spec,) * 8 + (P(),) * 5
    return jax.shard_map(
        functools.partial(shards, mesh.shape["dp"]),
        mesh=mesh,
        in_specs=in_specs,
        out_specs=out_specs,
        check_vma=False,
    )
```

time: 1630 us -> 769 us (0.47)
  waiting for transfers between devices: 1120 us -> 384 us
  matrix products: 266 us -> 83.9 us
  starting transfers between devices: 11.9 us -> 143 us
  other arithmetic: 137 us -> 51.3 us
  Pallas kernels: 0 us -> 67.4 us
  blocking collectives: 40.8 us -> 0 us
    reduce_scatter x12 -> x0, waiting for transfers between devices: 692 us -> none  [the longest x2 283 us: shards(): lax.psum_scatter(dense_grad, 'dp', scatter_dimension=1, tiled=True)]
    all_gather x12 -> x0, waiting for transfers between devices: 428 us -> none  [the longest x2 135 us: shards(): lax.all_gather(dense_low[current], 'dp', axis=1, tiled=True)]
    ppermute x0 -> x122, waiting for transfers between devices: none -> 384 us  [the longest x32 182 us: reduce(): lax.ppermute(parts[shift], 'dp', shift_pairs(self.total, size, stride, -s...]
    dot_general x36 -> x80, matrix products: 266 us -> 83.9 us  [dot(): lax.dot_general(left, right, dims, preferred_element_type=jnp.float32)]
    ppermute x0 -> x122, starting transfers between devices: none -> 143 us  [the longest x32 69.5 us: gather(): lax.ppermute(block, 'dp', shift_pairs(self.total, size, stride, shift))]
    pallas_call x0 -> x10, Pallas kernels: none -> 67.4 us  [the longest x6 33.7 us: move_columns(): pl.pallas_call(copy, out_shape=jax.ShapeDtypeStruct(wide.shape, wide.dtyp...]
    convert_element_type x10 -> x15, other arithmetic: 55.1 us -> 6.43 us  [the longest x6 2.04 us: reduce(): low = total.astype(jnp.bfloat16)]
    psum x1 -> x0, blocking collectives: 40.8 us -> none  [shards(): summed_list[current] = lax.psum((squares, vector_grad), ('dp', 'mp'))]
  transfers between devices with their start and end apart: 24 -> 122, of which waited for: 23 -> 50; matrix products, arithmetic and copies ran while one was open for 6% -> 17% of each run, Pallas kernels for 0% -> 5%
where the time goes in v1:
time: 769 us; the launch traced here: 760 us
  waiting for transfers between devices  384 us (50%)
  starting transfers between devices  143 us (19%)
  matrix products  83.9 us (11%)
  Pallas kernels  67.4 us (9%)
  other arithmetic  51.3 us (7%)
  local copies, waits for them, and re-layouts  27.6 us (4%)
    ppermute x32, waiting for transfers between devices, reduce(): lax.ppermute(parts[shift], 'dp', shift_pairs(self.total, size, stride, -s...  182 us
    ppermute x32, waiting for transfers between devices, gather(): lax.ppermute(block, 'dp', shift_pairs(self.total, size, stride, shift))  116 us
    dot_general x80, matrix products, dot(): lax.dot_general(left, right, dims, preferred_element_type=jnp.float32)  83.9 us
    ppermute x18, waiting for transfers between devices, chip_swap(): return lax.ppermute(values_in, 'mp', [(0, 2), (2, 0), (1, 3), (3, 1)])  70.4 us
    ppermute x32, starting transfers between devices, gather(): lax.ppermute(block, 'dp', shift_pairs(self.total, size, stride, shift))  69.5 us
    ppermute x32, starting transfers between devices, reduce(): lax.ppermute(parts[shift], 'dp', shift_pairs(self.total, size, stride, -s...  43 us
    pallas_call x6, Pallas kernels, move_columns(): pl.pallas_call(copy, out_shape=jax.ShapeDtypeStruct(wide.shape, wide.dtyp...  33.7 us
    unnamed x240, local copies, waits for them, and re-layouts  20 us
  transfers between devices with their start and end apart: 122, of which 50 were waited for; matrix products, arithmetic and copies ran while one was open for 17% of the time, Pallas kernels for 5%

profile of v1, /device:TPU:0, one launch (start us, length us, event | category | flops | bytes accessed | tf_op | source)
XLA Modules:
  0.0 760.2 jit_solution(8241871488833849917)
XLA Ops:
  2.8 5.0 collective-permute-start.37
  8.8 2.8 collective-permute-start.9
  18.9 4.6 move_columns.7
  25.5 6.0 move_columns.6
  36.3 6.0 move_columns.9
  49.2 5.1 collective-permute-done.8
  56.9 3.8 collective-permute-start.1
  62.4 3.8 collective-permute-start.2
  68.0 9.5 %collective-permute-done.1 = bf16[128,768]{1,0:T(8,128)(2,1)S(1)} collective-permute-done((bf16[128,768]{1,0:T(8,128)(2,1)S(1)}, bf16[128,768]{1,0:T(8,128)(2,1)S(1)}, u32[]{:S(2)}, u32[]{:S(2)}) %collective-permute-start.1) | collective-permute-done | bytes 196640 | tf_op jit(solution)/shard_map/ppermute | solution.py:287
  83.1 8.6 %collective-permute-start.46 = (bf16[128,1024]{1,0:T(8,128)(2,1)S(1)}, bf16[128,1024]{1,0:T(8,128)(2,1)S(1)}, u32[]{:S(2)}, u32[]{:S(2)}) collective-permute-start(bf16[128,1024]{1,0:T(8,128)(2,1)S(1)} %copy-done.46), channel_id=1, source_target_pairs={{0,8},{4,12},{8,16},{12,20},{16,24},{20,28},{24,0},{28,4},{1,9},{5... | collective-permute-start | bytes 786440 | tf_op jit(solution)/shard_map/ppermute | solution.py:287
  92.4 10.2 %collective-permute-done.46 = bf16[128,1024]{1,0:T(8,128)(2,1)S(1)} collective-permute-done((bf16[128,1024]{1,0:T(8,128)(2,1)S(1)}, bf16[128,1024]{1,0:T(8,128)(2,1)S(1)}, u32[]{:S(2)}, u32[]{:S(2)}) %collective-permute-start.46) | collective-permute-done | bytes 262176 | tf_op jit(solution)/shard_map/ppermute | solution.py:287
  102.6 3.0 collective-permute-start.47
  112.5 7.1 attend.2
  120.1 3.0 collective-permute-start.16
  123.1 4.9 collective-permute-done.18
  128.0 13.0 %collective-permute-start.15 = (bf16[128,1024]{1,0:T(8,128)(2,1)S(1)}, bf16[128,1024]{1,0:T(8,128)(2,1)S(1)}, u32[]{:S(2)}, u32[]{:S(2)}) collective-permute-start(bf16[128,1024]{1,0:T(8,128)(2,1)S(1)} %copy-done.45), channel_id=1, source_target_pairs={{0,16},{4,20},{8,24},{12,28},{16,0},{20,4},{24,8},{28,12},{1,17},{... | collective-permute-start | bytes 786440 | tf_op jit(solution)/shard_map/ppermute | solution.py:287
  143.2 10.2 %collective-permute-done.14 = bf16[128,1024]{1,0:T(8,128)(2,1)S(1)} collective-permute-done((bf16[128,1024]{1,0:T(8,128)(2,1)S(1)}, bf16[128,1024]{1,0:T(8,128)(2,1)S(1)}, u32[]{:S(2)}, u32[]{:S(2)}) %collective-permute-start.14) | collective-permute-done | bytes 262176 | tf_op jit(solution)/shard_map/ppermute | solution.py:287
  153.4 5.3 collective-permute-done.15
  158.8 5.3 collective-permute-start.43
  171.1 15.7 %collective-permute-done.43 = bf16[128,1024]{1,0:T(8,128)(2,1)S(1)} collective-permute-done((bf16[128,1024]{1,0:T(8,128)(2,1)S(1)}, bf16[128,1024]{1,0:T(8,128)(2,1)S(1)}, u32[]{:S(2)}, u32[]{:S(2)}) %collective-permute-start.43) | collective-permute-done | bytes 262176 | tf_op jit(solution)/shard_map/ppermute | solution.py:287
  190.0 3.0 collective-permute-done.31
  194.1 11.3 %collective-permute-done.24 = bf16[320,1024]{1,0:T(8,128)(2,1)S(1)} collective-permute-done((bf16[320,1024]{1,0:T(8,128)(2,1)S(1)}, bf16[320,1024]{1,0:T(8,128)(2,1)S(1)}, u32[]{:S(2)}, u32[]{:S(2)}) %collective-permute-start.24) | collective-permute-done | bytes 655392 | tf_op jit(solution)/shard_map/ppermute | solution.py:314
  205.5 9.9 %collective-permute-done.49 = bf16[512,1024]{1,0:T(8,128)(2,1)S(1)} collective-permute-done((bf16[512,1024]{1,0:T(8,128)(2,1)S(1)}, bf16[512,1024]{1,0:T(8,128)(2,1)S(1)}, u32[]{:S(2)}, u32[]{:S(2)}) %collective-permute-start.49) | collective-permute-done | bytes 1048608 | tf_op jit(solution)/shard_map/ppermute | solution.py:287
  218.1 19.7 %collective-permute-done.21 = bf16[512,1024]{1,0:T(8,128)(2,1)S(1)} collective-permute-done((bf16[512,1024]{1,0:T(8,128)(2,1)S(1)}, bf16[512,1024]{1,0:T(8,128)(2,1)S(1)}, u32[]{:S(2)}, u32[]{:S(2)}) %collective-permute-start.21) | collective-permute-done | bytes 1048608 | tf_op jit(solution)/shard_map/ppermute | solution.py:287
  238.0 22.4 %collective-permute-done.17 = bf16[512,1024]{1,0:T(8,128)(2,1)S(1)} collective-permute-done((bf16[512,1024]{1,0:T(8,128)(2,1)S(1)}, bf16[512,1024]{1,0:T(8,128)(2,1)S(1)}, u32[]{:S(2)}, u32[]{:S(2)}) %collective-permute-start.17) | collective-permute-done | bytes 1048608 | tf_op jit(solution)/shard_map/ppermute | solution.py:287
  275.3 12.5 %collective-permute-done.27 = bf16[320,1024]{1,0:T(8,128)(2,1)S(1)} collective-permute-done((bf16[320,1024]{1,0:T(8,128)(2,1)S(1)}, bf16[320,1024]{1,0:T(8,128)(2,1)S(1)}, u32[]{:S(2)}, u32[]{:S(2)}) %collective-permute-start.27) | collective-permute-done | bytes 655392 | tf_op jit(solution)/shard_map/ppermute | solution.py:314
  291.2 14.8 %collective-permute-done.33 = bf16[320,1024]{1,0:T(8,128)(2,1)S(1)} collective-permute-done((bf16[320,1024]{1,0:T(8,128)(2,1)S(1)}, bf16[320,1024]{1,0:T(8,128)(2,1)S(1)}, u32[]{:S(2)}, u32[]{:S(2)}) %collective-permute-start.33) | collective-permute-done | bytes 655392 | tf_op jit(solution)/shard_map/ppermute | solution.py:314
  308.8 7.0 attend.3
  325.0 12.2 %collective-permute-done.41 = bf16[320,1024]{1,0:T(8,128)(2,1)S(1)} collective-permute-done((bf16[320,1024]{1,0:T(8,128)(2,1)S(1)}, bf16[320,1024]{1,0:T(8,128)(2,1)S(1)}, u32[]{:S(2)}, u32[]{:S(2)}) %collective-permute-start.41) | collective-permute-done | bytes 655392 | tf_op jit(solution)/shard_map/ppermute | solution.py:314
  345.0 9.8 %collective-permute-done.52 = bf16[320,1024]{1,0:T(8,128)(2,1)S(1)} collective-permute-done((bf16[320,1024]{1,0:T(8,128)(2,1)S(1)}, bf16[320,1024]{1,0:T(8,128)(2,1)S(1)}, u32[]{:S(2)}, u32[]{:S(2)}) %collective-permute-start.52) | collective-permute-done | bytes 655392 | tf_op jit(solution)/shard_map/ppermute | solution.py:314
  374.9 19.3 %collective-permute-done.108 = bf16[512,1024]{1,0:T(8,128)(2,1)S(1)} collective-permute-done((bf16[512,1024]{1,0:T(8,128)(2,1)S(1)}, bf16[512,1024]{1,0:T(8,128)(2,1)S(1)}, u32[]{:S(2)}, u32[]{:S(2)}) %collective-permute-start.108) | collective-permute-done | bytes 1048608 | tf_op jit(solution)/shard_map/ppermute | solution.py:298
  396.7 19.5 %collective-permute-done.104 = bf16[512,1024]{1,0:T(8,128)(2,1)S(1)} collective-permute-done((bf16[512,1024]{1,0:T(8,128)(2,1)S(1)}, bf16[512,1024]{1,0:T(8,128)(2,1)S(1)}, u32[]{:S(2)}, u32[]{:S(2)}) %collective-permute-start.104) | collective-permute-done | bytes 1048608 | tf_op jit(solution)/shard_map/ppermute | solution.py:298
  417.9 12.2 %collective-permute-done.110 = bf16[128,1024]{1,0:T(8,128)(2,1)S(1)} collective-permute-done((bf16[128,1024]{1,0:T(8,128)(2,1)S(1)}, bf16[128,1024]{1,0:T(8,128)(2,1)S(1)}, u32[]{:S(2)}, u32[]{:S(2)}) %collective-permute-start.110) | collective-permute-done | bytes 262176 | tf_op jit(solution)/shard_map/ppermute | solution.py:298
  437.3 8.2 %collective-permute-done.105 = bf16[128,1024]{1,0:T(8,128)(2,1)S(1)} collective-permute-done((bf16[128,1024]{1,0:T(8,128)(2,1)S(1)}, bf16[128,1024]{1,0:T(8,128)(2,1)S(1)}, u32[]{:S(2)}, u32[]{:S(2)}) %collective-permute-start.105) | collective-permute-done | bytes 262176 | tf_op jit(solution)/shard_map/ppermute | solution.py:298
  446.5 7.0 collective-permute-done.106
  456.9 6.4 move_columns.8
  468.7 9.8 %attend_back.2 = (bf16[320,768]{1,0:T(8,128)(2,1)S(1)}, bf16[320,768]{1,0:T(8,128)(2,1)S(1)}, bf16[320,768]{1,0:T(8,128)(2,1)S(1)}, bf16[320,768]{1,0:T(8,128)(2,1)S(1)}) custom-call(s32[1]{0:T(128)} %bitcast.place_ref, f32[1280,256]{1,0:T(8,128)S(1)} %fusion.120.mask_ref, bf16[320,768]{1,0:T(8,128)(2,1)S(1)} %convolution_convert_fusion.47.refs_0_, ...), custom_call_target="tpu_custom_call" | custom-call | flops 3355443200 | bytes 5898240 | tf_op jit(solution)/shard_map/attend_back/pallas_call | solution.py:182
  490.3 5.8 collective-permute-done.100
  497.8 5.2 collective-permute-start.101
  505.9 3.2 collective-permute-done.103
  509.1 3.0 collective-permute-done.96
  512.4 5.2 collective-permute-start.97
  523.3 4.1 collective-permute-done.99
  527.5 5.4 collective-permute-done.98
  534.2 2.8 collective-permute-done.70
  556.6 18.3 %collective-permute-done.88 = bf16[512,1024]{1,0:T(8,128)(2,1)S(1)} collective-permute-done((bf16[512,1024]{1,0:T(8,128)(2,1)S(1)}, bf16[512,1024]{1,0:T(8,128)(2,1)S(1)}, u32[]{:S(2)}, u32[]{:S(2)}) %collective-permute-start.88) | collective-permute-done | bytes 1048608 | tf_op jit(solution)/shard_map/ppermute | solution.py:298
  575.3 3.2 collective-permute-start.89
  579.1 17.6 %collective-permute-done.92 = bf16[512,1024]{1,0:T(8,128)(2,1)S(1)} collective-permute-done((bf16[512,1024]{1,0:T(8,128)(2,1)S(1)}, bf16[512,1024]{1,0:T(8,128)(2,1)S(1)}, u32[]{:S(2)}, u32[]{:S(2)}) %collective-permute-start.92) | collective-permute-done | bytes 1048608 | tf_op jit(solution)/shard_map/ppermute | solution.py:298
  599.6 3.5 collective-permute-start.93
  607.8 4.7 collective-permute-done.90
  612.7 8.4 %collective-permute-done.95 = bf16[128,1024]{1,0:T(8,128)(2,1)S(1)} collective-permute-done((bf16[128,1024]{1,0:T(8,128)(2,1)S(1)}, bf16[128,1024]{1,0:T(8,128)(2,1)S(1)}, u32[]{:S(2)}, u32[]{:S(2)}) %collective-permute-start.95) | collective-permute-done | bytes 262176 | tf_op jit(solution)/shard_map/ppermute | solution.py:298
  621.1 12.3 %collective-permute-done.94 = bf16[128,1024]{1,0:T(8,128)(2,1)S(1)} collective-permute-done((bf16[128,1024]{1,0:T(8,128)(2,1)S(1)}, bf16[128,1024]{1,0:T(8,128)(2,1)S(1)}, u32[]{:S(2)}, u32[]{:S(2)}) %collective-permute-start.94) | collective-permute-done | bytes 262176 | tf_op jit(solution)/shard_map/ppermute | solution.py:298
  637.9 9.8 %attend_back.3 = (bf16[320,768]{1,0:T(8,128)(2,1)S(1)}, bf16[320,768]{1,0:T(8,128)(2,1)S(1)}, bf16[320,768]{1,0:T(8,128)(2,1)S(1)}, bf16[320,768]{1,0:T(8,128)(2,1)S(1)}) custom-call(s32[1]{0:T(128)} %bitcast.place_ref, f32[1280,256]{1,0:T(8,128)S(1)} %fusion.120.mask_ref, bf16[320,768]{1,0:T(8,128)(2,1)S(1)} %copy-done.1, bf16[320,768]{1,0:T(8,128)(2,1)S(1)} %copy-done.5, ...), custom_call_target="tpu_custom_call" | custom-call | flops 3355443200 | bytes 5898240 | tf_op jit(solution)/shard_map/attend_back/pallas_call | solution.py:182
  656.4 6.4 collective-permute-done.84
  663.4 3.3 collective-permute-start.85
  667.6 11.3 %collective-permute-done.80 = bf16[512,768]{1,0:T(8,128)(2,1)S(1)} collective-permute-done((bf16[512,768]{1,0:T(8,128)(2,1)S(1)}, bf16[512,768]{1,0:T(8,128)(2,1)S(1)}, u32[]{:S(2)}, u32[]{:S(2)}) %collective-permute-start.80) | collective-permute-done | bytes 786464 | tf_op jit(solution)/shard_map/ppermute | solution.py:298
  679.2 3.3 collective-permute-start.81
  683.2 7.2 collective-permute-done.81
  692.1 5.8 collective-permute-done.82
  708.4 2.9 collective-permute-done.115
  730.2 4.6 move_columns.11
  738.0 2.9 collective-permute-done.118
  745.1 3.7 collective-permute-done.120
  751.6 6.1 move_columns.10
  (648 shorter events, 248.7 us)
Async XLA Ops:
  2.8 59.6 %collective-permute-start.37 = (bf16[128,256]{1,0:T(8,128)(2,1)}, bf16[128,256]{1,0:T(8,128)(2,1)}, u32[]{:S(2)}, u32[]{:S(2)}) collective-permute-start(bf16[128,256]{1,0:T(8,128)(2,1)} %get-tuple-element.137), channel_id=1, source_target_pairs={{0,24},{4,28},{8,0},{12,4},{16,8},{20,12},{24,16},{28,20},{1,25},{... | collective-permute-start | bytes 196616 | tf_op jit(solution)/shard_map/ppermute | solution.py:287
  7.8 53.7 %collective-permute-start.36 = (bf16[128,256]{1,0:T(8,128)(2,1)}, bf16[128,256]{1,0:T(8,128)(2,1)}, u32[]{:S(2)}, u32[]{:S(2)}) collective-permute-start(bf16[128,256]{1,0:T(8,128)(2,1)} %get-tuple-element.137), channel_id=1, source_target_pairs={{0,16},{4,20},{8,24},{12,28},{16,0},{20,4},{24,8},{28,12},{1,17},{... | collective-permute-start | bytes 196616 | tf_op jit(solution)/shard_map/ppermute | solution.py:287
  7.8 49.1 %collective-permute-start.35 = (bf16[128,256]{1,0:T(8,128)(2,1)}, bf16[128,256]{1,0:T(8,128)(2,1)}, u32[]{:S(2)}, u32[]{:S(2)}) collective-permute-start(bf16[128,256]{1,0:T(8,128)(2,1)} %get-tuple-element.137), channel_id=1, source_target_pairs={{0,8},{4,12},{8,16},{12,20},{16,24},{20,28},{24,0},{28,4},{1,9},{5... | collective-permute-start | bytes 196616 | tf_op jit(solution)/shard_map/ppermute | solution.py:287
  8.8 38.6 %collective-permute-start.9 = (bf16[128,256]{1,0:T(8,128)(2,1)}, bf16[128,256]{1,0:T(8,128)(2,1)}, u32[]{:S(2)}, u32[]{:S(2)}) collective-permute-start(bf16[128,256]{1,0:T(8,128)(2,1)} %get-tuple-element.141), channel_id=1, source_target_pairs={{0,24},{4,28},{8,0},{12,4},{16,8},{20,12},{24,16},{28,20},{1,25},{... | collective-permute-start | bytes 196616 | tf_op jit(solution)/shard_map/ppermute | solution.py:287
  11.6 33.8 %collective-permute-start.7 = (bf16[128,256]{1,0:T(8,128)(2,1)}, bf16[128,256]{1,0:T(8,128)(2,1)}, u32[]{:S(2)}, u32[]{:S(2)}) collective-permute-start(bf16[128,256]{1,0:T(8,128)(2,1)} %get-tuple-element.141), channel_id=1, source_target_pairs={{0,8},{4,12},{8,16},{12,20},{16,24},{20,28},{24,0},{28,4},{1,9},{5... | collective-permute-start | bytes 196616 | tf_op jit(solution)/shard_map/ppermute | solution.py:287
  47.4 35.7 %collective-permute-start.29 = (bf16[128,768]{1,0:T(8,128)(2,1)S(1)}, bf16[128,768]{1,0:T(8,128)(2,1)S(1)}, u32[]{:S(2)}, u32[]{:S(2)}) collective-permute-start(bf16[128,768]{1,0:T(8,128)(2,1)S(1)} %get-tuple-element.169), channel_id=1, source_target_pairs={{0,16},{4,20},{8,24},{12,28},{16,0},{20,4},{24,8},{28,12},{1,17},{... | collective-permute-start | bytes 589832 | tf_op jit(solution)/shard_map/ppermute | solution.py:287
  54.3 27.2 %collective-permute-start.28 = (bf16[128,768]{1,0:T(8,128)(2,1)S(1)}, bf16[128,768]{1,0:T(8,128)(2,1)S(1)}, u32[]{:S(2)}, u32[]{:S(2)}) collective-permute-start(bf16[128,768]{1,0:T(8,128)(2,1)S(1)} %get-tuple-element.169), channel_id=1, source_target_pairs={{0,8},{4,12},{8,16},{12,20},{16,24},{20,28},{24,0},{28,4},{1,9},{5... | collective-permute-start | bytes 589832 | tf_op jit(solution)/shard_map/ppermute | solution.py:287
  56.9 20.5 %collective-permute-start.1 = (bf16[128,768]{1,0:T(8,128)(2,1)S(1)}, bf16[128,768]{1,0:T(8,128)(2,1)S(1)}, u32[]{:S(2)}, u32[]{:S(2)}) collective-permute-start(bf16[128,768]{1,0:T(8,128)(2,1)S(1)} %get-tuple-element.171), channel_id=1, source_target_pairs={{0,16},{4,20},{8,24},{12,28},{16,0},{20,4},{24,8},{28,12},{1,17},{... | collective-permute-start | bytes 589832 | tf_op jit(solution)/shard_map/ppermute | solution.py:287
  61.5 18.2 %collective-permute-start = (bf16[128,768]{1,0:T(8,128)(2,1)S(1)}, bf16[128,768]{1,0:T(8,128)(2,1)S(1)}, u32[]{:S(2)}, u32[]{:S(2)}) collective-permute-start(bf16[128,768]{1,0:T(8,128)(2,1)S(1)} %get-tuple-element.171), channel_id=1, source_target_pairs={{0,8},{4,12},{8,16},{12,20},{16,24},{20,28},{24,0},{28,4},{1,9},{5... | collective-permute-start | bytes 589832 | tf_op jit(solution)/shard_map/ppermute | solution.py:287
  62.4 17.4 %collective-permute-start.2 = (bf16[128,768]{1,0:T(8,128)(2,1)S(1)}, bf16[128,768]{1,0:T(8,128)(2,1)S(1)}, u32[]{:S(2)}, u32[]{:S(2)}) collective-permute-start(bf16[128,768]{1,0:T(8,128)(2,1)S(1)} %get-tuple-element.171), channel_id=1, source_target_pairs={{0,24},{4,28},{8,0},{12,4},{16,8},{20,12},{24,16},{28,20},{1,25},{... | collective-permute-start | bytes 589832 | tf_op jit(solution)/shard_map/ppermute | solution.py:287
  79.7 40.4 %collective-permute-start.48 = (bf16[128,1024]{1,0:T(8,128)(2,1)S(1)}, bf16[128,1024]{1,0:T(8,128)(2,1)S(1)}, u32[]{:S(2)}, u32[]{:S(2)}) collective-permute-start(bf16[128,1024]{1,0:T(8,128)(2,1)S(1)} %copy-done.46), channel_id=1, source_target_pairs={{0,24},{4,28},{8,0},{12,4},{16,8},{20,12},{24,16},{28,20},{1,25},{... | collective-permute-start | bytes 786440 | tf_op jit(solution)/shard_map/ppermute | solution.py:287
  79.8 28.5 %collective-permute-start.3 = (bf16[512,768]{1,0:T(8,128)(2,1)S(1)}, bf16[512,768]{1,0:T(8,128)(2,1)S(1)}, u32[]{:S(2)}, u32[]{:S(2)}) collective-permute-start(bf16[512,768]{1,0:T(8,128)(2,1)S(1)} %pad_maximum_fusion.26), channel_id=1, source_target_pairs={{0,4},{4,0},{8,12},{12,8},{16,20},{20,16},{24,28},{28,24},{1,5},{5... | collective-permute-start | bytes 2359304 | tf_op jit(solution)/shard_map/ppermute | solution.py:287
  81.5 24.3 %collective-permute-start.5 = (bf16[320,1024]{1,0:T(8,128)(2,1)S(1)}, bf16[320,1024]{1,0:T(8,128)(2,1)S(1)}, u32[]{:S(2)}, u32[]{:S(2)}) collective-permute-start(bf16[320,1024]{1,0:T(8,128)(2,1)S(1)} %add_convert_fusion.9), channel_id=1, source_target_pairs={{0,2},{2,0},{1,3},{3,1},{4,6},{6,4},{5,7},{7,5},{8,10},{10,8},{9,1... | collective-permute-start | bytes 1966088 | tf_op jit(solution)/shard_map/ppermute | solution.py:314
  83.1 19.5 %collective-permute-start.46 = (bf16[128,1024]{1,0:T(8,128)(2,1)S(1)}, bf16[128,1024]{1,0:T(8,128)(2,1)S(1)}, u32[]{:S(2)}, u32[]{:S(2)}) collective-permute-start(bf16[128,1024]{1,0:T(8,128)(2,1)S(1)} %copy-done.46), channel_id=1, source_target_pairs={{0,8},{4,12},{8,16},{12,20},{16,24},{20,28},{24,0},{28,4},{1,9},{5... | collective-permute-start | bytes 786440 | tf_op jit(solution)/shard_map/ppermute | solution.py:287
  102.6 17.4 %collective-permute-start.47 = (bf16[128,1024]{1,0:T(8,128)(2,1)S(1)}, bf16[128,1024]{1,0:T(8,128)(2,1)S(1)}, u32[]{:S(2)}, u32[]{:S(2)}) collective-permute-start(bf16[128,1024]{1,0:T(8,128)(2,1)S(1)} %copy-done.46), channel_id=1, source_target_pairs={{0,16},{4,20},{8,24},{12,28},{16,0},{20,4},{24,8},{28,12},{1,17},{... | collective-permute-start | bytes 786440 | tf_op jit(solution)/shard_map/ppermute | solution.py:287
  105.8 36.2 %collective-permute-start.20 = (bf16[128,1024]{1,0:T(8,128)(2,1)S(1)}, bf16[128,1024]{1,0:T(8,128)(2,1)S(1)}, u32[]{:S(2)}, u32[]{:S(2)}) collective-permute-start(bf16[128,1024]{1,0:T(8,128)(2,1)S(1)} %copy-done.47), channel_id=1, source_target_pairs={{0,24},{4,28},{8,0},{12,4},{16,8},{20,12},{24,16},{28,20},{1,25},{... | collective-permute-start | bytes 786440 | tf_op jit(solution)/shard_map/ppermute | solution.py:287
  110.1 31.0 %collective-permute-start.19 = (bf16[128,1024]{1,0:T(8,128)(2,1)S(1)}, bf16[128,1024]{1,0:T(8,128)(2,1)S(1)}, u32[]{:S(2)}, u32[]{:S(2)}) collective-permute-start(bf16[128,1024]{1,0:T(8,128)(2,1)S(1)} %copy-done.47), channel_id=1, source_target_pairs={{0,16},{4,20},{8,24},{12,28},{16,0},{20,4},{24,8},{28,12},{1,17},{... | collective-permute-start | bytes 786440 | tf_op jit(solution)/shard_map/ppermute | solution.py:287
  110.8 17.2 %collective-permute-start.18 = (bf16[128,1024]{1,0:T(8,128)(2,1)S(1)}, bf16[128,1024]{1,0:T(8,128)(2,1)S(1)}, u32[]{:S(2)}, u32[]{:S(2)}) collective-permute-start(bf16[128,1024]{1,0:T(8,128)(2,1)S(1)} %copy-done.47), channel_id=1, source_target_pairs={{0,8},{4,12},{8,16},{12,20},{16,24},{20,28},{24,0},{28,4},{1,9},{5... | collective-permute-start | bytes 786440 | tf_op jit(solution)/shard_map/ppermute | solution.py:287
  120.0 21.5 %collective-permute-start.12 = (bf16[320,1024]{1,0:T(8,128)(2,1)S(1)}, bf16[320,1024]{1,0:T(8,128)(2,1)S(1)}, u32[]{:S(2)}, u32[]{:S(2)}) collective-permute-start(bf16[320,1024]{1,0:T(8,128)(2,1)S(1)} %convolution_convert_fusion.40), channel_id=1, source_target_pairs={{0,1},{1,0},{2,3},{3,2},{4,5},{5,4},{6,7},{7,6},{8,9},{9,8},{10,11... | collective-permute-start | bytes 1966088 | tf_op jit(solution)/shard_map/ppermute | solution.py:310
  120.1 44.0 %collective-permute-start.16 = (bf16[128,1024]{1,0:T(8,128)(2,1)S(1)}, bf16[128,1024]{1,0:T(8,128)(2,1)S(1)}, u32[]{:S(2)}, u32[]{:S(2)}) collective-permute-start(bf16[128,1024]{1,0:T(8,128)(2,1)S(1)} %copy-done.45), channel_id=1, source_target_pairs={{0,24},{4,28},{8,0},{12,4},{16,8},{20,12},{24,16},{28,20},{1,25},{... | collective-permute-start | bytes 786440 | tf_op jit(solution)/shard_map/ppermute | solution.py:287
  128.0 30.7 %collective-permute-start.15 = (bf16[128,1024]{1,0:T(8,128)(2,1)S(1)}, bf16[128,1024]{1,0:T(8,128)(2,1)S(1)}, u32[]{:S(2)}, u32[]{:S(2)}) collective-permute-start(bf16[128,1024]{1,0:T(8,128)(2,1)S(1)} %copy-done.45), channel_id=1, source_target_pairs={{0,16},{4,20},{8,24},{12,28},{16,0},{20,4},{24,8},{28,12},{1,17},{... | collective-permute-start | bytes 786440 | tf_op jit(solution)/shard_map/ppermute | solution.py:287
  141.5 25.2 %collective-permute-start.11 = (bf16[320,1024]{1,0:T(8,128)(2,1)S(1)}, bf16[320,1024]{1,0:T(8,128)(2,1)S(1)}, u32[]{:S(2)}, u32[]{:S(2)}) collective-permute-start(bf16[320,1024]{1,0:T(8,128)(2,1)S(1)} %convolution_convert_fusion.42), channel_id=1, source_target_pairs={{0,1},{1,0},{2,3},{3,2},{4,5},{5,4},{6,7},{7,6},{8,9},{9,8},{10,11... | collective-permute-start | bytes 1966088 | tf_op jit(solution)/shard_map/ppermute | solution.py:310
  142.0 25.8 %collective-permute-start.13 = (bf16[320,1024]{1,0:T(8,128)(2,1)S(1)}, bf16[320,1024]{1,0:T(8,128)(2,1)S(1)}, u32[]{:S(2)}, u32[]{:S(2)}) collective-permute-start(bf16[320,1024]{1,0:T(8,128)(2,1)S(1)} %fusion.53), channel_id=1, source_target_pairs={{0,2},{2,0},{1,3},{3,1},{4,6},{6,4},{5,7},{7,5},{8,10},{10,8},{9,1... | collective-permute-start | bytes 1966088 | tf_op jit(solution)/shard_map/ppermute | solution.py:314
  158.8 28.0 %collective-permute-start.43 = (bf16[128,1024]{1,0:T(8,128)(2,1)S(1)}, bf16[128,1024]{1,0:T(8,128)(2,1)S(1)}, u32[]{:S(2)}, u32[]{:S(2)}) collective-permute-start(bf16[128,1024]{1,0:T(8,128)(2,1)S(1)} %get-tuple-element.124), channel_id=1, source_target_pairs={{0,16},{4,20},{8,24},{12,28},{16,0},{20,4},{24,8},{28,12},{1,17},{... | collective-permute-start | bytes 786440 | tf_op jit(solution)/shard_map/ppermute | solution.py:287
  164.1 23.6 %collective-permute-start.42 = (bf16[128,1024]{1,0:T(8,128)(2,1)S(1)}, bf16[128,1024]{1,0:T(8,128)(2,1)S(1)}, u32[]{:S(2)}, u32[]{:S(2)}) collective-permute-start(bf16[128,1024]{1,0:T(8,128)(2,1)S(1)} %get-tuple-element.124), channel_id=1, source_target_pairs={{0,8},{4,12},{8,16},{12,20},{16,24},{20,28},{24,0},{28,4},{1,9},{5... | collective-permute-start | bytes 786440 | tf_op jit(solution)/shard_map/ppermute | solution.py:287
  166.8 22.5 %collective-permute-start.38 = (bf16[512,256]{1,0:T(8,128)(2,1)S(1)}, bf16[512,256]{1,0:T(8,128)(2,1)S(1)}, u32[]{:S(2)}, u32[]{:S(2)}) collective-permute-start(bf16[512,256]{1,0:T(8,128)(2,1)S(1)} %pad_maximum_fusion.41), channel_id=1, source_target_pairs={{0,4},{4,0},{8,12},{12,8},{16,20},{20,16},{24,28},{28,24},{1,5},{5... | collective-permute-start | bytes 786440 | tf_op jit(solution)/shard_map/ppermute | solution.py:287
  167.8 25.1 %collective-permute-start.31 = (bf16[512,768]{1,0:T(8,128)(2,1)S(1)}, bf16[512,768]{1,0:T(8,128)(2,1)S(1)}, u32[]{:S(2)}, u32[]{:S(2)}) collective-permute-start(bf16[512,768]{1,0:T(8,128)(2,1)S(1)} %pad_maximum_fusion.27), channel_id=1, source_target_pairs={{0,4},{4,0},{8,12},{12,8},{16,20},{20,16},{24,28},{28,24},{1,5},{5... | collective-permute-start | bytes 2359304 | tf_op jit(solution)/shard_map/ppermute | solution.py:287
  169.8 45.6 %collective-permute-start.49 = (bf16[512,1024]{1,0:T(8,128)(2,1)S(1)}, bf16[512,1024]{1,0:T(8,128)(2,1)S(1)}, u32[]{:S(2)}, u32[]{:S(2)}) collective-permute-start(bf16[512,1024]{1,0:T(8,128)(2,1)S(1)} %pad_maximum_fusion.18), channel_id=1, source_target_pairs={{0,4},{4,0},{8,12},{12,8},{16,20},{20,16},{24,28},{28,24},{1,5},{5... | collective-permute-start | bytes 3145736 | tf_op jit(solution)/shard_map/ppermute | solution.py:287
  186.8 51.1 %collective-permute-start.21 = (bf16[512,1024]{1,0:T(8,128)(2,1)S(1)}, bf16[512,1024]{1,0:T(8,128)(2,1)S(1)}, u32[]{:S(2)}, u32[]{:S(2)}) collective-permute-start(bf16[512,1024]{1,0:T(8,128)(2,1)S(1)} %pad_maximum_fusion.16), channel_id=1, source_target_pairs={{0,4},{4,0},{8,12},{12,8},{16,20},{20,16},{24,28},{28,24},{1,5},{5... | collective-permute-start | bytes 3145736 | tf_op jit(solution)/shard_map/ppermute | solution.py:287
  187.7 17.7 %collective-permute-start.24 = (bf16[320,1024]{1,0:T(8,128)(2,1)S(1)}, bf16[320,1024]{1,0:T(8,128)(2,1)S(1)}, u32[]{:S(2)}, u32[]{:S(2)}) collective-permute-start(bf16[320,1024]{1,0:T(8,128)(2,1)S(1)} %add_convert_fusion.8), channel_id=1, source_target_pairs={{0,2},{2,0},{1,3},{3,1},{4,6},{6,4},{5,7},{7,5},{8,10},{10,8},{9,1... | collective-permute-start | bytes 1966088 | tf_op jit(solution)/shard_map/ppermute | solution.py:314
  189.3 71.0 %collective-permute-start.17 = (bf16[512,1024]{1,0:T(8,128)(2,1)S(1)}, bf16[512,1024]{1,0:T(8,128)(2,1)S(1)}, u32[]{:S(2)}, u32[]{:S(2)}) collective-permute-start(bf16[512,1024]{1,0:T(8,128)(2,1)S(1)} %pad_maximum_fusion.15), channel_id=1, source_target_pairs={{0,4},{4,0},{8,12},{12,8},{16,20},{20,16},{24,28},{28,24},{1,5},{5... | collective-permute-start | bytes 3145736 | tf_op jit(solution)/shard_map/ppermute | solution.py:287
  192.9 24.1 %collective-permute-start.58 = (bf16[320,1024]{1,0:T(8,128)(2,1)S(1)}, bf16[320,1024]{1,0:T(8,128)(2,1)S(1)}, u32[]{:S(2)}, u32[]{:S(2)}) collective-permute-start(bf16[320,1024]{1,0:T(8,128)(2,1)S(1)} %convert_element_type.703), channel_id=1, source_target_pairs={{0,2},{2,0},{1,3},{3,1},{4,6},{6,4},{5,7},{7,5},{8,10},{10,8},{9,1... | collective-permute-start | bytes 1966088 | tf_op jit(solution)/shard_map/ppermute | solution.py:314
  205.4 55.1 %collective-permute-start.25 = (bf16[320,1024]{1,0:T(8,128)(2,1)S(1)}, bf16[320,1024]{1,0:T(8,128)(2,1)S(1)}, u32[]{:S(2)}, u32[]{:S(2)}) collective-permute-start(bf16[320,1024]{1,0:T(8,128)(2,1)S(1)} %collective-permute-done.24), channel_id=1, source_target_pairs={{0,1},{1,0},{2,3},{3,2},{4,5},{5,4},{6,7},{7,6},{8,9},{9,8},{10,11... | collective-permute-start | bytes 1966088 | tf_op jit(solution)/shard_map/ppermute | solution.py:310
  215.4 75.4 %collective-permute-start.56 = (bf16[320,1024]{1,0:T(8,128)(2,1)S(1)}, bf16[320,1024]{1,0:T(8,128)(2,1)S(1)}, u32[]{:S(2)}, u32[]{:S(2)}) collective-permute-start(bf16[320,1024]{1,0:T(8,128)(2,1)S(1)} %convert_element_type.703), channel_id=1, source_target_pairs={{0,1},{1,0},{2,3},{3,2},{4,5},{5,4},{6,7},{7,6},{8,9},{9,8},{10,11... | collective-permute-start | bytes 1966088 | tf_op jit(solution)/shard_map/ppermute | solution.py:310
  217.1 73.6 %collective-permute-start.45 = (bf16[512,1024]{1,0:T(8,128)(2,1)S(1)}, bf16[512,1024]{1,0:T(8,128)(2,1)S(1)}, u32[]{:S(2)}, u32[]{:S(2)}) collective-permute-start(bf16[512,1024]{1,0:T(8,128)(2,1)S(1)} %pad_maximum_fusion.17), channel_id=1, source_target_pairs={{0,4},{4,0},{8,12},{12,8},{16,20},{20,16},{24,28},{28,24},{1,5},{5... | collective-permute-start | bytes 3145736 | tf_op jit(solution)/shard_map/ppermute | solution.py:287
  237.9 52.9 %collective-permute-start.59 = (bf16[320,1024]{1,0:T(8,128)(2,1)S(1)}, bf16[320,1024]{1,0:T(8,128)(2,1)S(1)}, u32[]{:S(2)}, u32[]{:S(2)}) collective-permute-start(bf16[320,1024]{1,0:T(8,128)(2,1)S(1)} %collective-permute-done.58), channel_id=1, source_target_pairs={{0,1},{1,0},{2,3},{3,2},{4,5},{5,4},{6,7},{7,6},{8,9},{9,8},{10,11... | collective-permute-start | bytes 1966088 | tf_op jit(solution)/shard_map/ppermute | solution.py:310
  270.6 17.2 %collective-permute-start.27 = (bf16[320,1024]{1,0:T(8,128)(2,1)S(1)}, bf16[320,1024]{1,0:T(8,128)(2,1)S(1)}, u32[]{:S(2)}, u32[]{:S(2)}) collective-permute-start(bf16[320,1024]{1,0:T(8,128)(2,1)S(1)} %fusion.46), channel_id=1, source_target_pairs={{0,2},{2,0},{1,3},{3,1},{4,6},{6,4},{5,7},{7,5},{8,10},{10,8},{9,1... | collective-permute-start | bytes 1966088 | tf_op jit(solution)/shard_map/ppermute | solution.py:314
  320.0 17.2 %collective-permute-start.41 = (bf16[320,1024]{1,0:T(8,128)(2,1)S(1)}, bf16[320,1024]{1,0:T(8,128)(2,1)S(1)}, u32[]{:S(2)}, u32[]{:S(2)}) collective-permute-start(bf16[320,1024]{1,0:T(8,128)(2,1)S(1)} %fusion.39), channel_id=1, source_target_pairs={{0,2},{2,0},{1,3},{3,1},{4,6},{6,4},{5,7},{7,5},{8,10},{10,8},{9,1... | collective-permute-start | bytes 1966088 | tf_op jit(solution)/shard_map/ppermute | solution.py:314
  344.5 88.5 %collective-permute-start.57 = (bf16[320,1024]{1,0:T(8,128)(2,1)S(1)}, bf16[320,1024]{1,0:T(8,128)(2,1)S(1)}, u32[]{:S(2)}, u32[]{:S(2)}) collective-permute-start(bf16[320,1024]{1,0:T(8,128)(2,1)S(1)} %convolution_convert_fusion.26), channel_id=1, source_target_pairs={{0,1},{1,0},{2,3},{3,2},{4,5},{5,4},{6,7},{7,6},{8,9},{9,8},{10,11... | collective-permute-start | bytes 1966088 | tf_op jit(solution)/shard_map/ppermute | solution.py:310
  368.2 26.0 %collective-permute-start.108 = (bf16[512,1024]{1,0:T(8,128)(2,1)S(1)}, bf16[512,1024]{1,0:T(8,128)(2,1)S(1)}, u32[]{:S(2)}, u32[]{:S(2)}) collective-permute-start(bf16[512,1024]{1,0:T(8,128)(2,1)S(1)} %convolution_convert_fusion), channel_id=1, source_target_pairs={{0,4},{4,0},{8,12},{12,8},{16,20},{20,16},{24,28},{28,24},{1,5},{5... | collective-permute-start | bytes 3145736 | tf_op jit(solution)/shard_map/ppermute | solution.py:298
  369.2 47.0 %collective-permute-start.104 = (bf16[512,1024]{1,0:T(8,128)(2,1)S(1)}, bf16[512,1024]{1,0:T(8,128)(2,1)S(1)}, u32[]{:S(2)}, u32[]{:S(2)}) collective-permute-start(bf16[512,1024]{1,0:T(8,128)(2,1)S(1)} %convolution_convert_fusion.2), channel_id=1, source_target_pairs={{0,4},{4,0},{8,12},{12,8},{16,20},{20,16},{24,28},{28,24},{1,5},{5... | collective-permute-start | bytes 3145736 | tf_op jit(solution)/shard_map/ppermute | solution.py:298
  372.9 60.3 %collective-permute-start.61 = (bf16[320,1024]{1,0:T(8,128)(2,1)S(1)}, bf16[320,1024]{1,0:T(8,128)(2,1)S(1)}, u32[]{:S(2)}, u32[]{:S(2)}) collective-permute-start(bf16[320,1024]{1,0:T(8,128)(2,1)S(1)} %fusion.26), channel_id=1, source_target_pairs={{0,2},{2,0},{1,3},{3,1},{4,6},{6,4},{5,7},{7,5},{8,10},{10,8},{9,1... | collective-permute-start | bytes 1966088 | tf_op jit(solution)/shard_map/ppermute | solution.py:314
  394.7 22.0 %collective-permute-start.109 = (bf16[128,1024]{1,0:T(8,128)(2,1)S(1)}, bf16[128,1024]{1,0:T(8,128)(2,1)S(1)}, u32[]{:S(2)}, u32[]{:S(2)}) collective-permute-start(bf16[128,1024]{1,0:T(8,128)(2,1)S(1)} %get-tuple-element.114), channel_id=1, source_target_pairs={{0,24},{4,28},{8,0},{12,4},{16,8},{20,12},{24,16},{28,20},{1,25},{... | collective-permute-start | bytes 786440 | tf_op jit(solution)/shard_map/ppermute | solution.py:298
  396.5 20.3 %collective-permute-start.111 = (bf16[128,1024]{1,0:T(8,128)(2,1)S(1)}, bf16[128,1024]{1,0:T(8,128)(2,1)S(1)}, u32[]{:S(2)}, u32[]{:S(2)}) collective-permute-start(bf16[128,1024]{1,0:T(8,128)(2,1)S(1)} %get-tuple-element.115), channel_id=1, source_target_pairs={{0,8},{4,12},{8,16},{12,20},{16,24},{20,28},{24,0},{28,4},{1,9},{5... | collective-permute-start | bytes 786440 | tf_op jit(solution)/shard_map/ppermute | solution.py:298
  416.7 38.0 %collective-permute-start.51 = (bf16[320,1024]{1,0:T(8,128)(2,1)S(1)}, bf16[320,1024]{1,0:T(8,128)(2,1)S(1)}, u32[]{:S(2)}, u32[]{:S(2)}) collective-permute-start(bf16[320,1024]{1,0:T(8,128)(2,1)S(1)} %convolution_convert_fusion.30), channel_id=1, source_target_pairs={{0,1},{1,0},{2,3},{3,2},{4,5},{5,4},{6,7},{7,6},{8,9},{9,8},{10,11... | collective-permute-start | bytes 1966088 | tf_op jit(solution)/shard_map/ppermute | solution.py:310
  416.8 38.0 %collective-permute-start.55 = (bf16[320,1024]{1,0:T(8,128)(2,1)S(1)}, bf16[320,1024]{1,0:T(8,128)(2,1)S(1)}, u32[]{:S(2)}, u32[]{:S(2)}) collective-permute-start(bf16[320,1024]{1,0:T(8,128)(2,1)S(1)} %fusion.32), channel_id=1, source_target_pairs={{0,2},{2,0},{1,3},{3,1},{4,6},{6,4},{5,7},{7,5},{8,10},{10,8},{9,1... | collective-permute-start | bytes 1966088 | tf_op jit(solution)/shard_map/ppermute | solution.py:314
  433.2 20.3 %collective-permute-start.106 = (bf16[128,1024]{1,0:T(8,128)(2,1)S(1)}, bf16[128,1024]{1,0:T(8,128)(2,1)S(1)}, u32[]{:S(2)}, u32[]{:S(2)}) collective-permute-start(bf16[128,1024]{1,0:T(8,128)(2,1)S(1)} %get-tuple-element.113), channel_id=1, source_target_pairs={{0,16},{4,20},{8,24},{12,28},{16,0},{20,4},{24,8},{28,12},{1,17},{... | collective-permute-start | bytes 786440 | tf_op jit(solution)/shard_map/ppermute | solution.py:298
  445.5 17.8 %collective-permute-start.63 = (bf16[320,1024]{1,0:T(8,128)(2,1)}, bf16[320,1024]{1,0:T(8,128)(2,1)}, u32[]{:S(2)}, u32[]{:S(2)}) collective-permute-start(bf16[320,1024]{1,0:T(8,128)(2,1)} %fusion.191), channel_id=1, source_target_pairs={{0,2},{2,0},{1,3},{3,1},{4,6},{6,4},{5,7},{7,5},{8,10},{10,8},{9,1... | collective-permute-start | bytes 1966088 | tf_op jit(solution)/shard_map/ppermute | solution.py:314
  488.7 29.7 %collective-permute-start.65 = (bf16[320,1024]{1,0:T(8,128)(2,1)S(1)}, bf16[320,1024]{1,0:T(8,128)(2,1)S(1)}, u32[]{:S(2)}, u32[]{:S(2)}) collective-permute-start(bf16[320,1024]{1,0:T(8,128)(2,1)S(1)} %convolution_convert_fusion.22), channel_id=1, source_target_pairs={{0,1},{1,0},{2,3},{3,2},{4,5},{5,4},{6,7},{7,6},{8,9},{9,8},{10,11... | collective-permute-start | bytes 1966088 | tf_op jit(solution)/shard_map/ppermute | solution.py:310
  489.2 22.9 %collective-permute-start.96 = (bf16[512,768]{1,0:T(8,128)(2,1)S(1)}, bf16[512,768]{1,0:T(8,128)(2,1)S(1)}, u32[]{:S(2)}, u32[]{:S(2)}) collective-permute-start(bf16[512,768]{1,0:T(8,128)(2,1)S(1)} %convolution_convert_fusion.8), channel_id=1, source_target_pairs={{0,4},{4,0},{8,12},{12,8},{16,20},{20,16},{24,28},{28,24},{1,5},{5... | collective-permute-start | bytes 2359304 | tf_op jit(solution)/shard_map/ppermute | solution.py:298
  539.5 60.1 %collective-permute-start.69 = (bf16[320,1024]{1,0:T(8,128)(2,1)S(1)}, bf16[320,1024]{1,0:T(8,128)(2,1)S(1)}, u32[]{:S(2)}, u32[]{:S(2)}) collective-permute-start(bf16[320,1024]{1,0:T(8,128)(2,1)S(1)} %convolution_convert_fusion.18), channel_id=1, source_target_pairs={{0,1},{1,0},{2,3},{3,2},{4,5},{5,4},{6,7},{7,6},{8,9},{9,8},{10,11... | collective-permute-start | bytes 1966088 | tf_op jit(solution)/shard_map/ppermute | solution.py:310
  548.8 26.0 %collective-permute-start.88 = (bf16[512,1024]{1,0:T(8,128)(2,1)S(1)}, bf16[512,1024]{1,0:T(8,128)(2,1)S(1)}, u32[]{:S(2)}, u32[]{:S(2)}) collective-permute-start(bf16[512,1024]{1,0:T(8,128)(2,1)S(1)} %convolution_convert_fusion.6), channel_id=1, source_target_pairs={{0,4},{4,0},{8,12},{12,8},{16,20},{20,16},{24,28},{28,24},{1,5},{5... | collective-permute-start | bytes 3145736 | tf_op jit(solution)/shard_map/ppermute | solution.py:298
  551.7 45.1 %collective-permute-start.92 = (bf16[512,1024]{1,0:T(8,128)(2,1)S(1)}, bf16[512,1024]{1,0:T(8,128)(2,1)S(1)}, u32[]{:S(2)}, u32[]{:S(2)}) collective-permute-start(bf16[512,1024]{1,0:T(8,128)(2,1)S(1)} %convolution_convert_fusion.4), channel_id=1, source_target_pairs={{0,4},{4,0},{8,12},{12,8},{16,20},{20,16},{24,28},{28,24},{1,5},{5... | collective-permute-start | bytes 3145736 | tf_op jit(solution)/shard_map/ppermute | solution.py:298
  555.5 47.6 %collective-permute-start.73 = (bf16[320,1024]{1,0:T(8,128)(2,1)S(1)}, bf16[320,1024]{1,0:T(8,128)(2,1)S(1)}, u32[]{:S(2)}, u32[]{:S(2)}) collective-permute-start(bf16[320,1024]{1,0:T(8,128)(2,1)S(1)} %fusion.15), channel_id=1, source_target_pairs={{0,2},{2,0},{1,3},{3,1},{4,6},{6,4},{5,7},{7,5},{8,10},{10,8},{9,1... | collective-permute-start | bytes 1966088 | tf_op jit(solution)/shard_map/ppermute | solution.py:314
  575.3 30.9 %collective-permute-start.89 = (bf16[128,1024]{1,0:T(8,128)(2,1)S(1)}, bf16[128,1024]{1,0:T(8,128)(2,1)S(1)}, u32[]{:S(2)}, u32[]{:S(2)}) collective-permute-start(bf16[128,1024]{1,0:T(8,128)(2,1)S(1)} %get-tuple-element.117), channel_id=1, source_target_pairs={{0,24},{4,28},{8,0},{12,4},{16,8},{20,12},{24,16},{28,20},{1,25},{... | collective-permute-start | bytes 786440 | tf_op jit(solution)/shard_map/ppermute | solution.py:298
  578.5 28.3 %collective-permute-start.91 = (bf16[128,1024]{1,0:T(8,128)(2,1)S(1)}, bf16[128,1024]{1,0:T(8,128)(2,1)S(1)}, u32[]{:S(2)}, u32[]{:S(2)}) collective-permute-start(bf16[128,1024]{1,0:T(8,128)(2,1)S(1)} %get-tuple-element.118), channel_id=1, source_target_pairs={{0,8},{4,12},{8,16},{12,20},{16,24},{20,28},{24,0},{28,4},{1,9},{5... | collective-permute-start | bytes 786440 | tf_op jit(solution)/shard_map/ppermute | solution.py:298
  603.1 18.0 %collective-permute-start.95 = (bf16[128,1024]{1,0:T(8,128)(2,1)S(1)}, bf16[128,1024]{1,0:T(8,128)(2,1)S(1)}, u32[]{:S(2)}, u32[]{:S(2)}) collective-permute-start(bf16[128,1024]{1,0:T(8,128)(2,1)S(1)} %get-tuple-element.121), channel_id=1, source_target_pairs={{0,8},{4,12},{8,16},{12,20},{16,24},{20,28},{24,0},{28,4},{1,9},{5... | collective-permute-start | bytes 786440 | tf_op jit(solution)/shard_map/ppermute | solution.py:298
  606.2 27.3 %collective-permute-start.94 = (bf16[128,1024]{1,0:T(8,128)(2,1)S(1)}, bf16[128,1024]{1,0:T(8,128)(2,1)S(1)}, u32[]{:S(2)}, u32[]{:S(2)}) collective-permute-start(bf16[128,1024]{1,0:T(8,128)(2,1)S(1)} %get-tuple-element.122), channel_id=1, source_target_pairs={{0,16},{4,20},{8,24},{12,28},{16,0},{20,4},{24,8},{28,12},{1,17},{... | collective-permute-start | bytes 786440 | tf_op jit(solution)/shard_map/ppermute | solution.py:298
  606.8 28.5 %collective-permute-start.75 = (bf16[320,1024]{1,0:T(8,128)(2,1)S(1)}, bf16[320,1024]{1,0:T(8,128)(2,1)S(1)}, u32[]{:S(2)}, u32[]{:S(2)}) collective-permute-start(bf16[320,1024]{1,0:T(8,128)(2,1)S(1)} %fusion.192), channel_id=1, source_target_pairs={{0,2},{2,0},{1,3},{3,1},{4,6},{6,4},{5,7},{7,5},{8,10},{10,8},{9,1... | collective-permute-start | bytes 1966088 | tf_op jit(solution)/shard_map/ppermute | solution.py:314
  612.5 23.6 %collective-permute-start.74 = (bf16[320,1024]{1,0:T(8,128)(2,1)S(1)}, bf16[320,1024]{1,0:T(8,128)(2,1)S(1)}, u32[]{:S(2)}, u32[]{:S(2)}) collective-permute-start(bf16[320,1024]{1,0:T(8,128)(2,1)S(1)} %fusion.192), channel_id=1, source_target_pairs={{0,1},{1,0},{2,3},{3,2},{4,5},{5,4},{6,7},{7,6},{8,9},{9,8},{10,11... | collective-permute-start | bytes 1966088 | tf_op jit(solution)/shard_map/ppermute | solution.py:310
  654.6 24.3 %collective-permute-start.80 = (bf16[512,768]{1,0:T(8,128)(2,1)S(1)}, bf16[512,768]{1,0:T(8,128)(2,1)S(1)}, u32[]{:S(2)}, u32[]{:S(2)}) collective-permute-start(bf16[512,768]{1,0:T(8,128)(2,1)S(1)} %convolution_convert_fusion.10), channel_id=1, source_target_pairs={{0,4},{4,0},{8,12},{12,8},{16,20},{20,16},{24,28},{28,24},{1,5},{5... | collective-permute-start | bytes 2359304 | tf_op jit(solution)/shard_map/ppermute | solution.py:298
  663.4 19.1 %collective-permute-start.85 = (bf16[128,256]{1,0:T(8,128)(2,1)S(1)}, bf16[128,256]{1,0:T(8,128)(2,1)S(1)}, u32[]{:S(2)}, u32[]{:S(2)}) collective-permute-start(bf16[128,256]{1,0:T(8,128)(2,1)S(1)} %get-tuple-element.166), channel_id=1, source_target_pairs={{0,24},{4,28},{8,0},{12,4},{16,8},{20,12},{24,16},{28,20},{1,25},{... | collective-permute-start | bytes 196616 | tf_op jit(solution)/shard_map/ppermute | solution.py:298
  666.7 16.4 %collective-permute-start.87 = (bf16[128,256]{1,0:T(8,128)(2,1)S(1)}, bf16[128,256]{1,0:T(8,128)(2,1)S(1)}, u32[]{:S(2)}, u32[]{:S(2)}) collective-permute-start(bf16[128,256]{1,0:T(8,128)(2,1)S(1)} %get-tuple-element.167), channel_id=1, source_target_pairs={{0,8},{4,12},{8,16},{12,20},{16,24},{20,28},{24,0},{28,4},{1,9},{5... | collective-permute-start | bytes 196616 | tf_op jit(solution)/shard_map/ppermute | solution.py:298
  705.0 22.4 %collective-permute-start.77 = (bf16[320,1024]{1,0:T(8,128)(2,1)S(1)}, bf16[320,1024]{1,0:T(8,128)(2,1)S(1)}, u32[]{:S(2)}, u32[]{:S(2)}) collective-permute-start(bf16[320,1024]{1,0:T(8,128)(2,1)S(1)} %convolution_convert_fusion.14), channel_id=1, source_target_pairs={{0,1},{1,0},{2,3},{3,2},{4,5},{5,4},{6,7},{7,6},{8,9},{9,8},{10,11... | collective-permute-start | bytes 1966088 | tf_op jit(solution)/shard_map/ppermute | solution.py:310
  (159 other events, 1557.3 us)

commit v2 on v1

v2 whole, which is shorter than its diff:
```python
import functools

import jax
import jax.numpy as jnp
from jax import lax
from jax.experimental import pallas as pl
from jax.experimental.pallas import tpu as pltpu
from jax.sharding import PartitionSpec as P

D = 1024
HEADS = 16
HD = 64
FF = 4096
STEP = 10


EPS_NORM = 1e-06
BETA_ONE = 0.9
BETA_TWO = 0.999
ADAM_EPS = 1e-06
WEIGHT_DECAY = 0.01
LEARN_RATE = 0.5
MASKED = -1000000000.0

QUERIES = 128
REACH = 64
WINDOW = QUERIES + 2 * REACH

NT = (((1,), (1,)), ((), ()))
TN = (((0,), (0,)), ((), ()))


VMEM_SPEC = pl.BlockSpec(memory_space=pltpu.VMEM)
SMEM_SPEC = pl.BlockSpec(memory_space=pltpu.SMEM)
ANY_SPEC = pl.BlockSpec(memory_space=pl.ANY)


def struct(shape, kind=jnp.bfloat16):
    return jax.ShapeDtypeStruct(shape, kind)


class Order:
    def __init__(self):
        self.earlier = []

    def settle(self, value):
        self.earlier = self.earlier + [value]
        return value

    def __call__(
        self, name, body, ins, outs, room, in_specs=None, out_specs=None, grid_spec=None, scratch=(), aliases=None
    ):
        extra = list(self.earlier)
        scalars = 0 if grid_spec is None else grid_spec[0]

        def wrapped(*refs):
            return body(*refs[: len(ins)], *refs[len(ins) + len(extra) :])

        in_specs = (in_specs or [VMEM_SPEC] * len(ins)) + [ANY_SPEC] * len(extra)
        out_specs = out_specs or [VMEM_SPEC] * len(outs)
        size = sum(array.size * jnp.dtype(array.dtype).itemsize for array in (*ins, *outs))
        places = dict(out_shape=outs, in_specs=in_specs, out_specs=out_specs, scratch_shapes=scratch)
        if grid_spec is not None:
            del places["in_specs"], places["out_specs"], places["scratch_shapes"]
            places["grid_spec"] = pltpu.PrefetchScalarGridSpec(
                num_scalar_prefetch=scalars,
                grid=grid_spec[1],
                in_specs=in_specs,
                out_specs=out_specs,
            )
        result = pl.pallas_call(
            wrapped,
            **places,
            input_output_aliases=aliases or {},
            cost_estimate=pl.CostEstimate(flops=size, bytes_accessed=size, transcendentals=0),
            compiler_params=pltpu.CompilerParams(vmem_limit_bytes=room << 20),
            name=name,
        )(*ins, *extra)
        self.earlier = [result[-1]]
        return result


def add_kernel(here, far, out):
    out[...] = (here[...].astype(jnp.float32) + far[...].astype(jnp.float32)).astype(out.dtype)


def add(run, here, far, kind):
    return run("add", add_kernel, [here, far], [struct(here.shape, kind)], 4)[0]


def cast_kernel(*refs):
    out, begin = refs[-1], 0
    for ref in refs[:-1]:
        out[:, begin : begin + ref.shape[1]] = ref[...].astype(out.dtype)
        begin += ref.shape[1]


def cast(run, *parts):
    across = sum(part.shape[1] for part in parts)
    return run("cast", cast_kernel, parts, [struct((parts[0].shape[0], across))], 6)[0]


def join_kernel(here, far, *outs):
    rows, begin = here.shape[0], 0
    for out in outs:
        columns = slice(begin, begin + out.shape[1])
        out[:rows, :] = here[:, columns]
        out[rows:, :] = far[:, columns]
        begin += out.shape[1]


def join(run, here, far, spans):
    outs = [struct((2 * here.shape[0], span)) for span in spans]
    return run("join", join_kernel, [here, far], outs, 10)


def adam_part(gradient, weight, first, second, decay):
    first_new = BETA_ONE * first + (1.0 - BETA_ONE) * gradient
    second_new = BETA_TWO * second + (1.0 - BETA_TWO) * gradient * gradient
    step_dir = (
        first_new
        / (1.0 - BETA_ONE**STEP)
        / (jnp.sqrt(second_new / (1.0 - BETA_TWO**STEP)) + ADAM_EPS)
        + decay * weight
    )
    return (first_new, second_new, step_dir)


def dot(left, right, dims=(((1,), (0,)), ((), ()))):
    return lax.dot_general(left, right, dims, preferred_element_type=jnp.float32)


def head_lanes(rows, width, value):
    lane_head = lax.broadcasted_iota(jnp.int32, (rows, width), 1) // HD
    return [
        jnp.where(lane_head == head, value, 0.0).astype(jnp.float32) for head in range(width // HD)
    ]


def block_shares(query_wide, keys_in, mask):
    heads_here = query_wide.shape[0] // QUERIES
    scores = dot(query_wide, keys_in, NT).reshape(heads_here, QUERIES, WINDOW)
    scores = jnp.where((mask > 0.5)[None], scores, MASKED)
    powered = jnp.exp(scores - jnp.max(scores, axis=-1, keepdims=True))
    shares = powered * (1.0 / jnp.sum(powered, axis=-1, keepdims=True))
    return shares.reshape(heads_here * QUERIES, WINDOW)


def fold_heads(wide, lanes):
    total = wide[:QUERIES] * lanes[0]
    for head in range(1, len(lanes)):
        total += wide[head * QUERIES : (head + 1) * QUERIES] * lanes[head]
    return total


def places_of(place_ref, pieces, rows):
    half = rows // 2
    found = []
    for piece in range(pieces):
        chip, stream = divmod(piece, 2)
        for core in range(2):
            block = jnp.bitwise_xor(place_ref[0], 2 * chip + core)
            found.append((piece, core * half, pl.multiple_of(block * rows + stream * half, 32)))
    return found


def in_token_order(place_ref, refs, store, start):
    rows = refs[0].shape[0]
    for piece, row, token in places_of(place_ref, len(refs), rows):
        store[pl.ds(token + start, rows // 2), :] = refs[piece][pl.ds(row, rows // 2), :]


def attend_kernel(pieces, place_ref, mask_ref, *refs):
    ins, outs, (all_in, all_out) = refs[:pieces], refs[pieces : 2 * pieces], refs[2 * pieces :]
    count, width = all_out.shape
    all_in[:REACH, :] = jnp.zeros((REACH, 3 * width), jnp.bfloat16)
    all_in[REACH + count :, :] = jnp.zeros((REACH, 3 * width), jnp.bfloat16)
    in_token_order(place_ref, ins, all_in, REACH)
    scaled = [lane.astype(jnp.bfloat16) for lane in head_lanes(QUERIES, width, HD ** (-0.5))]
    plain = head_lanes(QUERIES, width, 1.0)

    @pl.loop(0, count // QUERIES, unroll=count // QUERIES)
    def _(block):
        base = pl.multiple_of(block * QUERIES, QUERIES)
        query = all_in[pl.ds(base + REACH, QUERIES), :width]
        keys_in = all_in[pl.ds(base, WINDOW), width : 2 * width]
        values_in = all_in[pl.ds(base, WINDOW), 2 * width :]
        query_wide = jnp.concatenate([query * lane for lane in scaled], axis=0)
        shares = block_shares(query_wide, keys_in, mask_ref[pl.ds(base, QUERIES), :])
        wide = dot(shares.astype(jnp.bfloat16), values_in)
        all_out[pl.ds(base, QUERIES), :] = fold_heads(wide, plain).astype(jnp.bfloat16)

    rows = outs[0].shape[0]
    for piece, row, token in places_of(place_ref, pieces, rows):
        outs[piece][pl.ds(row, rows // 2), :] = all_out[pl.ds(token, rows // 2), :]


def attend_back_kernel(pieces, place_ref, mask_ref, *refs):
    ins, grads, outs = refs[:pieces], refs[pieces : 2 * pieces], refs[2 * pieces : 3 * pieces]
    all_in, all_grad, query_sum, key_sum, value_sum = refs[3 * pieces :]
    count, width = all_grad.shape
    all_in[:REACH, :] = jnp.zeros((REACH, 3 * width), jnp.bfloat16)
    all_in[REACH + count :, :] = jnp.zeros((REACH, 3 * width), jnp.bfloat16)
    in_token_order(place_ref, ins, all_in, REACH)
    in_token_order(place_ref, grads, all_grad, 0)
    key_sum[...] = jnp.zeros_like(key_sum)
    value_sum[...] = jnp.zeros_like(value_sum)
    scaled = [lane.astype(jnp.bfloat16) for lane in head_lanes(QUERIES, width, HD ** (-0.5))]
    plain_low = [lane.astype(jnp.bfloat16) for lane in head_lanes(QUERIES, width, 1.0)]
    scaled_wide = head_lanes(QUERIES, width, HD ** (-0.5))

    @pl.loop(0, count // QUERIES, unroll=count // QUERIES)
    def _(block):
        base = pl.multiple_of(block * QUERIES, QUERIES)
        query = all_in[pl.ds(base + REACH, QUERIES), :width]
        keys_in = all_in[pl.ds(base, WINDOW), width : 2 * width]
        values_in = all_in[pl.ds(base, WINDOW), 2 * width :]
        grad = all_grad[pl.ds(base, QUERIES), :]
        query_wide = jnp.concatenate([query * lane for lane in scaled], axis=0)
        grad_wide = jnp.concatenate([grad * lane for lane in plain_low], axis=0)
        shares = block_shares(query_wide, keys_in, mask_ref[pl.ds(base, QUERIES), :])
        grad_shares = dot(grad_wide, values_in, NT)
        inner = jnp.sum(grad_shares * shares, axis=-1, keepdims=True)
        grad_scores = (shares * (grad_shares - inner)).astype(jnp.bfloat16)
        query_sum[pl.ds(base, QUERIES), :] = fold_heads(dot(grad_scores, keys_in), scaled_wide)
        key_sum[pl.ds(base, WINDOW), :] += dot(grad_scores, query_wide, TN)
        value_sum[pl.ds(base, WINDOW), :] += dot(shares.astype(jnp.bfloat16), grad_wide, TN)

    rows = outs[0].shape[0]
    for piece, row, token in places_of(place_ref, pieces, rows):
        here, there = pl.ds(row, rows // 2), pl.ds(token + REACH, rows // 2)
        out = outs[piece]
        out[here, :width] = query_sum[pl.ds(token, rows // 2), :].astype(jnp.bfloat16)
        out[here, width : 2 * width] = key_sum[there, :].astype(jnp.bfloat16)
        out[here, 2 * width :] = value_sum[there, :].astype(jnp.bfloat16)


def attend(run, place, mask, projected):
    pieces = len(projected)
    rows, width = projected[0].shape[0], projected[0].shape[1] // 3
    count = rows * pieces
    return run(
        "attend",
        functools.partial(attend_kernel, pieces),
        [place, mask, *projected],
        [struct((rows, width))] * pieces,
        12,
        in_specs=[SMEM_SPEC] + [VMEM_SPEC] * (1 + pieces),
        scratch=[
            pltpu.VMEM((count + 2 * REACH, 3 * width), jnp.bfloat16),
            pltpu.VMEM((count, width), jnp.bfloat16),
        ],
    )


def attend_back(run, place, mask, projected, grads):
    pieces = len(projected)
    rows, width = projected[0].shape[0], projected[0].shape[1] // 3
    count = rows * pieces
    return run(
        "attend_back",
        functools.partial(attend_back_kernel, pieces),
        [place, mask, *projected, *grads],
        [struct((rows, 3 * width))] * pieces,
        20,
        in_specs=[SMEM_SPEC] + [VMEM_SPEC] * (1 + 2 * pieces),
        scratch=[
            pltpu.VMEM((count + 2 * REACH, 3 * width), jnp.bfloat16),
            pltpu.VMEM((count, width), jnp.bfloat16),
            pltpu.VMEM((count, width), jnp.float32),
            pltpu.VMEM((count + 2 * REACH, width), jnp.float32),
            pltpu.VMEM((count + 2 * REACH, width), jnp.float32),
        ],
    )


def crop_mask(segments):
    blocks = segments.shape[0] // QUERIES
    edge = jnp.full((REACH,), -1, segments.dtype)
    padded = jnp.concatenate([edge, segments, edge])
    keys_of = jnp.stack([padded[b * QUERIES : b * QUERIES + WINDOW] for b in range(blocks)])
    same = segments.reshape(blocks, QUERIES)[:, :, None] == keys_of[:, None, :]
    return same.astype(jnp.float32).reshape(blocks * QUERIES, WINDOW)


def row_step(count):
    return 32 if count % 32 == 0 else count


def normalised(value):
    centre = value - jnp.mean(value, axis=-1, keepdims=True)
    spread_of = jnp.mean(centre * centre, axis=-1, keepdims=True)
    scale = lax.rsqrt(spread_of + EPS_NORM)
    return centre * scale, scale


def norm_kernel(row, terms, params_ref, value_ref, *refs):
    *term_refs, out_ref, low_ref = refs if terms else (None, *refs)
    step = row_step(value_ref.shape[0])

    @pl.loop(0, value_ref.shape[0] // step, unroll=value_ref.shape[0] // step)
    def _(index):
        here = pl.ds(pl.multiple_of(index * step, step), step)
        value = value_ref[here, :]
        if terms:
            for ref in term_refs:
                value = value + ref[here, :].astype(jnp.float32)
            out_ref[here, :] = value
        gain, shift = params_ref[row : row + 1, :], params_ref[row + 1 : row + 2, :]
        low_ref[here, :] = (normalised(value)[0] * gain + shift).astype(jnp.bfloat16)


def norm(run, params, row, value, *terms):
    wide = [struct(value.shape, jnp.float32)] if terms else []
    result = run(
        "norm",
        functools.partial(norm_kernel, row, len(terms)),
        [params, value, *terms],
        wide + [struct(value.shape)],
        6,
    )
    return result if terms else result[0]


def norm_back_kernel(
    row, params_ref, stream_ref, value_ref, first, second, sums_ref, out_ref, low_ref
):
    step = row_step(value_ref.shape[0])
    width = value_ref.shape[1]
    sums_ref[...] = jnp.zeros_like(sums_ref)

    @pl.loop(0, value_ref.shape[0] // step, unroll=value_ref.shape[0] // step)
    def _(index):
        here = pl.ds(pl.multiple_of(index * step, step), step)
        grad = first[here, :].astype(jnp.float32) + second[here, :].astype(jnp.float32)
        unit, scale = normalised(value_ref[here, :])
        along = grad * unit
        sums_ref[:8, :] += jnp.sum(along.reshape(step // 8, 8, width), axis=0)
        sums_ref[8:, :] += jnp.sum(grad.reshape(step // 8, 8, width), axis=0)
        gain = params_ref[row : row + 1, :]
        pushed = grad * gain
        inner = jnp.mean(pushed * unit, axis=-1, keepdims=True)
        term = scale * (pushed - jnp.mean(pushed, axis=-1, keepdims=True) - unit * inner)
        total = stream_ref[here, :] + term
        out_ref[here, :] = total
        low_ref[here, :] = total.astype(jnp.bfloat16)


def norm_back(run, params, row, stream_grad, value, *terms):
    return run(
        "norm_back",
        functools.partial(norm_back_kernel, row),
        [params, stream_grad, value, *terms],
        [
            struct((16, value.shape[1]), jnp.float32),
            struct(value.shape, jnp.float32),
            struct(value.shape),
        ],
        8,
    )


COLUMNS = 256


def two_halves(both, weights, here):
    first, second = weights
    half = first.shape[0]
    return dot(both[:, :half], first[:, here]) + dot(both[:, half:], second[:, here])


def project_kernel(begin, mine, facing, first, second, out):
    both = jnp.concatenate([mine[...], facing[...]], axis=0)
    for start in range(0, out.shape[1], COLUMNS):
        here = slice(begin + start, begin + start + COLUMNS)
        out[:, start : start + COLUMNS] = two_halves(both, (first, second), here).astype(
            jnp.bfloat16
        )


def project(run, mine, facing, first, second, begin, width):
    outs = [struct((2 * mine.shape[0], width))]
    body = functools.partial(project_kernel, begin)
    return run("project", body, [mine, facing, first, second], outs, 10)[0]


def widen_kernel(mine, facing, first, second, active, slope):
    both = jnp.concatenate([mine[...], facing[...]], axis=0)
    for start in range(0, active.shape[1], COLUMNS):
        here = slice(start, start + COLUMNS)
        hidden = two_halves(both, (first, second), here)
        below = 0.5 + 0.5 * lax.erf(hidden * (0.5**0.5))
        density = jnp.exp(-0.5 * hidden * hidden) * 0.3989422804014327
        active[:, here] = (hidden * below).astype(jnp.bfloat16)
        slope[:, here] = (below + hidden * density).astype(jnp.bfloat16)


def widen(run, mine, facing, first, second):
    outs = [struct((2 * mine.shape[0], first.shape[1]))] * 2
    return run("widen", widen_kernel, [mine, facing, first, second], outs, 10)


def bend_kernel(mine, facing, first, second, slope, out):
    both = jnp.concatenate([mine[...], facing[...]], axis=0)
    for start in range(0, out.shape[1], COLUMNS):
        here = slice(start, start + COLUMNS)
        grad = two_halves(both, (first, second), here)
        out[:, here] = (grad * slope[:, here].astype(jnp.float32)).astype(jnp.bfloat16)


def bend_back(run, mine, facing, first, second, slope):
    return run("bend_back", bend_kernel, [mine, facing, first, second, slope], [struct(slope.shape)], 10)[0]


def narrow_kernel(begin, piece, first, second, kept, sent):
    half = kept.shape[0]
    columns = slice(begin, begin + piece.shape[1])
    for index, weights in enumerate((first, second)):
        for start in range(0, weights.shape[0], COLUMNS):
            there = index * weights.shape[0] + start
            here = slice(there, there + COLUMNS)
            rows = weights[start : start + COLUMNS, columns]
            both = dot(piece[...], rows, NT).astype(jnp.bfloat16)
            kept[:, here] = both[:half]
            sent[:, here] = both[half:]


def narrow(run, piece, first, second, begin):
    outs = [struct((piece.shape[0] // 2, 2 * first.shape[0]))] * 2
    return run("narrow", functools.partial(narrow_kernel, begin), [piece, first, second], outs, 10)


def weight_terms_kernel(counts, columns, *refs):
    ins = refs[: sum(map(sum, counts))]
    kept, sent, all_left, all_right = refs[len(ins) :]
    begin = 0
    for lefts, rights in counts:
        left, right, ins = ins[:lefts], ins[lefts : lefts + rights], ins[lefts + rights :]
        for store, parts in ((all_left, left), (all_right, right)):
            row = 0
            for part in parts:
                store[row : row + part.shape[0], : part.shape[1]] = part[...]
                row += part.shape[0]
        wide = right[0].shape[1]
        for out, spans in zip((sent, kept), columns[::-1]):
            row = 0
            for first, last in spans:
                for start in range(0, wide, COLUMNS):
                    out[row : row + last - first, begin + start : begin + start + COLUMNS] = dot(
                        all_left[:, first:last], all_right[:, start : start + COLUMNS], TN
                    ).astype(jnp.bfloat16)
                row += last - first
        begin += wide


def weight_terms(run, pairs, columns):
    counts = tuple((len(left), len(right)) for left, right in pairs)
    flat = [array for left, right in pairs for array in (*left, *right)]
    total = sum(array.shape[0] for array in pairs[0][0])
    across = sum(right[0].shape[1] for _, right in pairs)
    return run(
        "weight_terms",
        functools.partial(weight_terms_kernel, counts, columns),
        flat,
        [struct((sum(last - first for first, last in spans), across)) for spans in columns],
        24,
        scratch=[
            pltpu.VMEM((total, pairs[0][0][0].shape[1]), jnp.bfloat16),
            pltpu.VMEM((total, max(right[0].shape[1] for _, right in pairs)), jnp.bfloat16),
        ],
    )


def fold_kernel(many, *refs):
    heres, fars, (kept, sent) = refs[:many], refs[many : 2 * many], refs[2 * many :]
    rows = kept.shape[0]
    begin = 0
    for here, far in zip(heres, fars):
        columns = slice(begin, begin + here.shape[1])
        for out, part in ((sent, slice(rows, None)), (kept, slice(0, rows))):
            out[:, columns] = (
                here[part, :].astype(jnp.float32) + far[part, :].astype(jnp.float32)
            ).astype(jnp.bfloat16)
        begin += here.shape[1]


def fold(run, heres, fars):
    across = sum(array.shape[1] for array in heres)
    outs = [struct((heres[0].shape[0] // 2, across))] * 2
    return run("fold", functools.partial(fold_kernel, len(heres)), [*heres, *fars], outs, 12)


def moments_kernel(at, kept, far, weights, first, second, *refs):
    first_new, second_new, step_out, squares = refs[-4:]
    grad = kept[...].astype(jnp.float32) + far[...].astype(jnp.float32)
    weight = weights[...].reshape(grad.shape)
    new_first, new_second, step = adam_part(
        grad, weight, first[...].reshape(grad.shape), second[...].reshape(grad.shape), WEIGHT_DECAY
    )
    for out, value in ((first_new, new_first), (second_new, new_second), (step_out, step)):
        out[...] = value.reshape(out.shape)
    for place, value in enumerate((weight, step)):
        squares[0, place : place + 1, :] = jnp.sum(value * value, axis=0, keepdims=True)


def moments(run, names, layer, kept, far, weights, first, second, before):
    rows, wide = weights.shape[2:]
    spec = pl.BlockSpec((1, 1, rows, wide), lambda n, at: (layer, at[n], 0, 0))
    grad_spec = pl.BlockSpec((rows, wide), lambda n, at: (0, n))
    before = list(before or [])
    return run(
        "moments",
        moments_kernel,
        [jnp.array(names, jnp.int32), kept, far, weights, first, second, *before],
        [struct(weights.shape, jnp.float32)] * 3 + [struct((len(names), 2, wide), jnp.float32)],
        12,
        in_specs=[grad_spec, grad_spec, spec, spec, spec] + [ANY_SPEC] * len(before),
        out_specs=[spec, spec, spec, pl.BlockSpec((1, 2, wide), lambda n, at: (n, 0, 0))],
        grid_spec=(1, (len(names),)),
        aliases={6 + i: i for i in range(len(before))},
    )


def apply_kernel(trust, weights, step, new, low):
    layer, name = pl.program_id(0), pl.program_id(1)
    value = weights[...] - LEARN_RATE * trust[layer, name] * step[...]
    new[...] = value
    low[...] = value.astype(jnp.bfloat16)


def apply(run, trust, weights, step):
    layers, names, rows, wide = weights.shape
    spec = pl.BlockSpec((1, 1, rows, wide), lambda layer, name: (layer, name, 0, 0))
    return run(
        "apply",
        apply_kernel,
        [trust, weights, step],
        [struct(weights.shape, jnp.float32), struct(weights.shape)],
        8,
        in_specs=[SMEM_SPEC, spec, spec],
        out_specs=[spec, spec],
        grid_spec=(0, (layers, names)),
    )


def move_columns(run, wides, order, out_rows, back):
    width, kind = wides[0].shape[1], wides[0].dtype
    blocks = order.shape[0]
    block = width // blocks
    if block % 128:
        if back:
            order = jnp.argsort(order)
        columns = (order[:, None] * block + jnp.arange(block)[None, :]).reshape(-1)
        moved = jnp.take(jnp.concatenate(wides, axis=0), columns, axis=1)
        starts = [sum(out_rows[:i]) for i in range(len(out_rows))]
        return [moved[start : start + rows] for start, rows in zip(starts, out_rows)]

    def copy(order_ref, *refs):
        ins, outs = refs[: len(wides)], refs[len(wides) :]
        step = min(ref.shape[0] for ref in refs)
        for row in range(0, sum(out_rows), step):
            source, target, from_row, to_row = ins, outs, row, row
            index = 0
            while from_row >= source[index].shape[0]:
                from_row -= source[index].shape[0]
                index += 1
            source, index = source[index], 0
            while to_row >= target[index].shape[0]:
                to_row -= target[index].shape[0]
                index += 1
            target = target[index]
            for place in range(blocks):
                there = pl.ds(pl.multiple_of(order_ref[place] * block, 128), block)
                here = pl.ds(place * block, block)
                from_columns, to_columns = (here, there) if back else (there, here)
                target[pl.ds(to_row, step), to_columns] = source[pl.ds(from_row, step), from_columns]

    return run(
        "move_columns",
        copy,
        [order, *wides],
        [struct((rows, width), kind) for rows in out_rows],
        6,
        in_specs=[SMEM_SPEC] + [VMEM_SPEC] * len(wides),
    )


class Rows:
    def __init__(self, total, run):
        self.total, self.run = total, run
        self.strides = [1 << bit for bit in reversed(range(total.bit_length() - 1))]

    def offsets(self):
        places = [0]
        for stride in self.strides:
            places = places + [place ^ stride for place in places]
        return places

    def order(self):
        return jnp.bitwise_xor(
            jnp.array(self.offsets(), jnp.int32), lax.axis_index("dp").astype(jnp.int32)
        )

    def swap(self, values, stride):
        return lax.ppermute(
            values, "dp", [(source, source ^ stride) for source in range(self.total)]
        )

class Gather:
    def __init__(self, rows, spans, *maps):
        self.rows, self.run, self.spans = rows, rows.run, spans
        self.block = cast(self.run, *maps)
        self.there, self.wholes = None, [None] * len(spans)

    def send(self):
        self.there = self.rows.swap(self.block, self.rows.strides[0])

    def take(self):
        for stride in self.rows.strides[1:-1]:
            (self.block,) = join(self.run, self.block, self.there, [self.block.shape[1]])
            if stride == self.rows.strides[-2]:
                return
            self.there = self.rows.swap(self.block, stride)

    def send_near(self):
        self.there = self.rows.swap(self.block, self.rows.strides[-2])

    def take_near(self):
        self.block = join(self.run, self.block, self.there, self.spans)

    def send_last(self, span=0):
        self.wholes[span] = (
            self.block[span],
            self.rows.swap(self.block[span], self.rows.strides[-1]),
        )

    def take_last(self, span=0):
        here, there = self.wholes[span]
        self.wholes[span] = (here, self.run.settle(there))
        return self.wholes[span]


class Reduce:
    def __init__(self, rows):
        self.rows, self.run = rows, rows.run
        self.kept, self.there = [], []

    def send(self, pairs):
        width = pairs[0][0][0].shape[1]
        columns = (((0, width // 2),), ((width // 2, width),))
        keep, away = weight_terms(self.run, pairs, columns)
        self.kept.append(keep)
        self.there.append(self.rows.swap(away, self.rows.strides[-1]))

    def settle(self, group=0):
        self.there[group] = self.run.settle(self.there[group])

    def pass_on(self, level):
        stride = self.rows.strides[-1 - level]
        keep, away = fold(self.run, self.kept, self.there)
        self.kept, self.there = [keep], [self.rows.swap(away, stride)]

    def finish(self):
        for level in range(3, len(self.rows.strides)):
            self.pass_on(level)
        return self.kept[0], self.there[0]


def core_swap(values_in):
    return lax.ppermute(values_in, "mp", [(0, 1), (1, 0), (2, 3), (3, 2)])


def chip_swap(values_in):
    return lax.ppermute(values_in, "mp", [(0, 2), (2, 0), (1, 3), (3, 1)])


def total_everywhere(value, rows_total):
    value = value + core_swap(value)
    value = value + chip_swap(value)
    stride = 1
    while stride < rows_total:
        value = value + lax.ppermute(
            value, "dp", [(source, source ^ stride) for source in range(rows_total)]
        )
        stride *= 2
    return value


def shards(
    rows_total,
    tokens,
    cotangent,
    segments,
    attention_weights,
    attention_first,
    attention_second,
    dense_weights,
    dense_first,
    dense_second,
    norm_params,
    norm_first,
    norm_second,
):
    layers = attention_weights.shape[0]
    width = attention_weights.shape[3]
    run = Order()
    rows = Rows(rows_total, run)
    order = rows.order()
    place = lax.axis_index("mp").astype(jnp.int32).reshape(1)
    count = tokens.shape[0]
    half = count // 2
    both = range(2)

    wide = dense_weights.shape[3]
    settle = run.settle

    def mixer(current, first, last):
        return [attention_weights[current, s] for s in range(first, last)]

    class Exchange:
        def __init__(self):
            self.mine, self.facing = [None, None], [None, None]
            self.beyond, self.beyond_facing = [None, None], [None, None]

        def send(self, part, value):
            self.mine[part] = value
            self.beyond[part] = chip_swap(value)
            self.facing[part] = core_swap(value)

        def near(self, part):
            self.facing[part] = settle(self.facing[part])
            return self.mine[part], self.facing[part]

        def far(self, part):
            self.beyond[part] = settle(self.beyond[part])
            self.beyond_facing[part] = core_swap(self.beyond[part])

        def pieces(self):
            return [
                array
                for near, far in ((self.mine, self.facing), (self.beyond, self.beyond_facing))
                for part in both
                for array in (near[part], far[part])
            ]

    class Collect:
        def __init__(self, weights, begin):
            self.weights, self.begin = weights, begin
            self.near, self.there = [None, None], [None, None]

        def send(self, part, far_piece, near_piece):
            terms = []
            for piece in (far_piece, near_piece):
                kept, sent = narrow(run, piece, *self.weights, self.begin)
                terms.append((kept, core_swap(sent)))
            self.there[part] = chip_swap(add(run, *terms[0], jnp.bfloat16))
            self.near[part] = add(run, *terms[1], jnp.float32)

        def terms(self, part):
            return self.near[part], self.there[part]

    inputs_way = Gather(rows, [3 * width], *mixer(0, 0, 3))
    inputs_way.send()
    output_way = Gather(rows, [width], *mixer(0, 3, 4))
    (params_here,) = move_columns(
        run, [norm_params.reshape(layers * 4, D)], order, [layers * 4], False
    )
    stream = move_columns(run, [tokens], order, [half, half], False)
    normed = Exchange()
    for part in both:
        normed.send(part, norm(run, params_here, 0, stream[part]))
    inputs_way.take()
    inputs_way.send_near()
    output_way.send()
    up_way = Gather(rows, [wide], dense_weights[0, 0])
    down_way = Gather(rows, [wide], dense_weights[0, 1])
    for part in both:
        normed.near(part)
    normed.far(0)
    inputs_way.take_near()
    inputs_way.send_last()
    output_way.take()
    output_way.send_near()
    up_way.send()
    normed.far(1)
    stream_grad = list(move_columns(run, [cotangent], order, [half, half], False))
    back = Exchange()
    back.send(0, cast(run, stream_grad[0]))
    output_way.take_near()
    output_way.send_last()
    mask = crop_mask(segments)
    back.near(0)
    up_way.take()
    up_way.send_near()
    down_way.send()
    back.far(0)
    back.send(1, cast(run, stream_grad[1]))
    inputs_map, inputs_begin = inputs_way.take_last(), 0
    back.near(1)

    mixer_way = Gather(rows, [4 * width], *mixer(1, 0, 4)) if layers > 1 else None
    dense_way = (
        Gather(rows, [wide, wide], dense_weights[1, 0], dense_weights[1, 1]) if layers > 1 else None
    )
    saved_forward, copies = [], []
    for current in range(layers):
        row = 4 * current
        first = current == 0
        projected = [None] * 4

        def project_inputs(*values):
            return project(run, *values, inputs_begin, 3 * width)

        for part in both:
            projected[part] = project_inputs(*normed.near(part), *inputs_map)
        for part in both:
            if not first:
                normed.far(part)
            projected[2 + part] = project_inputs(
                normed.beyond[part], normed.beyond_facing[part], *inputs_map
            )
        if not first:
            dense_way.take_near()
            dense_way.send_last(0)
        attended = attend(run, place, mask, projected)
        if first:
            back.far(1)
            output_map, output_begin = output_way.take_last(), 0
            up_way.take_near()
            up_way.send_last()
            down_way.take()
            down_way.send_near()
        mixed = Collect(output_map, output_begin)
        for part in both:
            mixed.send(part, attended[2 + part], attended[part])
        if first:
            mixer_way.send()
            down_way.take_near()
        middle, normed_two = [None] * 2, Exchange()
        active, slope = [None] * 4, [None] * 4
        for part in both:
            middle[part], low = norm(run, params_here, row + 2, stream[part], *mixed.terms(part))
            normed_two.send(part, low)
            normed_two.near(part)
        if first:
            mixer_way.take()
            mixer_way.send_near()
            up_map = up_way.take_last()
            down_way.send_last()
        else:
            up_map = dense_way.take_last(0)
            dense_way.send_last(1)
        for part in both:
            active[part], slope[part] = widen(run, *normed_two.near(part), *up_map)
        for part in both:
            normed_two.far(part)
            if first and part == 0:
                mixer_way.take_near()
                dense_way.send()
            active[2 + part], slope[2 + part] = widen(
                run, normed_two.beyond[part], normed_two.beyond_facing[part], *up_map
            )
        if first:
            down_map = down_way.take_last()
            mixer_way.send_last()
        else:
            down_map = dense_way.take_last(1)
        saved_forward.append((stream, normed, projected, attended, middle, normed_two, active, slope))
        copies.append((inputs_map, inputs_begin, output_map, output_begin, up_map, down_map))
        if current + 1 < layers:
            widened = Collect(down_map, 0)
            for part in both:
                widened.send(part, active[2 + part], active[part])
            dense_way.take()
            dense_way.send_near()
            stream, normed = [None, None], Exchange()
            for part in both:
                stream[part], low = norm(
                    run, params_here, row + 4, middle[part], *widened.terms(part)
                )
                normed.send(part, low)
                normed.near(part)
            inputs_map = mixer_way.take_last()
            output_map, inputs_begin, output_begin = inputs_map, 0, 3 * width

    dense_grads, mixer_grads = [None] * layers, [None] * layers
    vector_list = [[None, None] for _ in range(layers)]
    mixer_state, dense_state = None, None
    squares_list = [[None] * 6 for _ in range(layers)]

    def dense_moments(current, names, reduced):
        nonlocal dense_state
        *dense_state, squares = moments(
            run, names, current, *reduced.finish(),
            dense_weights, dense_first, dense_second, dense_state,
        )
        for place, name in enumerate(names):
            squares_list[current][4 + name] = squares[place]

    def mixer_moments(current, reduced):
        nonlocal mixer_state
        *mixer_state, squares = moments(
            run, (0, 1, 2, 3), current, *reduced.finish(),
            attention_weights, attention_first, attention_second, mixer_state,
        )
        for name in range(4):
            squares_list[current][name] = squares[name]

    def eight_rows(vectors):
        total = vectors[0] + vectors[1]
        return jnp.sum(total.reshape(2, 8, D), axis=1)

    for current in reversed(range(layers)):
        row = 4 * current
        newest = current == layers - 1
        stream_in, normed, projected, attended, middle, normed_two, active, slope = saved_forward[
            current
        ]
        inputs_map, inputs_begin, output_map, output_begin, up_map, down_map = copies[current]
        grad_hidden = [None] * 4
        for part in both:
            grad_hidden[part] = bend_back(run, *back.near(part), *down_map, slope[part])
        if not newest:
            mixer_grads[current + 1].settle()
            mixer_grads[current + 1].pass_on(1)
        for part in both:
            if not newest:
                back.far(part)
            grad_hidden[2 + part] = bend_back(
                run, back.beyond[part], back.beyond_facing[part], *down_map, slope[2 + part],
            )
        raised = Collect(up_map, 0)
        for part in both:
            raised.send(part, grad_hidden[2 + part], grad_hidden[part])
        if not newest:
            dense_grads[current + 1].pass_on(2)
        dense_grads[current] = [Reduce(rows), Reduce(rows)]
        dense_grads[current][0].send([(back.pieces(), active)])
        vectors = [None, None]
        turned = Exchange()
        for part in both:
            vectors[part], stream_grad[part], low = norm_back(
                run,
                params_here,
                row + 2,
                stream_grad[part],
                middle[part],
                *raised.terms(part),
            )
            turned.send(part, low)
            turned.near(part)
            if part == 0:
                if newest:
                    dense_grads[current][0].send([(normed_two.pieces(), grad_hidden)])
                else:
                    mixer_grads[current + 1].pass_on(2)
        if not newest:
            dense_grads[current][1].send([(normed_two.pieces(), grad_hidden)])
        vector_list[current][1] = eight_rows(vectors)
        grad_attended = [None] * 4

        def project_back(*values):
            return project(run, *values, output_begin, width)

        for part in both:
            grad_attended[part] = project_back(*turned.near(part), *output_map)
        for part in both:
            turned.far(part)
            grad_attended[2 + part] = project_back(
                turned.beyond[part], turned.beyond_facing[part], *output_map
            )
        if newest:
            dense_grads[current][0].settle(0)
        else:
            dense_moments(current + 1, (1, 0), dense_grads[current + 1])
            dense_grads[current][0].pass_on(1)
        grad_projected = attend_back(run, place, mask, projected, grad_attended)
        lowered = Collect(inputs_map, inputs_begin)
        for part in both:
            lowered.send(part, grad_projected[2 + part], grad_projected[part])
        if newest:
            dense_grads[current] = dense_grads[current][0]
            dense_grads[current].settle(1)
            dense_grads[current].pass_on(1)
        else:
            mixer_moments(current + 1, mixer_grads[current + 1])
            dense_grads[current][0].pass_on(2)
        mixer_grads[current] = Reduce(rows)
        mixer_grads[current].send([(normed.pieces(), grad_projected), (turned.pieces(), attended)])
        back = Exchange()
        for part in both:
            vectors[part], stream_grad[part], low = norm_back(
                run,
                params_here,
                row,
                stream_grad[part],
                stream_in[part],
                *lowered.terms(part),
            )
            if current:
                back.send(part, low)
                back.near(part)
        vector_list[current][0] = eight_rows(vectors)

    dense_grads[0][1].pass_on(1)
    dense_moments(0, (1,), dense_grads[0][0])
    widened = Collect(copies[-1][5], 0)
    active, middle = saved_forward[-1][6], saved_forward[-1][4]
    for part in both:
        widened.send(part, active[2 + part], active[part])
    (grad_tokens,) = move_columns(run, stream_grad, order, [count], True)
    vector_rows = [pair for entry in vector_list for pair in entry]
    (vectors,) = move_columns(
        run, [jnp.concatenate(vector_rows)], order, [layers * 4], True
    )
    dense_grads[0][1].pass_on(2)
    mixer_grads[0].settle()
    mixer_grads[0].pass_on(1)

    def finish(*values):
        parts = [
            values[i] + (values[i + 1] + values[i + 2].astype(jnp.float32)) for i in (0, 3)
        ]
        return move_columns(run, parts, order, [count], True)

    (outcome,) = finish(middle[0], *widened.terms(0), middle[1], *widened.terms(1))
    mixer_grads[0].pass_on(2)
    dense_moments(0, (0,), dense_grads[0][1])
    total_vectors = total_everywhere(vectors, rows_total).reshape(layers, 4, D)
    mixer_moments(0, mixer_grads[0])
    total_squares = total_everywhere(
        jnp.stack(
            [jnp.sum(value, axis=1) for entry in squares_list for value in entry]
        ).reshape(layers, 6, 2),
        rows_total,
    )
    sizes_all = jnp.sqrt(total_squares[:, :, 0])
    moves_all = jnp.sqrt(total_squares[:, :, 1])
    trust_all = sizes_all / moves_all
    mixer_new, mixer_copy = apply(run, trust_all[:, :4], attention_weights, mixer_state[2])
    dense_new, dense_copy = apply(run, trust_all[:, 4:], dense_weights, dense_state[2])
    params_first, params_second, params_step = adam_part(
        total_vectors, norm_params, norm_first, norm_second, 0.0
    )
    params_size = jnp.sqrt(jnp.sum(norm_params * norm_params, axis=-1))
    params_move = jnp.sqrt(jnp.sum(params_step * params_step, axis=-1))
    params_new = norm_params - LEARN_RATE * (params_size / params_move)[:, :, None] * params_step
    mixer_entries = float(D * HEADS * HD) ** 0.5
    dense_entries = float(D * FF) ** 0.5
    entry_roots = jnp.array([mixer_entries] * 4 + [dense_entries] * 2, jnp.float32)
    norms = jnp.stack([sizes_all / entry_roots[None, :], moves_all / entry_roots[None, :]], axis=-1)
    second_norm_grad = total_vectors[:, 2:4]
    return (
        outcome,
        grad_tokens,
        mixer_new,
        mixer_state[0],
        mixer_state[1],
        mixer_copy,
        dense_new,
        dense_state[0],
        dense_state[1],
        dense_copy,
        params_new,
        params_first,
        params_second,
        norms,
        second_norm_grad,
    )


def solution(mesh):
    rows_spec = P(("dp", "mp"), None)
    weight_spec = P(None, None, "dp", "mp")
    in_specs = (rows_spec, rows_spec, P("dp")) + (weight_spec,) * 6 + (P(),) * 3
    out_specs = (rows_spec,) * 2 + (weight_spec,) * 8 + (P(),) * 5
    return jax.shard_map(
        functools.partial(shards, mesh.shape["dp"]),
        mesh=mesh,
        in_specs=in_specs,
        out_specs=out_specs,
        check_vma=False,
    )
```

time: 769 us -> 567 us (0.74)
  waiting for transfers between devices: 384 us -> 276 us
  matrix products: 83.9 us -> 0 us
  Pallas kernels: 67.4 us -> 136 us
  other arithmetic: 51.3 us -> 5.1 us
  starting transfers between devices: 143 us -> 101 us
  local copies, waits for them, and re-layouts: 27.6 us -> 35.3 us
    ppermute x64 -> x35, waiting for transfers between devices: 298 us -> 126 us  [swap(): lax.ppermute(values, 'dp', [(source, source ^ stride) for source in range...]
    dot_general x80 -> x0, matrix products: 83.9 us -> none  [dot(): lax.dot_general(left, right, dims, preferred_element_type=jnp.float32)]
    ppermute x64 -> x35, starting transfers between devices: 112 us -> 39.1 us  [swap(): lax.ppermute(values, 'dp', [(source, source ^ stride) for source in range...]
    pallas_call x10 -> x165, Pallas kernels: 67.4 us -> 136 us  [__call__(): pl.pallas_call(wrapped, **places, input_output_aliases=aliases or {}, cos...]
    ppermute x18 -> x34, waiting for transfers between devices: 70.4 us -> 128 us  [chip_swap(): return lax.ppermute(values_in, 'mp', [(0, 2), (2, 0), (1, 3), (3, 1)])]
    ppermute x18 -> x34, starting transfers between devices: 19.6 us -> 38.6 us  [chip_swap(): return lax.ppermute(values_in, 'mp', [(0, 2), (2, 0), (1, 3), (3, 1)])]
    reduce_sum x13 -> x9, other arithmetic: 12.4 us -> 0.82 us  [the longest x5 0.69 us: shards(): jnp.sum(value, axis=1)]
    convert_element_type x18 -> x0, other arithmetic: 11.1 us -> none  [the longest x1 2.14 us: shards(): dense_new.astype(jnp.bfloat16)]
  transfers between devices with their start and end apart: 122 -> 141, of which waited for: 50 -> 69; matrix products, arithmetic and copies ran while one was open for 17% -> 1% of each run, Pallas kernels for 5% -> 21%
where the time goes in v2:
time: 567 us; the launch traced here: 557 us
  waiting for transfers between devices  276 us (49%)
  Pallas kernels  136 us (24%)
  starting transfers between devices  101 us (18%)
  local copies, waits for them, and re-layouts  35.3 us (6%)
    pallas_call x165, Pallas kernels, __call__(): pl.pallas_call(wrapped, **places, input_output_aliases=aliases or {}, cos...  136 us
    ppermute x34, waiting for transfers between devices, chip_swap(): return lax.ppermute(values_in, 'mp', [(0, 2), (2, 0), (1, 3), (3, 1)])  128 us
    ppermute x35, waiting for transfers between devices, swap(): lax.ppermute(values, 'dp', [(source, source ^ stride) for source in range...  126 us
    ppermute x35, starting transfers between devices, swap(): lax.ppermute(values, 'dp', [(source, source ^ stride) for source in range...  39.1 us
    ppermute x34, starting transfers between devices, chip_swap(): return lax.ppermute(values_in, 'mp', [(0, 2), (2, 0), (1, 3), (3, 1)])  38.6 us
    unnamed x235, local copies, waits for them, and re-layouts  29.8 us
    ppermute x66, starting transfers between devices, core_swap(): return lax.ppermute(values_in, 'mp', [(0, 1), (1, 0), (2, 3), (3, 2)])  12.1 us
    ppermute x6, waiting for transfers between devices, total_everywhere(): lax.ppermute(value, 'dp', [(source, source ^ stride) for source in range(...  11.9 us
  transfers between devices with their start and end apart: 141, of which 69 were waited for; matrix products, arithmetic and copies ran while one was open for 1% of the time, Pallas kernels for 21%

profile of v2, /device:TPU:0, one launch (start us, length us, event | category | flops | bytes accessed | tf_op | source)
XLA Modules:
  0.0 557.0 jit_solution(10451865787209234717)
XLA Ops:
  0.7 2.2 slice_bitcast_fusion.4
  2.9 4.1 collective-permute-start.1
  9.8 6.3 %collective-permute-done.1.refs_1_ = bf16[128,768]{1,0:T(8,128)(2,1)S(1)} collective-permute-done((bf16[128,768]{1,0:T(8,128)(2,1)S(1)}, bf16[128,768]{1,0:T(8,128)(2,1)S(1)}, u32[]{:S(2)}, u32[]{:S(2)}) %collective-permute-start.1) | collective-permute-done | bytes 196640 | tf_op jit(solution)/shard_map/ppermute | solution.py:605
  21.4 6.6 %collective-permute-done.4.refs_5_.refs_0_.refs_4_ = bf16[160,1024]{1,0:T(8,128)(2,1)S(1)} collective-permute-done((bf16[160,1024]{1,0:T(8,128)(2,1)S(1)}, bf16[160,1024]{1,0:T(8,128)(2,1)S(1)}, u32[]{:S(2)}, u32[]{:S(2)}) %collective-permute-start.4) | collective-permute-done | bytes 327712 | tf_op jit(solution)/shard_map/ppermute | solution.py:674
  31.1 3.4 collective-permute-start.6
  34.4 2.9 collective-permute-done.6.refs_1_
  39.9 2.2 collective-permute-start.8
  42.2 8.7 %collective-permute-done.9.refs_1_ = bf16[256,256]{1,0:T(8,128)(2,1)S(1)} collective-permute-done((bf16[256,256]{1,0:T(8,128)(2,1)S(1)}, bf16[256,256]{1,0:T(8,128)(2,1)S(1)}, u32[]{:S(2)}, u32[]{:S(2)}) %collective-permute-start.9) | collective-permute-done | bytes 131104 | tf_op jit(solution)/shard_map/ppermute | solution.py:605
  50.9 3.6 collective-permute-done.8.refs_1_
  58.7 2.2 collective-permute-start.16
  69.7 2.9 attend.2
  72.7 3.9 collective-permute-done.17.refs_1_
  84.6 9.6 %collective-permute-done.22.refs_1_ = bf16[256,1024]{1,0:T(8,128)(2,1)S(1)} collective-permute-done((bf16[256,1024]{1,0:T(8,128)(2,1)S(1)}, bf16[256,1024]{1,0:T(8,128)(2,1)S(1)}, u32[]{:S(2)}, u32[]{:S(2)}) %collective-permute-start.22) | collective-permute-done | bytes 524320 | tf_op jit(solution)/shard_map/ppermute | solution.py:605
  98.1 6.7 %collective-permute-done.28.refs_3_ = bf16[160,1024]{1,0:T(8,128)(2,1)S(1)} collective-permute-done((bf16[160,1024]{1,0:T(8,128)(2,1)S(1)}, bf16[160,1024]{1,0:T(8,128)(2,1)S(1)}, u32[]{:S(2)}, u32[]{:S(2)}) %collective-permute-start.28) | collective-permute-done | bytes 327712 | tf_op jit(solution)/shard_map/ppermute | solution.py:674
  105.7 5.6 %collective-permute-done.27.refs_1_ = bf16[128,1024]{1,0:T(8,128)(2,1)S(1)} collective-permute-done((bf16[128,1024]{1,0:T(8,128)(2,1)S(1)}, bf16[128,1024]{1,0:T(8,128)(2,1)S(1)}, u32[]{:S(2)}, u32[]{:S(2)}) %collective-permute-start.27) | collective-permute-done | bytes 262176 | tf_op jit(solution)/shard_map/ppermute | solution.py:605
  113.0 2.8 collective-permute-done.31.refs_3_.refs_0_.refs_4_
  116.1 6.2 %collective-permute-done.34.refs_0_.refs_5_.refs_6_ = bf16[160,1024]{1,0:T(8,128)(2,1)S(1)} collective-permute-done((bf16[160,1024]{1,0:T(8,128)(2,1)S(1)}, bf16[160,1024]{1,0:T(8,128)(2,1)S(1)}, u32[]{:S(2)}, u32[]{:S(2)}) %collective-permute-start.34) | collective-permute-done | bytes 327712 | tf_op jit(solution)/shard_map/ppermute | solution.py:674
  129.2 13.7 %collective-permute-done.30.refs_2_.refs_4_.refs_3_ = bf16[512,1024]{1,0:T(8,128)(2,1)S(1)} collective-permute-done((bf16[512,1024]{1,0:T(8,128)(2,1)S(1)}, bf16[512,1024]{1,0:T(8,128)(2,1)S(1)}, u32[]{:S(2)}, u32[]{:S(2)}) %collective-permute-start.30) | collective-permute-done | bytes 1048608 | tf_op jit(solution)/shard_map/ppermute | solution.py:605
  151.4 19.8 %collective-permute-done.39.refs_1_ = bf16[128,2048]{1,0:T(8,128)(2,1)S(1)} collective-permute-done((bf16[128,2048]{1,0:T(8,128)(2,1)S(1)}, bf16[128,2048]{1,0:T(8,128)(2,1)S(1)}, u32[]{:S(2)}, u32[]{:S(2)}) %collective-permute-start.39) | collective-permute-done | bytes 524320 | tf_op jit(solution)/shard_map/ppermute | solution.py:605
  173.8 8.5 %collective-permute-done.44.refs_3_ = bf16[160,1024]{1,0:T(8,128)(2,1)S(1)} collective-permute-done((bf16[160,1024]{1,0:T(8,128)(2,1)S(1)}, bf16[160,1024]{1,0:T(8,128)(2,1)S(1)}, u32[]{:S(2)}, u32[]{:S(2)}) %collective-permute-start.44) | collective-permute-done | bytes 327712 | tf_op jit(solution)/shard_map/ppermute | solution.py:674
  184.1 5.1 collective-permute-done.46.refs_0_.refs_5_.refs_4_
  189.3 6.6 %collective-permute-done.48.refs_0_.refs_5_.refs_6_ = bf16[160,1024]{1,0:T(8,128)(2,1)S(1)} collective-permute-done((bf16[160,1024]{1,0:T(8,128)(2,1)S(1)}, bf16[160,1024]{1,0:T(8,128)(2,1)S(1)}, u32[]{:S(2)}, u32[]{:S(2)}) %collective-permute-start.48) | collective-permute-done | bytes 327712 | tf_op jit(solution)/shard_map/ppermute | solution.py:674
  198.8 3.0 attend.3
  209.2 7.5 %collective-permute-done.53.refs_3_ = bf16[160,1024]{1,0:T(8,128)(2,1)S(1)} collective-permute-done((bf16[160,1024]{1,0:T(8,128)(2,1)S(1)}, bf16[160,1024]{1,0:T(8,128)(2,1)S(1)}, u32[]{:S(2)}, u32[]{:S(2)}) %collective-permute-start.53) | collective-permute-done | bytes 327712 | tf_op jit(solution)/shard_map/ppermute | solution.py:674
  219.2 8.5 %collective-permute-done.58.refs_3_ = bf16[160,1024]{1,0:T(8,128)(2,1)S(1)} collective-permute-done((bf16[160,1024]{1,0:T(8,128)(2,1)S(1)}, bf16[160,1024]{1,0:T(8,128)(2,1)S(1)}, u32[]{:S(2)}, u32[]{:S(2)}) %collective-permute-start.58) | collective-permute-done | bytes 327712 | tf_op jit(solution)/shard_map/ppermute | solution.py:674
  229.5 5.1 collective-permute-done.61.refs_0_.refs_5_.refs_4_
  234.7 6.6 %collective-permute-done.63.refs_0_.refs_5_.refs_6_ = bf16[160,1024]{1,0:T(8,128)(2,1)S(1)} collective-permute-done((bf16[160,1024]{1,0:T(8,128)(2,1)S(1)}, bf16[160,1024]{1,0:T(8,128)(2,1)S(1)}, u32[]{:S(2)}, u32[]{:S(2)}) %collective-permute-start.63) | collective-permute-done | bytes 327712 | tf_op jit(solution)/shard_map/ppermute | solution.py:674
  247.0 4.9 collective-permute-done.60.refs_3_.refs_6_.refs_2_
  266.1 4.1 weight_terms.6
  270.8 3.2 collective-permute-done.69.refs_4_
  278.5 2.9 weight_terms.7
  281.4 5.5 collective-permute-done.73.refs_4_
  289.6 4.3 collective-permute-done.75.refs_0_.refs_5_.refs_16_
  294.0 6.6 %collective-permute-done.77.refs_0_.refs_5_.refs_18_ = bf16[160,1024]{1,0:T(8,128)(2,1)S(1)} collective-permute-done((bf16[160,1024]{1,0:T(8,128)(2,1)S(1)}, bf16[160,1024]{1,0:T(8,128)(2,1)S(1)}, u32[]{:S(2)}, u32[]{:S(2)}) %collective-permute-start.77) | collective-permute-done | bytes 327712 | tf_op jit(solution)/shard_map/ppermute | solution.py:674
  302.5 7.7 %attend_back.2 = (bf16[320,768]{1,0:T(8,128)(2,1)S(1)}, bf16[320,768]{1,0:T(8,128)(2,1)S(1)}, bf16[320,768]{1,0:T(8,128)(2,1)S(1)}, bf16[320,768]{1,0:T(8,128)(2,1)S(1)}) custom-call(s32[1]{0:T(128)} %bitcast.4.refs_0_, f32[1280,256]{1,0:T(8,128)S(1)} %fusion.refs_1_, bf16[320,768]{1,0:T(8,128)(2,1)S(1)} %project.20.refs_4_.refs_2_, ...), custom_call_target="tpu_custom_call" | custom-call | flops 5898244 | bytes 5898244 | tf_op jit(solution)/shard_map/attend_back/pallas_call | solution.py:71
  319.2 3.2 weight_terms.8
  323.0 2.8 collective-permute-done.82.refs_4_
  328.5 8.5 %collective-permute-done.87.refs_4_ = bf16[160,1024]{1,0:T(8,128)(2,1)S(1)} collective-permute-done((bf16[160,1024]{1,0:T(8,128)(2,1)S(1)}, bf16[160,1024]{1,0:T(8,128)(2,1)S(1)}, u32[]{:S(2)}, u32[]{:S(2)}) %collective-permute-start.87) | collective-permute-done | bytes 327712 | tf_op jit(solution)/shard_map/ppermute | solution.py:674
  341.1 2.9 collective-permute-done.89.refs_0_.refs_6_.refs_4_
  344.0 6.6 %collective-permute-done.91.refs_0_.refs_6_ = bf16[160,1024]{1,0:T(8,128)(2,1)S(1)} collective-permute-done((bf16[160,1024]{1,0:T(8,128)(2,1)S(1)}, bf16[160,1024]{1,0:T(8,128)(2,1)S(1)}, u32[]{:S(2)}, u32[]{:S(2)}) %collective-permute-start.91) | collective-permute-done | bytes 327712 | tf_op jit(solution)/shard_map/ppermute | solution.py:674
  366.1 3.3 weight_terms.9
  373.3 3.0 collective-permute-done.102.refs_1_
  376.4 5.4 collective-permute-done.101.refs_4_
  383.9 2.6 collective-permute-start.100
  386.5 2.3 collective-permute-done.107.refs_0_.refs_5_.refs_16_
  388.8 6.6 %collective-permute-done.105.refs_0_.refs_5_.refs_18_ = bf16[160,1024]{1,0:T(8,128)(2,1)S(1)} collective-permute-done((bf16[160,1024]{1,0:T(8,128)(2,1)S(1)}, bf16[160,1024]{1,0:T(8,128)(2,1)S(1)}, u32[]{:S(2)}, u32[]{:S(2)}) %collective-permute-start.105) | collective-permute-done | bytes 327712 | tf_op jit(solution)/shard_map/ppermute | solution.py:674
  395.4 2.9 weight_terms.10
  400.8 8.0 %collective-permute-done.100.refs_2_ = bf16[128,2048]{1,0:T(8,128)(2,1)S(1)} collective-permute-done((bf16[128,2048]{1,0:T(8,128)(2,1)S(1)}, bf16[128,2048]{1,0:T(8,128)(2,1)S(1)}, u32[]{:S(2)}, u32[]{:S(2)}) %collective-permute-start.100) | collective-permute-done | bytes 524320 | tf_op jit(solution)/shard_map/ppermute | solution.py:605
  408.8 2.5 moments.5
  411.6 7.4 %attend_back.3 = (bf16[320,768]{1,0:T(8,128)(2,1)S(1)}, bf16[320,768]{1,0:T(8,128)(2,1)S(1)}, bf16[320,768]{1,0:T(8,128)(2,1)S(1)}, bf16[320,768]{1,0:T(8,128)(2,1)S(1)}) custom-call(s32[1]{0:T(128)} %bitcast.4.refs_0_, f32[1280,256]{1,0:T(8,128)S(1)} %fusion.refs_1_, bf16[320,768]{1,0:T(8,128)(2,1)S(1)} %project.16.refs_4_.refs_2_, ...), custom_call_target="tpu_custom_call" | custom-call | flops 5898244 | bytes 5898244 | tf_op jit(solution)/shard_map/attend_back/pallas_call | solution.py:71
  428.1 10.2 %collective-permute-done.111.refs_2_ = bf16[128,1024]{1,0:T(8,128)(2,1)S(1)} collective-permute-done((bf16[128,1024]{1,0:T(8,128)(2,1)S(1)}, bf16[128,1024]{1,0:T(8,128)(2,1)S(1)}, u32[]{:S(2)}, u32[]{:S(2)}) %collective-permute-start.111) | collective-permute-done | bytes 262176 | tf_op jit(solution)/shard_map/ppermute | solution.py:605
  438.4 2.5 moments.6
  441.1 3.4 collective-permute-start.116
  444.6 4.1 weight_terms.11
  450.7 5.5 collective-permute-done.116.refs_2_
  470.0 4.2 collective-permute-done.127.refs_1_
  481.7 13.5 %collective-permute-done.128.refs_1_ = bf16[256,1024]{1,0:T(8,128)(2,1)S(1)} collective-permute-done((bf16[256,1024]{1,0:T(8,128)(2,1)S(1)}, bf16[256,1024]{1,0:T(8,128)(2,1)S(1)}, u32[]{:S(2)}, u32[]{:S(2)}) %collective-permute-start.128) | collective-permute-done | bytes 524320 | tf_op jit(solution)/shard_map/ppermute | solution.py:605
  498.4 3.4 collective-permute-done.138
  506.5 2.9 collective-permute-start.140
  525.8 3.8 moments.9
  536.5 3.0 collective-permute-done.133
  543.2 2.9 collective-permute-start.135
  549.6 3.4 apply.2
  554.0 2.8 apply.3
  (670 shorter events, 216.7 us)
Async XLA Ops:
  2.9 13.2 %collective-permute-start.1 = (bf16[128,768]{1,0:T(8,128)(2,1)S(1)}, bf16[128,768]{1,0:T(8,128)(2,1)S(1)}, u32[]{:S(2)}, u32[]{:S(2)}) collective-permute-start(bf16[128,768]{1,0:T(8,128)(2,1)S(1)} %cast.8.refs_1_.refs_0_), channel_id=1, source_target_pairs={{0,16},{4,20},{8,24},{12,28},{16,0},{20,4},{24,8},{28,12},{1,17},{... | collective-permute-start | bytes 589832 | tf_op jit(solution)/shard_map/ppermute | solution.py:605
  16.1 11.9 %collective-permute-start.2 = (bf16[256,768]{1,0:T(8,128)(2,1)S(1)}, bf16[256,768]{1,0:T(8,128)(2,1)S(1)}, u32[]{:S(2)}, u32[]{:S(2)}) collective-permute-start(bf16[256,768]{1,0:T(8,128)(2,1)S(1)} %join.12.refs_1_.refs_0_), channel_id=1, source_target_pairs={{0,8},{4,12},{8,0},{12,4},{16,24},{20,28},{24,16},{28,20},{1,9},{5... | collective-permute-start | bytes 1179656 | tf_op jit(solution)/shard_map/ppermute | solution.py:605
  17.4 10.6 %collective-permute-start.4 = (bf16[160,1024]{1,0:T(8,128)(2,1)S(1)}, bf16[160,1024]{1,0:T(8,128)(2,1)S(1)}, u32[]{:S(2)}, u32[]{:S(2)}) collective-permute-start(bf16[160,1024]{1,0:T(8,128)(2,1)S(1)} %norm.8.refs_2_.refs_0_), channel_id=1, source_target_pairs={{0,2},{2,0},{1,3},{3,1},{4,6},{6,4},{5,7},{7,5},{8,10},{10,8},{9,1... | collective-permute-start | bytes 983048 | tf_op jit(solution)/shard_map/ppermute | solution.py:674
  19.0 18.4 %collective-permute-start.7 = (bf16[160,1024]{1,0:T(8,128)(2,1)S(1)}, bf16[160,1024]{1,0:T(8,128)(2,1)}, u32[]{:S(2)}, u32[]{:S(2)}) collective-permute-start(bf16[160,1024]{1,0:T(8,128)(2,1)S(1)} %norm.9.refs_2_.refs_0_), channel_id=1, source_target_pairs={{0,2},{2,0},{1,3},{3,1},{4,6},{6,4},{5,7},{7,5},{8,10},{10,8},{9,1... | collective-permute-start | bytes 983048 | tf_op jit(solution)/shard_map/ppermute | solution.py:674
  29.6 29.1 %collective-permute-start.5 = (bf16[512,768]{1,0:T(8,128)(2,1)S(1)}, bf16[512,768]{1,0:T(8,128)(2,1)S(1)}, u32[]{:S(2)}, u32[]{:S(2)}) collective-permute-start(bf16[512,768]{1,0:T(8,128)(2,1)S(1)} %join.13.refs_2_.refs_1_), channel_id=1, source_target_pairs={{0,4},{4,0},{8,12},{12,8},{16,20},{20,16},{24,28},{28,24},{1,5},{5... | collective-permute-start | bytes 2359304 | tf_op jit(solution)/shard_map/ppermute | solution.py:605
  38.2 16.3 %collective-permute-start.10 = (bf16[160,1024]{1,0:T(8,128)(2,1)S(1)}, bf16[160,1024]{1,0:T(8,128)(2,1)S(1)}, u32[]{:S(2)}, u32[]{:S(2)}) collective-permute-start(bf16[160,1024]{1,0:T(8,128)(2,1)S(1)} %cast.12.refs_2_.refs_0_), channel_id=1, source_target_pairs={{0,1},{1,0},{2,3},{3,2},{4,5},{5,4},{6,7},{7,6},{8,9},{9,8},{10,11... | collective-permute-start | bytes 983048 | tf_op jit(solution)/shard_map/ppermute | solution.py:670
  38.3 17.1 %collective-permute-start.11 = (bf16[160,1024]{1,0:T(8,128)(2,1)S(1)}, bf16[160,1024]{1,0:T(8,128)(2,1)S(1)}, u32[]{:S(2)}, u32[]{:S(2)}) collective-permute-start(bf16[160,1024]{1,0:T(8,128)(2,1)S(1)} %cast.12.refs_2_.refs_0_), channel_id=1, source_target_pairs={{0,2},{2,0},{1,3},{3,1},{4,6},{6,4},{5,7},{7,5},{8,10},{10,8},{9,1... | collective-permute-start | bytes 983048 | tf_op jit(solution)/shard_map/ppermute | solution.py:674
  39.9 14.6 %collective-permute-start.8 = (bf16[128,1024]{1,0:T(8,128)(2,1)S(1)}, bf16[128,1024]{1,0:T(8,128)(2,1)S(1)}, u32[]{:S(2)}, u32[]{:S(2)}) collective-permute-start(bf16[128,1024]{1,0:T(8,128)(2,1)S(1)} %cast.10.refs_1_.refs_0_), channel_id=1, source_target_pairs={{0,16},{4,20},{8,24},{12,28},{16,0},{20,4},{24,8},{28,12},{1,17},{... | collective-permute-start | bytes 786440 | tf_op jit(solution)/shard_map/ppermute | solution.py:605
  56.3 20.2 %collective-permute-start.17 = (bf16[256,1024]{1,0:T(8,128)(2,1)}, bf16[256,1024]{1,0:T(8,128)(2,1)}, u32[]{:S(2)}, u32[]{:S(2)}) collective-permute-start(bf16[256,1024]{1,0:T(8,128)(2,1)} %join.16.refs_1_.refs_0_), channel_id=1, source_target_pairs={{0,8},{4,12},{8,0},{12,4},{16,24},{20,28},{24,16},{28,20},{1,9},{5... | collective-permute-start | bytes 1572872 | tf_op jit(solution)/shard_map/ppermute | solution.py:605
  56.4 11.6 %collective-permute-start.14 = (bf16[160,1024]{1,0:T(8,128)(2,1)}, bf16[160,1024]{1,0:T(8,128)(2,1)}, u32[]{:S(2)}, u32[]{:S(2)}) collective-permute-start(bf16[160,1024]{1,0:T(8,128)(2,1)} %collective-permute-done.7.refs_3_.refs_0_.refs_6_), channel_id=1, source_target_pairs={{0,1},{1,0},{2,3},{3,2},{4,5},{5,4},{6,7},{7,6},{8,9},{9,8},{10,11... | collective-permute-start | bytes 983048 | tf_op jit(solution)/shard_map/ppermute | solution.py:670
  57.5 15.2 %collective-permute-start.18 = (bf16[160,1024]{1,0:T(8,128)(2,1)}, bf16[160,1024]{1,0:T(8,128)(2,1)}, u32[]{:S(2)}, u32[]{:S(2)}) collective-permute-start(bf16[160,1024]{1,0:T(8,128)(2,1)} %cast.13.refs_4_.refs_0_.refs_2_), channel_id=1, source_target_pairs={{0,2},{2,0},{1,3},{3,1},{4,6},{6,4},{5,7},{7,5},{8,10},{10,8},{9,1... | collective-permute-start | bytes 983048 | tf_op jit(solution)/shard_map/ppermute | solution.py:674
  58.1 14.6 %collective-permute-start.15 = (bf16[512,256]{1,0:T(8,128)(2,1)S(1)}, bf16[512,256]{1,0:T(8,128)(2,1)S(1)}, u32[]{:S(2)}, u32[]{:S(2)}) collective-permute-start(bf16[512,256]{1,0:T(8,128)(2,1)S(1)} %join.15.refs_2_.refs_1_), channel_id=1, source_target_pairs={{0,4},{4,0},{8,12},{12,8},{16,20},{20,16},{24,28},{28,24},{1,5},{5... | collective-permute-start | bytes 786440 | tf_op jit(solution)/shard_map/ppermute | solution.py:605
  58.7 19.2 %collective-permute-start.16 = (bf16[128,1024]{1,0:T(8,128)(2,1)}, bf16[128,1024]{1,0:T(8,128)(2,1)}, u32[]{:S(2)}, u32[]{:S(2)}) collective-permute-start(bf16[128,1024]{1,0:T(8,128)(2,1)} %cast.11.refs_2_.refs_0_), channel_id=1, source_target_pairs={{0,16},{4,20},{8,24},{12,28},{16,0},{20,4},{24,8},{28,12},{1,17},{... | collective-permute-start | bytes 786440 | tf_op jit(solution)/shard_map/ppermute | solution.py:605
  80.3 13.9 %collective-permute-start.22 = (bf16[256,1024]{1,0:T(8,128)(2,1)S(1)}, bf16[256,1024]{1,0:T(8,128)(2,1)S(1)}, u32[]{:S(2)}, u32[]{:S(2)}) collective-permute-start(bf16[256,1024]{1,0:T(8,128)(2,1)S(1)} %join.18.refs_3_.refs_0_), channel_id=1, source_target_pairs={{0,8},{4,12},{8,0},{12,4},{16,24},{20,28},{24,16},{28,20},{1,9},{5... | collective-permute-start | bytes 1572872 | tf_op jit(solution)/shard_map/ppermute | solution.py:605
  83.0 11.3 %collective-permute-start.21 = (bf16[160,1024]{1,0:T(8,128)(2,1)S(1)}, bf16[160,1024]{1,0:T(8,128)(2,1)S(1)}, u32[]{:S(2)}, u32[]{:S(2)}) collective-permute-start(bf16[160,1024]{1,0:T(8,128)(2,1)S(1)} %add.146.refs_2_), channel_id=1, source_target_pairs={{0,2},{2,0},{1,3},{3,1},{4,6},{6,4},{5,7},{7,5},{8,10},{10,8},{9,1... | collective-permute-start | bytes 983048 | tf_op jit(solution)/shard_map/ppermute | solution.py:674
  95.2 27.1 %collective-permute-start.26 = (bf16[512,1024]{1,0:T(8,128)(2,1)S(1)}, bf16[512,1024]{1,0:T(8,128)(2,1)S(1)}, u32[]{:S(2)}, u32[]{:S(2)}) collective-permute-start(bf16[512,1024]{1,0:T(8,128)(2,1)S(1)} %join.17.refs_2_.refs_1_), channel_id=1, source_target_pairs={{0,4},{4,0},{8,12},{12,8},{16,20},{20,16},{24,28},{28,24},{1,5},{5... | collective-permute-start | bytes 3145736 | tf_op jit(solution)/shard_map/ppermute | solution.py:605
  95.7 47.2 %collective-permute-start.30 = (bf16[512,1024]{1,0:T(8,128)(2,1)S(1)}, bf16[512,1024]{1,0:T(8,128)(2,1)S(1)}, u32[]{:S(2)}, u32[]{:S(2)}) collective-permute-start(bf16[512,1024]{1,0:T(8,128)(2,1)S(1)} %join.19.refs_4_.refs_1_.refs_2_), channel_id=1, source_target_pairs={{0,4},{4,0},{8,12},{12,8},{16,20},{20,16},{24,28},{28,24},{1,5},{5... | collective-permute-start | bytes 3145736 | tf_op jit(solution)/shard_map/ppermute | solution.py:605
  97.3 14.0 %collective-permute-start.27 = (bf16[128,1024]{1,0:T(8,128)(2,1)S(1)}, bf16[128,1024]{1,0:T(8,128)(2,1)S(1)}, u32[]{:S(2)}, u32[]{:S(2)}) collective-permute-start(bf16[128,1024]{1,0:T(8,128)(2,1)S(1)} %cast.14.refs_2_.refs_0_), channel_id=1, source_target_pairs={{0,16},{4,20},{8,24},{12,28},{16,0},{20,4},{24,8},{28,12},{1,17},{... | collective-permute-start | bytes 786440 | tf_op jit(solution)/shard_map/ppermute | solution.py:605
  111.3 11.0 %collective-permute-start.34 = (bf16[160,1024]{1,0:T(8,128)(2,1)S(1)}, bf16[160,1024]{1,0:T(8,128)(2,1)S(1)}, u32[]{:S(2)}, u32[]{:S(2)}) collective-permute-start(bf16[160,1024]{1,0:T(8,128)(2,1)S(1)} %get-tuple-element.227.refs_2_.refs_0_), channel_id=1, source_target_pairs={{0,2},{2,0},{1,3},{3,1},{4,6},{6,4},{5,7},{7,5},{8,10},{10,8},{9,1... | collective-permute-start | bytes 983048 | tf_op jit(solution)/shard_map/ppermute | solution.py:674
  112.9 13.6 %collective-permute-start.33 = (bf16[256,1024]{1,0:T(8,128)(2,1)S(1)}, bf16[256,1024]{1,0:T(8,128)(2,1)S(1)}, u32[]{:S(2)}, u32[]{:S(2)}) collective-permute-start(bf16[256,1024]{1,0:T(8,128)(2,1)S(1)} %join.20.refs_4_.refs_0_), channel_id=1, source_target_pairs={{0,8},{4,12},{8,0},{12,4},{16,24},{20,28},{24,16},{28,20},{1,9},{5... | collective-permute-start | bytes 1572872 | tf_op jit(solution)/shard_map/ppermute | solution.py:605
  115.7 10.8 %collective-permute-start.32 = (bf16[160,1024]{1,0:T(8,128)(2,1)S(1)}, bf16[160,1024]{1,0:T(8,128)(2,1)S(1)}, u32[]{:S(2)}, u32[]{:S(2)}) collective-permute-start(bf16[160,1024]{1,0:T(8,128)(2,1)S(1)} %collective-permute-done.31.refs_3_.refs_0_.refs_4_), channel_id=1, source_target_pairs={{0,1},{1,0},{2,3},{3,2},{4,5},{5,4},{6,7},{7,6},{8,9},{9,8},{10,11... | collective-permute-start | bytes 983048 | tf_op jit(solution)/shard_map/ppermute | solution.py:670
  145.4 25.8 %collective-permute-start.39 = (bf16[128,2048]{1,0:T(8,128)(2,1)S(1)}, bf16[128,2048]{1,0:T(8,128)(2,1)S(1)}, u32[]{:S(2)}, u32[]{:S(2)}) collective-permute-start(bf16[128,2048]{1,0:T(8,128)(2,1)S(1)} %cast.15.refs_4_.refs_0_), channel_id=1, source_target_pairs={{0,16},{4,20},{8,24},{12,28},{16,0},{20,4},{24,8},{28,12},{1,17},{... | collective-permute-start | bytes 1572872 | tf_op jit(solution)/shard_map/ppermute | solution.py:605
  149.1 22.2 %collective-permute-start.38 = (bf16[160,1024]{1,0:T(8,128)(2,1)S(1)}, bf16[160,1024]{1,0:T(8,128)(2,1)S(1)}, u32[]{:S(2)}, u32[]{:S(2)}) collective-permute-start(bf16[160,1024]{1,0:T(8,128)(2,1)S(1)} %add.150.refs_2_), channel_id=1, source_target_pairs={{0,2},{2,0},{1,3},{3,1},{4,6},{6,4},{5,7},{7,5},{8,10},{10,8},{9,1... | collective-permute-start | bytes 983048 | tf_op jit(solution)/shard_map/ppermute | solution.py:674
  150.6 45.2 %collective-permute-start.43 = (bf16[512,1024]{1,0:T(8,128)(2,1)S(1)}, bf16[512,1024]{1,0:T(8,128)(2,1)S(1)}, u32[]{:S(2)}, u32[]{:S(2)}) collective-permute-start(bf16[512,1024]{1,0:T(8,128)(2,1)S(1)} %join.21.refs_4_.refs_2_.refs_1_), channel_id=1, source_target_pairs={{0,4},{4,0},{8,12},{12,8},{16,20},{20,16},{24,28},{28,24},{1,5},{5... | collective-permute-start | bytes 3145736 | tf_op jit(solution)/shard_map/ppermute | solution.py:605
  171.2 27.5 %collective-permute-start.50 = (bf16[256,2048]{1,0:T(8,128)(2,1)S(1)}, bf16[256,2048]{1,0:T(8,128)(2,1)S(1)}, u32[]{:S(2)}, u32[]{:S(2)}) collective-permute-start(bf16[256,2048]{1,0:T(8,128)(2,1)S(1)} %join.22.refs_4_.refs_0_), channel_id=1, source_target_pairs={{0,8},{4,12},{8,0},{12,4},{16,24},{20,28},{24,16},{28,20},{1,9},{5... | collective-permute-start | bytes 3145736 | tf_op jit(solution)/shard_map/ppermute | solution.py:605
  173.3 16.0 %collective-permute-start.46 = (bf16[160,1024]{1,0:T(8,128)(2,1)S(1)}, bf16[160,1024]{1,0:T(8,128)(2,1)S(1)}, u32[]{:S(2)}, u32[]{:S(2)}) collective-permute-start(bf16[160,1024]{1,0:T(8,128)(2,1)S(1)} %get-tuple-element.245.refs_4_.refs_0_), channel_id=1, source_target_pairs={{0,2},{2,0},{1,3},{3,1},{4,6},{6,4},{5,7},{7,5},{8,10},{10,8},{9,1... | collective-permute-start | bytes 983048 | tf_op jit(solution)/shard_map/ppermute | solution.py:674
  182.6 13.3 %collective-permute-start.48 = (bf16[160,1024]{1,0:T(8,128)(2,1)S(1)}, bf16[160,1024]{1,0:T(8,128)(2,1)S(1)}, u32[]{:S(2)}, u32[]{:S(2)}) collective-permute-start(bf16[160,1024]{1,0:T(8,128)(2,1)S(1)} %get-tuple-element.247.refs_4_.refs_0_.refs_2_), channel_id=1, source_target_pairs={{0,2},{2,0},{1,3},{3,1},{4,6},{6,4},{5,7},{7,5},{8,10},{10,8},{9,1... | collective-permute-start | bytes 983048 | tf_op jit(solution)/shard_map/ppermute | solution.py:674
  184.1 11.7 %collective-permute-start.45 = (bf16[160,1024]{1,0:T(8,128)(2,1)S(1)}, bf16[160,1024]{1,0:T(8,128)(2,1)S(1)}, u32[]{:S(2)}, u32[]{:S(2)}) collective-permute-start(bf16[160,1024]{1,0:T(8,128)(2,1)S(1)} %get-tuple-element.247.refs_4_.refs_0_.refs_2_), channel_id=1, source_target_pairs={{0,1},{1,0},{2,3},{3,2},{4,5},{5,4},{6,7},{7,6},{8,9},{9,8},{10,11... | collective-permute-start | bytes 983048 | tf_op jit(solution)/shard_map/ppermute | solution.py:670
  203.9 37.4 %collective-permute-start.57 = (bf16[512,1024]{1,0:T(8,128)(2,1)S(1)}, bf16[512,1024]{1,0:T(8,128)(2,1)S(1)}, u32[]{:S(2)}, u32[]{:S(2)}) collective-permute-start(bf16[512,1024]{1,0:T(8,128)(2,1)S(1)} %get-tuple-element.263.refs_2_.refs_1_), channel_id=1, source_target_pairs={{0,4},{4,0},{8,12},{12,8},{16,20},{20,16},{24,28},{28,24},{1,5},{5... | collective-permute-start | bytes 3145736 | tf_op jit(solution)/shard_map/ppermute | solution.py:605
  208.5 43.5 %collective-permute-start.60 = (bf16[512,1024]{1,0:T(8,128)(2,1)S(1)}, bf16[512,1024]{1,0:T(8,128)(2,1)S(1)}, u32[]{:S(2)}, u32[]{:S(2)}) collective-permute-start(bf16[512,1024]{1,0:T(8,128)(2,1)S(1)} %get-tuple-element.248.refs_6_.refs_2_.refs_1_), channel_id=1, source_target_pairs={{0,4},{4,0},{8,12},{12,8},{16,20},{20,16},{24,28},{28,24},{1,5},{5... | collective-permute-start | bytes 3145736 | tf_op jit(solution)/shard_map/ppermute | solution.py:605
  218.7 16.0 %collective-permute-start.61 = (bf16[160,1024]{1,0:T(8,128)(2,1)S(1)}, bf16[160,1024]{1,0:T(8,128)(2,1)S(1)}, u32[]{:S(2)}, u32[]{:S(2)}) collective-permute-start(bf16[160,1024]{1,0:T(8,128)(2,1)S(1)} %get-tuple-element.262.refs_4_.refs_0_), channel_id=1, source_target_pairs={{0,2},{2,0},{1,3},{3,1},{4,6},{6,4},{5,7},{7,5},{8,10},{10,8},{9,1... | collective-permute-start | bytes 983048 | tf_op jit(solution)/shard_map/ppermute | solution.py:674
  228.0 13.3 %collective-permute-start.63 = (bf16[160,1024]{1,0:T(8,128)(2,1)S(1)}, bf16[160,1024]{1,0:T(8,128)(2,1)S(1)}, u32[]{:S(2)}, u32[]{:S(2)}) collective-permute-start(bf16[160,1024]{1,0:T(8,128)(2,1)S(1)} %get-tuple-element.265.refs_4_.refs_0_.refs_2_), channel_id=1, source_target_pairs={{0,2},{2,0},{1,3},{3,1},{4,6},{6,4},{5,7},{7,5},{8,10},{10,8},{9,1... | collective-permute-start | bytes 983048 | tf_op jit(solution)/shard_map/ppermute | solution.py:674
  229.5 12.2 %collective-permute-start.59 = (bf16[160,1024]{1,0:T(8,128)(2,1)S(1)}, bf16[160,1024]{1,0:T(8,128)(2,1)S(1)}, u32[]{:S(2)}, u32[]{:S(2)}) collective-permute-start(bf16[160,1024]{1,0:T(8,128)(2,1)S(1)} %get-tuple-element.265.refs_4_.refs_0_.refs_2_), channel_id=1, source_target_pairs={{0,1},{1,0},{2,3},{3,2},{4,5},{5,4},{6,7},{7,6},{8,9},{9,8},{10,11... | collective-permute-start | bytes 983048 | tf_op jit(solution)/shard_map/ppermute | solution.py:670
  241.3 13.4 %collective-permute-start.65 = (bf16[160,1024]{1,0:T(8,128)(2,1)S(1)}, bf16[160,1024]{1,0:T(8,128)(2,1)S(1)}, u32[]{:S(2)}, u32[]{:S(2)}) collective-permute-start(bf16[160,1024]{1,0:T(8,128)(2,1)S(1)} %copy-done.41), channel_id=1, source_target_pairs={{0,1},{1,0},{2,3},{3,2},{4,5},{5,4},{6,7},{7,6},{8,9},{9,8},{10,11... | collective-permute-start | bytes 983048 | tf_op jit(solution)/shard_map/ppermute | solution.py:670
  241.8 13.7 %collective-permute-start.66 = (bf16[160,1024]{1,0:T(8,128)(2,1)}, bf16[160,1024]{1,0:T(8,128)(2,1)S(1)}, u32[]{:S(2)}, u32[]{:S(2)}) collective-permute-start(bf16[160,1024]{1,0:T(8,128)(2,1)} %collective-permute-done.18.refs_3_.refs_0_.refs_6_), channel_id=1, source_target_pairs={{0,1},{1,0},{2,3},{3,2},{4,5},{5,4},{6,7},{7,6},{8,9},{9,8},{10,11... | collective-permute-start | bytes 983048 | tf_op jit(solution)/shard_map/ppermute | solution.py:670
  270.2 32.3 %collective-permute-start.79 = (bf16[512,1024]{1,0:T(8,128)(2,1)}, bf16[512,1024]{1,0:T(8,128)(2,1)S(1)}, u32[]{:S(2)}, u32[]{:S(2)}) collective-permute-start(bf16[512,1024]{1,0:T(8,128)(2,1)} %get-tuple-element.282.refs_5_), channel_id=1, source_target_pairs={{0,4},{4,0},{8,12},{12,8},{16,20},{20,16},{24,28},{28,24},{1,5},{5... | collective-permute-start | bytes 3145736 | tf_op jit(solution)/shard_map/ppermute | solution.py:605
  277.9 16.0 %collective-permute-start.75 = (bf16[160,1024]{1,0:T(8,128)(2,1)S(1)}, bf16[160,1024]{1,0:T(8,128)(2,1)S(1)}, u32[]{:S(2)}, u32[]{:S(2)}) collective-permute-start(bf16[160,1024]{1,0:T(8,128)(2,1)S(1)} %get-tuple-element.284.refs_12_.refs_0_), channel_id=1, source_target_pairs={{0,2},{2,0},{1,3},{3,1},{4,6},{6,4},{5,7},{7,5},{8,10},{10,8},{9,1... | collective-permute-start | bytes 983048 | tf_op jit(solution)/shard_map/ppermute | solution.py:674
  287.5 13.0 %collective-permute-start.77 = (bf16[160,1024]{1,0:T(8,128)(2,1)S(1)}, bf16[160,1024]{1,0:T(8,128)(2,1)S(1)}, u32[]{:S(2)}, u32[]{:S(2)}) collective-permute-start(bf16[160,1024]{1,0:T(8,128)(2,1)S(1)} %get-tuple-element.287.refs_4_.refs_0_.refs_14_), channel_id=1, source_target_pairs={{0,2},{2,0},{1,3},{3,1},{4,6},{6,4},{5,7},{7,5},{8,10},{10,8},{9,1... | collective-permute-start | bytes 983048 | tf_op jit(solution)/shard_map/ppermute | solution.py:674
  289.1 29.0 %collective-permute-start.83 = (bf16[512,1024]{1,0:T(8,128)(2,1)S(1)}, bf16[512,1024]{1,0:T(8,128)(2,1)S(1)}, u32[]{:S(2)}, u32[]{:S(2)}) collective-permute-start(bf16[512,1024]{1,0:T(8,128)(2,1)S(1)} %get-tuple-element.286.refs_5_), channel_id=1, source_target_pairs={{0,4},{4,0},{8,12},{12,8},{16,20},{20,16},{24,28},{28,24},{1,5},{5... | collective-permute-start | bytes 3145736 | tf_op jit(solution)/shard_map/ppermute | solution.py:605
  289.6 10.9 %collective-permute-start.74 = (bf16[160,1024]{1,0:T(8,128)(2,1)S(1)}, bf16[160,1024]{1,0:T(8,128)(2,1)S(1)}, u32[]{:S(2)}, u32[]{:S(2)}) collective-permute-start(bf16[160,1024]{1,0:T(8,128)(2,1)S(1)} %get-tuple-element.287.refs_4_.refs_0_.refs_14_), channel_id=1, source_target_pairs={{0,1},{1,0},{2,3},{3,2},{4,5},{5,4},{6,7},{7,6},{8,9},{9,8},{10,11... | collective-permute-start | bytes 983048 | tf_op jit(solution)/shard_map/ppermute | solution.py:670
  322.4 29.9 %collective-permute-start.94 = (bf16[512,1024]{1,0:T(8,128)(2,1)S(1)}, bf16[512,1024]{1,0:T(8,128)(2,1)S(1)}, u32[]{:S(2)}, u32[]{:S(2)}) collective-permute-start(bf16[512,1024]{1,0:T(8,128)(2,1)S(1)} %get-tuple-element.303.refs_5_), channel_id=1, source_target_pairs={{0,4},{4,0},{8,12},{12,8},{16,20},{20,16},{24,28},{28,24},{1,5},{5... | collective-permute-start | bytes 3145736 | tf_op jit(solution)/shard_map/ppermute | solution.py:605
  328.0 16.0 %collective-permute-start.89 = (bf16[160,1024]{1,0:T(8,128)(2,1)S(1)}, bf16[160,1024]{1,0:T(8,128)(2,1)S(1)}, u32[]{:S(2)}, u32[]{:S(2)}) collective-permute-start(bf16[160,1024]{1,0:T(8,128)(2,1)S(1)} %get-tuple-element.304.refs_5_.refs_0_), channel_id=1, source_target_pairs={{0,2},{2,0},{1,3},{3,1},{4,6},{6,4},{5,7},{7,5},{8,10},{10,8},{9,1... | collective-permute-start | bytes 983048 | tf_op jit(solution)/shard_map/ppermute | solution.py:674
  337.5 13.0 %collective-permute-start.91 = (bf16[160,1024]{1,0:T(8,128)(2,1)S(1)}, bf16[160,1024]{1,0:T(8,128)(2,1)S(1)}, u32[]{:S(2)}, u32[]{:S(2)}) collective-permute-start(bf16[160,1024]{1,0:T(8,128)(2,1)S(1)} %get-tuple-element.306.refs_5_.refs_0_.refs_2_), channel_id=1, source_target_pairs={{0,2},{2,0},{1,3},{3,1},{4,6},{6,4},{5,7},{7,5},{8,10},{10,8},{9,1... | collective-permute-start | bytes 983048 | tf_op jit(solution)/shard_map/ppermute | solution.py:674
  339.1 25.4 %collective-permute-start.93 = (bf16[256,2048]{1,0:T(8,128)(2,1)S(1)}, bf16[256,2048]{1,0:T(8,128)(2,1)S(1)}, u32[]{:S(2)}, u32[]{:S(2)}) collective-permute-start(bf16[256,2048]{1,0:T(8,128)(2,1)S(1)} %get-tuple-element.302.refs_24_), channel_id=1, source_target_pairs={{0,8},{4,12},{8,0},{12,4},{16,24},{20,28},{24,16},{28,20},{1,9},{5... | collective-permute-start | bytes 3145736 | tf_op jit(solution)/shard_map/ppermute | solution.py:605
  362.3 14.0 %collective-permute-start.102 = (bf16[256,1024]{1,0:T(8,128)(2,1)S(1)}, bf16[256,1024]{1,0:T(8,128)(2,1)S(1)}, u32[]{:S(2)}, u32[]{:S(2)}) collective-permute-start(bf16[256,1024]{1,0:T(8,128)(2,1)S(1)} %get-tuple-element.309.refs_5_), channel_id=1, source_target_pairs={{0,8},{4,12},{8,0},{12,4},{16,24},{20,28},{24,16},{28,20},{1,9},{5... | collective-permute-start | bytes 1572872 | tf_op jit(solution)/shard_map/ppermute | solution.py:605
  369.4 41.9 %collective-permute-start.99 = (bf16[512,1024]{1,0:T(8,128)(2,1)S(1)}, bf16[512,1024]{1,0:T(8,128)(2,1)S(1)}, u32[]{:S(2)}, u32[]{:S(2)}) collective-permute-start(bf16[512,1024]{1,0:T(8,128)(2,1)S(1)} %get-tuple-element.320.refs_5_), channel_id=1, source_target_pairs={{0,4},{4,0},{8,12},{12,8},{16,20},{20,16},{24,28},{28,24},{1,5},{5... | collective-permute-start | bytes 3145736 | tf_op jit(solution)/shard_map/ppermute | solution.py:605
  372.8 16.0 %collective-permute-start.107 = (bf16[160,1024]{1,0:T(8,128)(2,1)S(1)}, bf16[160,1024]{1,0:T(8,128)(2,1)S(1)}, u32[]{:S(2)}, u32[]{:S(2)}) collective-permute-start(bf16[160,1024]{1,0:T(8,128)(2,1)S(1)} %get-tuple-element.325.refs_2_.refs_0_.refs_12_), channel_id=1, source_target_pairs={{0,2},{2,0},{1,3},{3,1},{4,6},{6,4},{5,7},{7,5},{8,10},{10,8},{9,1... | collective-permute-start | bytes 983048 | tf_op jit(solution)/shard_map/ppermute | solution.py:674
  382.3 13.0 %collective-permute-start.105 = (bf16[160,1024]{1,0:T(8,128)(2,1)S(1)}, bf16[160,1024]{1,0:T(8,128)(2,1)S(1)}, u32[]{:S(2)}, u32[]{:S(2)}) collective-permute-start(bf16[160,1024]{1,0:T(8,128)(2,1)S(1)} %get-tuple-element.327.refs_12_.refs_0_.refs_14_), channel_id=1, source_target_pairs={{0,2},{2,0},{1,3},{3,1},{4,6},{6,4},{5,7},{7,5},{8,10},{10,8},{9,1... | collective-permute-start | bytes 983048 | tf_op jit(solution)/shard_map/ppermute | solution.py:674
  383.9 24.9 %collective-permute-start.100 = (bf16[128,2048]{1,0:T(8,128)(2,1)S(1)}, bf16[128,2048]{1,0:T(8,128)(2,1)S(1)}, u32[]{:S(2)}, u32[]{:S(2)}) collective-permute-start(bf16[128,2048]{1,0:T(8,128)(2,1)S(1)} %get-tuple-element.318.refs_12_), channel_id=1, source_target_pairs={{0,16},{4,20},{8,24},{12,28},{16,0},{20,4},{24,8},{28,12},{1,17},{... | collective-permute-start | bytes 1572872 | tf_op jit(solution)/shard_map/ppermute | solution.py:605
  388.8 11.3 %collective-permute-start.108 = (bf16[160,1024]{1,0:T(8,128)(2,1)S(1)}, bf16[160,1024]{1,0:T(8,128)(2,1)S(1)}, u32[]{:S(2)}, u32[]{:S(2)}) collective-permute-start(bf16[160,1024]{1,0:T(8,128)(2,1)S(1)} %collective-permute-done.107.refs_0_.refs_5_.refs_16_), channel_id=1, source_target_pairs={{0,1},{1,0},{2,3},{3,2},{4,5},{5,4},{6,7},{7,6},{8,9},{9,8},{10,11... | collective-permute-start | bytes 983048 | tf_op jit(solution)/shard_map/ppermute | solution.py:670
  398.3 52.2 %collective-permute-start.117 = (bf16[512,1024]{1,0:T(8,128)(2,1)S(1)}, bf16[512,1024]{1,0:T(8,128)(2,1)S(1)}, u32[]{:S(2)}, u32[]{:S(2)}) collective-permute-start(bf16[512,1024]{1,0:T(8,128)(2,1)S(1)} %get-tuple-element.328.refs_4_), channel_id=1, source_target_pairs={{0,4},{4,0},{8,12},{12,8},{16,20},{20,16},{24,28},{28,24},{1,5},{5... | collective-permute-start | bytes 3145736 | tf_op jit(solution)/shard_map/ppermute | solution.py:605
  421.0 19.9 %collective-permute-start.110 = (bf16[256,1024]{1,0:T(8,128)(2,1)S(1)}, bf16[256,1024]{1,0:T(8,128)(2,1)S(1)}, u32[]{:S(2)}, u32[]{:S(2)}) collective-permute-start(bf16[256,1024]{1,0:T(8,128)(2,1)S(1)} %get-tuple-element.331.refs_10_), channel_id=1, source_target_pairs={{0,8},{4,12},{8,0},{12,4},{16,24},{20,28},{24,16},{28,20},{1,9},{5... | collective-permute-start | bytes 1572872 | tf_op jit(solution)/shard_map/ppermute | solution.py:605
  424.4 13.9 %collective-permute-start.111 = (bf16[128,1024]{1,0:T(8,128)(2,1)S(1)}, bf16[128,1024]{1,0:T(8,128)(2,1)S(1)}, u32[]{:S(2)}, u32[]{:S(2)}) collective-permute-start(bf16[128,1024]{1,0:T(8,128)(2,1)S(1)} %get-tuple-element.326.refs_5_), channel_id=1, source_target_pairs={{0,16},{4,20},{8,24},{12,28},{16,0},{20,4},{24,8},{28,12},{1,17},{... | collective-permute-start | bytes 786440 | tf_op jit(solution)/shard_map/ppermute | solution.py:605
  425.9 23.4 %collective-permute-start.119 = (bf16[160,1024]{1,0:T(8,128)(2,1)S(1)}, bf16[160,1024]{1,0:T(8,128)(2,1)S(1)}, u32[]{:S(2)}, u32[]{:S(2)}) collective-permute-start(bf16[160,1024]{1,0:T(8,128)(2,1)S(1)} %add.170.refs_2_), channel_id=1, source_target_pairs={{0,2},{2,0},{1,3},{3,1},{4,6},{6,4},{5,7},{7,5},{8,10},{10,8},{9,1... | collective-permute-start | bytes 983048 | tf_op jit(solution)/shard_map/ppermute | solution.py:674
  426.5 23.3 %collective-permute-start.118 = (bf16[160,1024]{1,0:T(8,128)(2,1)S(1)}, bf16[160,1024]{1,0:T(8,128)(2,1)S(1)}, u32[]{:S(2)}, u32[]{:S(2)}) collective-permute-start(bf16[160,1024]{1,0:T(8,128)(2,1)S(1)} %add.172.refs_2_), channel_id=1, source_target_pairs={{0,2},{2,0},{1,3},{3,1},{4,6},{6,4},{5,7},{7,5},{8,10},{10,8},{9,1... | collective-permute-start | bytes 983048 | tf_op jit(solution)/shard_map/ppermute | solution.py:674
  441.1 15.1 %collective-permute-start.116 = (bf16[128,1024]{1,0:T(8,128)(2,1)S(1)}, bf16[128,1024]{1,0:T(8,128)(2,1)S(1)}, u32[]{:S(2)}, u32[]{:S(2)}) collective-permute-start(bf16[128,1024]{1,0:T(8,128)(2,1)S(1)} %get-tuple-element.347.refs_24_), channel_id=1, source_target_pairs={{0,16},{4,20},{8,24},{12,28},{16,0},{20,4},{24,8},{28,12},{1,17},{... | collective-permute-start | bytes 786440 | tf_op jit(solution)/shard_map/ppermute | solution.py:605
  448.7 27.1 %collective-permute-start.126 = (bf16[512,1024]{1,0:T(8,128)(2,1)S(1)}, bf16[512,1024]{1,0:T(8,128)(2,1)S(1)}, u32[]{:S(2)}, u32[]{:S(2)}) collective-permute-start(bf16[512,1024]{1,0:T(8,128)(2,1)S(1)} %get-tuple-element.354.refs_5_), channel_id=1, source_target_pairs={{0,4},{4,0},{8,12},{12,8},{16,20},{20,16},{24,28},{28,24},{1,5},{5... | collective-permute-start | bytes 3145736 | tf_op jit(solution)/shard_map/ppermute | solution.py:605
  459.9 14.3 %collective-permute-start.127 = (bf16[256,1024]{1,0:T(8,128)(2,1)S(1)}, bf16[256,1024]{1,0:T(8,128)(2,1)S(1)}, u32[]{:S(2)}, u32[]{:S(2)}) collective-permute-start(bf16[256,1024]{1,0:T(8,128)(2,1)S(1)} %get-tuple-element.357.refs_9_), channel_id=1, source_target_pairs={{0,8},{4,12},{8,0},{12,4},{16,24},{20,28},{24,16},{28,20},{1,9},{5... | collective-permute-start | bytes 1572872 | tf_op jit(solution)/shard_map/ppermute | solution.py:605
  462.7 15.2 %collective-permute-start.122 = (bf16[160,1024]{1,0:T(8,128)(2,1)S(1)}, bf16[160,1024]{1,0:T(8,128)(2,1)S(1)}, u32[]{:S(2)}, u32[]{:S(2)}) collective-permute-start(bf16[160,1024]{1,0:T(8,128)(2,1)S(1)} %add.174.refs_2_), channel_id=1, source_target_pairs={{0,2},{2,0},{1,3},{3,1},{4,6},{6,4},{5,7},{7,5},{8,10},{10,8},{9,1... | collective-permute-start | bytes 983048 | tf_op jit(solution)/shard_map/ppermute | solution.py:674
  464.4 15.3 %collective-permute-start.125 = (bf16[160,1024]{1,0:T(8,128)(2,1)S(1)}, bf16[160,1024]{1,0:T(8,128)(2,1)S(1)}, u32[]{:S(2)}, u32[]{:S(2)}) collective-permute-start(bf16[160,1024]{1,0:T(8,128)(2,1)S(1)} %add.176.refs_2_), channel_id=1, source_target_pairs={{0,2},{2,0},{1,3},{3,1},{4,6},{6,4},{5,7},{7,5},{8,10},{10,8},{9,1... | collective-permute-start | bytes 983048 | tf_op jit(solution)/shard_map/ppermute | solution.py:674
  474.9 37.8 %collective-permute-start.130 = (bf16[128,1024]{1,0:T(8,128)(2,1)}, bf16[128,1024]{1,0:T(8,128)(2,1)}, u32[]{:S(2)}, u32[]{:S(2)}) collective-permute-start(bf16[128,1024]{1,0:T(8,128)(2,1)} %get-tuple-element.379.refs_2_), channel_id=1, source_target_pairs={{0,16},{4,20},{8,24},{12,28},{16,0},{20,4},{24,8},{28,12},{1,17},{... | collective-permute-start | bytes 786440 | tf_op jit(solution)/shard_map/ppermute | solution.py:605
  476.0 19.1 %collective-permute-start.128 = (bf16[256,1024]{1,0:T(8,128)(2,1)S(1)}, bf16[256,1024]{1,0:T(8,128)(2,1)S(1)}, u32[]{:S(2)}, u32[]{:S(2)}) collective-permute-start(bf16[256,1024]{1,0:T(8,128)(2,1)S(1)} %get-tuple-element.380.refs_3_), channel_id=1, source_target_pairs={{0,8},{4,12},{8,0},{12,4},{16,24},{20,28},{24,16},{28,20},{1,9},{5... | collective-permute-start | bytes 1572872 | tf_op jit(solution)/shard_map/ppermute | solution.py:605
  478.1 19.7 %collective-permute-start.137 = (f32[8,1024]{1,0:T(8,128)S(1)}, f32[8,1024]{1,0:T(8,128)S(1)}, u32[]{:S(2)}, u32[]{:S(2)}) collective-permute-start(f32[8,1024]{1,0:T(8,128)S(1)} %add.118), channel_id=1, source_target_pairs={{0,2},{2,0},{1,3},{3,1},{4,6},{6,4},{5,7},{7,5},{8,10},{10,8},{9,1... | collective-permute-start | bytes 98312 | tf_op jit(solution)/shard_map/ppermute | solution.py:674
  497.2 24.9 %collective-permute-start.129 = (bf16[128,1024]{1,0:T(8,128)(2,1)}, bf16[128,1024]{1,0:T(8,128)(2,1)}, u32[]{:S(2)}, u32[]{:S(2)}) collective-permute-start(bf16[128,1024]{1,0:T(8,128)(2,1)} %get-tuple-element.383.refs_9_), channel_id=1, source_target_pairs={{0,16},{4,20},{8,24},{12,28},{16,0},{20,4},{24,8},{28,12},{1,17},{... | collective-permute-start | bytes 786440 | tf_op jit(solution)/shard_map/ppermute | solution.py:605
  (194 other events, 1413.2 us)

commit v3 on v2

v3 whole, which is shorter than its diff:
```python
import functools

import jax
import jax.numpy as jnp
from jax import lax
from jax.experimental import pallas as pl
from jax.experimental.pallas import tpu as pltpu
from jax.sharding import PartitionSpec as P

D = 1024
HEADS = 16
HD = 64
FF = 4096
STEP = 10


EPS_NORM = 1e-06
BETA_ONE = 0.9
BETA_TWO = 0.999
ADAM_EPS = 1e-06
WEIGHT_DECAY = 0.01
LEARN_RATE = 0.5
MASKED = -1000000000.0

QUERIES = 128
REACH = 64
WINDOW = QUERIES + 2 * REACH

NT = (((1,), (1,)), ((), ()))
TN = (((0,), (0,)), ((), ()))


VMEM_SPEC = pl.BlockSpec(memory_space=pltpu.VMEM)
SMEM_SPEC = pl.BlockSpec(memory_space=pltpu.SMEM)
ANY_SPEC = pl.BlockSpec(memory_space=pl.ANY)


def struct(shape, kind=jnp.bfloat16):
    return jax.ShapeDtypeStruct(shape, kind)


TOKEN = struct((8, 128), jnp.float32)


class Order:
    def __init__(self):
        self.token, self.earlier = None, []

    def settle(self, value):
        self.earlier = self.earlier + [value]
        return value

    def mark(self):
        self("mark", lambda: None, [], [], 2)

    def __call__(
        self, name, body, ins, outs, room, in_specs=None, out_specs=None, grid_spec=None, scratch=(), aliases=None
    ):
        before = [] if self.token is None else [self.token]
        extra = before + list(self.earlier)
        scalars = 0 if grid_spec is None else grid_spec[0]

        def wrapped(*refs):
            token = refs[len(ins) + len(extra) + len(outs)]
            token[...] = jnp.zeros(TOKEN.shape, TOKEN.dtype)
            refs = refs[: len(ins)] + refs[len(ins) + len(extra) :]
            return body(*refs[: len(ins) + len(outs)], *refs[len(ins) + len(outs) + 1 :])

        if grid_spec is None:
            token_spec = VMEM_SPEC
        else:
            token_spec = pl.BlockSpec(TOKEN.shape, lambda *grid: (0, 0))
        in_specs = (in_specs or [VMEM_SPEC] * len(ins)) + [token_spec] * len(before)
        in_specs = in_specs + [ANY_SPEC] * len(self.earlier)
        out_specs = (out_specs or [VMEM_SPEC] * len(outs)) + [token_spec]
        if grid_spec is None:
            places = dict(in_specs=in_specs, out_specs=out_specs, scratch_shapes=scratch)
        else:
            places = dict(
                grid_spec=pltpu.PrefetchScalarGridSpec(
                    num_scalar_prefetch=scalars,
                    grid=grid_spec[1],
                    in_specs=in_specs,
                    out_specs=out_specs,
                )
            )
        *result, self.token = pl.pallas_call(
            wrapped,
            out_shape=[*outs, TOKEN],
            **places,
            input_output_aliases=aliases or {},
            cost_estimate=pl.CostEstimate(flops=1, bytes_accessed=1, transcendentals=0),
            compiler_params=pltpu.CompilerParams(vmem_limit_bytes=room << 20),
            name=name,
        )(*ins, *extra)
        self.earlier = []
        return result


def add(run, here, far, kind, *more):
    body = functools.partial(sum_kernel, 2 + len(more))
    return run("add", body, [here, far, *more], [struct(here.shape, kind)], 4)[0]


def sum_kernel(count, *refs):
    total = refs[0][...].astype(jnp.float32)
    for ref in refs[1:count]:
        total = total + ref[...].astype(jnp.float32)
    refs[-1][...] = total.astype(refs[-1].dtype)


def add_halves_kernel(kept, first, second, out):
    half = first.shape[0]
    for here, part in ((slice(0, half), first), (slice(half, None), second)):
        total = kept[here, :].astype(jnp.float32) + part[...].astype(jnp.float32)
        out[here, :] = total.astype(out.dtype)


def add_halves(run, kept, parts, kind):
    return run("add", add_halves_kernel, [kept, *parts], [struct(kept.shape, kind)], 6)[0]


def cast_kernel(ref, out, first, second):
    low = ref[...].astype(out.dtype)
    out[...] = low
    first[...] = low[: first.shape[0]]
    second[...] = low[first.shape[0] :]


def cast(run, wide):
    rows, width = wide.shape
    outs = [struct((rows, width)), *[struct((rows // 2, width))] * 2]
    low, *parts = run("cast", cast_kernel, [wide], outs, 6)
    return low, parts


def block_kernel(ref, out):
    out[...] = ref[...].reshape(out.shape).astype(out.dtype)


def cast_blocks(run, weights, layer, first, last):
    rows, wide = weights.shape[2:]
    return run(
        "cast",
        block_kernel,
        [weights],
        [struct((rows, (last - first) * wide))],
        6,
        in_specs=[pl.BlockSpec((1, 1, rows, wide), lambda n: (layer, first + n, 0, 0))],
        out_specs=[pl.BlockSpec((rows, wide), lambda n: (0, n))],
        grid_spec=(0, (last - first,)),
    )[0]


def join_kernel(begin, here, far, out):
    rows = here.shape[0]
    columns = slice(begin, begin + out.shape[1])
    out[:rows, :] = here[:, columns]
    out[rows:, :] = far[:, columns]


def join(run, here, far, begin, width):
    outs = [struct((2 * here.shape[0], width))]
    return run("join", functools.partial(join_kernel, begin), [here, far], outs, 10)[0]


def adam_part(gradient, weight, first, second, decay):
    first_new = BETA_ONE * first + (1.0 - BETA_ONE) * gradient
    second_new = BETA_TWO * second + (1.0 - BETA_TWO) * gradient * gradient
    step_dir = (
        first_new
        / (1.0 - BETA_ONE**STEP)
        / (jnp.sqrt(second_new / (1.0 - BETA_TWO**STEP)) + ADAM_EPS)
        + decay * weight
    )
    return (first_new, second_new, step_dir)


def dot(left, right, dims=(((1,), (0,)), ((), ()))):
    return lax.dot_general(left, right, dims, preferred_element_type=jnp.float32)


def head_lanes(rows, width, value):
    lane_head = lax.broadcasted_iota(jnp.int32, (rows, width), 1) // HD
    return [
        jnp.where(lane_head == head, value, 0.0).astype(jnp.float32) for head in range(width // HD)
    ]


def block_shares(query_wide, keys_in, mask):
    heads_here = query_wide.shape[0] // QUERIES
    scores = dot(query_wide, keys_in, NT).reshape(heads_here, QUERIES, WINDOW)
    scores = jnp.where((mask > 0.5)[None], scores, MASKED)
    powered = jnp.exp(scores - jnp.max(scores, axis=-1, keepdims=True))
    shares = powered * (1.0 / jnp.sum(powered, axis=-1, keepdims=True))
    return shares.reshape(heads_here * QUERIES, WINDOW)


def fold_heads(wide, lanes):
    total = wide[:QUERIES] * lanes[0]
    for head in range(1, len(lanes)):
        total += wide[head * QUERIES : (head + 1) * QUERIES] * lanes[head]
    return total


def places_of(place_ref, pieces, rows):
    half = rows // 2
    found = []
    for piece in range(pieces):
        for core in range(2):
            block = jnp.bitwise_xor(place_ref[0], 2 * piece + core)
            found.append((piece, core * half, pl.multiple_of(block * half, 32)))
    return found


def in_token_order(place_ref, refs, store, start):
    rows = refs[0].shape[0]
    for piece, row, token in places_of(place_ref, len(refs), rows):
        store[pl.ds(token + start, rows // 2), :] = refs[piece][pl.ds(row, rows // 2), :]


def attend_kernel(pieces, place_ref, mask_ref, *refs):
    ins, outs, (all_in, all_out) = refs[:pieces], refs[pieces : 2 * pieces], refs[2 * pieces :]
    count, width = all_out.shape
    all_in[:REACH, :] = jnp.zeros((REACH, 3 * width), jnp.bfloat16)
    all_in[REACH + count :, :] = jnp.zeros((REACH, 3 * width), jnp.bfloat16)
    in_token_order(place_ref, ins, all_in, REACH)
    scaled = [lane.astype(jnp.bfloat16) for lane in head_lanes(QUERIES, width, HD ** (-0.5))]
    plain = head_lanes(QUERIES, width, 1.0)

    @pl.loop(0, count // QUERIES, unroll=count // QUERIES)
    def _(block):
        base = pl.multiple_of(block * QUERIES, QUERIES)
        query = all_in[pl.ds(base + REACH, QUERIES), :width]
        keys_in = all_in[pl.ds(base, WINDOW), width : 2 * width]
        values_in = all_in[pl.ds(base, WINDOW), 2 * width :]
        query_wide = jnp.concatenate([query * lane for lane in scaled], axis=0)
        shares = block_shares(query_wide, keys_in, mask_ref[pl.ds(base, QUERIES), :])
        wide = dot(shares.astype(jnp.bfloat16), values_in)
        all_out[pl.ds(base, QUERIES), :] = fold_heads(wide, plain).astype(jnp.bfloat16)

    rows = outs[0].shape[0]
    for piece, row, token in places_of(place_ref, pieces, rows):
        outs[piece][pl.ds(row, rows // 2), :] = all_out[pl.ds(token, rows // 2), :]


def attend_back_kernel(pieces, place_ref, mask_ref, *refs):
    ins, grads, outs = refs[:pieces], refs[pieces : 2 * pieces], refs[2 * pieces : 3 * pieces]
    all_in, all_grad, query_sum, key_sum, value_sum = refs[3 * pieces :]
    count, width = all_grad.shape
    all_in[:REACH, :] = jnp.zeros((REACH, 3 * width), jnp.bfloat16)
    all_in[REACH + count :, :] = jnp.zeros((REACH, 3 * width), jnp.bfloat16)
    in_token_order(place_ref, ins, all_in, REACH)
    in_token_order(place_ref, grads, all_grad, 0)
    key_sum[...] = jnp.zeros_like(key_sum)
    value_sum[...] = jnp.zeros_like(value_sum)
    scaled = [lane.astype(jnp.bfloat16) for lane in head_lanes(QUERIES, width, HD ** (-0.5))]
    plain_low = [lane.astype(jnp.bfloat16) for lane in head_lanes(QUERIES, width, 1.0)]
    scaled_wide = head_lanes(QUERIES, width, HD ** (-0.5))

    @pl.loop(0, count // QUERIES, unroll=count // QUERIES)
    def _(block):
        base = pl.multiple_of(block * QUERIES, QUERIES)
        query = all_in[pl.ds(base + REACH, QUERIES), :width]
        keys_in = all_in[pl.ds(base, WINDOW), width : 2 * width]
        values_in = all_in[pl.ds(base, WINDOW), 2 * width :]
        grad = all_grad[pl.ds(base, QUERIES), :]
        query_wide = jnp.concatenate([query * lane for lane in scaled], axis=0)
        grad_wide = jnp.concatenate([grad * lane for lane in plain_low], axis=0)
        shares = block_shares(query_wide, keys_in, mask_ref[pl.ds(base, QUERIES), :])
        grad_shares = dot(grad_wide, values_in, NT)
        inner = jnp.sum(grad_shares * shares, axis=-1, keepdims=True)
        grad_scores = (shares * (grad_shares - inner)).astype(jnp.bfloat16)
        query_sum[pl.ds(base, QUERIES), :] = fold_heads(dot(grad_scores, keys_in), scaled_wide)
        key_sum[pl.ds(base, WINDOW), :] += dot(grad_scores, query_wide, TN)
        value_sum[pl.ds(base, WINDOW), :] += dot(shares.astype(jnp.bfloat16), grad_wide, TN)

    rows = outs[0].shape[0]
    for piece, row, token in places_of(place_ref, pieces, rows):
        here, there = pl.ds(row, rows // 2), pl.ds(token + REACH, rows // 2)
        out = outs[piece]
        out[here, :width] = query_sum[pl.ds(token, rows // 2), :].astype(jnp.bfloat16)
        out[here, width : 2 * width] = key_sum[there, :].astype(jnp.bfloat16)
        out[here, 2 * width :] = value_sum[there, :].astype(jnp.bfloat16)


def attend(run, place, mask, projected):
    pieces = len(projected)
    rows, width = projected[0].shape[0], projected[0].shape[1] // 3
    count = rows * pieces
    return run(
        "attend",
        functools.partial(attend_kernel, pieces),
        [place, mask, *projected],
        [struct((rows, width))] * pieces,
        12,
        in_specs=[SMEM_SPEC] + [VMEM_SPEC] * (1 + pieces),
        scratch=[
            pltpu.VMEM((count + 2 * REACH, 3 * width), jnp.bfloat16),
            pltpu.VMEM((count, width), jnp.bfloat16),
        ],
    )


def attend_back(run, place, mask, projected, grads):
    pieces = len(projected)
    rows, width = projected[0].shape[0], projected[0].shape[1] // 3
    count = rows * pieces
    return run(
        "attend_back",
        functools.partial(attend_back_kernel, pieces),
        [place, mask, *projected, *grads],
        [struct((rows, 3 * width))] * pieces,
        20,
        in_specs=[SMEM_SPEC] + [VMEM_SPEC] * (1 + 2 * pieces),
        scratch=[
            pltpu.VMEM((count + 2 * REACH, 3 * width), jnp.bfloat16),
            pltpu.VMEM((count, width), jnp.bfloat16),
            pltpu.VMEM((count, width), jnp.float32),
            pltpu.VMEM((count + 2 * REACH, width), jnp.float32),
            pltpu.VMEM((count + 2 * REACH, width), jnp.float32),
        ],
    )


def crop_mask(segments):
    blocks = segments.shape[0] // QUERIES
    edge = jnp.full((REACH,), -1, segments.dtype)
    padded = jnp.concatenate([edge, segments, edge])
    keys_of = jnp.stack([padded[b * QUERIES : b * QUERIES + WINDOW] for b in range(blocks)])
    same = segments.reshape(blocks, QUERIES)[:, :, None] == keys_of[:, None, :]
    return same.astype(jnp.float32).reshape(blocks * QUERIES, WINDOW)


def row_step(count):
    return 32 if count % 32 == 0 else count


def normalised(value):
    centre = value - jnp.mean(value, axis=-1, keepdims=True)
    spread_of = jnp.mean(centre * centre, axis=-1, keepdims=True)
    scale = lax.rsqrt(spread_of + EPS_NORM)
    return centre * scale, scale


def norm_kernel(row, terms, params_ref, value_ref, *refs):
    *outs, all_low, first_low, second_low = refs[terms:]
    half = first_low.shape[0]
    step = row_step(half)
    gain, shift = params_ref[row : row + 1, :], params_ref[row + 1 : row + 2, :]
    for start in range(0, 2 * half, step):
        here = slice(start, start + step)
        value = value_ref[here, :]
        if terms:
            value = value + refs[0][here, :].astype(jnp.float32)
            value = value + refs[1][here, :].astype(jnp.float32)
            outs[0][here, :] = value
        low = (normalised(value)[0] * gain + shift).astype(jnp.bfloat16)
        all_low[here, :] = low
        if start < half:
            first_low[here, :] = low
        else:
            second_low[start - half : start - half + step, :] = low


def norm(run, params, row, value, *terms):
    wide = [struct(value.shape, jnp.float32)] if terms else []
    low = [struct(value.shape), *[struct((value.shape[0] // 2, value.shape[1]))] * 2]
    body = functools.partial(norm_kernel, row, len(terms))
    *stream, whole, first, second = run("norm", body, [params, value, *terms], wide + low, 6)
    return (*stream, (whole, [first, second]))


def norm_back_kernel(
    row, params_ref, stream_ref, value_ref, near, far, sums_ref, out_ref, all_low, first_low, second_low
):
    half = first_low.shape[0]
    step = row_step(half)
    width = value_ref.shape[1]
    gain = params_ref[row : row + 1, :]
    sums_ref[...] = jnp.zeros_like(sums_ref)
    for start in range(0, 2 * half, step):
        here = slice(start, start + step)
        grad = near[here, :].astype(jnp.float32) + far[here, :].astype(jnp.float32)
        unit, scale = normalised(value_ref[here, :])
        along = grad * unit
        sums_ref[:8, :] += jnp.sum(along.reshape(step // 8, 8, width), axis=0)
        sums_ref[8:, :] += jnp.sum(grad.reshape(step // 8, 8, width), axis=0)
        pushed = grad * gain
        inner = jnp.mean(pushed * unit, axis=-1, keepdims=True)
        term = scale * (pushed - jnp.mean(pushed, axis=-1, keepdims=True) - unit * inner)
        total = stream_ref[here, :] + term
        out_ref[here, :] = total
        low = total.astype(jnp.bfloat16)
        all_low[here, :] = low
        if start < half:
            first_low[here, :] = low
        else:
            second_low[start - half : start - half + step, :] = low


def norm_back(run, params, row, stream_grad, value, *terms):
    sums, stream, whole, first, second = run(
        "norm_back",
        functools.partial(norm_back_kernel, row),
        [params, stream_grad, value, *terms],
        [
            struct((16, value.shape[1]), jnp.float32),
            struct(value.shape, jnp.float32),
            struct(value.shape),
            *[struct((value.shape[0] // 2, value.shape[1]))] * 2,
        ],
        8,
    )
    return sums, stream, (whole, [first, second])


COLUMNS = 256


def two_halves(both, weights, here):
    first, second = weights
    half = first.shape[0]
    return dot(both[:, :half], first[:, here]) + dot(both[:, half:], second[:, here])


def project_kernel(begin, a, b, c, first, second, out):
    both = jnp.concatenate([a[...], b[...], c[...]], axis=0)
    for start in range(0, out.shape[1], COLUMNS):
        here = slice(begin + start, begin + start + COLUMNS)
        out[:, start : start + COLUMNS] = two_halves(both, (first, second), here).astype(
            jnp.bfloat16
        )


def project(run, piece, first, second, begin, width):
    outs = [struct((sum(part.shape[0] for part in piece), width))]
    body = functools.partial(project_kernel, begin)
    return run("project", body, [*piece, first, second], outs, 14)[0]


def widen_kernel(begin, a, b, c, first, second, active, slope):
    both = jnp.concatenate([a[...], b[...], c[...]], axis=0)
    for start in range(0, active.shape[1], COLUMNS):
        here = slice(start, start + COLUMNS)
        hidden = two_halves(both, (first, second), slice(begin + start, begin + start + COLUMNS))
        below = 0.5 + 0.5 * lax.erf(hidden * (0.5**0.5))
        density = jnp.exp(-0.5 * hidden * hidden) * 0.3989422804014327
        active[:, here] = (hidden * below).astype(jnp.bfloat16)
        slope[:, here] = (below + hidden * density).astype(jnp.bfloat16)


def widen(run, piece, first, second, begin, width):
    outs = [struct((sum(part.shape[0] for part in piece), width))] * 2
    return run("widen", functools.partial(widen_kernel, begin), [*piece, first, second], outs, 14)


def bend_kernel(begin, a, b, c, first, second, slope, out):
    both = jnp.concatenate([a[...], b[...], c[...]], axis=0)
    for start in range(0, out.shape[1], COLUMNS):
        here = slice(start, start + COLUMNS)
        grad = two_halves(both, (first, second), slice(begin + start, begin + start + COLUMNS))
        out[:, here] = (grad * slope[:, here].astype(jnp.float32)).astype(jnp.bfloat16)


def bend_back(run, piece, first, second, begin, slope):
    return run("bend_back", functools.partial(bend_kernel, begin), [*piece, first, second, slope], [struct(slope.shape)], 14)[0]


def narrow_kernel(begin, piece, first, second, kept, sent, sent_more):
    half = kept.shape[0]
    part = sent.shape[0]
    columns = slice(begin, begin + piece.shape[1])
    for index, weights in enumerate((first, second)):
        for start in range(0, weights.shape[0], COLUMNS):
            there = index * weights.shape[0] + start
            here = slice(there, there + COLUMNS)
            rows = weights[start : start + COLUMNS, columns]
            both = dot(piece[...], rows, NT).astype(jnp.bfloat16)
            kept[:, here] = both[:half]
            sent[:, here] = both[half : half + part]
            sent_more[:, here] = both[half + part :]


def narrow(run, piece, first, second, begin):
    rows, width = piece.shape[0] // 2, 2 * first.shape[0]
    outs = [struct((rows, width)), *[struct((rows // 2, width))] * 2]
    kept, *sent = run("narrow", functools.partial(narrow_kernel, begin), [piece, first, second], outs, 14)
    return kept, sent


def weight_terms_kernel(counts, columns, *refs):
    ins = refs[: sum(map(sum, counts))]
    kept, sent, all_left, all_right = refs[len(ins) :]
    begin = 0
    for lefts, rights in counts:
        left, right, ins = ins[:lefts], ins[lefts : lefts + rights], ins[lefts + rights :]
        for store, parts in ((all_left, left), (all_right, right)):
            row = 0
            for part in parts:
                store[row : row + part.shape[0], : part.shape[1]] = part[...]
                row += part.shape[0]
        wide = right[0].shape[1]
        for out, spans in zip((sent, kept), columns[::-1]):
            row = 0
            for first, last in spans:
                for start in range(0, wide, COLUMNS):
                    out[row : row + last - first, begin + start : begin + start + COLUMNS] = dot(
                        all_left[:, first:last], all_right[:, start : start + COLUMNS], TN
                    ).astype(jnp.bfloat16)
                row += last - first
        begin += wide


def weight_terms(run, pairs, columns):
    counts = tuple((len(left), len(right)) for left, right in pairs)
    flat = [array for left, right in pairs for array in (*left, *right)]
    total = sum(array.shape[0] for array in pairs[0][0])
    across = sum(right[0].shape[1] for _, right in pairs)
    return run(
        "weight_terms",
        functools.partial(weight_terms_kernel, counts, columns),
        flat,
        [struct((sum(last - first for first, last in spans), across)) for spans in columns],
        24,
        scratch=[
            pltpu.VMEM((total, pairs[0][0][0].shape[1]), jnp.bfloat16),
            pltpu.VMEM((total, max(right[0].shape[1] for _, right in pairs)), jnp.bfloat16),
        ],
    )


def fold_kernel(many, *refs):
    heres, fars, (kept, sent) = refs[:many], refs[many : 2 * many], refs[2 * many :]
    rows = kept.shape[0]
    begin = 0
    for here, far in zip(heres, fars):
        columns = slice(begin, begin + here.shape[1])
        for out, part in ((sent, slice(rows, None)), (kept, slice(0, rows))):
            out[:, columns] = (
                here[part, :].astype(jnp.float32) + far[part, :].astype(jnp.float32)
            ).astype(jnp.bfloat16)
        begin += here.shape[1]


def fold(run, heres, fars):
    across = sum(array.shape[1] for array in heres)
    outs = [struct((heres[0].shape[0] // 2, across))] * 2
    return run("fold", functools.partial(fold_kernel, len(heres)), [*heres, *fars], outs, 12)


def moments_kernel(at, kept, far, weights, first, second, *refs):
    first_new, second_new, step_out, squares = refs[-4:]
    grad = kept[...].astype(jnp.float32) + far[...].astype(jnp.float32)
    weight = weights[...].reshape(grad.shape)
    new_first, new_second, step = adam_part(
        grad, weight, first[...].reshape(grad.shape), second[...].reshape(grad.shape), WEIGHT_DECAY
    )
    for out, value in ((first_new, new_first), (second_new, new_second), (step_out, step)):
        out[...] = value.reshape(out.shape)
    for place, value in enumerate((weight, step)):
        squares[0, place : place + 1, :] = jnp.sum(value * value, axis=0, keepdims=True)


def moments(run, names, layer, kept, far, weights, first, second, before):
    rows, wide = weights.shape[2:]
    spec = pl.BlockSpec((1, 1, rows, wide), lambda n, at: (layer, at[n], 0, 0))
    grad_spec = pl.BlockSpec((rows, wide), lambda n, at: (0, n))
    before = list(before or [])
    return run(
        "moments",
        moments_kernel,
        [jnp.array(names, jnp.int32), kept, far, weights, first, second, *before],
        [struct(weights.shape, jnp.float32)] * 3 + [struct((len(names), 2, wide), jnp.float32)],
        12,
        in_specs=[grad_spec, grad_spec, spec, spec, spec] + [ANY_SPEC] * len(before),
        out_specs=[spec, spec, spec, pl.BlockSpec((1, 2, wide), lambda n, at: (n, 0, 0))],
        grid_spec=(1, (len(names),)),
        aliases={6 + i: i for i in range(len(before))},
    )


def squares_kernel(places, *refs):
    out = refs[-1]
    for ref, rows in zip(refs[:-1], places):
        for index, row in enumerate(rows):
            sums = jnp.sum(ref[index], axis=-1, keepdims=True)
            out[2 * row : 2 * row + 2, :] = jnp.broadcast_to(sums, (2, out.shape[1]))


def squares_of(run, places, *column_sums):
    rows = 2 * sum(map(len, places))
    body = functools.partial(squares_kernel, places)
    return run("squares_of", body, list(column_sums), [struct((rows, 128), jnp.float32)], 4)[0]


def apply_kernel(begin, total, weights, step, new, low):
    row = 2 * (6 * pl.program_id(0) + begin + pl.program_id(1))
    size, move = jnp.sqrt(total[pl.ds(row, 1), :1]), jnp.sqrt(total[pl.ds(row + 1, 1), :1])
    rate = LEARN_RATE * (size / move)
    value = weights[...].reshape(weights.shape[2:]) - rate * step[...].reshape(step.shape[2:])
    new[...] = value.reshape(new.shape)
    low[...] = value.astype(jnp.bfloat16).reshape(low.shape)


def apply(run, begin, total, weights, step):
    layers, names, rows, wide = weights.shape
    spec = pl.BlockSpec((1, 1, rows, wide), lambda layer, name: (layer, name, 0, 0))
    return run(
        "apply",
        functools.partial(apply_kernel, begin),
        [total, weights, step],
        [struct(weights.shape, jnp.float32), struct(weights.shape)],
        8,
        in_specs=[pl.BlockSpec(total.shape, lambda layer, name: (0, 0)), spec, spec],
        out_specs=[spec, spec],
        grid_spec=(0, (layers, names)),
    )


def move_columns(run, wides, order, out_rows, back):
    width, kind = wides[0].shape[1], wides[0].dtype
    blocks = order.shape[0]
    block = width // blocks
    if block % 128:
        if back:
            order = jnp.argsort(order)
        columns = (order[:, None] * block + jnp.arange(block)[None, :]).reshape(-1)
        moved = jnp.take(jnp.concatenate(wides, axis=0), columns, axis=1)
        starts = [sum(out_rows[:i]) for i in range(len(out_rows))]
        return [moved[start : start + rows] for start, rows in zip(starts, out_rows)]

    def copy(order_ref, *refs):
        ins, outs = refs[: len(wides)], refs[len(wides) :]
        step = min(ref.shape[0] for ref in refs)
        for row in range(0, sum(out_rows), step):
            source, target, from_row, to_row = ins, outs, row, row
            index = 0
            while from_row >= source[index].shape[0]:
                from_row -= source[index].shape[0]
                index += 1
            source, index = source[index], 0
            while to_row >= target[index].shape[0]:
                to_row -= target[index].shape[0]
                index += 1
            target = target[index]
            for place in range(blocks):
                there = pl.ds(pl.multiple_of(order_ref[place] * block, 128), block)
                here = pl.ds(place * block, block)
                from_columns, to_columns = (here, there) if back else (there, here)
                target[pl.ds(to_row, step), to_columns] = source[pl.ds(from_row, step), from_columns]

    return run(
        "move_columns",
        copy,
        [order, *wides],
        [struct((rows, width), kind) for rows in out_rows],
        6,
        in_specs=[SMEM_SPEC] + [VMEM_SPEC] * len(wides),
    )


class Rows:
    def __init__(self, total, run):
        self.total, self.run = total, run
        self.strides = [1 << bit for bit in reversed(range(total.bit_length() - 1))]

    def order(self):
        places = [0]
        for stride in self.strides:
            places = places + [place ^ stride for place in places]
        return jnp.bitwise_xor(
            jnp.array(places, jnp.int32), lax.axis_index("dp").astype(jnp.int32)
        )

    def swap(self, values, stride):
        return lax.ppermute(
            values, "dp", [(source, source ^ stride) for source in range(self.total)]
        )


class Gather:
    def __init__(self, rows, weights, layer, first, last, spans):
        self.rows, self.run, self.spans = rows, rows.run, spans
        self.what = (weights, layer, first, last)
        self.width = sum(spans)
        self.wholes = [None] * len(spans)

    def far(self):
        self.block = cast_blocks(self.run, *self.what)
        self.there = self.rows.swap(self.block, self.rows.strides[0])

    def near(self):
        for stride in self.rows.strides[1:-1]:
            self.run.settle(self.there)
            self.block = join(self.run, self.block, self.there, 0, self.width)
            self.there = self.rows.swap(self.block, stride)

    def last(self, span=0):
        part = join(self.run, self.block, self.there, sum(self.spans[:span]), self.spans[span])
        self.wholes[span] = (part, self.rows.swap(part, self.rows.strides[-1]))

    def take(self, span=0):
        self.run.settle(self.wholes[span][1])
        return self.wholes[span]


def stack_kernel(*refs):
    out, begin = refs[-1], 0
    for here, far in zip(refs[:-1:2], refs[1:-1:2]):
        columns = slice(begin, begin + here.shape[1])
        out[: here.shape[0], columns] = here[...]
        out[here.shape[0] :, columns] = far[...]
        begin += here.shape[1]


def stack(run, *pairs):
    flat = [array for pair in pairs for array in pair]
    across = sum(here.shape[1] for here, _ in pairs)
    return run("stack", stack_kernel, flat, [struct((2 * flat[0].shape[0], across))], 12)[0]


class GatherBoth:
    def __init__(self, rows, weights, layer):
        self.ways = [
            Gather(rows, weights, layer, name, name + 1, [weights.shape[3]]) for name in range(2)
        ]
        self.rows, self.run = rows, rows.run

    def near(self):
        for way in self.ways:
            for stride in self.rows.strides[1:-2]:
                way.block = join(self.run, way.block, way.there, 0, way.width)
                way.there = self.rows.swap(way.block, stride)
        self.block = stack(self.run, *[(way.block, way.there) for way in self.ways])
        self.there = self.rows.swap(self.block, self.rows.strides[-2])

    def last(self):
        self.whole = stack(self.run, (self.block, self.there))
        self.there = self.rows.swap(self.whole, self.rows.strides[-1])

    def take(self):
        self.run.settle(self.there)
        return self.whole, self.there


class Reduce:
    def __init__(self, rows):
        self.rows, self.run = rows, rows.run
        self.kept, self.there = [], []

    def send(self, *pairs):
        columns = (((0, D // 2),), ((D // 2, D),))
        keep, away = weight_terms(self.run, pairs, columns)
        self.kept.append(keep)
        self.there.append(self.rows.swap(away, self.rows.strides[-1]))

    def settle(self, group=0):
        self.run.settle(self.there[group])

    def near(self):
        self.pass_on(self.rows.strides[-2])

    def far(self):
        for stride in reversed(self.rows.strides[:-2]):
            self.pass_on(stride)

    def pass_on(self, stride):
        keep, away = fold(self.run, self.kept, self.there)
        self.kept, self.there = [keep], [self.rows.swap(away, stride)]

    def terms(self):
        return self.kept[0], self.there[0]


def core_swap(values_in):
    return lax.ppermute(values_in, "mp", [(0, 1), (1, 0), (2, 3), (3, 2)])


def chip_swap(values_in):
    return lax.ppermute(values_in, "mp", [(0, 2), (2, 0), (1, 3), (3, 1)])


class Exchange:
    def __init__(self, run, mine):
        self.run, (self.mine, parts) = run, mine
        self.beyond = chip_swap(self.mine)
        self.facing = [core_swap(part) for part in parts]

    def near(self):
        return [self.mine, *self.facing]

    def pass_on(self):
        self.relay, parts = cast(self.run, self.beyond)
        self.beyond_facing = [core_swap(part) for part in parts]

    def far(self):
        return [self.relay, *self.beyond_facing]

    def pieces(self):
        return self.near() + self.far()


def collect(run, near_piece, far_piece, weights, begin):
    far_kept, far_sent = narrow(run, far_piece, *weights, begin)
    far_sent = [core_swap(part) for part in far_sent]
    kept, sent = narrow(run, near_piece, *weights, begin)
    there = chip_swap(add_halves(run, far_kept, far_sent, jnp.bfloat16))
    sent = [core_swap(part) for part in sent]
    return add_halves(run, kept, sent, jnp.float32), there


def shards(
    rows_total,
    tokens,
    cotangent,
    segments,
    attention_weights,
    attention_first,
    attention_second,
    dense_weights,
    dense_first,
    dense_second,
    norm_params,
    norm_first,
    norm_second,
):
    layers = attention_weights.shape[0]
    width, wide = attention_weights.shape[3], dense_weights.shape[3]
    run = Order()
    settle = run.settle
    rows = Rows(rows_total, run)
    order = rows.order()
    place = lax.axis_index("mp").astype(jnp.int32).reshape(1)
    mask = crop_mask(segments)
    count = tokens.shape[0]

    inputs_way = Gather(rows, attention_weights, 0, 0, 3, [3 * width])
    output_way = Gather(rows, attention_weights, 0, 3, 4, [width])
    up_way = Gather(rows, dense_weights, 0, 0, 1, [wide])
    down_way = Gather(rows, dense_weights, 0, 1, 2, [wide])
    mixer_way = Gather(rows, attention_weights, 1, 0, 4, [4 * width])
    dense_way = GatherBoth(rows, dense_weights, 1)

    inputs_way.far()
    (params_here,) = move_columns(
        run, [norm_params.reshape(layers * 4, D)], order, [layers * 4], False
    )
    (stream,) = move_columns(run, [tokens], order, [count], False)
    normed = Exchange(run, *norm(run, params_here, 0, stream))
    inputs_way.near()
    output_way.far()
    inputs_way.last()
    up_way.far()
    output_way.near()
    normed.pass_on()
    (stream_grad,) = move_columns(run, [cotangent], order, [count], False)
    back = Exchange(run, cast(run, stream_grad))
    output_way.last()
    up_way.near()
    inputs_map = inputs_way.take()
    projected = [project(run, normed.near(), *inputs_map, 0, 3 * width)]
    projected.append(project(run, normed.far(), *inputs_map, 0, 3 * width))
    down_way.far()
    attended = attend(run, place, mask, projected)
    back.pass_on()
    up_way.last()
    output_map = output_way.take()

    saved = []
    settle(down_way.there)
    mixed = collect(run, attended[0], attended[1], output_map, 0)
    down_way.near()
    mixer_way.far()
    dense_way.ways[0].far()
    middle, low = norm(run, params_here, 2, stream, *mixed)
    normed_two = Exchange(run, low)
    down_way.last()
    mixer_way.near()
    settle(dense_way.ways[0].there)
    dense_way.ways[1].far()
    up_map = (*up_way.take(), 0)
    active, slope = [None, None], [None, None]
    active[0], slope[0] = widen(run, normed_two.near(), *up_map, wide)
    settle(mixer_way.there)
    settle(dense_way.ways[1].there)
    normed_two.pass_on()
    active[1], slope[1] = widen(run, normed_two.far(), *up_map, wide)
    down_map = (*down_way.take(), 0)
    saved.append((stream, normed, projected, attended, middle, normed_two, active, slope))
    saved[-1] += ((*inputs_map, 0), (*output_map, 0), up_map, down_map)

    widened = collect(run, *active, down_map[:2], down_map[2])
    mixer_way.last()
    dense_way.near()
    stream, low = norm(run, params_here, 4, middle, *widened)
    normed = Exchange(run, low)
    dense_way.last()
    inputs_map = mixer_way.take()
    projected = [project(run, normed.near(), *inputs_map, 0, 3 * width)]
    normed.pass_on()
    projected.append(project(run, normed.far(), *inputs_map, 0, 3 * width))
    attended = attend(run, place, mask, projected)

    mixed = collect(run, attended[0], attended[1], inputs_map, 3 * width)
    middle, low = norm(run, params_here, 6, stream, *mixed)
    normed_two = Exchange(run, low)
    dense_map = dense_way.take()
    up_map, down_map = (*dense_map, 0), (*dense_map, wide)
    active, slope = [None, None], [None, None]
    active[0], slope[0] = widen(run, normed_two.near(), *up_map, wide)
    grad_hidden = [bend_back(run, back.near(), *down_map, slope[0])]
    normed_two.pass_on()
    active[1], slope[1] = widen(run, normed_two.far(), *up_map, wide)
    saved.append((stream, normed, projected, attended, middle, normed_two, active, slope))
    saved[-1] += ((*inputs_map, 0), (*inputs_map, 3 * width), up_map, down_map)

    mixer_state, dense_state = None, None
    squares, places, vectors = [], [], [None] * (2 * layers)

    def dense_moments(layer, names, terms):
        nonlocal dense_state
        *dense_state, sums = moments(
            run, names, layer, *terms, dense_weights, dense_first, dense_second, dense_state
        )
        squares.append(sums)
        places.append([6 * layer + 4 + name for name in names])

    def mixer_moments(layer, terms):
        nonlocal mixer_state
        *mixer_state, sums = moments(
            run, (0, 1, 2, 3), layer, *terms,
            attention_weights, attention_first, attention_second, mixer_state,
        )
        squares.append(sums)
        places.append([6 * layer + name for name in range(4)])

    def weight_grad(*pairs):
        reduced = Reduce(rows)
        reduced.send(*pairs)
        return reduced

    stream_in, normed, projected, attended, middle, normed_two, active, slope = saved[1][:8]
    inputs_map, output_map, up_map, down_map = saved[1][8:]
    grad_hidden.append(bend_back(run, back.far(), *down_map, slope[1]))
    raised = collect(run, *grad_hidden, up_map[:2], up_map[2])
    down_later = weight_grad((back.pieces(), active))
    up_later = weight_grad((normed_two.pieces(), grad_hidden))
    vectors[3], stream_grad, low = norm_back(run, params_here, 6, stream_grad, middle, *raised)
    turned = Exchange(run, low)
    down_later.near()
    grad_attended = [project(run, turned.near(), *output_map, width)]
    turned.pass_on()
    grad_attended.append(project(run, turned.far(), *output_map, width))
    grad_projected = attend_back(run, place, mask, projected, grad_attended)

    down_later.settle()
    lowered = collect(run, *grad_projected, inputs_map[:2], inputs_map[2])
    down_later.far()
    up_later.near()
    mixer_later = weight_grad((normed.pieces(), grad_projected), (turned.pieces(), attended))
    vectors[2], stream_grad, low = norm_back(run, params_here, 4, stream_grad, stream_in, *lowered)
    back = Exchange(run, low)

    stream_in, normed, projected, attended, middle, normed_two, active, slope = saved[0][:8]
    inputs_map, output_map, up_map, down_map = saved[0][8:]
    grad_hidden = [bend_back(run, back.near(), *down_map, slope[0])]
    mixer_later.settle()
    up_later.settle()
    down_later.settle()
    back.pass_on()
    grad_hidden.append(bend_back(run, back.far(), *down_map, slope[1]))
    raised = collect(run, *grad_hidden, up_map[:2], up_map[2])
    mixer_later.near()
    up_later.far()
    down_grad = weight_grad((back.pieces(), active))
    dense_moments(1, (1,), down_later.terms())
    up_later.settle()
    vectors[1], stream_grad, low = norm_back(run, params_here, 2, stream_grad, middle, *raised)
    turned = Exchange(run, low)
    mixer_later.far()
    up_grad = weight_grad((normed_two.pieces(), grad_hidden))
    grad_attended = [project(run, turned.near(), *output_map, width)]
    dense_moments(1, (0,), up_later.terms())
    down_grad.near()
    mixer_later.settle()
    turned.pass_on()
    grad_attended.append(project(run, turned.far(), *output_map, width))
    grad_projected = attend_back(run, place, mask, projected, grad_attended)

    down_grad.settle()
    lowered = collect(run, *grad_projected, inputs_map[:2], inputs_map[2])
    mixer_grad = weight_grad((normed.pieces(), grad_projected), (turned.pieces(), attended))
    down_grad.far()
    up_grad.near()
    mixer_moments(1, mixer_later.terms())
    down_grad.settle()
    vectors[0], stream_grad, low = norm_back(run, params_here, 0, stream_grad, stream_in, *lowered)

    up_grad.far()
    middle, active, down_map = saved[-1][4], saved[-1][6], saved[-1][11]
    widened = collect(run, *active, down_map[:2], down_map[2])
    mixer_grad.near()
    dense_moments(0, (1,), down_grad.terms())
    all_rows = jnp.concatenate([jnp.sum(sums.reshape(2, 8, D), axis=1) for sums in vectors])
    (all_rows,) = move_columns(run, [all_rows], order, [layers * 4], True)
    all_rows = add(run, all_rows, core_swap(all_rows), jnp.float32)
    (grad_tokens,) = move_columns(run, [stream_grad], order, [count], True)
    mixer_grad.far()
    last_stream = add(run, middle, widened[0], jnp.float32, widened[1])
    all_rows = add(run, all_rows, chip_swap(all_rows), jnp.float32)
    for stride in reversed(rows.strides):
        all_rows = add(run, all_rows, rows.swap(all_rows, stride), jnp.float32)
    (outcome,) = move_columns(run, [last_stream], order, [count], True)
    dense_moments(0, (0,), up_grad.terms())
    mixer_moments(0, mixer_grad.terms())
    all_squares = squares_of(run, places, *squares)
    all_squares = add(run, all_squares, core_swap(all_squares), jnp.float32)
    all_squares = add(run, all_squares, chip_swap(all_squares), jnp.float32)
    for stride in reversed(rows.strides):
        all_squares = add(run, all_squares, rows.swap(all_squares, stride), jnp.float32)
    all_vectors = all_rows
    mixer_new, mixer_copy = apply(run, 0, all_squares, attention_weights, mixer_state[2])
    dense_new, dense_copy = apply(run, 4, all_squares, dense_weights, dense_state[2])

    total_squares = all_squares[:, 0].reshape(layers, 6, 2)
    total_vectors = all_vectors.reshape(layers, 4, D)
    sizes_all = jnp.sqrt(total_squares[:, :, 0])
    moves_all = jnp.sqrt(total_squares[:, :, 1])
    params_first, params_second, params_step = adam_part(
        total_vectors, norm_params, norm_first, norm_second, 0.0
    )
    params_size = jnp.sqrt(jnp.sum(norm_params * norm_params, axis=-1))
    params_move = jnp.sqrt(jnp.sum(params_step * params_step, axis=-1))
    params_new = norm_params - LEARN_RATE * (params_size / params_move)[:, :, None] * params_step
    mixer_entries = float(D * HEADS * HD) ** 0.5
    dense_entries = float(D * FF) ** 0.5
    entry_roots = jnp.array([mixer_entries] * 4 + [dense_entries] * 2, jnp.float32)
    norms = jnp.stack([sizes_all / entry_roots[None, :], moves_all / entry_roots[None, :]], axis=-1)
    second_norm_grad = total_vectors[:, 2:4]
    return (
        outcome,
        grad_tokens,
        mixer_new,
        mixer_state[0],
        mixer_state[1],
        mixer_copy,
        dense_new,
        dense_state[0],
        dense_state[1],
        dense_copy,
        params_new,
        params_first,
        params_second,
        norms,
        second_norm_grad,
    )


def solution(mesh):
    rows_spec = P(("dp", "mp"), None)
    weight_spec = P(None, None, "dp", "mp")
    in_specs = (rows_spec, rows_spec, P("dp")) + (weight_spec,) * 6 + (P(),) * 3
    out_specs = (rows_spec,) * 2 + (weight_spec,) * 8 + (P(),) * 5
    return jax.shard_map(
        functools.partial(shards, mesh.shape["dp"]),
        mesh=mesh,
        in_specs=in_specs,
        out_specs=out_specs,
        check_vma=False,
    )
```

time: 567 us -> 496 us (0.87)
  waiting for transfers between devices: 276 us -> 238 us
  local copies, waits for them, and re-layouts: 35.3 us -> 21 us
  starting transfers between devices: 101 us -> 86.7 us
    ppermute x34 -> x18, waiting for transfers between devices: 128 us -> 56.7 us  [chip_swap(): return lax.ppermute(values_in, 'mp', [(0, 2), (2, 0), (1, 3), (3, 1)])]
    ppermute x35 -> x43, waiting for transfers between devices: 126 us -> 162 us  [swap(): lax.ppermute(values, 'dp', [(source, source ^ stride) for source in range...]
    ppermute x34 -> x18, starting transfers between devices: 38.6 us -> 16.6 us  [chip_swap(): return lax.ppermute(values_in, 'mp', [(0, 2), (2, 0), (1, 3), (3, 1)])]
    ppermute x35 -> x43, starting transfers between devices: 39.1 us -> 53.4 us  [swap(): lax.ppermute(values, 'dp', [(source, source ^ stride) for source in range...]
    ppermute x6 -> x0, waiting for transfers between devices: 11.9 us -> none  [total_everywhere(): lax.ppermute(value, 'dp', [(source, source ^ stride) for source in range(...]
    ppermute x6 -> x0, starting transfers between devices: 10.9 us -> none  [total_everywhere(): lax.ppermute(value, 'dp', [(source, source ^ stride) for source in range(...]
    unnamed x235 -> x184, local copies, waits for them, and re-layouts: 29.8 us -> 19.2 us
    ppermute x66, waiting for transfers between devices: 11 us -> 18.9 us  [core_swap(): return lax.ppermute(values_in, 'mp', [(0, 1), (1, 0), (2, 3), (3, 2)])]
  transfers between devices with their start and end apart: 141 -> 127, of which waited for: 69 -> 65; matrix products, arithmetic and copies ran while one was open for 1% -> 1% of each run, Pallas kernels for 21% -> 24%
where the time goes in v3:
time: 496 us; the launch traced here: 489 us
  waiting for transfers between devices  238 us (48%)
  Pallas kernels  137 us (28%)
  starting transfers between devices  86.7 us (17%)
  local copies, waits for them, and re-layouts  21 us (4%)
    ppermute x43, waiting for transfers between devices, swap(): lax.ppermute(values, 'dp', [(source, source ^ stride) for source in range...  162 us
    pallas_call x132, Pallas kernels, __call__(): pl.pallas_call(wrapped, out_shape=[*outs, TOKEN], **places, input_output_...  137 us
    ppermute x18, waiting for transfers between devices, chip_swap(): return lax.ppermute(values_in, 'mp', [(0, 2), (2, 0), (1, 3), (3, 1)])  56.7 us
    ppermute x43, starting transfers between devices, swap(): lax.ppermute(values, 'dp', [(source, source ^ stride) for source in range...  53.4 us
    unnamed x184, local copies, waits for them, and re-layouts  19.2 us
    ppermute x66, waiting for transfers between devices, core_swap(): return lax.ppermute(values_in, 'mp', [(0, 1), (1, 0), (2, 3), (3, 2)])  18.9 us
    ppermute x66, starting transfers between devices, core_swap(): return lax.ppermute(values_in, 'mp', [(0, 1), (1, 0), (2, 3), (3, 2)])  16.7 us
    ppermute x18, starting transfers between devices, chip_swap(): return lax.ppermute(values_in, 'mp', [(0, 2), (2, 0), (1, 3), (3, 1)])  16.6 us
  transfers between devices with their start and end apart: 127, of which 65 were waited for; matrix products, arithmetic and copies ran while one was open for 1% of the time, Pallas kernels for 24%

profile of v3, /device:TPU:0, one launch (start us, length us, event | category | flops | bytes accessed | tf_op | source)
XLA Modules:
  0.0 488.7 jit_solution(3120986687113978315)
XLA Ops:
  3.1 4.0 collective-permute-start.2
  12.8 3.7 collective-permute-done.2.refs_1_.refs_3_
  19.9 7.9 %collective-permute-done.3.refs_1_ = bf16[256,768]{1,0:T(8,128)(2,1)S(1)} collective-permute-done((bf16[256,768]{1,0:T(8,128)(2,1)S(1)}, bf16[256,768]{1,0:T(8,128)(2,1)S(1)}, u32[]{:S(2)}, u32[]{:S(2)}) %collective-permute-start.3) | collective-permute-done | bytes 393248 | tf_op jit(solution)/shard_map/ppermute | solution.py:677
  29.3 3.3 collective-permute-start.6
  32.7 4.1 collective-permute-done.6.refs_1_.refs_3_
  36.8 6.4 %collective-permute-start.7 = (bf16[256,256]{1,0:T(8,128)(2,1)S(1)}, bf16[256,256]{1,0:T(8,128)(2,1)S(1)}, u32[]{:S(2)}, u32[]{:S(2)}) collective-permute-start(bf16[256,256]{1,0:T(8,128)(2,1)S(1)} %get-tuple-element.416.refs_0_), channel_id=1, source_target_pairs={{0,8},{4,12},{8,0},{12,4},{16,24},{20,28},{24,16},{28,20},{1,9},{5... | collective-permute-start | bytes 393224 | tf_op jit(solution)/shard_map/ppermute | solution.py:677
  49.0 1.7 collective-permute-done.7.refs_1_
  58.6 4.0 collective-permute-start.14
  65.2 2.9 attend.2
  69.5 3.2 collective-permute-done.12.refs_1_
  83.8 3.0 collective-permute-start.23
  86.9 10.1 %collective-permute-done.19.refs_3_ = bf16[320,1024]{1,0:T(8,128)(2,1)S(1)} collective-permute-done((bf16[320,1024]{1,0:T(8,128)(2,1)S(1)}, bf16[320,1024]{1,0:T(8,128)(2,1)S(1)}, u32[]{:S(2)}, u32[]{:S(2)}) %collective-permute-start.19) | collective-permute-done | bytes 655392 | tf_op jit(solution)/shard_map/ppermute | solution.py:781
  97.5 9.8 %collective-permute-done.24.refs_1_ = bf16[256,1024]{1,0:T(8,128)(2,1)S(1)} collective-permute-done((bf16[256,1024]{1,0:T(8,128)(2,1)S(1)}, bf16[256,1024]{1,0:T(8,128)(2,1)S(1)}, u32[]{:S(2)}, u32[]{:S(2)}) %collective-permute-start.24) | collective-permute-done | bytes 524320 | tf_op jit(solution)/shard_map/ppermute | solution.py:677
  112.5 2.3 widen.4
  114.8 12.5 %collective-permute-done.29.refs_3_ = bf16[128,1024]{1,0:T(8,128)(2,1)S(1)} collective-permute-done((bf16[128,1024]{1,0:T(8,128)(2,1)S(1)}, bf16[128,1024]{1,0:T(8,128)(2,1)S(1)}, u32[]{:S(2)}, u32[]{:S(2)}) %collective-permute-start.29) | collective-permute-done | bytes 262176 | tf_op jit(solution)/shard_map/ppermute | solution.py:677
  127.3 2.2 collective-permute-done.28.refs_2_.refs_1_
  131.8 2.3 widen.5
  141.5 14.0 %collective-permute-done.36.refs_3_ = bf16[320,1024]{1,0:T(8,128)(2,1)S(1)} collective-permute-done((bf16[320,1024]{1,0:T(8,128)(2,1)S(1)}, bf16[320,1024]{1,0:T(8,128)(2,1)S(1)}, u32[]{:S(2)}, u32[]{:S(2)}) %collective-permute-start.36) | collective-permute-done | bytes 655392 | tf_op jit(solution)/shard_map/ppermute | solution.py:781
  157.0 8.6 %collective-permute-done.40.refs_1_ = bf16[256,2048]{1,0:T(8,128)(2,1)S(1)} collective-permute-done((bf16[256,2048]{1,0:T(8,128)(2,1)S(1)}, bf16[256,2048]{1,0:T(8,128)(2,1)S(1)}, u32[]{:S(2)}, u32[]{:S(2)}) %collective-permute-start.40) | collective-permute-done | bytes 1048608 | tf_op jit(solution)/shard_map/ppermute | solution.py:677
  167.6 4.5 collective-permute-done.41.refs_0_
  175.9 2.9 attend.3
  184.4 14.1 %collective-permute-done.48.refs_3_ = bf16[320,1024]{1,0:T(8,128)(2,1)S(1)} collective-permute-done((bf16[320,1024]{1,0:T(8,128)(2,1)S(1)}, bf16[320,1024]{1,0:T(8,128)(2,1)S(1)}, u32[]{:S(2)}, u32[]{:S(2)}) %collective-permute-start.48) | collective-permute-done | bytes 655392 | tf_op jit(solution)/shard_map/ppermute | solution.py:781
  201.3 11.4 %collective-permute-done.51.refs_4_.refs_6_.refs_2_ = bf16[512,2048]{1,0:T(8,128)(2,1)S(1)} collective-permute-done((bf16[512,2048]{1,0:T(8,128)(2,1)S(1)}, bf16[512,2048]{1,0:T(8,128)(2,1)S(1)}, u32[]{:S(2)}, u32[]{:S(2)}) %collective-permute-start.51) | collective-permute-done | bytes 2097184 | tf_op jit(solution)/shard_map/ppermute | solution.py:677
  212.7 2.3 widen.6
  215.1 2.6 bend_back.4
  220.0 2.3 widen.7
  223.9 1.7 narrow.22
  231.2 4.0 weight_terms.6
  239.8 3.0 weight_terms.7
  242.8 3.7 collective-permute-done.63.refs_4_
  247.8 2.3 norm_back.4
  251.0 10.7 %collective-permute-done.66.refs_1_ = bf16[512,1024]{1,0:T(8,128)(2,1)} collective-permute-done((bf16[512,1024]{1,0:T(8,128)(2,1)}, bf16[512,1024]{1,0:T(8,128)(2,1)}, u32[]{:S(2)}, u32[]{:S(2)}) %collective-permute-start.66) | collective-permute-done | bytes 1048608 | tf_op jit(solution)/shard_map/ppermute | solution.py:677
  268.9 7.6 %attend_back.2 = (bf16[640,768]{1,0:T(8,128)(2,1)S(1)}, bf16[640,768]{1,0:T(8,128)(2,1)S(1)}, f32[8,128]{1,0:T(8,128)S(1)}) custom-call(s32[1]{0:T(128)} %bitcast.refs_0_, f32[1280,256]{1,0:T(8,128)S(1)} %fusion.refs_1_, bf16[640,768]{1,0:T(8,128)(2,1)S(1)} %get-tuple-element.501.refs_2_, bf16[640,768]{1,0:T(8,128)(2,1)S(1)} %get-tuple-element.507.refs_3_, ...), custom_call_target="tpu_custom_call" | custom-call | flops 1 | bytes 1 | tf_op jit(solution)/shard_map/attend_back/pallas_call | solution.py:87
  282.2 5.6 %collective-permute-done.76.refs_1_ = bf16[512,1024]{1,0:T(8,128)(2,1)S(1)} collective-permute-done((bf16[512,1024]{1,0:T(8,128)(2,1)S(1)}, bf16[512,1024]{1,0:T(8,128)(2,1)S(1)}, u32[]{:S(2)}, u32[]{:S(2)}) %collective-permute-start.76) | collective-permute-done | bytes 1048608 | tf_op jit(solution)/shard_map/ppermute | solution.py:677
  288.8 4.4 weight_terms.8
  294.1 4.0 collective-permute-done.75.refs_4_
  304.3 14.2 %collective-permute-done.82.refs_4_.refs_2_ = bf16[128,1024]{1,0:T(8,128)(2,1)S(1)} collective-permute-done((bf16[128,1024]{1,0:T(8,128)(2,1)S(1)}, bf16[128,1024]{1,0:T(8,128)(2,1)S(1)}, u32[]{:S(2)}, u32[]{:S(2)}) %collective-permute-start.82) | collective-permute-done | bytes 262176 | tf_op jit(solution)/shard_map/ppermute | solution.py:677
  330.1 2.9 weight_terms.9
  337.6 11.6 %collective-permute-done.91.refs_6_.refs_2_ = bf16[128,1024]{1,0:T(8,128)(2,1)S(1)} collective-permute-done((bf16[128,1024]{1,0:T(8,128)(2,1)S(1)}, bf16[128,1024]{1,0:T(8,128)(2,1)S(1)}, u32[]{:S(2)}, u32[]{:S(2)}) %collective-permute-start.91) | collective-permute-done | bytes 262176 | tf_op jit(solution)/shard_map/ppermute | solution.py:677
  351.8 3.0 collective-permute-done.89.refs_1_
  356.2 3.0 weight_terms.10
  363.8 4.8 collective-permute-done.98.refs_2_
  372.3 7.6 %attend_back.3 = (bf16[640,768]{1,0:T(8,128)(2,1)S(1)}, bf16[640,768]{1,0:T(8,128)(2,1)S(1)}, f32[8,128]{1,0:T(8,128)S(1)}) custom-call(s32[1]{0:T(128)} %bitcast.refs_0_, f32[1280,256]{1,0:T(8,128)S(1)} %fusion.refs_1_, bf16[640,768]{1,0:T(8,128)(2,1)S(1)} %copy-done.20, bf16[640,768]{1,0:T(8,128)(2,1)S(1)} %copy-done.23, ...), custom_call_target="tpu_custom_call" | custom-call | flops 1 | bytes 1 | tf_op jit(solution)/shard_map/attend_back/pallas_call | solution.py:87
  385.4 4.0 weight_terms.11
  391.7 2.5 collective-permute-start.107
  394.2 2.6 moments.8
  396.8 11.7 %collective-permute-done.107.refs_6_.refs_2_ = bf16[128,1024]{1,0:T(8,128)(2,1)S(1)} collective-permute-done((bf16[128,1024]{1,0:T(8,128)(2,1)S(1)}, bf16[128,1024]{1,0:T(8,128)(2,1)S(1)}, u32[]{:S(2)}, u32[]{:S(2)}) %collective-permute-start.107) | collective-permute-done | bytes 262176 | tf_op jit(solution)/shard_map/ppermute | solution.py:677
  408.5 2.0 norm_back.7
  417.0 2.9 collective-permute-start.114
  423.0 1.8 move_columns.10
  424.8 13.0 %collective-permute-done.114.refs_1_ = bf16[256,1024]{1,0:T(8,128)(2,1)S(1)} collective-permute-done((bf16[256,1024]{1,0:T(8,128)(2,1)S(1)}, bf16[256,1024]{1,0:T(8,128)(2,1)S(1)}, u32[]{:S(2)}, u32[]{:S(2)}) %collective-permute-start.114) | collective-permute-done | bytes 524320 | tf_op jit(solution)/shard_map/ppermute | solution.py:677
  439.3 2.7 collective-permute-done.116.refs_1_
  442.8 3.0 collective-permute-done.117.refs_1_
  445.9 2.4 collective-permute-start.118
  448.2 4.0 collective-permute-done.118.refs_1_
  452.7 4.4 collective-permute-done.119.refs_1_
  457.1 1.8 move_columns.11
  460.0 2.4 moments.11
  465.5 2.9 collective-permute-done.123.refs_1_
  469.8 2.3 collective-permute-done.124.refs_1_
  472.1 3.7 collective-permute-done.125.refs_1_
  477.6 2.8 collective-permute-done.126.refs_1_
  482.3 3.0 apply.2
  485.3 2.3 apply.3
  (527 shorter events, 167.5 us)
Async XLA Ops:
  3.1 13.4 %collective-permute-start.2 = (bf16[128,768]{1,0:T(8,128)(2,1)}, bf16[128,768]{1,0:T(8,128)(2,1)S(1)}, u32[]{:S(2)}, u32[]{:S(2)}) collective-permute-start(bf16[128,768]{1,0:T(8,128)(2,1)} %get-tuple-element.406.refs_0_), channel_id=1, source_target_pairs={{0,16},{4,20},{8,24},{12,28},{16,0},{20,4},{24,8},{28,12},{1,17},{... | collective-permute-start | bytes 589832 | tf_op jit(solution)/shard_map/ppermute | solution.py:677
  17.5 10.4 %collective-permute-start.3 = (bf16[256,768]{1,0:T(8,128)(2,1)S(1)}, bf16[256,768]{1,0:T(8,128)(2,1)S(1)}, u32[]{:S(2)}, u32[]{:S(2)}) collective-permute-start(bf16[256,768]{1,0:T(8,128)(2,1)S(1)} %get-tuple-element.408.refs_0_), channel_id=1, source_target_pairs={{0,8},{4,12},{8,0},{12,4},{16,24},{20,28},{24,16},{28,20},{1,9},{5... | collective-permute-start | bytes 1179656 | tf_op jit(solution)/shard_map/ppermute | solution.py:677
  18.4 18.4 %collective-permute-start.8 = (bf16[320,1024]{1,0:T(8,128)(2,1)S(1)}, bf16[320,1024]{1,0:T(8,128)(2,1)S(1)}, u32[]{:S(2)}, u32[]{:S(2)}) collective-permute-start(bf16[320,1024]{1,0:T(8,128)(2,1)S(1)} %get-tuple-element.403.refs_0_), channel_id=1, source_target_pairs={{0,2},{2,0},{1,3},{3,1},{4,6},{6,4},{5,7},{7,5},{8,10},{10,8},{9,1... | collective-permute-start | bytes 1966088 | tf_op jit(solution)/shard_map/ppermute | solution.py:781
  27.9 24.9 %collective-permute-start.4 = (bf16[512,768]{1,0:T(8,128)(2,1)S(1)}, bf16[512,768]{1,0:T(8,128)(2,1)S(1)}, u32[]{:S(2)}, u32[]{:S(2)}) collective-permute-start(bf16[512,768]{1,0:T(8,128)(2,1)S(1)} %get-tuple-element.411.refs_3_.refs_1_), channel_id=1, source_target_pairs={{0,4},{4,0},{8,12},{12,8},{16,20},{20,16},{24,28},{28,24},{1,5},{5... | collective-permute-start | bytes 2359304 | tf_op jit(solution)/shard_map/ppermute | solution.py:677
  29.3 18.2 %collective-permute-start = (bf16[160,1024]{1,0:T(8,128)(2,1)S(1)}, bf16[160,1024]{1,0:T(8,128)(2,1)S(1)}, u32[]{:S(2)}, u32[]{:S(2)}) collective-permute-start(bf16[160,1024]{1,0:T(8,128)(2,1)S(1)} %get-tuple-element.404), channel_id=1, source_target_pairs={{0,1},{1,0},{2,3},{3,2},{4,5},{5,4},{6,7},{7,6},{8,9},{9,8},{10,11... | collective-permute-start | bytes 983048 | tf_op jit(solution)/shard_map/ppermute | solution.py:777
  29.3 7.5 %collective-permute-start.6 = (bf16[128,256]{1,0:T(8,128)(2,1)S(1)}, bf16[128,256]{1,0:T(8,128)(2,1)S(1)}, u32[]{:S(2)}, u32[]{:S(2)}) collective-permute-start(bf16[128,256]{1,0:T(8,128)(2,1)S(1)} %get-tuple-element.414.refs_0_), channel_id=1, source_target_pairs={{0,16},{4,20},{8,24},{12,28},{16,0},{20,4},{24,8},{28,12},{1,17},{... | collective-permute-start | bytes 196616 | tf_op jit(solution)/shard_map/ppermute | solution.py:677
  32.6 18.3 %collective-permute-start.5 = (bf16[128,1024]{1,0:T(8,128)(2,1)S(1)}, bf16[128,1024]{1,0:T(8,128)(2,1)S(1)}, u32[]{:S(2)}, u32[]{:S(2)}) collective-permute-start(bf16[128,1024]{1,0:T(8,128)(2,1)S(1)} %get-tuple-element.413.refs_0_), channel_id=1, source_target_pairs={{0,16},{4,20},{8,24},{12,28},{16,0},{20,4},{24,8},{28,12},{1,17},{... | collective-permute-start | bytes 786440 | tf_op jit(solution)/shard_map/ppermute | solution.py:677
  36.8 16.1 %collective-permute-start.1 = (bf16[160,1024]{1,0:T(8,128)(2,1)S(1)}, bf16[160,1024]{1,0:T(8,128)(2,1)S(1)}, u32[]{:S(2)}, u32[]{:S(2)}) collective-permute-start(bf16[160,1024]{1,0:T(8,128)(2,1)S(1)} %get-tuple-element.405), channel_id=1, source_target_pairs={{0,1},{1,0},{2,3},{3,2},{4,5},{5,4},{6,7},{7,6},{8,9},{9,8},{10,11... | collective-permute-start | bytes 983048 | tf_op jit(solution)/shard_map/ppermute | solution.py:777
  36.8 14.0 %collective-permute-start.7 = (bf16[256,256]{1,0:T(8,128)(2,1)S(1)}, bf16[256,256]{1,0:T(8,128)(2,1)S(1)}, u32[]{:S(2)}, u32[]{:S(2)}) collective-permute-start(bf16[256,256]{1,0:T(8,128)(2,1)S(1)} %get-tuple-element.416.refs_0_), channel_id=1, source_target_pairs={{0,8},{4,12},{8,0},{12,4},{16,24},{20,28},{24,16},{28,20},{1,9},{5... | collective-permute-start | bytes 393224 | tf_op jit(solution)/shard_map/ppermute | solution.py:677
  47.5 20.6 %collective-permute-start.13 = (bf16[320,1024]{1,0:T(8,128)(2,1)}, bf16[320,1024]{1,0:T(8,128)(2,1)}, u32[]{:S(2)}, u32[]{:S(2)}) collective-permute-start(bf16[320,1024]{1,0:T(8,128)(2,1)} %get-tuple-element.436.refs_0_), channel_id=1, source_target_pairs={{0,2},{2,0},{1,3},{3,1},{4,6},{6,4},{5,7},{7,5},{8,10},{10,8},{9,1... | collective-permute-start | bytes 1966088 | tf_op jit(solution)/shard_map/ppermute | solution.py:781
  52.8 19.8 %collective-permute-start.12 = (bf16[256,1024]{1,0:T(8,128)(2,1)}, bf16[256,1024]{1,0:T(8,128)(2,1)}, u32[]{:S(2)}, u32[]{:S(2)}) collective-permute-start(bf16[256,1024]{1,0:T(8,128)(2,1)} %get-tuple-element.435.refs_0_), channel_id=1, source_target_pairs={{0,8},{4,12},{8,0},{12,4},{16,24},{20,28},{24,16},{28,20},{1,9},{5... | collective-permute-start | bytes 1572872 | tf_op jit(solution)/shard_map/ppermute | solution.py:677
  52.9 21.1 %collective-permute-start.11 = (bf16[512,256]{1,0:T(8,128)(2,1)}, bf16[512,256]{1,0:T(8,128)(2,1)S(1)}, u32[]{:S(2)}, u32[]{:S(2)}) collective-permute-start(bf16[512,256]{1,0:T(8,128)(2,1)} %get-tuple-element.433.refs_1_.refs_3_), channel_id=1, source_target_pairs={{0,4},{4,0},{8,12},{12,8},{16,20},{20,16},{24,28},{28,24},{1,5},{5... | collective-permute-start | bytes 786440 | tf_op jit(solution)/shard_map/ppermute | solution.py:677
  58.6 16.1 %collective-permute-start.14 = (bf16[128,1024]{1,0:T(8,128)(2,1)}, bf16[128,1024]{1,0:T(8,128)(2,1)}, u32[]{:S(2)}, u32[]{:S(2)}) collective-permute-start(bf16[128,1024]{1,0:T(8,128)(2,1)} %get-tuple-element.440.refs_0_), channel_id=1, source_target_pairs={{0,16},{4,20},{8,24},{12,28},{16,0},{20,4},{24,8},{28,12},{1,17},{... | collective-permute-start | bytes 786440 | tf_op jit(solution)/shard_map/ppermute | solution.py:677
  78.8 30.8 %collective-permute-start.22 = (bf16[512,1024]{1,0:T(8,128)(2,1)S(1)}, bf16[512,1024]{1,0:T(8,128)(2,1)S(1)}, u32[]{:S(2)}, u32[]{:S(2)}) collective-permute-start(bf16[512,1024]{1,0:T(8,128)(2,1)S(1)} %get-tuple-element.460.refs_3_.refs_1_), channel_id=1, source_target_pairs={{0,4},{4,0},{8,12},{12,8},{16,20},{20,16},{24,28},{28,24},{1,5},{5... | collective-permute-start | bytes 3145736 | tf_op jit(solution)/shard_map/ppermute | solution.py:677
  80.5 16.5 %collective-permute-start.19 = (bf16[320,1024]{1,0:T(8,128)(2,1)S(1)}, bf16[320,1024]{1,0:T(8,128)(2,1)S(1)}, u32[]{:S(2)}, u32[]{:S(2)}) collective-permute-start(bf16[320,1024]{1,0:T(8,128)(2,1)S(1)} %get-tuple-element.451), channel_id=1, source_target_pairs={{0,2},{2,0},{1,3},{3,1},{4,6},{6,4},{5,7},{7,5},{8,10},{10,8},{9,1... | collective-permute-start | bytes 1966088 | tf_op jit(solution)/shard_map/ppermute | solution.py:781
  83.3 24.0 %collective-permute-start.24 = (bf16[256,1024]{1,0:T(8,128)(2,1)S(1)}, bf16[256,1024]{1,0:T(8,128)(2,1)S(1)}, u32[]{:S(2)}, u32[]{:S(2)}) collective-permute-start(bf16[256,1024]{1,0:T(8,128)(2,1)S(1)} %get-tuple-element.462.refs_0_), channel_id=1, source_target_pairs={{0,8},{4,12},{8,0},{12,4},{16,24},{20,28},{24,16},{28,20},{1,9},{5... | collective-permute-start | bytes 1572872 | tf_op jit(solution)/shard_map/ppermute | solution.py:677
  83.8 25.7 %collective-permute-start.23 = (bf16[128,1024]{1,0:T(8,128)(2,1)S(1)}, bf16[128,1024]{1,0:T(8,128)(2,1)S(1)}, u32[]{:S(2)}, u32[]{:S(2)}) collective-permute-start(bf16[128,1024]{1,0:T(8,128)(2,1)S(1)} %get-tuple-element.461.refs_0_), channel_id=1, source_target_pairs={{0,16},{4,20},{8,24},{12,28},{16,0},{20,4},{24,8},{28,12},{1,17},{... | collective-permute-start | bytes 786440 | tf_op jit(solution)/shard_map/ppermute | solution.py:677
  86.8 22.7 %collective-permute-start.25 = (bf16[128,1024]{1,0:T(8,128)(2,1)S(1)}, bf16[128,1024]{1,0:T(8,128)(2,1)S(1)}, u32[]{:S(2)}, u32[]{:S(2)}) collective-permute-start(bf16[128,1024]{1,0:T(8,128)(2,1)S(1)} %get-tuple-element.466.refs_0_), channel_id=1, source_target_pairs={{0,16},{4,20},{8,24},{12,28},{16,0},{20,4},{24,8},{28,12},{1,17},{... | collective-permute-start | bytes 786440 | tf_op jit(solution)/shard_map/ppermute | solution.py:677
  107.4 26.8 %collective-permute-start.26 = (bf16[512,1024]{1,0:T(8,128)(2,1)S(1)}, bf16[512,1024]{1,0:T(8,128)(2,1)S(1)}, u32[]{:S(2)}, u32[]{:S(2)}) collective-permute-start(bf16[512,1024]{1,0:T(8,128)(2,1)S(1)} %get-tuple-element.469.refs_1_.refs_3_), channel_id=1, source_target_pairs={{0,4},{4,0},{8,12},{12,8},{16,20},{20,16},{24,28},{28,24},{1,5},{5... | collective-permute-start | bytes 3145736 | tf_op jit(solution)/shard_map/ppermute | solution.py:677
  107.8 21.7 %collective-permute-start.27 = (bf16[320,1024]{1,0:T(8,128)(2,1)S(1)}, bf16[320,1024]{1,0:T(8,128)(2,1)S(1)}, u32[]{:S(2)}, u32[]{:S(2)}) collective-permute-start(bf16[320,1024]{1,0:T(8,128)(2,1)S(1)} %get-tuple-element.457.refs_0_), channel_id=1, source_target_pairs={{0,2},{2,0},{1,3},{3,1},{4,6},{6,4},{5,7},{7,5},{8,10},{10,8},{9,1... | collective-permute-start | bytes 1966088 | tf_op jit(solution)/shard_map/ppermute | solution.py:781
  109.5 20.0 %collective-permute-start.28 = (bf16[256,1024]{1,0:T(8,128)(2,1)S(1)}, bf16[256,1024]{1,0:T(8,128)(2,1)S(1)}, u32[]{:S(2)}, u32[]{:S(2)}) collective-permute-start(bf16[256,1024]{1,0:T(8,128)(2,1)S(1)} %get-tuple-element.471.refs_0_), channel_id=1, source_target_pairs={{0,8},{4,12},{8,0},{12,4},{16,24},{20,28},{24,16},{28,20},{1,9},{5... | collective-permute-start | bytes 1572872 | tf_op jit(solution)/shard_map/ppermute | solution.py:677
  111.1 16.2 %collective-permute-start.29 = (bf16[128,1024]{1,0:T(8,128)(2,1)S(1)}, bf16[128,1024]{1,0:T(8,128)(2,1)S(1)}, u32[]{:S(2)}, u32[]{:S(2)}) collective-permute-start(bf16[128,1024]{1,0:T(8,128)(2,1)S(1)} %get-tuple-element.472.refs_2_), channel_id=1, source_target_pairs={{0,16},{4,20},{8,24},{12,28},{16,0},{20,4},{24,8},{28,12},{1,17},{... | collective-permute-start | bytes 786440 | tf_op jit(solution)/shard_map/ppermute | solution.py:677
  138.6 16.8 %collective-permute-start.36 = (bf16[320,1024]{1,0:T(8,128)(2,1)S(1)}, bf16[320,1024]{1,0:T(8,128)(2,1)S(1)}, u32[]{:S(2)}, u32[]{:S(2)}) collective-permute-start(bf16[320,1024]{1,0:T(8,128)(2,1)S(1)} %get-tuple-element.489), channel_id=1, source_target_pairs={{0,2},{2,0},{1,3},{3,1},{4,6},{6,4},{5,7},{7,5},{8,10},{10,8},{9,1... | collective-permute-start | bytes 1966088 | tf_op jit(solution)/shard_map/ppermute | solution.py:781
  140.4 25.3 %collective-permute-start.40 = (bf16[256,2048]{1,0:T(8,128)(2,1)S(1)}, bf16[256,2048]{1,0:T(8,128)(2,1)S(1)}, u32[]{:S(2)}, u32[]{:S(2)}) collective-permute-start(bf16[256,2048]{1,0:T(8,128)(2,1)S(1)} %get-tuple-element.498.refs_0_), channel_id=1, source_target_pairs={{0,8},{4,12},{8,0},{12,4},{16,24},{20,28},{24,16},{28,20},{1,9},{5... | collective-permute-start | bytes 3145736 | tf_op jit(solution)/shard_map/ppermute | solution.py:677
  140.7 25.6 %collective-permute-start.39 = (bf16[512,1024]{1,0:T(8,128)(2,1)S(1)}, bf16[512,1024]{1,0:T(8,128)(2,1)S(1)}, u32[]{:S(2)}, u32[]{:S(2)}) collective-permute-start(bf16[512,1024]{1,0:T(8,128)(2,1)S(1)} %get-tuple-element.497.refs_3_.refs_1_), channel_id=1, source_target_pairs={{0,4},{4,0},{8,12},{12,8},{16,20},{20,16},{24,28},{28,24},{1,5},{5... | collective-permute-start | bytes 3145736 | tf_op jit(solution)/shard_map/ppermute | solution.py:677
  156.0 16.0 %collective-permute-start.41 = (bf16[320,1024]{1,0:T(8,128)(2,1)S(1)}, bf16[320,1024]{1,0:T(8,128)(2,1)S(1)}, u32[]{:S(2)}, u32[]{:S(2)}) collective-permute-start(bf16[320,1024]{1,0:T(8,128)(2,1)S(1)} %get-tuple-element.494.refs_0_), channel_id=1, source_target_pairs={{0,2},{2,0},{1,3},{3,1},{4,6},{6,4},{5,7},{7,5},{8,10},{10,8},{9,1... | collective-permute-start | bytes 1966088 | tf_op jit(solution)/shard_map/ppermute | solution.py:781
  156.5 9.8 %collective-permute-start.37 = (bf16[160,1024]{1,0:T(8,128)(2,1)S(1)}, bf16[160,1024]{1,0:T(8,128)(2,1)S(1)}, u32[]{:S(2)}, u32[]{:S(2)}) collective-permute-start(bf16[160,1024]{1,0:T(8,128)(2,1)S(1)} %get-tuple-element.495), channel_id=1, source_target_pairs={{0,1},{1,0},{2,3},{3,2},{4,5},{5,4},{6,7},{7,6},{8,9},{9,8},{10,11... | collective-permute-start | bytes 983048 | tf_op jit(solution)/shard_map/ppermute | solution.py:777
  156.5 9.8 %collective-permute-start.38 = (bf16[160,1024]{1,0:T(8,128)(2,1)S(1)}, bf16[160,1024]{1,0:T(8,128)(2,1)S(1)}, u32[]{:S(2)}, u32[]{:S(2)}) collective-permute-start(bf16[160,1024]{1,0:T(8,128)(2,1)S(1)} %get-tuple-element.496), channel_id=1, source_target_pairs={{0,1},{1,0},{2,3},{3,2},{4,5},{5,4},{6,7},{7,6},{8,9},{9,8},{10,11... | collective-permute-start | bytes 983048 | tf_op jit(solution)/shard_map/ppermute | solution.py:777
  165.8 46.9 %collective-permute-start.51 = (bf16[512,2048]{1,0:T(8,128)(2,1)S(1)}, bf16[512,2048]{1,0:T(8,128)(2,1)S(1)}, u32[]{:S(2)}, u32[]{:S(2)}) collective-permute-start(bf16[512,2048]{1,0:T(8,128)(2,1)S(1)} %get-tuple-element.528.refs_3_.refs_1_), channel_id=1, source_target_pairs={{0,4},{4,0},{8,12},{12,8},{16,20},{20,16},{24,28},{28,24},{1,5},{5... | collective-permute-start | bytes 6291464 | tf_op jit(solution)/shard_map/ppermute | solution.py:677
  181.7 16.8 %collective-permute-start.48 = (bf16[320,1024]{1,0:T(8,128)(2,1)S(1)}, bf16[320,1024]{1,0:T(8,128)(2,1)S(1)}, u32[]{:S(2)}, u32[]{:S(2)}) collective-permute-start(bf16[320,1024]{1,0:T(8,128)(2,1)S(1)} %get-tuple-element.522), channel_id=1, source_target_pairs={{0,2},{2,0},{1,3},{3,1},{4,6},{6,4},{5,7},{7,5},{8,10},{10,8},{9,1... | collective-permute-start | bytes 1966088 | tf_op jit(solution)/shard_map/ppermute | solution.py:781
  199.2 18.6 %collective-permute-start.52 = (bf16[320,1024]{1,0:T(8,128)(2,1)S(1)}, bf16[320,1024]{1,0:T(8,128)(2,1)S(1)}, u32[]{:S(2)}, u32[]{:S(2)}) collective-permute-start(bf16[320,1024]{1,0:T(8,128)(2,1)S(1)} %get-tuple-element.525.refs_0_), channel_id=1, source_target_pairs={{0,2},{2,0},{1,3},{3,1},{4,6},{6,4},{5,7},{7,5},{8,10},{10,8},{9,1... | collective-permute-start | bytes 1966088 | tf_op jit(solution)/shard_map/ppermute | solution.py:781
  199.8 15.3 %collective-permute-start.53 = (bf16[160,1024]{1,0:T(8,128)(2,1)S(1)}, bf16[160,1024]{1,0:T(8,128)(2,1)S(1)}, u32[]{:S(2)}, u32[]{:S(2)}) collective-permute-start(bf16[160,1024]{1,0:T(8,128)(2,1)S(1)} %copy-done.85), channel_id=1, source_target_pairs={{0,1},{1,0},{2,3},{3,2},{4,5},{5,4},{6,7},{7,6},{8,9},{9,8},{10,11... | collective-permute-start | bytes 983048 | tf_op jit(solution)/shard_map/ppermute | solution.py:777
  200.8 14.3 %collective-permute-start.54 = (bf16[160,1024]{1,0:T(8,128)(2,1)S(1)}, bf16[160,1024]{1,0:T(8,128)(2,1)S(1)}, u32[]{:S(2)}, u32[]{:S(2)}) collective-permute-start(bf16[160,1024]{1,0:T(8,128)(2,1)S(1)} %copy-done.83), channel_id=1, source_target_pairs={{0,1},{1,0},{2,3},{3,2},{4,5},{5,4},{6,7},{7,6},{8,9},{9,8},{10,11... | collective-permute-start | bytes 983048 | tf_op jit(solution)/shard_map/ppermute | solution.py:777
  229.4 17.1 %collective-permute-start.63 = (bf16[320,1024]{1,0:T(8,128)(2,1)}, bf16[320,1024]{1,0:T(8,128)(2,1)}, u32[]{:S(2)}, u32[]{:S(2)}) collective-permute-start(bf16[320,1024]{1,0:T(8,128)(2,1)} %get-tuple-element.559), channel_id=1, source_target_pairs={{0,2},{2,0},{1,3},{3,1},{4,6},{6,4},{5,7},{7,5},{8,10},{10,8},{9,1... | collective-permute-start | bytes 1966088 | tf_op jit(solution)/shard_map/ppermute | solution.py:781
  236.2 25.5 %collective-permute-start.66 = (bf16[512,1024]{1,0:T(8,128)(2,1)}, bf16[512,1024]{1,0:T(8,128)(2,1)}, u32[]{:S(2)}, u32[]{:S(2)}) collective-permute-start(bf16[512,1024]{1,0:T(8,128)(2,1)} %get-tuple-element.568), channel_id=1, source_target_pairs={{0,4},{4,0},{8,12},{12,8},{16,20},{20,16},{24,28},{28,24},{1,5},{5... | collective-permute-start | bytes 3145736 | tf_op jit(solution)/shard_map/ppermute | solution.py:677
  250.1 16.0 %collective-permute-start.67 = (bf16[320,1024]{1,0:T(8,128)(2,1)S(1)}, bf16[320,1024]{1,0:T(8,128)(2,1)S(1)}, u32[]{:S(2)}, u32[]{:S(2)}) collective-permute-start(bf16[320,1024]{1,0:T(8,128)(2,1)S(1)} %get-tuple-element.564.refs_0_.refs_8_), channel_id=1, source_target_pairs={{0,2},{2,0},{1,3},{3,1},{4,6},{6,4},{5,7},{7,5},{8,10},{10,8},{9,1... | collective-permute-start | bytes 1966088 | tf_op jit(solution)/shard_map/ppermute | solution.py:781
  250.5 14.3 %collective-permute-start.64 = (bf16[160,1024]{1,0:T(8,128)(2,1)S(1)}, bf16[160,1024]{1,0:T(8,128)(2,1)S(1)}, u32[]{:S(2)}, u32[]{:S(2)}) collective-permute-start(bf16[160,1024]{1,0:T(8,128)(2,1)S(1)} %get-tuple-element.565), channel_id=1, source_target_pairs={{0,1},{1,0},{2,3},{3,2},{4,5},{5,4},{6,7},{7,6},{8,9},{9,8},{10,11... | collective-permute-start | bytes 983048 | tf_op jit(solution)/shard_map/ppermute | solution.py:777
  250.5 14.3 %collective-permute-start.65 = (bf16[160,1024]{1,0:T(8,128)(2,1)S(1)}, bf16[160,1024]{1,0:T(8,128)(2,1)S(1)}, u32[]{:S(2)}, u32[]{:S(2)}) collective-permute-start(bf16[160,1024]{1,0:T(8,128)(2,1)S(1)} %get-tuple-element.566), channel_id=1, source_target_pairs={{0,1},{1,0},{2,3},{3,2},{4,5},{5,4},{6,7},{7,6},{8,9},{9,8},{10,11... | collective-permute-start | bytes 983048 | tf_op jit(solution)/shard_map/ppermute | solution.py:777
  263.2 13.3 %collective-permute-start.70 = (bf16[256,1024]{1,0:T(8,128)(2,1)S(1)}, bf16[256,1024]{1,0:T(8,128)(2,1)S(1)}, u32[]{:S(2)}, u32[]{:S(2)}) collective-permute-start(bf16[256,1024]{1,0:T(8,128)(2,1)S(1)} %get-tuple-element.582), channel_id=1, source_target_pairs={{0,8},{4,12},{8,0},{12,4},{16,24},{20,28},{24,16},{28,20},{1,9},{5... | collective-permute-start | bytes 1572872 | tf_op jit(solution)/shard_map/ppermute | solution.py:677
  263.6 24.1 %collective-permute-start.76 = (bf16[512,1024]{1,0:T(8,128)(2,1)S(1)}, bf16[512,1024]{1,0:T(8,128)(2,1)S(1)}, u32[]{:S(2)}, u32[]{:S(2)}) collective-permute-start(bf16[512,1024]{1,0:T(8,128)(2,1)S(1)} %copy-done.79), channel_id=1, source_target_pairs={{0,4},{4,0},{8,12},{12,8},{16,20},{20,16},{24,28},{28,24},{1,5},{5... | collective-permute-start | bytes 3145736 | tf_op jit(solution)/shard_map/ppermute | solution.py:677
  281.1 17.0 %collective-permute-start.75 = (bf16[320,1024]{1,0:T(8,128)(2,1)}, bf16[320,1024]{1,0:T(8,128)(2,1)S(1)}, u32[]{:S(2)}, u32[]{:S(2)}) collective-permute-start(bf16[320,1024]{1,0:T(8,128)(2,1)} %get-tuple-element.593), channel_id=1, source_target_pairs={{0,2},{2,0},{1,3},{3,1},{4,6},{6,4},{5,7},{7,5},{8,10},{10,8},{9,1... | collective-permute-start | bytes 1966088 | tf_op jit(solution)/shard_map/ppermute | solution.py:781
  293.2 26.7 %collective-permute-start.80 = (bf16[512,1024]{1,0:T(8,128)(2,1)}, bf16[512,1024]{1,0:T(8,128)(2,1)S(1)}, u32[]{:S(2)}, u32[]{:S(2)}) collective-permute-start(bf16[512,1024]{1,0:T(8,128)(2,1)} %get-tuple-element.608), channel_id=1, source_target_pairs={{0,4},{4,0},{8,12},{12,8},{16,20},{20,16},{24,28},{28,24},{1,5},{5... | collective-permute-start | bytes 3145736 | tf_op jit(solution)/shard_map/ppermute | solution.py:677
  299.1 20.8 %collective-permute-start.79 = (bf16[320,1024]{1,0:T(8,128)(2,1)S(1)}, bf16[320,1024]{1,0:T(8,128)(2,1)S(1)}, u32[]{:S(2)}, u32[]{:S(2)}) collective-permute-start(bf16[320,1024]{1,0:T(8,128)(2,1)S(1)} %get-tuple-element.601.refs_0_), channel_id=1, source_target_pairs={{0,2},{2,0},{1,3},{3,1},{4,6},{6,4},{5,7},{7,5},{8,10},{10,8},{9,1... | collective-permute-start | bytes 1966088 | tf_op jit(solution)/shard_map/ppermute | solution.py:781
  299.9 20.0 %collective-permute-start.81 = (bf16[256,1024]{1,0:T(8,128)(2,1)S(1)}, bf16[256,1024]{1,0:T(8,128)(2,1)S(1)}, u32[]{:S(2)}, u32[]{:S(2)}) collective-permute-start(bf16[256,1024]{1,0:T(8,128)(2,1)S(1)} %copy-done.81), channel_id=1, source_target_pairs={{0,8},{4,12},{8,0},{12,4},{16,24},{20,28},{24,16},{28,20},{1,9},{5... | collective-permute-start | bytes 1572872 | tf_op jit(solution)/shard_map/ppermute | solution.py:677
  301.5 17.0 %collective-permute-start.82 = (bf16[128,1024]{1,0:T(8,128)(2,1)S(1)}, bf16[128,1024]{1,0:T(8,128)(2,1)S(1)}, u32[]{:S(2)}, u32[]{:S(2)}) collective-permute-start(bf16[128,1024]{1,0:T(8,128)(2,1)S(1)} %get-tuple-element.610), channel_id=1, source_target_pairs={{0,16},{4,20},{8,24},{12,28},{16,0},{20,4},{24,8},{28,12},{1,17},{... | collective-permute-start | bytes 786440 | tf_op jit(solution)/shard_map/ppermute | solution.py:677
  328.1 21.1 %collective-permute-start.90 = (bf16[320,1024]{1,0:T(8,128)(2,1)S(1)}, bf16[320,1024]{1,0:T(8,128)(2,1)S(1)}, u32[]{:S(2)}, u32[]{:S(2)}) collective-permute-start(bf16[320,1024]{1,0:T(8,128)(2,1)S(1)} %get-tuple-element.633), channel_id=1, source_target_pairs={{0,2},{2,0},{1,3},{3,1},{4,6},{6,4},{5,7},{7,5},{8,10},{10,8},{9,1... | collective-permute-start | bytes 1966088 | tf_op jit(solution)/shard_map/ppermute | solution.py:781
  333.1 29.4 %collective-permute-start.93 = (bf16[512,1024]{1,0:T(8,128)(2,1)S(1)}, bf16[512,1024]{1,0:T(8,128)(2,1)S(1)}, u32[]{:S(2)}, u32[]{:S(2)}) collective-permute-start(bf16[512,1024]{1,0:T(8,128)(2,1)S(1)} %get-tuple-element.646), channel_id=1, source_target_pairs={{0,4},{4,0},{8,12},{12,8},{16,20},{20,16},{24,28},{28,24},{1,5},{5... | collective-permute-start | bytes 3145736 | tf_op jit(solution)/shard_map/ppermute | solution.py:677
  334.5 14.7 %collective-permute-start.91 = (bf16[128,1024]{1,0:T(8,128)(2,1)S(1)}, bf16[128,1024]{1,0:T(8,128)(2,1)S(1)}, u32[]{:S(2)}, u32[]{:S(2)}) collective-permute-start(bf16[128,1024]{1,0:T(8,128)(2,1)S(1)} %get-tuple-element.640), channel_id=1, source_target_pairs={{0,16},{4,20},{8,24},{12,28},{16,0},{20,4},{24,8},{28,12},{1,17},{... | collective-permute-start | bytes 786440 | tf_op jit(solution)/shard_map/ppermute | solution.py:677
  336.3 18.5 %collective-permute-start.89 = (bf16[256,1024]{1,0:T(8,128)(2,1)S(1)}, bf16[256,1024]{1,0:T(8,128)(2,1)S(1)}, u32[]{:S(2)}, u32[]{:S(2)}) collective-permute-start(bf16[256,1024]{1,0:T(8,128)(2,1)S(1)} %get-tuple-element.630), channel_id=1, source_target_pairs={{0,8},{4,12},{8,0},{12,4},{16,24},{20,28},{24,16},{28,20},{1,9},{5... | collective-permute-start | bytes 1572872 | tf_op jit(solution)/shard_map/ppermute | solution.py:677
  350.5 18.1 %collective-permute-start.97 = (bf16[320,1024]{1,0:T(8,128)(2,1)S(1)}, bf16[320,1024]{1,0:T(8,128)(2,1)S(1)}, u32[]{:S(2)}, u32[]{:S(2)}) collective-permute-start(bf16[320,1024]{1,0:T(8,128)(2,1)S(1)} %get-tuple-element.651.refs_0_.refs_8_), channel_id=1, source_target_pairs={{0,2},{2,0},{1,3},{3,1},{4,6},{6,4},{5,7},{7,5},{8,10},{10,8},{9,1... | collective-permute-start | bytes 1966088 | tf_op jit(solution)/shard_map/ppermute | solution.py:781
  351.3 7.9 %collective-permute-start.94 = (bf16[160,1024]{1,0:T(8,128)(2,1)S(1)}, bf16[160,1024]{1,0:T(8,128)(2,1)S(1)}, u32[]{:S(2)}, u32[]{:S(2)}) collective-permute-start(bf16[160,1024]{1,0:T(8,128)(2,1)S(1)} %get-tuple-element.652), channel_id=1, source_target_pairs={{0,1},{1,0},{2,3},{3,2},{4,5},{5,4},{6,7},{7,6},{8,9},{9,8},{10,11... | collective-permute-start | bytes 983048 | tf_op jit(solution)/shard_map/ppermute | solution.py:777
  351.3 8.6 %collective-permute-start.95 = (bf16[160,1024]{1,0:T(8,128)(2,1)S(1)}, bf16[160,1024]{1,0:T(8,128)(2,1)S(1)}, u32[]{:S(2)}, u32[]{:S(2)}) collective-permute-start(bf16[160,1024]{1,0:T(8,128)(2,1)S(1)} %get-tuple-element.653), channel_id=1, source_target_pairs={{0,1},{1,0},{2,3},{3,2},{4,5},{5,4},{6,7},{7,6},{8,9},{9,8},{10,11... | collective-permute-start | bytes 983048 | tf_op jit(solution)/shard_map/ppermute | solution.py:777
  354.9 13.7 %collective-permute-start.98 = (bf16[128,1024]{1,0:T(8,128)(2,1)S(1)}, bf16[128,1024]{1,0:T(8,128)(2,1)S(1)}, u32[]{:S(2)}, u32[]{:S(2)}) collective-permute-start(bf16[128,1024]{1,0:T(8,128)(2,1)S(1)} %get-tuple-element.661), channel_id=1, source_target_pairs={{0,16},{4,20},{8,24},{12,28},{16,0},{20,4},{24,8},{28,12},{1,17},{... | collective-permute-start | bytes 786440 | tf_op jit(solution)/shard_map/ppermute | solution.py:677
  359.1 32.2 %collective-permute-start.92 = (bf16[512,1024]{1,0:T(8,128)(2,1)}, bf16[512,1024]{1,0:T(8,128)(2,1)S(1)}, u32[]{:S(2)}, u32[]{:S(2)}) collective-permute-start(bf16[512,1024]{1,0:T(8,128)(2,1)} %get-tuple-element.644), channel_id=1, source_target_pairs={{0,4},{4,0},{8,12},{12,8},{16,20},{20,16},{24,28},{28,24},{1,5},{5... | collective-permute-start | bytes 3145736 | tf_op jit(solution)/shard_map/ppermute | solution.py:677
  362.7 17.2 %collective-permute-start.96 = (bf16[256,1024]{1,0:T(8,128)(2,1)S(1)}, bf16[256,1024]{1,0:T(8,128)(2,1)S(1)}, u32[]{:S(2)}, u32[]{:S(2)}) collective-permute-start(bf16[256,1024]{1,0:T(8,128)(2,1)S(1)} %get-tuple-element.658), channel_id=1, source_target_pairs={{0,8},{4,12},{8,0},{12,4},{16,24},{20,28},{24,16},{28,20},{1,9},{5... | collective-permute-start | bytes 1572872 | tf_op jit(solution)/shard_map/ppermute | solution.py:677
  389.3 27.5 %collective-permute-start.113 = (bf16[512,1024]{1,0:T(8,128)(2,1)}, bf16[512,1024]{1,0:T(8,128)(2,1)S(1)}, u32[]{:S(2)}, u32[]{:S(2)}) collective-permute-start(bf16[512,1024]{1,0:T(8,128)(2,1)} %get-tuple-element.706), channel_id=1, source_target_pairs={{0,4},{4,0},{8,12},{12,8},{16,20},{20,16},{24,28},{28,24},{1,5},{5... | collective-permute-start | bytes 3145736 | tf_op jit(solution)/shard_map/ppermute | solution.py:677
  389.9 18.6 %collective-permute-start.106 = (bf16[320,1024]{1,0:T(8,128)(2,1)S(1)}, bf16[320,1024]{1,0:T(8,128)(2,1)S(1)}, u32[]{:S(2)}, u32[]{:S(2)}) collective-permute-start(bf16[320,1024]{1,0:T(8,128)(2,1)S(1)} %get-tuple-element.687), channel_id=1, source_target_pairs={{0,2},{2,0},{1,3},{3,1},{4,6},{6,4},{5,7},{7,5},{8,10},{10,8},{9,1... | collective-permute-start | bytes 1966088 | tf_op jit(solution)/shard_map/ppermute | solution.py:781
  391.6 19.1 %collective-permute-start.105 = (bf16[256,1024]{1,0:T(8,128)(2,1)S(1)}, bf16[256,1024]{1,0:T(8,128)(2,1)S(1)}, u32[]{:S(2)}, u32[]{:S(2)}) collective-permute-start(bf16[256,1024]{1,0:T(8,128)(2,1)S(1)} %get-tuple-element.684), channel_id=1, source_target_pairs={{0,8},{4,12},{8,0},{12,4},{16,24},{20,28},{24,16},{28,20},{1,9},{5... | collective-permute-start | bytes 1572872 | tf_op jit(solution)/shard_map/ppermute | solution.py:677
  391.7 16.8 %collective-permute-start.107 = (bf16[128,1024]{1,0:T(8,128)(2,1)S(1)}, bf16[128,1024]{1,0:T(8,128)(2,1)S(1)}, u32[]{:S(2)}, u32[]{:S(2)}) collective-permute-start(bf16[128,1024]{1,0:T(8,128)(2,1)S(1)} %get-tuple-element.691), channel_id=1, source_target_pairs={{0,16},{4,20},{8,24},{12,28},{16,0},{20,4},{24,8},{28,12},{1,17},{... | collective-permute-start | bytes 786440 | tf_op jit(solution)/shard_map/ppermute | solution.py:677
  415.2 23.8 %collective-permute-start.112 = (bf16[320,1024]{1,0:T(8,128)(2,1)S(1)}, bf16[320,1024]{1,0:T(8,128)(2,1)S(1)}, u32[]{:S(2)}, u32[]{:S(2)}) collective-permute-start(bf16[320,1024]{1,0:T(8,128)(2,1)S(1)} %get-tuple-element.704), channel_id=1, source_target_pairs={{0,2},{2,0},{1,3},{3,1},{4,6},{6,4},{5,7},{7,5},{8,10},{10,8},{9,1... | collective-permute-start | bytes 1966088 | tf_op jit(solution)/shard_map/ppermute | solution.py:781
  417.0 20.7 %collective-permute-start.114 = (bf16[256,1024]{1,0:T(8,128)(2,1)S(1)}, bf16[256,1024]{1,0:T(8,128)(2,1)S(1)}, u32[]{:S(2)}, u32[]{:S(2)}) collective-permute-start(bf16[256,1024]{1,0:T(8,128)(2,1)S(1)} %get-tuple-element.709), channel_id=1, source_target_pairs={{0,8},{4,12},{8,0},{12,4},{16,24},{20,28},{24,16},{28,20},{1,9},{5... | collective-permute-start | bytes 1572872 | tf_op jit(solution)/shard_map/ppermute | solution.py:677
  421.8 37.1 %collective-permute-start.120 = (bf16[128,1024]{1,0:T(8,128)(2,1)S(1)}, bf16[128,1024]{1,0:T(8,128)(2,1)S(1)}, u32[]{:S(2)}, u32[]{:S(2)}) collective-permute-start(bf16[128,1024]{1,0:T(8,128)(2,1)S(1)} %get-tuple-element.743), channel_id=1, source_target_pairs={{0,16},{4,20},{8,24},{12,28},{16,0},{20,4},{24,8},{28,12},{1,17},{... | collective-permute-start | bytes 786440 | tf_op jit(solution)/shard_map/ppermute | solution.py:677
  437.9 22.1 %collective-permute-start.121 = (bf16[128,1024]{1,0:T(8,128)(2,1)S(1)}, bf16[128,1024]{1,0:T(8,128)(2,1)S(1)}, u32[]{:S(2)}, u32[]{:S(2)}) collective-permute-start(bf16[128,1024]{1,0:T(8,128)(2,1)S(1)} %get-tuple-element.750), channel_id=1, source_target_pairs={{0,16},{4,20},{8,24},{12,28},{16,0},{20,4},{24,8},{28,12},{1,17},{... | collective-permute-start | bytes 786440 | tf_op jit(solution)/shard_map/ppermute | solution.py:677
  445.9 6.4 %collective-permute-start.118 = (f32[8,1024]{1,0:T(8,128)S(1)}, f32[8,1024]{1,0:T(8,128)S(1)}, u32[]{:S(2)}, u32[]{:S(2)}) collective-permute-start(f32[8,1024]{1,0:T(8,128)S(1)} %get-tuple-element.731.refs_0_), channel_id=1, source_target_pairs={{0,8},{4,12},{8,0},{12,4},{16,24},{20,28},{24,16},{28,20},{1,9},{5... | collective-permute-start | bytes 98312 | tf_op jit(solution)/shard_map/ppermute | solution.py:677
  (154 other events, 648.3 us)

commit v4 on v3

--- a/solution.py
+++ b/solution.py
@@ -418,60 +418,71 @@
 COLUMNS = 256
 
 
-def two_halves(both, weights, here):
-    first, second = weights
-    half = first.shape[0]
-    return dot(both[:, :half], first[:, here]) + dot(both[:, half:], second[:, here])
-
-
-def project_kernel(begin, a, b, c, first, second, out):
+def by_parts(both, weights, here):
+    total, row = 0.0, 0
+    for part in weights:
+        total = total + dot(both[:, row : row + part.shape[0]], part[:, here])
+        row += part.shape[0]
+    return total
+
+
+def project_kernel(begin, many, a, b, c, *refs):
+    weights, (out,) = refs[:many], refs[many:]
     both = jnp.concatenate([a[...], b[...], c[...]], axis=0)
     for start in range(0, out.shape[1], COLUMNS):
         here = slice(begin + start, begin + start + COLUMNS)
-        out[:, start : start + COLUMNS] = two_halves(both, (first, second), here).astype(
+        out[:, start : start + COLUMNS] = by_parts(both, weights, here).astype(
             jnp.bfloat16
         )
 
 
-def project(run, piece, first, second, begin, width):
+def project(run, piece, *rest):
+    *weights, begin, width = rest
     outs = [struct((sum(part.shape[0] for part in piece), width))]
-    body = functools.partial(project_kernel, begin)
-    return run("project", body, [*piece, first, second], outs, 14)[0]
-
-
-def widen_kernel(begin, a, b, c, first, second, active, slope):
+    body = functools.partial(project_kernel, begin, len(weights))
+    return run("project", body, [*piece, *weights], outs, 14)[0]
+
+
+def widen_kernel(begin, many, a, b, c, *refs):
+    weights, (active, slope) = refs[:many], refs[many:]
     both = jnp.concatenate([a[...], b[...], c[...]], axis=0)
     for start in range(0, active.shape[1], COLUMNS):
         here = slice(start, start + COLUMNS)
-        hidden = two_halves(both, (first, second), slice(begin + start, begin + start + COLUMNS))
+        hidden = by_parts(both, weights, slice(begin + start, begin + start + COLUMNS))
         below = 0.5 + 0.5 * lax.erf(hidden * (0.5**0.5))
         density = jnp.exp(-0.5 * hidden * hidden) * 0.3989422804014327
         active[:, here] = (hidden * below).astype(jnp.bfloat16)
         slope[:, here] = (below + hidden * density).astype(jnp.bfloat16)
 
 
-def widen(run, piece, first, second, begin, width):
+def widen(run, piece, *rest):
+    *weights, begin, width = rest
     outs = [struct((sum(part.shape[0] for part in piece), width))] * 2
-    return run("widen", functools.partial(widen_kernel, begin), [*piece, first, second], outs, 14)
-
-
-def bend_kernel(begin, a, b, c, first, second, slope, out):
+    body = functools.partial(widen_kernel, begin, len(weights))
+    return run("widen", body, [*piece, *weights], outs, 14)
+
+
+def bend_kernel(begin, many, a, b, c, *refs):
+    weights, (slope, out) = refs[:many], refs[many:]
     both = jnp.concatenate([a[...], b[...], c[...]], axis=0)
     for start in range(0, out.shape[1], COLUMNS):
         here = slice(start, start + COLUMNS)
-        grad = two_halves(both, (first, second), slice(begin + start, begin + start + COLUMNS))
+        grad = by_parts(both, weights, slice(begin + start, begin + start + COLUMNS))
         out[:, here] = (grad * slope[:, here].astype(jnp.float32)).astype(jnp.bfloat16)
 
 
-def bend_back(run, piece, first, second, begin, slope):
-    return run("bend_back", functools.partial(bend_kernel, begin), [*piece, first, second, slope], [struct(slope.shape)], 14)[0]
-
-
-def narrow_kernel(begin, piece, first, second, kept, sent, sent_more):
+def bend_back(run, piece, *rest):
+    *weights, begin, slope = rest
+    body = functools.partial(bend_kernel, begin, len(weights))
+    return run("bend_back", body, [*piece, *weights, slope], [struct(slope.shape)], 14)[0]
+
+
+def narrow_kernel(begin, many, piece, *refs):
+    weights_parts, (kept, sent, sent_more) = refs[:many], refs[many:]
     half = kept.shape[0]
     part = sent.shape[0]
     columns = slice(begin, begin + piece.shape[1])
-    for index, weights in enumerate((first, second)):
+    for index, weights in enumerate(weights_parts):
         for start in range(0, weights.shape[0], COLUMNS):
             there = index * weights.shape[0] + start
             here = slice(there, there + COLUMNS)
@@ -482,10 +493,12 @@
             sent_more[:, here] = both[half + part :]
 
 
-def narrow(run, piece, first, second, begin):
-    rows, width = piece.shape[0] // 2, 2 * first.shape[0]
+def narrow(run, piece, *rest):
+    *weights, begin = rest
+    rows, width = piece.shape[0] // 2, sum(part.shape[0] for part in weights)
     outs = [struct((rows, width)), *[struct((rows // 2, width))] * 2]
-    kept, *sent = run("narrow", functools.partial(narrow_kernel, begin), [piece, first, second], outs, 14)
+    body = functools.partial(narrow_kernel, begin, len(weights))
+    kept, *sent = run("narrow", body, [piece, *weights], outs, 14)
     return kept, sent
 
 
@@ -580,24 +593,42 @@
     )
 
 
-def squares_kernel(places, *refs):
+def squares_place(index):
+    return 8 + index // 8, index % 8 * 128
+
+
+def squares_kernel(places, vectors, *refs):
     out = refs[-1]
-    for ref, rows in zip(refs[:-1], places):
-        for index, row in enumerate(rows):
+    out[:8, :] = vectors[...]
+    out[8:, :] = jnp.zeros_like(out[8:, :])
+    for ref, names in zip(refs[:-1], places):
+        for index, name in enumerate(names):
             sums = jnp.sum(ref[index], axis=-1, keepdims=True)
-            out[2 * row : 2 * row + 2, :] = jnp.broadcast_to(sums, (2, out.shape[1]))
-
-
-def squares_of(run, places, *column_sums):
-    rows = 2 * sum(map(len, places))
+            for part in range(2):
+                row, lane = squares_place(2 * name + part)
+                out[row : row + 1, lane : lane + 128] = jnp.broadcast_to(
+                    sums[part : part + 1], (1, 128)
+                )
+
+
+def sums_of(run, places, vectors, *column_sums):
     body = functools.partial(squares_kernel, places)
-    return run("squares_of", body, list(column_sums), [struct((rows, 128), jnp.float32)], 4)[0]
+    return run("sums_of", body, [vectors, *column_sums], [struct((16, D), jnp.float32)], 4)[0]
 
 
 def apply_kernel(begin, total, weights, step, new, low):
-    row = 2 * (6 * pl.program_id(0) + begin + pl.program_id(1))
-    size, move = jnp.sqrt(total[pl.ds(row, 1), :1]), jnp.sqrt(total[pl.ds(row + 1, 1), :1])
-    rate = LEARN_RATE * (size / move)
+    index = 2 * (6 * pl.program_id(0) + begin + pl.program_id(1))
+
+    numbers = total[8:, :]
+    here_row = lax.broadcasted_iota(jnp.int32, numbers.shape, 0) + 8
+    here_lane = lax.broadcasted_iota(jnp.int32, numbers.shape, 1)
+
+    def root(at):
+        row, lane = squares_place(at)
+        chosen = jnp.where((here_row == row) & (here_lane == lane), numbers, 0.0)
+        return jnp.sqrt(jnp.sum(jnp.sum(chosen, axis=0, keepdims=True), axis=1, keepdims=True))
+
+    rate = LEARN_RATE * (root(index) / root(index + 1))
     value = weights[...].reshape(weights.shape[2:]) - rate * step[...].reshape(step.shape[2:])
     new[...] = value.reshape(new.shape)
     low[...] = value.astype(jnp.bfloat16).reshape(low.shape)
@@ -703,6 +734,19 @@
     def take(self, span=0):
         self.run.settle(self.wholes[span][1])
         return self.wholes[span]
+
+    def early(self):
+        self.ahead = self.rows.swap(self.block, self.rows.strides[-1])
+
+    def late(self):
+        shape = struct(self.there.shape)
+        (self.behind,) = self.run("copy", block_kernel, [self.there], [shape], 6)
+        self.behind_there = self.rows.swap(self.behind, self.rows.strides[-1])
+
+    def take_parts(self):
+        self.run.settle(self.ahead)
+        self.run.settle(self.behind_there)
+        return self.block, self.behind, self.ahead, self.behind_there
 
 
 def stack_kernel(*refs):
@@ -852,12 +896,12 @@
     output_way.far()
     inputs_way.last()
     up_way.far()
-    output_way.near()
     normed.pass_on()
     (stream_grad,) = move_columns(run, [cotangent], order, [count], False)
     back = Exchange(run, cast(run, stream_grad))
+    output_way.near()
+    up_way.near()
     output_way.last()
-    up_way.near()
     inputs_map = inputs_way.take()
     projected = [project(run, normed.near(), *inputs_map, 0, 3 * width)]
     projected.append(project(run, normed.far(), *inputs_map, 0, 3 * width))
@@ -871,11 +915,12 @@
     settle(down_way.there)
     mixed = collect(run, attended[0], attended[1], output_map, 0)
     down_way.near()
+    down_way.early()
     mixer_way.far()
     dense_way.ways[0].far()
     middle, low = norm(run, params_here, 2, stream, *mixed)
     normed_two = Exchange(run, low)
-    down_way.last()
+    down_way.late()
     mixer_way.near()
     settle(dense_way.ways[0].there)
     dense_way.ways[1].far()
@@ -884,19 +929,21 @@
     active[0], slope[0] = widen(run, normed_two.near(), *up_map, wide)
     settle(mixer_way.there)
     settle(dense_way.ways[1].there)
+    settle(down_way.ahead)
     normed_two.pass_on()
+    mixer_way.last()
+    dense_way.near()
     active[1], slope[1] = widen(run, normed_two.far(), *up_map, wide)
-    down_map = (*down_way.take(), 0)
+    down_map = (*down_way.take_parts(), 0)
     saved.append((stream, normed, projected, attended, middle, normed_two, active, slope))
     saved[-1] += ((*inputs_map, 0), (*output_map, 0), up_map, down_map)
 
-    widened = collect(run, *active, down_map[:2], down_map[2])
-    mixer_way.last()
-    dense_way.near()
+    widened = collect(run, *active, down_map[:-1], down_map[-1])
+    settle(dense_way.there)
+    inputs_map = mixer_way.take()
     stream, low = norm(run, params_here, 4, middle, *widened)
     normed = Exchange(run, low)
     dense_way.last()
-    inputs_map = mixer_way.take()
     projected = [project(run, normed.near(), *inputs_map, 0, 3 * width)]
     normed.pass_on()
     projected.append(project(run, normed.far(), *inputs_map, 0, 3 * width))
@@ -943,7 +990,7 @@
     stream_in, normed, projected, attended, middle, normed_two, active, slope = saved[1][:8]
     inputs_map, output_map, up_map, down_map = saved[1][8:]
     grad_hidden.append(bend_back(run, back.far(), *down_map, slope[1]))
-    raised = collect(run, *grad_hidden, up_map[:2], up_map[2])
+    raised = collect(run, *grad_hidden, up_map[:-1], up_map[-1])
     down_later = weight_grad((back.pieces(), active))
     up_later = weight_grad((normed_two.pieces(), grad_hidden))
     vectors[3], stream_grad, low = norm_back(run, params_here, 6, stream_grad, middle, *raised)
@@ -955,7 +1002,7 @@
     grad_projected = attend_back(run, place, mask, projected, grad_attended)
 
     down_later.settle()
-    lowered = collect(run, *grad_projected, inputs_map[:2], inputs_map[2])
+    lowered = collect(run, *grad_projected, inputs_map[:-1], inputs_map[-1])
     down_later.far()
     up_later.near()
     mixer_later = weight_grad((normed.pieces(), grad_projected), (turned.pieces(), attended))
@@ -970,7 +1017,7 @@
     down_later.settle()
     back.pass_on()
     grad_hidden.append(bend_back(run, back.far(), *down_map, slope[1]))
-    raised = collect(run, *grad_hidden, up_map[:2], up_map[2])
+    raised = collect(run, *grad_hidden, up_map[:-1], up_map[-1])
     mixer_later.near()
     up_later.far()
     down_grad = weight_grad((back.pieces(), active))
@@ -988,9 +1035,9 @@
     grad_attended.append(project(run, turned.far(), *output_map, width))
     grad_projected = attend_back(run, place, mask, projected, grad_attended)
 
+    mixer_grad = weight_grad((normed.pieces(), grad_projected), (turned.pieces(), attended))
     down_grad.settle()
-    lowered = collect(run, *grad_projected, inputs_map[:2], inputs_map[2])
-    mixer_grad = weight_grad((normed.pieces(), grad_projected), (turned.pieces(), attended))
+    lowered = collect(run, *grad_projected, inputs_map[:-1], inputs_map[-1])
     down_grad.far()
     up_grad.near()
     mixer_moments(1, mixer_later.terms())
@@ -998,33 +1045,28 @@
     vectors[0], stream_grad, low = norm_back(run, params_here, 0, stream_grad, stream_in, *lowered)
 
     up_grad.far()
-    middle, active, down_map = saved[-1][4], saved[-1][6], saved[-1][11]
-    widened = collect(run, *active, down_map[:2], down_map[2])
     mixer_grad.near()
-    dense_moments(0, (1,), down_grad.terms())
     all_rows = jnp.concatenate([jnp.sum(sums.reshape(2, 8, D), axis=1) for sums in vectors])
     (all_rows,) = move_columns(run, [all_rows], order, [layers * 4], True)
-    all_rows = add(run, all_rows, core_swap(all_rows), jnp.float32)
+    dense_moments(0, (1,), down_grad.terms())
     (grad_tokens,) = move_columns(run, [stream_grad], order, [count], True)
+    middle, active, down_map = saved[-1][4], saved[-1][6], saved[-1][11]
+    widened = collect(run, *active, down_map[:-1], down_map[-1])
     mixer_grad.far()
+    dense_moments(0, (0,), up_grad.terms())
     last_stream = add(run, middle, widened[0], jnp.float32, widened[1])
-    all_rows = add(run, all_rows, chip_swap(all_rows), jnp.float32)
+    (outcome,) = move_columns(run, [last_stream], order, [count], True)
+    mixer_moments(0, mixer_grad.terms())
+    total = sums_of(run, places, all_rows, *squares)
+    total = add(run, total, core_swap(total), jnp.float32)
+    total = add(run, total, chip_swap(total), jnp.float32)
     for stride in reversed(rows.strides):
-        all_rows = add(run, all_rows, rows.swap(all_rows, stride), jnp.float32)
-    (outcome,) = move_columns(run, [last_stream], order, [count], True)
-    dense_moments(0, (0,), up_grad.terms())
-    mixer_moments(0, mixer_grad.terms())
-    all_squares = squares_of(run, places, *squares)
-    all_squares = add(run, all_squares, core_swap(all_squares), jnp.float32)
-    all_squares = add(run, all_squares, chip_swap(all_squares), jnp.float32)
-    for stride in reversed(rows.strides):
-        all_squares = add(run, all_squares, rows.swap(all_squares, stride), jnp.float32)
-    all_vectors = all_rows
-    mixer_new, mixer_copy = apply(run, 0, all_squares, attention_weights, mixer_state[2])
-    dense_new, dense_copy = apply(run, 4, all_squares, dense_weights, dense_state[2])
-
-    total_squares = all_squares[:, 0].reshape(layers, 6, 2)
-    total_vectors = all_vectors.reshape(layers, 4, D)
+        total = add(run, total, rows.swap(total, stride), jnp.float32)
+    mixer_new, mixer_copy = apply(run, 0, total, attention_weights, mixer_state[2])
+    dense_new, dense_copy = apply(run, 4, total, dense_weights, dense_state[2])
+
+    total_vectors = total[: 4 * layers].reshape(layers, 4, D)
+    total_squares = total[8 : 8 + 3].reshape(24, 128)[:, 0].reshape(layers, 6, 2)
     sizes_all = jnp.sqrt(total_squares[:, :, 0])
     moves_all = jnp.sqrt(total_squares[:, :, 1])
     params_first, params_second, params_step = adam_part(

time: 496 us -> 491 us (0.990)
    ppermute x66 -> x65, waiting for transfers between devices: 18.9 us -> 16.1 us  [core_swap(): return lax.ppermute(values_in, 'mp', [(0, 1), (1, 0), (2, 3), (3, 2)])]
    unnamed x184 -> x189, local copies, waits for them, and re-layouts: 19.2 us -> 21.4 us
    ppermute x18 -> x17, starting transfers between devices: 16.6 us -> 15 us  [chip_swap(): return lax.ppermute(values_in, 'mp', [(0, 2), (2, 0), (1, 3), (3, 1)])]
    pallas_call x132 -> x127, Pallas kernels: 137 us -> 136 us  [__call__(): pl.pallas_call(wrapped, out_shape=[*outs, TOKEN], **places, input_output_...]
    ppermute x43 -> x41, waiting for transfers between devices: 162 us -> 161 us  [swap(): lax.ppermute(values, 'dp', [(source, source ^ stride) for source in range...]
    ppermute x66 -> x65, starting transfers between devices: 16.7 us -> 16.3 us  [core_swap(): return lax.ppermute(values_in, 'mp', [(0, 1), (1, 0), (2, 3), (3, 2)])]
    ppermute x18 -> x17, waiting for transfers between devices: 56.7 us -> 57.1 us  [chip_swap(): return lax.ppermute(values_in, 'mp', [(0, 2), (2, 0), (1, 3), (3, 1)])]
    ppermute x43 -> x41, starting transfers between devices: 53.4 us -> 53.4 us  [swap(): lax.ppermute(values, 'dp', [(source, source ^ stride) for source in range...]
  transfers between devices with their start and end apart: 127 -> 123, of which waited for: 65 -> 61; matrix products, arithmetic and copies ran while one was open for 1% -> 0% of each run, Pallas kernels for 24% -> 23%
where the time goes in v4:
time: 491 us; the launch traced here: 484 us
  waiting for transfers between devices  234 us (48%)
  Pallas kernels  136 us (28%)
  starting transfers between devices  84.6 us (17%)
  local copies, waits for them, and re-layouts  23.1 us (5%)
    ppermute x41, waiting for transfers between devices, swap(): lax.ppermute(values, 'dp', [(source, source ^ stride) for source in range...  161 us
    pallas_call x127, Pallas kernels, __call__(): pl.pallas_call(wrapped, out_shape=[*outs, TOKEN], **places, input_output_...  136 us
    ppermute x17, waiting for transfers between devices, chip_swap(): return lax.ppermute(values_in, 'mp', [(0, 2), (2, 0), (1, 3), (3, 1)])  57.1 us
    ppermute x41, starting transfers between devices, swap(): lax.ppermute(values, 'dp', [(source, source ^ stride) for source in range...  53.4 us
    unnamed x189, local copies, waits for them, and re-layouts  21.4 us
    ppermute x65, starting transfers between devices, core_swap(): return lax.ppermute(values_in, 'mp', [(0, 1), (1, 0), (2, 3), (3, 2)])  16.3 us
    ppermute x65, waiting for transfers between devices, core_swap(): return lax.ppermute(values_in, 'mp', [(0, 1), (1, 0), (2, 3), (3, 2)])  16.1 us
    ppermute x17, starting transfers between devices, chip_swap(): return lax.ppermute(values_in, 'mp', [(0, 2), (2, 0), (1, 3), (3, 1)])  15 us
  transfers between devices with their start and end apart: 123, of which 61 were waited for; matrix products, arithmetic and copies ran while one was open for 0% of the time, Pallas kernels for 23%

profile of v4, /device:TPU:0, one launch (start us, length us, event | category | flops | bytes accessed | tf_op | source)
XLA Modules:
  0.0 483.7 jit_solution(488926715455833885)
XLA Ops:
  3.1 4.0 collective-permute-start.2
  12.8 3.7 collective-permute-done.2.refs_1_.refs_3_
  19.9 7.9 %collective-permute-done.3.refs_1_ = bf16[256,768]{1,0:T(8,128)(2,1)S(1)} collective-permute-done((bf16[256,768]{1,0:T(8,128)(2,1)S(1)}, bf16[256,768]{1,0:T(8,128)(2,1)S(1)}, u32[]{:S(2)}, u32[]{:S(2)}) %collective-permute-start.3) | collective-permute-done | bytes 393248 | tf_op jit(solution)/shard_map/ppermute | solution.py:708
  29.8 3.3 collective-permute-start.8
  34.7 3.3 collective-permute-start.5
  42.3 5.8 %collective-permute-done.5.refs_1_.refs_3_ = bf16[128,256]{1,0:T(8,128)(2,1)S(1)} collective-permute-done((bf16[128,256]{1,0:T(8,128)(2,1)S(1)}, bf16[128,256]{1,0:T(8,128)(2,1)S(1)}, u32[]{:S(2)}, u32[]{:S(2)}) %collective-permute-start.5) | collective-permute-done | bytes 65568 | tf_op jit(solution)/shard_map/ppermute | solution.py:708
  51.8 2.9 collective-permute-done.7.refs_1_
  62.0 3.4 collective-permute-start.14
  67.9 2.9 attend.2
  73.7 2.5 collective-permute-done.14.refs_5_.refs_1_.refs_3_
  85.1 3.2 collective-permute-start.23
  88.5 10.4 %collective-permute-done.19.refs_3_ = bf16[320,1024]{1,0:T(8,128)(2,1)S(1)} collective-permute-done((bf16[320,1024]{1,0:T(8,128)(2,1)S(1)}, bf16[320,1024]{1,0:T(8,128)(2,1)S(1)}, u32[]{:S(2)}, u32[]{:S(2)}) %collective-permute-start.19) | collective-permute-done | bytes 655392 | tf_op jit(solution)/shard_map/ppermute | solution.py:825
  99.9 9.4 %collective-permute-done.24.refs_0_ = bf16[256,1024]{1,0:T(8,128)(2,1)S(1)} collective-permute-done((bf16[256,1024]{1,0:T(8,128)(2,1)S(1)}, bf16[256,1024]{1,0:T(8,128)(2,1)S(1)}, u32[]{:S(2)}, u32[]{:S(2)}) %collective-permute-start.24) | collective-permute-done | bytes 524320 | tf_op jit(solution)/shard_map/ppermute | solution.py:708
  111.6 3.0 collective-permute-start.30
  115.2 2.3 widen.4
  118.6 5.5 %collective-permute-done.26.refs_4_.refs_3_.refs_6_.refs_5_ = bf16[256,1024]{1,0:T(8,128)(2,1)S(1)} collective-permute-done((bf16[256,1024]{1,0:T(8,128)(2,1)S(1)}, bf16[256,1024]{1,0:T(8,128)(2,1)S(1)}, u32[]{:S(2)}, u32[]{:S(2)}) %collective-permute-start.26) | collective-permute-done | bytes 524320 | tf_op jit(solution)/shard_map/ppermute | solution.py:708
  124.1 3.9 collective-permute-done.30.refs_3_
  130.6 1.9 collective-permute-start.38
  133.0 2.3 widen.5
  141.9 13.9 %collective-permute-done.38.refs_5_.refs_1_ = bf16[256,2048]{1,0:T(8,128)(2,1)S(1)} collective-permute-done((bf16[256,2048]{1,0:T(8,128)(2,1)S(1)}, bf16[256,2048]{1,0:T(8,128)(2,1)S(1)}, u32[]{:S(2)}, u32[]{:S(2)}) %collective-permute-start.38) | collective-permute-done | bytes 1048608 | tf_op jit(solution)/shard_map/ppermute | solution.py:708
  162.6 11.2 %collective-permute-done.42.refs_0_ = bf16[320,1024]{1,0:T(8,128)(2,1)S(1)} collective-permute-done((bf16[320,1024]{1,0:T(8,128)(2,1)S(1)}, bf16[320,1024]{1,0:T(8,128)(2,1)S(1)}, u32[]{:S(2)}, u32[]{:S(2)}) %collective-permute-start.42) | collective-permute-done | bytes 655392 | tf_op jit(solution)/shard_map/ppermute | solution.py:825
  177.7 2.9 attend.3
  186.4 13.9 %collective-permute-done.49.refs_3_ = bf16[320,1024]{1,0:T(8,128)(2,1)S(1)} collective-permute-done((bf16[320,1024]{1,0:T(8,128)(2,1)S(1)}, bf16[320,1024]{1,0:T(8,128)(2,1)S(1)}, u32[]{:S(2)}, u32[]{:S(2)}) %collective-permute-start.49) | collective-permute-done | bytes 655392 | tf_op jit(solution)/shard_map/ppermute | solution.py:825
  202.1 3.2 collective-permute-done.52.refs_4_.refs_6_.refs_2_
  205.3 2.3 widen.6
  207.7 2.6 bend_back.4
  210.3 6.5 %collective-permute-done.53.refs_0_ = bf16[320,1024]{1,0:T(8,128)(2,1)S(1)} collective-permute-done((bf16[320,1024]{1,0:T(8,128)(2,1)S(1)}, bf16[320,1024]{1,0:T(8,128)(2,1)S(1)}, u32[]{:S(2)}, u32[]{:S(2)}) %collective-permute-start.53) | collective-permute-done | bytes 655392 | tf_op jit(solution)/shard_map/ppermute | solution.py:825
  219.1 2.3 widen.7
  230.4 4.0 weight_terms.6
  238.0 3.0 weight_terms.7
  241.0 4.6 collective-permute-done.64.refs_4_
  246.9 2.3 norm_back.4
  250.5 10.4 %collective-permute-done.67.refs_1_ = bf16[512,1024]{1,0:T(8,128)(2,1)} collective-permute-done((bf16[512,1024]{1,0:T(8,128)(2,1)}, bf16[512,1024]{1,0:T(8,128)(2,1)}, u32[]{:S(2)}, u32[]{:S(2)}) %collective-permute-start.67) | collective-permute-done | bytes 1048608 | tf_op jit(solution)/shard_map/ppermute | solution.py:708
  268.0 7.6 %attend_back.2 = (bf16[640,768]{1,0:T(8,128)(2,1)S(1)}, bf16[640,768]{1,0:T(8,128)(2,1)S(1)}, f32[8,128]{1,0:T(8,128)S(1)}) custom-call(s32[1]{0:T(128)} %bitcast.refs_0_, f32[1280,256]{1,0:T(8,128)S(1)} %fusion.refs_1_, bf16[640,768]{1,0:T(8,128)(2,1)S(1)} %get-tuple-element.491.refs_2_, bf16[640,768]{1,0:T(8,128)(2,1)S(1)} %get-tuple-element.497.refs_3_, ...), custom_call_target="tpu_custom_call" | custom-call | flops 1 | bytes 1 | tf_op jit(solution)/shard_map/attend_back/pallas_call | solution.py:87
  281.3 5.5 %collective-permute-done.77.refs_1_ = bf16[512,1024]{1,0:T(8,128)(2,1)S(1)} collective-permute-done((bf16[512,1024]{1,0:T(8,128)(2,1)S(1)}, bf16[512,1024]{1,0:T(8,128)(2,1)S(1)}, u32[]{:S(2)}, u32[]{:S(2)}) %collective-permute-start.77) | collective-permute-done | bytes 1048608 | tf_op jit(solution)/shard_map/ppermute | solution.py:708
  287.8 3.4 weight_terms.8
  292.5 4.7 collective-permute-done.76.refs_4_
  303.7 13.6 %collective-permute-done.83.refs_4_.refs_2_ = bf16[128,1024]{1,0:T(8,128)(2,1)S(1)} collective-permute-done((bf16[128,1024]{1,0:T(8,128)(2,1)S(1)}, bf16[128,1024]{1,0:T(8,128)(2,1)S(1)}, u32[]{:S(2)}, u32[]{:S(2)}) %collective-permute-start.83) | collective-permute-done | bytes 262176 | tf_op jit(solution)/shard_map/ppermute | solution.py:708
  329.2 2.9 weight_terms.9
  332.8 2.5 collective-permute-start.91
  336.9 10.6 %collective-permute-done.91.refs_6_.refs_2_ = bf16[128,1024]{1,0:T(8,128)(2,1)S(1)} collective-permute-done((bf16[128,1024]{1,0:T(8,128)(2,1)S(1)}, bf16[128,1024]{1,0:T(8,128)(2,1)S(1)}, u32[]{:S(2)}, u32[]{:S(2)}) %collective-permute-start.91) | collective-permute-done | bytes 262176 | tf_op jit(solution)/shard_map/ppermute | solution.py:708
  350.6 2.4 collective-permute-done.94.refs_1_
  353.2 1.8 collective-permute-start.97
  355.0 2.9 weight_terms.10
  362.8 4.0 collective-permute-done.97.refs_2_
  370.6 7.6 %attend_back.3 = (bf16[640,768]{1,0:T(8,128)(2,1)S(1)}, bf16[640,768]{1,0:T(8,128)(2,1)S(1)}, f32[8,128]{1,0:T(8,128)S(1)}) custom-call(s32[1]{0:T(128)} %bitcast.refs_0_, f32[1280,256]{1,0:T(8,128)S(1)} %fusion.refs_1_, bf16[640,768]{1,0:T(8,128)(2,1)S(1)} %copy-done.20, bf16[640,768]{1,0:T(8,128)(2,1)S(1)} %copy-done.23, ...), custom_call_target="tpu_custom_call" | custom-call | flops 1 | bytes 1 | tf_op jit(solution)/shard_map/attend_back/pallas_call | solution.py:87
  378.3 3.0 weight_terms.11
  384.9 1.9 collective-permute-start.108
  388.6 2.5 collective-permute-start.107
  391.2 2.6 moments.8
  393.8 11.6 %collective-permute-done.107.refs_6_.refs_2_ = bf16[128,1024]{1,0:T(8,128)(2,1)S(1)} collective-permute-done((bf16[128,1024]{1,0:T(8,128)(2,1)S(1)}, bf16[128,1024]{1,0:T(8,128)(2,1)S(1)}, u32[]{:S(2)}, u32[]{:S(2)}) %collective-permute-start.107) | collective-permute-done | bytes 262176 | tf_op jit(solution)/shard_map/ppermute | solution.py:708
  405.4 2.0 norm_back.7
  407.8 2.5 collective-permute-done.108.refs_1_
  419.6 2.8 collective-permute-start.115
  422.6 13.1 %collective-permute-done.116.refs_1_ = bf16[256,1024]{1,0:T(8,128)(2,1)S(1)} collective-permute-done((bf16[256,1024]{1,0:T(8,128)(2,1)S(1)}, bf16[256,1024]{1,0:T(8,128)(2,1)S(1)}, u32[]{:S(2)}, u32[]{:S(2)}) %collective-permute-start.116) | collective-permute-done | bytes 524320 | tf_op jit(solution)/shard_map/ppermute | solution.py:708
  439.1 1.8 move_columns.11
  440.9 8.9 %collective-permute-done.117.refs_2_ = bf16[128,1024]{1,0:T(8,128)(2,1)S(1)} collective-permute-done((bf16[128,1024]{1,0:T(8,128)(2,1)S(1)}, bf16[128,1024]{1,0:T(8,128)(2,1)S(1)}, u32[]{:S(2)}, u32[]{:S(2)}) %collective-permute-start.117) | collective-permute-done | bytes 262176 | tf_op jit(solution)/shard_map/ppermute | solution.py:708
  449.8 2.4 moments.11
  455.4 3.5 collective-permute-done.119.refs_1_
  459.7 3.5 collective-permute-done.120.refs_1_
  463.3 4.3 collective-permute-done.121.refs_1_
  468.0 5.0 %collective-permute-done.122.refs_1_ = f32[16,1024]{1,0:T(8,128)S(1)} collective-permute-done((f32[16,1024]{1,0:T(8,128)S(1)}, f32[16,1024]{1,0:T(8,128)S(1)}, u32[]{:S(2)}, u32[]{:S(2)}) %collective-permute-start.122) | collective-permute-done | bytes 65568 | tf_op jit(solution)/shard_map/ppermute | solution.py:708
  475.4 3.4 apply.2
  478.8 2.5 apply.3
  (521 shorter events, 169.4 us)
Async XLA Ops:
  3.1 13.4 %collective-permute-start.2 = (bf16[128,768]{1,0:T(8,128)(2,1)}, bf16[128,768]{1,0:T(8,128)(2,1)S(1)}, u32[]{:S(2)}, u32[]{:S(2)}) collective-permute-start(bf16[128,768]{1,0:T(8,128)(2,1)} %get-tuple-element.396.refs_0_), channel_id=1, source_target_pairs={{0,16},{4,20},{8,24},{12,28},{16,0},{20,4},{24,8},{28,12},{1,17},{... | collective-permute-start | bytes 589832 | tf_op jit(solution)/shard_map/ppermute | solution.py:708
  17.5 10.4 %collective-permute-start.3 = (bf16[256,768]{1,0:T(8,128)(2,1)S(1)}, bf16[256,768]{1,0:T(8,128)(2,1)S(1)}, u32[]{:S(2)}, u32[]{:S(2)}) collective-permute-start(bf16[256,768]{1,0:T(8,128)(2,1)S(1)} %get-tuple-element.398.refs_0_), channel_id=1, source_target_pairs={{0,8},{4,12},{8,0},{12,4},{16,24},{20,28},{24,16},{28,20},{1,9},{5... | collective-permute-start | bytes 1179656 | tf_op jit(solution)/shard_map/ppermute | solution.py:708
  18.4 16.4 %collective-permute-start.6 = (bf16[320,1024]{1,0:T(8,128)(2,1)S(1)}, bf16[320,1024]{1,0:T(8,128)(2,1)S(1)}, u32[]{:S(2)}, u32[]{:S(2)}) collective-permute-start(bf16[320,1024]{1,0:T(8,128)(2,1)S(1)} %get-tuple-element.393.refs_0_), channel_id=1, source_target_pairs={{0,2},{2,0},{1,3},{3,1},{4,6},{6,4},{5,7},{7,5},{8,10},{10,8},{9,1... | collective-permute-start | bytes 1966088 | tf_op jit(solution)/shard_map/ppermute | solution.py:825
  27.9 28.4 %collective-permute-start.4 = (bf16[512,768]{1,0:T(8,128)(2,1)S(1)}, bf16[512,768]{1,0:T(8,128)(2,1)S(1)}, u32[]{:S(2)}, u32[]{:S(2)}) collective-permute-start(bf16[512,768]{1,0:T(8,128)(2,1)S(1)} %get-tuple-element.401.refs_3_.refs_1_), channel_id=1, source_target_pairs={{0,4},{4,0},{8,12},{12,8},{16,20},{20,16},{24,28},{28,24},{1,5},{5... | collective-permute-start | bytes 2359304 | tf_op jit(solution)/shard_map/ppermute | solution.py:708
  29.3 20.3 %collective-permute-start = (bf16[160,1024]{1,0:T(8,128)(2,1)S(1)}, bf16[160,1024]{1,0:T(8,128)(2,1)S(1)}, u32[]{:S(2)}, u32[]{:S(2)}) collective-permute-start(bf16[160,1024]{1,0:T(8,128)(2,1)S(1)} %get-tuple-element.394), channel_id=1, source_target_pairs={{0,1},{1,0},{2,3},{3,2},{4,5},{5,4},{6,7},{7,6},{8,9},{9,8},{10,11... | collective-permute-start | bytes 983048 | tf_op jit(solution)/shard_map/ppermute | solution.py:821
  29.3 21.1 %collective-permute-start.1 = (bf16[160,1024]{1,0:T(8,128)(2,1)S(1)}, bf16[160,1024]{1,0:T(8,128)(2,1)S(1)}, u32[]{:S(2)}, u32[]{:S(2)}) collective-permute-start(bf16[160,1024]{1,0:T(8,128)(2,1)S(1)} %get-tuple-element.395), channel_id=1, source_target_pairs={{0,1},{1,0},{2,3},{3,2},{4,5},{5,4},{6,7},{7,6},{8,9},{9,8},{10,11... | collective-permute-start | bytes 983048 | tf_op jit(solution)/shard_map/ppermute | solution.py:821
  29.8 20.6 %collective-permute-start.8 = (bf16[128,1024]{1,0:T(8,128)(2,1)S(1)}, bf16[128,1024]{1,0:T(8,128)(2,1)S(1)}, u32[]{:S(2)}, u32[]{:S(2)}) collective-permute-start(bf16[128,1024]{1,0:T(8,128)(2,1)S(1)} %get-tuple-element.410.refs_0_), channel_id=1, source_target_pairs={{0,16},{4,20},{8,24},{12,28},{16,0},{20,4},{24,8},{28,12},{1,17},{... | collective-permute-start | bytes 786440 | tf_op jit(solution)/shard_map/ppermute | solution.py:708
  34.7 13.3 %collective-permute-start.5 = (bf16[128,256]{1,0:T(8,128)(2,1)S(1)}, bf16[128,256]{1,0:T(8,128)(2,1)S(1)}, u32[]{:S(2)}, u32[]{:S(2)}) collective-permute-start(bf16[128,256]{1,0:T(8,128)(2,1)S(1)} %get-tuple-element.402.refs_0_), channel_id=1, source_target_pairs={{0,16},{4,20},{8,24},{12,28},{16,0},{20,4},{24,8},{28,12},{1,17},{... | collective-permute-start | bytes 196616 | tf_op jit(solution)/shard_map/ppermute | solution.py:708
  48.1 22.8 %collective-permute-start.13 = (bf16[320,1024]{1,0:T(8,128)(2,1)}, bf16[320,1024]{1,0:T(8,128)(2,1)}, u32[]{:S(2)}, u32[]{:S(2)}) collective-permute-start(bf16[320,1024]{1,0:T(8,128)(2,1)} %get-tuple-element.426.refs_0_), channel_id=1, source_target_pairs={{0,2},{2,0},{1,3},{3,1},{4,6},{6,4},{5,7},{7,5},{8,10},{10,8},{9,1... | collective-permute-start | bytes 1966088 | tf_op jit(solution)/shard_map/ppermute | solution.py:825
  49.6 5.0 %collective-permute-start.7 = (bf16[256,256]{1,0:T(8,128)(2,1)S(1)}, bf16[256,256]{1,0:T(8,128)(2,1)S(1)}, u32[]{:S(2)}, u32[]{:S(2)}) collective-permute-start(bf16[256,256]{1,0:T(8,128)(2,1)S(1)} %get-tuple-element.409.refs_0_), channel_id=1, source_target_pairs={{0,8},{4,12},{8,0},{12,4},{16,24},{20,28},{24,16},{28,20},{1,9},{5... | collective-permute-start | bytes 393224 | tf_op jit(solution)/shard_map/ppermute | solution.py:708
  50.4 8.6 %collective-permute-start.9 = (bf16[160,1024]{1,0:T(8,128)(2,1)S(1)}, bf16[160,1024]{1,0:T(8,128)(2,1)S(1)}, u32[]{:S(2)}, u32[]{:S(2)}) collective-permute-start(bf16[160,1024]{1,0:T(8,128)(2,1)S(1)} %get-tuple-element.416), channel_id=1, source_target_pairs={{0,1},{1,0},{2,3},{3,2},{4,5},{5,4},{6,7},{7,6},{8,9},{9,8},{10,11... | collective-permute-start | bytes 983048 | tf_op jit(solution)/shard_map/ppermute | solution.py:821
  50.4 8.6 %collective-permute-start.10 = (bf16[160,1024]{1,0:T(8,128)(2,1)S(1)}, bf16[160,1024]{1,0:T(8,128)(2,1)S(1)}, u32[]{:S(2)}, u32[]{:S(2)}) collective-permute-start(bf16[160,1024]{1,0:T(8,128)(2,1)S(1)} %get-tuple-element.417), channel_id=1, source_target_pairs={{0,1},{1,0},{2,3},{3,2},{4,5},{5,4},{6,7},{7,6},{8,9},{9,8},{10,11... | collective-permute-start | bytes 983048 | tf_op jit(solution)/shard_map/ppermute | solution.py:821
  54.7 17.8 %collective-permute-start.12 = (bf16[256,1024]{1,0:T(8,128)(2,1)}, bf16[256,1024]{1,0:T(8,128)(2,1)}, u32[]{:S(2)}, u32[]{:S(2)}) collective-permute-start(bf16[256,1024]{1,0:T(8,128)(2,1)} %get-tuple-element.425.refs_0_), channel_id=1, source_target_pairs={{0,8},{4,12},{8,0},{12,4},{16,24},{20,28},{24,16},{28,20},{1,9},{5... | collective-permute-start | bytes 1572872 | tf_op jit(solution)/shard_map/ppermute | solution.py:708
  56.3 17.4 %collective-permute-start.11 = (bf16[512,256]{1,0:T(8,128)(2,1)}, bf16[512,256]{1,0:T(8,128)(2,1)S(1)}, u32[]{:S(2)}, u32[]{:S(2)}) collective-permute-start(bf16[512,256]{1,0:T(8,128)(2,1)} %get-tuple-element.423.refs_1_.refs_3_), channel_id=1, source_target_pairs={{0,4},{4,0},{8,12},{12,8},{16,20},{20,16},{24,28},{28,24},{1,5},{5... | collective-permute-start | bytes 786440 | tf_op jit(solution)/shard_map/ppermute | solution.py:708
  62.0 14.2 %collective-permute-start.14 = (bf16[128,1024]{1,0:T(8,128)(2,1)}, bf16[128,1024]{1,0:T(8,128)(2,1)}, u32[]{:S(2)}, u32[]{:S(2)}) collective-permute-start(bf16[128,1024]{1,0:T(8,128)(2,1)} %get-tuple-element.430.refs_0_), channel_id=1, source_target_pairs={{0,16},{4,20},{8,24},{12,28},{16,0},{20,4},{24,8},{28,12},{1,17},{... | collective-permute-start | bytes 786440 | tf_op jit(solution)/shard_map/ppermute | solution.py:708
  78.3 33.3 %collective-permute-start.22 = (bf16[512,1024]{1,0:T(8,128)(2,1)S(1)}, bf16[512,1024]{1,0:T(8,128)(2,1)S(1)}, u32[]{:S(2)}, u32[]{:S(2)}) collective-permute-start(bf16[512,1024]{1,0:T(8,128)(2,1)S(1)} %get-tuple-element.450.refs_3_.refs_1_), channel_id=1, source_target_pairs={{0,4},{4,0},{8,12},{12,8},{16,20},{20,16},{24,28},{28,24},{1,5},{5... | collective-permute-start | bytes 3145736 | tf_op jit(solution)/shard_map/ppermute | solution.py:708
  82.0 16.8 %collective-permute-start.19 = (bf16[320,1024]{1,0:T(8,128)(2,1)S(1)}, bf16[320,1024]{1,0:T(8,128)(2,1)S(1)}, u32[]{:S(2)}, u32[]{:S(2)}) collective-permute-start(bf16[320,1024]{1,0:T(8,128)(2,1)S(1)} %get-tuple-element.441), channel_id=1, source_target_pairs={{0,2},{2,0},{1,3},{3,1},{4,6},{6,4},{5,7},{7,5},{8,10},{10,8},{9,1... | collective-permute-start | bytes 1966088 | tf_op jit(solution)/shard_map/ppermute | solution.py:825
  84.7 24.6 %collective-permute-start.24 = (bf16[256,1024]{1,0:T(8,128)(2,1)S(1)}, bf16[256,1024]{1,0:T(8,128)(2,1)S(1)}, u32[]{:S(2)}, u32[]{:S(2)}) collective-permute-start(bf16[256,1024]{1,0:T(8,128)(2,1)S(1)} %get-tuple-element.452.refs_1_.refs_3_), channel_id=1, source_target_pairs={{0,8},{4,12},{8,0},{12,4},{16,24},{20,28},{24,16},{28,20},{1,9},{5... | collective-permute-start | bytes 1572872 | tf_op jit(solution)/shard_map/ppermute | solution.py:708
  85.1 24.2 %collective-permute-start.23 = (bf16[128,1024]{1,0:T(8,128)(2,1)S(1)}, bf16[128,1024]{1,0:T(8,128)(2,1)S(1)}, u32[]{:S(2)}, u32[]{:S(2)}) collective-permute-start(bf16[128,1024]{1,0:T(8,128)(2,1)S(1)} %get-tuple-element.451.refs_0_), channel_id=1, source_target_pairs={{0,16},{4,20},{8,24},{12,28},{16,0},{20,4},{24,8},{28,12},{1,17},{... | collective-permute-start | bytes 786440 | tf_op jit(solution)/shard_map/ppermute | solution.py:708
  88.4 23.2 %collective-permute-start.25 = (bf16[128,1024]{1,0:T(8,128)(2,1)S(1)}, bf16[128,1024]{1,0:T(8,128)(2,1)S(1)}, u32[]{:S(2)}, u32[]{:S(2)}) collective-permute-start(bf16[128,1024]{1,0:T(8,128)(2,1)S(1)} %get-tuple-element.456.refs_0_), channel_id=1, source_target_pairs={{0,16},{4,20},{8,24},{12,28},{16,0},{20,4},{24,8},{28,12},{1,17},{... | collective-permute-start | bytes 786440 | tf_op jit(solution)/shard_map/ppermute | solution.py:708
  99.3 30.4 %collective-permute-start.28 = (bf16[320,1024]{1,0:T(8,128)(2,1)S(1)}, bf16[320,1024]{1,0:T(8,128)(2,1)S(1)}, u32[]{:S(2)}, u32[]{:S(2)}) collective-permute-start(bf16[320,1024]{1,0:T(8,128)(2,1)S(1)} %get-tuple-element.447.refs_0_), channel_id=1, source_target_pairs={{0,2},{2,0},{1,3},{3,1},{4,6},{6,4},{5,7},{7,5},{8,10},{10,8},{9,1... | collective-permute-start | bytes 1966088 | tf_op jit(solution)/shard_map/ppermute | solution.py:825
  109.4 14.8 %collective-permute-start.26 = (bf16[256,1024]{1,0:T(8,128)(2,1)S(1)}, bf16[256,1024]{1,0:T(8,128)(2,1)S(1)}, u32[]{:S(2)}, u32[]{:S(2)}) collective-permute-start(bf16[256,1024]{1,0:T(8,128)(2,1)S(1)} %get-tuple-element.452.refs_1_.refs_3_), channel_id=1, source_target_pairs={{0,4},{4,0},{8,12},{12,8},{16,20},{20,16},{24,28},{28,24},{1,5},{5... | collective-permute-start | bytes 1572872 | tf_op jit(solution)/shard_map/ppermute | solution.py:708
  111.6 18.2 %collective-permute-start.29 = (bf16[256,1024]{1,0:T(8,128)(2,1)S(1)}, bf16[256,1024]{1,0:T(8,128)(2,1)S(1)}, u32[]{:S(2)}, u32[]{:S(2)}) collective-permute-start(bf16[256,1024]{1,0:T(8,128)(2,1)S(1)} %get-tuple-element.461.refs_0_), channel_id=1, source_target_pairs={{0,8},{4,12},{8,0},{12,4},{16,24},{20,28},{24,16},{28,20},{1,9},{5... | collective-permute-start | bytes 1572872 | tf_op jit(solution)/shard_map/ppermute | solution.py:708
  111.6 16.4 %collective-permute-start.30 = (bf16[128,1024]{1,0:T(8,128)(2,1)S(1)}, bf16[128,1024]{1,0:T(8,128)(2,1)S(1)}, u32[]{:S(2)}, u32[]{:S(2)}) collective-permute-start(bf16[128,1024]{1,0:T(8,128)(2,1)S(1)} %get-tuple-element.462.refs_2_), channel_id=1, source_target_pairs={{0,16},{4,20},{8,24},{12,28},{16,0},{20,4},{24,8},{28,12},{1,17},{... | collective-permute-start | bytes 786440 | tf_op jit(solution)/shard_map/ppermute | solution.py:708
  114.7 20.7 %collective-permute-start.27 = (bf16[256,1024]{1,0:T(8,128)(2,1)S(1)}, bf16[256,1024]{1,0:T(8,128)(2,1)S(1)}, u32[]{:S(2)}, u32[]{:S(2)}) collective-permute-start(bf16[256,1024]{1,0:T(8,128)(2,1)S(1)} %get-tuple-element.459.refs_2_.refs_4_), channel_id=1, source_target_pairs={{0,4},{4,0},{8,12},{12,8},{16,20},{20,16},{24,28},{28,24},{1,5},{5... | collective-permute-start | bytes 1572872 | tf_op jit(solution)/shard_map/ppermute | solution.py:708
  130.6 25.3 %collective-permute-start.38 = (bf16[256,2048]{1,0:T(8,128)(2,1)S(1)}, bf16[256,2048]{1,0:T(8,128)(2,1)S(1)}, u32[]{:S(2)}, u32[]{:S(2)}) collective-permute-start(bf16[256,2048]{1,0:T(8,128)(2,1)S(1)} %get-tuple-element.483.refs_0_), channel_id=1, source_target_pairs={{0,8},{4,12},{8,0},{12,4},{16,24},{20,28},{24,16},{28,20},{1,9},{5... | collective-permute-start | bytes 3145736 | tf_op jit(solution)/shard_map/ppermute | solution.py:708
  132.4 25.0 %collective-permute-start.39 = (bf16[512,1024]{1,0:T(8,128)(2,1)S(1)}, bf16[512,1024]{1,0:T(8,128)(2,1)S(1)}, u32[]{:S(2)}, u32[]{:S(2)}) collective-permute-start(bf16[512,1024]{1,0:T(8,128)(2,1)S(1)} %get-tuple-element.484.refs_3_.refs_1_), channel_id=1, source_target_pairs={{0,4},{4,0},{8,12},{12,8},{16,20},{20,16},{24,28},{28,24},{1,5},{5... | collective-permute-start | bytes 3145736 | tf_op jit(solution)/shard_map/ppermute | solution.py:708
  139.3 18.2 %collective-permute-start.37 = (bf16[320,1024]{1,0:T(8,128)(2,1)S(1)}, bf16[320,1024]{1,0:T(8,128)(2,1)S(1)}, u32[]{:S(2)}, u32[]{:S(2)}) collective-permute-start(bf16[320,1024]{1,0:T(8,128)(2,1)S(1)} %get-tuple-element.481), channel_id=1, source_target_pairs={{0,2},{2,0},{1,3},{3,1},{4,6},{6,4},{5,7},{7,5},{8,10},{10,8},{9,1... | collective-permute-start | bytes 1966088 | tf_op jit(solution)/shard_map/ppermute | solution.py:825
  158.0 15.8 %collective-permute-start.42 = (bf16[320,1024]{1,0:T(8,128)(2,1)S(1)}, bf16[320,1024]{1,0:T(8,128)(2,1)S(1)}, u32[]{:S(2)}, u32[]{:S(2)}) collective-permute-start(bf16[320,1024]{1,0:T(8,128)(2,1)S(1)} %get-tuple-element.486.refs_0_), channel_id=1, source_target_pairs={{0,2},{2,0},{1,3},{3,1},{4,6},{6,4},{5,7},{7,5},{8,10},{10,8},{9,1... | collective-permute-start | bytes 1966088 | tf_op jit(solution)/shard_map/ppermute | solution.py:825
  158.7 46.6 %collective-permute-start.52 = (bf16[512,2048]{1,0:T(8,128)(2,1)S(1)}, bf16[512,2048]{1,0:T(8,128)(2,1)S(1)}, u32[]{:S(2)}, u32[]{:S(2)}) collective-permute-start(bf16[512,2048]{1,0:T(8,128)(2,1)S(1)} %get-tuple-element.518.refs_3_.refs_1_), channel_id=1, source_target_pairs={{0,4},{4,0},{8,12},{12,8},{16,20},{20,16},{24,28},{28,24},{1,5},{5... | collective-permute-start | bytes 6291464 | tf_op jit(solution)/shard_map/ppermute | solution.py:708
  183.5 16.8 %collective-permute-start.49 = (bf16[320,1024]{1,0:T(8,128)(2,1)S(1)}, bf16[320,1024]{1,0:T(8,128)(2,1)S(1)}, u32[]{:S(2)}, u32[]{:S(2)}) collective-permute-start(bf16[320,1024]{1,0:T(8,128)(2,1)S(1)} %get-tuple-element.512), channel_id=1, source_target_pairs={{0,2},{2,0},{1,3},{3,1},{4,6},{6,4},{5,7},{7,5},{8,10},{10,8},{9,1... | collective-permute-start | bytes 1966088 | tf_op jit(solution)/shard_map/ppermute | solution.py:825
  200.8 16.0 %collective-permute-start.53 = (bf16[320,1024]{1,0:T(8,128)(2,1)S(1)}, bf16[320,1024]{1,0:T(8,128)(2,1)S(1)}, u32[]{:S(2)}, u32[]{:S(2)}) collective-permute-start(bf16[320,1024]{1,0:T(8,128)(2,1)S(1)} %get-tuple-element.515.refs_0_), channel_id=1, source_target_pairs={{0,2},{2,0},{1,3},{3,1},{4,6},{6,4},{5,7},{7,5},{8,10},{10,8},{9,1... | collective-permute-start | bytes 1966088 | tf_op jit(solution)/shard_map/ppermute | solution.py:825
  202.1 5.6 %collective-permute-start.54 = (bf16[160,1024]{1,0:T(8,128)(2,1)S(1)}, bf16[160,1024]{1,0:T(8,128)(2,1)S(1)}, u32[]{:S(2)}, u32[]{:S(2)}) collective-permute-start(bf16[160,1024]{1,0:T(8,128)(2,1)S(1)} %copy-done.87), channel_id=1, source_target_pairs={{0,1},{1,0},{2,3},{3,2},{4,5},{5,4},{6,7},{7,6},{8,9},{9,8},{10,11... | collective-permute-start | bytes 983048 | tf_op jit(solution)/shard_map/ppermute | solution.py:821
  228.5 17.1 %collective-permute-start.64 = (bf16[320,1024]{1,0:T(8,128)(2,1)}, bf16[320,1024]{1,0:T(8,128)(2,1)}, u32[]{:S(2)}, u32[]{:S(2)}) collective-permute-start(bf16[320,1024]{1,0:T(8,128)(2,1)} %get-tuple-element.549), channel_id=1, source_target_pairs={{0,2},{2,0},{1,3},{3,1},{4,6},{6,4},{5,7},{7,5},{8,10},{10,8},{9,1... | collective-permute-start | bytes 1966088 | tf_op jit(solution)/shard_map/ppermute | solution.py:825
  235.4 25.4 %collective-permute-start.67 = (bf16[512,1024]{1,0:T(8,128)(2,1)}, bf16[512,1024]{1,0:T(8,128)(2,1)}, u32[]{:S(2)}, u32[]{:S(2)}) collective-permute-start(bf16[512,1024]{1,0:T(8,128)(2,1)} %get-tuple-element.558), channel_id=1, source_target_pairs={{0,4},{4,0},{8,12},{12,8},{16,20},{20,16},{24,28},{28,24},{1,5},{5... | collective-permute-start | bytes 3145736 | tf_op jit(solution)/shard_map/ppermute | solution.py:708
  249.2 16.0 %collective-permute-start.68 = (bf16[320,1024]{1,0:T(8,128)(2,1)S(1)}, bf16[320,1024]{1,0:T(8,128)(2,1)S(1)}, u32[]{:S(2)}, u32[]{:S(2)}) collective-permute-start(bf16[320,1024]{1,0:T(8,128)(2,1)S(1)} %get-tuple-element.554.refs_0_.refs_8_), channel_id=1, source_target_pairs={{0,2},{2,0},{1,3},{3,1},{4,6},{6,4},{5,7},{7,5},{8,10},{10,8},{9,1... | collective-permute-start | bytes 1966088 | tf_op jit(solution)/shard_map/ppermute | solution.py:825
  250.0 13.8 %collective-permute-start.65 = (bf16[160,1024]{1,0:T(8,128)(2,1)S(1)}, bf16[160,1024]{1,0:T(8,128)(2,1)S(1)}, u32[]{:S(2)}, u32[]{:S(2)}) collective-permute-start(bf16[160,1024]{1,0:T(8,128)(2,1)S(1)} %get-tuple-element.555), channel_id=1, source_target_pairs={{0,1},{1,0},{2,3},{3,2},{4,5},{5,4},{6,7},{7,6},{8,9},{9,8},{10,11... | collective-permute-start | bytes 983048 | tf_op jit(solution)/shard_map/ppermute | solution.py:821
  250.0 13.8 %collective-permute-start.66 = (bf16[160,1024]{1,0:T(8,128)(2,1)S(1)}, bf16[160,1024]{1,0:T(8,128)(2,1)S(1)}, u32[]{:S(2)}, u32[]{:S(2)}) collective-permute-start(bf16[160,1024]{1,0:T(8,128)(2,1)S(1)} %get-tuple-element.556), channel_id=1, source_target_pairs={{0,1},{1,0},{2,3},{3,2},{4,5},{5,4},{6,7},{7,6},{8,9},{9,8},{10,11... | collective-permute-start | bytes 983048 | tf_op jit(solution)/shard_map/ppermute | solution.py:821
  262.3 13.2 %collective-permute-start.71 = (bf16[256,1024]{1,0:T(8,128)(2,1)S(1)}, bf16[256,1024]{1,0:T(8,128)(2,1)S(1)}, u32[]{:S(2)}, u32[]{:S(2)}) collective-permute-start(bf16[256,1024]{1,0:T(8,128)(2,1)S(1)} %get-tuple-element.572), channel_id=1, source_target_pairs={{0,8},{4,12},{8,0},{12,4},{16,24},{20,28},{24,16},{28,20},{1,9},{5... | collective-permute-start | bytes 1572872 | tf_op jit(solution)/shard_map/ppermute | solution.py:708
  262.7 24.1 %collective-permute-start.77 = (bf16[512,1024]{1,0:T(8,128)(2,1)S(1)}, bf16[512,1024]{1,0:T(8,128)(2,1)S(1)}, u32[]{:S(2)}, u32[]{:S(2)}) collective-permute-start(bf16[512,1024]{1,0:T(8,128)(2,1)S(1)} %copy-done.81), channel_id=1, source_target_pairs={{0,4},{4,0},{8,12},{12,8},{16,20},{20,16},{24,28},{28,24},{1,5},{5... | collective-permute-start | bytes 3145736 | tf_op jit(solution)/shard_map/ppermute | solution.py:708
  280.2 17.0 %collective-permute-start.76 = (bf16[320,1024]{1,0:T(8,128)(2,1)}, bf16[320,1024]{1,0:T(8,128)(2,1)S(1)}, u32[]{:S(2)}, u32[]{:S(2)}) collective-permute-start(bf16[320,1024]{1,0:T(8,128)(2,1)} %get-tuple-element.583), channel_id=1, source_target_pairs={{0,2},{2,0},{1,3},{3,1},{4,6},{6,4},{5,7},{7,5},{8,10},{10,8},{9,1... | collective-permute-start | bytes 1966088 | tf_op jit(solution)/shard_map/ppermute | solution.py:825
  291.3 27.7 %collective-permute-start.81 = (bf16[512,1024]{1,0:T(8,128)(2,1)S(1)}, bf16[512,1024]{1,0:T(8,128)(2,1)S(1)}, u32[]{:S(2)}, u32[]{:S(2)}) collective-permute-start(bf16[512,1024]{1,0:T(8,128)(2,1)S(1)} %get-tuple-element.599), channel_id=1, source_target_pairs={{0,4},{4,0},{8,12},{12,8},{16,20},{20,16},{24,28},{28,24},{1,5},{5... | collective-permute-start | bytes 3145736 | tf_op jit(solution)/shard_map/ppermute | solution.py:708
  298.2 20.8 %collective-permute-start.80 = (bf16[320,1024]{1,0:T(8,128)(2,1)S(1)}, bf16[320,1024]{1,0:T(8,128)(2,1)S(1)}, u32[]{:S(2)}, u32[]{:S(2)}) collective-permute-start(bf16[320,1024]{1,0:T(8,128)(2,1)S(1)} %get-tuple-element.592.refs_0_), channel_id=1, source_target_pairs={{0,2},{2,0},{1,3},{3,1},{4,6},{6,4},{5,7},{7,5},{8,10},{10,8},{9,1... | collective-permute-start | bytes 1966088 | tf_op jit(solution)/shard_map/ppermute | solution.py:825
  299.0 20.0 %collective-permute-start.82 = (bf16[256,1024]{1,0:T(8,128)(2,1)S(1)}, bf16[256,1024]{1,0:T(8,128)(2,1)S(1)}, u32[]{:S(2)}, u32[]{:S(2)}) collective-permute-start(bf16[256,1024]{1,0:T(8,128)(2,1)S(1)} %copy-done.83), channel_id=1, source_target_pairs={{0,8},{4,12},{8,0},{12,4},{16,24},{20,28},{24,16},{28,20},{1,9},{5... | collective-permute-start | bytes 1572872 | tf_op jit(solution)/shard_map/ppermute | solution.py:708
  300.6 16.6 %collective-permute-start.83 = (bf16[128,1024]{1,0:T(8,128)(2,1)S(1)}, bf16[128,1024]{1,0:T(8,128)(2,1)S(1)}, u32[]{:S(2)}, u32[]{:S(2)}) collective-permute-start(bf16[128,1024]{1,0:T(8,128)(2,1)S(1)} %get-tuple-element.601), channel_id=1, source_target_pairs={{0,16},{4,20},{8,24},{12,28},{16,0},{20,4},{24,8},{28,12},{1,17},{... | collective-permute-start | bytes 786440 | tf_op jit(solution)/shard_map/ppermute | solution.py:708
  327.2 20.3 %collective-permute-start.90 = (bf16[320,1024]{1,0:T(8,128)(2,1)S(1)}, bf16[320,1024]{1,0:T(8,128)(2,1)S(1)}, u32[]{:S(2)}, u32[]{:S(2)}) collective-permute-start(bf16[320,1024]{1,0:T(8,128)(2,1)S(1)} %get-tuple-element.619), channel_id=1, source_target_pairs={{0,2},{2,0},{1,3},{3,1},{4,6},{6,4},{5,7},{7,5},{8,10},{10,8},{9,1... | collective-permute-start | bytes 1966088 | tf_op jit(solution)/shard_map/ppermute | solution.py:825
  332.2 28.4 %collective-permute-start.96 = (bf16[512,1024]{1,0:T(8,128)(2,1)S(1)}, bf16[512,1024]{1,0:T(8,128)(2,1)S(1)}, u32[]{:S(2)}, u32[]{:S(2)}) collective-permute-start(bf16[512,1024]{1,0:T(8,128)(2,1)S(1)} %get-tuple-element.640), channel_id=1, source_target_pairs={{0,4},{4,0},{8,12},{12,8},{16,20},{20,16},{24,28},{28,24},{1,5},{5... | collective-permute-start | bytes 3145736 | tf_op jit(solution)/shard_map/ppermute | solution.py:708
  332.8 14.7 %collective-permute-start.91 = (bf16[128,1024]{1,0:T(8,128)(2,1)S(1)}, bf16[128,1024]{1,0:T(8,128)(2,1)S(1)}, u32[]{:S(2)}, u32[]{:S(2)}) collective-permute-start(bf16[128,1024]{1,0:T(8,128)(2,1)S(1)} %get-tuple-element.628), channel_id=1, source_target_pairs={{0,16},{4,20},{8,24},{12,28},{16,0},{20,4},{24,8},{28,12},{1,17},{... | collective-permute-start | bytes 786440 | tf_op jit(solution)/shard_map/ppermute | solution.py:708
  335.4 17.7 %collective-permute-start.94 = (bf16[256,1024]{1,0:T(8,128)(2,1)S(1)}, bf16[256,1024]{1,0:T(8,128)(2,1)S(1)}, u32[]{:S(2)}, u32[]{:S(2)}) collective-permute-start(bf16[256,1024]{1,0:T(8,128)(2,1)S(1)} %get-tuple-element.634), channel_id=1, source_target_pairs={{0,8},{4,12},{8,0},{12,4},{16,24},{20,28},{24,16},{28,20},{1,9},{5... | collective-permute-start | bytes 1572872 | tf_op jit(solution)/shard_map/ppermute | solution.py:708
  348.8 18.0 %collective-permute-start.95 = (bf16[320,1024]{1,0:T(8,128)(2,1)S(1)}, bf16[320,1024]{1,0:T(8,128)(2,1)S(1)}, u32[]{:S(2)}, u32[]{:S(2)}) collective-permute-start(bf16[320,1024]{1,0:T(8,128)(2,1)S(1)} %get-tuple-element.630.refs_0_.refs_8_), channel_id=1, source_target_pairs={{0,2},{2,0},{1,3},{3,1},{4,6},{6,4},{5,7},{7,5},{8,10},{10,8},{9,1... | collective-permute-start | bytes 1966088 | tf_op jit(solution)/shard_map/ppermute | solution.py:825
  350.1 7.9 %collective-permute-start.92 = (bf16[160,1024]{1,0:T(8,128)(2,1)S(1)}, bf16[160,1024]{1,0:T(8,128)(2,1)S(1)}, u32[]{:S(2)}, u32[]{:S(2)}) collective-permute-start(bf16[160,1024]{1,0:T(8,128)(2,1)S(1)} %get-tuple-element.631), channel_id=1, source_target_pairs={{0,1},{1,0},{2,3},{3,2},{4,5},{5,4},{6,7},{7,6},{8,9},{9,8},{10,11... | collective-permute-start | bytes 983048 | tf_op jit(solution)/shard_map/ppermute | solution.py:821
  350.1 7.9 %collective-permute-start.93 = (bf16[160,1024]{1,0:T(8,128)(2,1)S(1)}, bf16[160,1024]{1,0:T(8,128)(2,1)S(1)}, u32[]{:S(2)}, u32[]{:S(2)}) collective-permute-start(bf16[160,1024]{1,0:T(8,128)(2,1)S(1)} %get-tuple-element.632), channel_id=1, source_target_pairs={{0,1},{1,0},{2,3},{3,2},{4,5},{5,4},{6,7},{7,6},{8,9},{9,8},{10,11... | collective-permute-start | bytes 983048 | tf_op jit(solution)/shard_map/ppermute | solution.py:821
  353.2 13.6 %collective-permute-start.97 = (bf16[128,1024]{1,0:T(8,128)(2,1)S(1)}, bf16[128,1024]{1,0:T(8,128)(2,1)S(1)}, u32[]{:S(2)}, u32[]{:S(2)}) collective-permute-start(bf16[128,1024]{1,0:T(8,128)(2,1)S(1)} %get-tuple-element.648), channel_id=1, source_target_pairs={{0,16},{4,20},{8,24},{12,28},{16,0},{20,4},{24,8},{28,12},{1,17},{... | collective-permute-start | bytes 786440 | tf_op jit(solution)/shard_map/ppermute | solution.py:708
  360.8 20.5 %collective-permute-start.100 = (bf16[256,1024]{1,0:T(8,128)(2,1)S(1)}, bf16[256,1024]{1,0:T(8,128)(2,1)S(1)}, u32[]{:S(2)}, u32[]{:S(2)}) collective-permute-start(bf16[256,1024]{1,0:T(8,128)(2,1)S(1)} %get-tuple-element.659), channel_id=1, source_target_pairs={{0,8},{4,12},{8,0},{12,4},{16,24},{20,28},{24,16},{28,20},{1,9},{5... | collective-permute-start | bytes 1572872 | tf_op jit(solution)/shard_map/ppermute | solution.py:708
  362.1 26.1 %collective-permute-start.106 = (bf16[512,1024]{1,0:T(8,128)(2,1)S(1)}, bf16[512,1024]{1,0:T(8,128)(2,1)S(1)}, u32[]{:S(2)}, u32[]{:S(2)}) collective-permute-start(bf16[512,1024]{1,0:T(8,128)(2,1)S(1)} %get-tuple-element.673), channel_id=1, source_target_pairs={{0,4},{4,0},{8,12},{12,8},{16,20},{20,16},{24,28},{28,24},{1,5},{5... | collective-permute-start | bytes 3145736 | tf_op jit(solution)/shard_map/ppermute | solution.py:708
  384.9 25.4 %collective-permute-start.108 = (bf16[512,1024]{1,0:T(8,128)(2,1)S(1)}, bf16[512,1024]{1,0:T(8,128)(2,1)S(1)}, u32[]{:S(2)}, u32[]{:S(2)}) collective-permute-start(bf16[512,1024]{1,0:T(8,128)(2,1)S(1)} %get-tuple-element.690), channel_id=1, source_target_pairs={{0,4},{4,0},{8,12},{12,8},{16,20},{20,16},{24,28},{28,24},{1,5},{5... | collective-permute-start | bytes 3145736 | tf_op jit(solution)/shard_map/ppermute | solution.py:708
  387.0 18.5 %collective-permute-start.105 = (bf16[320,1024]{1,0:T(8,128)(2,1)S(1)}, bf16[320,1024]{1,0:T(8,128)(2,1)S(1)}, u32[]{:S(2)}, u32[]{:S(2)}) collective-permute-start(bf16[320,1024]{1,0:T(8,128)(2,1)S(1)} %get-tuple-element.670), channel_id=1, source_target_pairs={{0,2},{2,0},{1,3},{3,1},{4,6},{6,4},{5,7},{7,5},{8,10},{10,8},{9,1... | collective-permute-start | bytes 1966088 | tf_op jit(solution)/shard_map/ppermute | solution.py:825
  388.5 19.1 %collective-permute-start.109 = (bf16[256,1024]{1,0:T(8,128)(2,1)S(1)}, bf16[256,1024]{1,0:T(8,128)(2,1)S(1)}, u32[]{:S(2)}, u32[]{:S(2)}) collective-permute-start(bf16[256,1024]{1,0:T(8,128)(2,1)S(1)} %get-tuple-element.692), channel_id=1, source_target_pairs={{0,8},{4,12},{8,0},{12,4},{16,24},{20,28},{24,16},{28,20},{1,9},{5... | collective-permute-start | bytes 1572872 | tf_op jit(solution)/shard_map/ppermute | solution.py:708
  388.6 16.8 %collective-permute-start.107 = (bf16[128,1024]{1,0:T(8,128)(2,1)S(1)}, bf16[128,1024]{1,0:T(8,128)(2,1)S(1)}, u32[]{:S(2)}, u32[]{:S(2)}) collective-permute-start(bf16[128,1024]{1,0:T(8,128)(2,1)S(1)} %get-tuple-element.679), channel_id=1, source_target_pairs={{0,16},{4,20},{8,24},{12,28},{16,0},{20,4},{24,8},{28,12},{1,17},{... | collective-permute-start | bytes 786440 | tf_op jit(solution)/shard_map/ppermute | solution.py:708
  416.1 19.5 %collective-permute-start.116 = (bf16[256,1024]{1,0:T(8,128)(2,1)S(1)}, bf16[256,1024]{1,0:T(8,128)(2,1)S(1)}, u32[]{:S(2)}, u32[]{:S(2)}) collective-permute-start(bf16[256,1024]{1,0:T(8,128)(2,1)S(1)} %get-tuple-element.716), channel_id=1, source_target_pairs={{0,8},{4,12},{8,0},{12,4},{16,24},{20,28},{24,16},{28,20},{1,9},{5... | collective-permute-start | bytes 1572872 | tf_op jit(solution)/shard_map/ppermute | solution.py:708
  418.3 19.5 %collective-permute-start.114 = (bf16[320,1024]{1,0:T(8,128)(2,1)S(1)}, bf16[320,1024]{1,0:T(8,128)(2,1)S(1)}, u32[]{:S(2)}, u32[]{:S(2)}) collective-permute-start(bf16[320,1024]{1,0:T(8,128)(2,1)S(1)} %get-tuple-element.709), channel_id=1, source_target_pairs={{0,2},{2,0},{1,3},{3,1},{4,6},{6,4},{5,7},{7,5},{8,10},{10,8},{9,1... | collective-permute-start | bytes 1966088 | tf_op jit(solution)/shard_map/ppermute | solution.py:825
  419.6 17.1 %collective-permute-start.115 = (bf16[128,1024]{1,0:T(8,128)(2,1)S(1)}, bf16[128,1024]{1,0:T(8,128)(2,1)S(1)}, u32[]{:S(2)}, u32[]{:S(2)}) collective-permute-start(bf16[128,1024]{1,0:T(8,128)(2,1)S(1)} %get-tuple-element.711), channel_id=1, source_target_pairs={{0,16},{4,20},{8,24},{12,28},{16,0},{20,4},{24,8},{28,12},{1,17},{... | collective-permute-start | bytes 786440 | tf_op jit(solution)/shard_map/ppermute | solution.py:708
  435.7 14.0 %collective-permute-start.117 = (bf16[128,1024]{1,0:T(8,128)(2,1)S(1)}, bf16[128,1024]{1,0:T(8,128)(2,1)S(1)}, u32[]{:S(2)}, u32[]{:S(2)}) collective-permute-start(bf16[128,1024]{1,0:T(8,128)(2,1)S(1)} %get-tuple-element.731), channel_id=1, source_target_pairs={{0,16},{4,20},{8,24},{12,28},{16,0},{20,4},{24,8},{28,12},{1,17},{... | collective-permute-start | bytes 786440 | tf_op jit(solution)/shard_map/ppermute | solution.py:708
  467.6 5.4 %collective-permute-start.122 = (f32[16,1024]{1,0:T(8,128)S(1)}, f32[16,1024]{1,0:T(8,128)S(1)}, u32[]{:S(2)}, u32[]{:S(2)}) collective-permute-start(f32[16,1024]{1,0:T(8,128)S(1)} %get-tuple-element.746.refs_0_), channel_id=1, source_target_pairs={{0,16},{4,20},{8,24},{12,28},{16,0},{20,4},{24,8},{28,12},{1,17},{... | collective-permute-start | bytes 196616 | tf_op jit(solution)/shard_map/ppermute | solution.py:708
  (152 other events, 680.0 us)

commit v5 on v4

--- a/solution.py
+++ b/solution.py
@@ -564,21 +564,25 @@
 
 def moments_kernel(at, kept, far, weights, first, second, *refs):
     first_new, second_new, step_out, squares = refs[-4:]
-    grad = kept[...].astype(jnp.float32) + far[...].astype(jnp.float32)
-    weight = weights[...].reshape(grad.shape)
-    new_first, new_second, step = adam_part(
-        grad, weight, first[...].reshape(grad.shape), second[...].reshape(grad.shape), WEIGHT_DECAY
-    )
-    for out, value in ((first_new, new_first), (second_new, new_second), (step_out, step)):
-        out[...] = value.reshape(out.shape)
-    for place, value in enumerate((weight, step)):
-        squares[0, place : place + 1, :] = jnp.sum(value * value, axis=0, keepdims=True)
+    wide = weights.shape[3]
+    for name in range(weights.shape[1]):
+        here = slice(name * wide, name * wide + wide)
+        grad = kept[:, here].astype(jnp.float32) + far[:, here].astype(jnp.float32)
+        weight = weights[0, name]
+        new_first, new_second, step = adam_part(
+            grad, weight, first[0, name], second[0, name], WEIGHT_DECAY
+        )
+        for out, value in ((first_new, new_first), (second_new, new_second), (step_out, step)):
+            out[0, name] = value
+        for place, value in enumerate((weight, step)):
+            squares[name, place : place + 1, :] = jnp.sum(value * value, axis=0, keepdims=True)
 
 
 def moments(run, names, layer, kept, far, weights, first, second, before):
     rows, wide = weights.shape[2:]
-    spec = pl.BlockSpec((1, 1, rows, wide), lambda n, at: (layer, at[n], 0, 0))
-    grad_spec = pl.BlockSpec((rows, wide), lambda n, at: (0, n))
+    many = len(names) if tuple(names) == tuple(range(weights.shape[1])) else 1
+    spec = pl.BlockSpec((1, many, rows, wide), lambda n, at: (layer, at[n], 0, 0))
+    grad_spec = pl.BlockSpec((rows, many * wide), lambda n, at: (0, n))
     before = list(before or [])
     return run(
         "moments",
@@ -587,8 +591,8 @@
         [struct(weights.shape, jnp.float32)] * 3 + [struct((len(names), 2, wide), jnp.float32)],
         12,
         in_specs=[grad_spec, grad_spec, spec, spec, spec] + [ANY_SPEC] * len(before),
-        out_specs=[spec, spec, spec, pl.BlockSpec((1, 2, wide), lambda n, at: (n, 0, 0))],
-        grid_spec=(1, (len(names),)),
+        out_specs=[spec, spec, spec, pl.BlockSpec((many, 2, wide), lambda n, at: (n, 0, 0))],
+        grid_spec=(1, (len(names) // many,)),
         aliases={6 + i: i for i in range(len(before))},
     )
 
@@ -617,7 +621,7 @@
 
 
 def apply_kernel(begin, total, weights, step, new, low):
-    index = 2 * (6 * pl.program_id(0) + begin + pl.program_id(1))
+    first = 2 * (6 * pl.program_id(0) + begin)
 
     numbers = total[8:, :]
     here_row = lax.broadcasted_iota(jnp.int32, numbers.shape, 0) + 8
@@ -628,24 +632,25 @@
         chosen = jnp.where((here_row == row) & (here_lane == lane), numbers, 0.0)
         return jnp.sqrt(jnp.sum(jnp.sum(chosen, axis=0, keepdims=True), axis=1, keepdims=True))
 
-    rate = LEARN_RATE * (root(index) / root(index + 1))
-    value = weights[...].reshape(weights.shape[2:]) - rate * step[...].reshape(step.shape[2:])
-    new[...] = value.reshape(new.shape)
-    low[...] = value.astype(jnp.bfloat16).reshape(low.shape)
+    for name in range(weights.shape[1]):
+        rate = LEARN_RATE * (root(first + 2 * name) / root(first + 2 * name + 1))
+        value = weights[0, name] - rate * step[0, name]
+        new[0, name] = value
+        low[0, name] = value.astype(jnp.bfloat16)
 
 
 def apply(run, begin, total, weights, step):
     layers, names, rows, wide = weights.shape
-    spec = pl.BlockSpec((1, 1, rows, wide), lambda layer, name: (layer, name, 0, 0))
+    spec = pl.BlockSpec((1, names, rows, wide), lambda layer: (layer, 0, 0, 0))
     return run(
         "apply",
         functools.partial(apply_kernel, begin),
         [total, weights, step],
         [struct(weights.shape, jnp.float32), struct(weights.shape)],
-        8,
-        in_specs=[pl.BlockSpec(total.shape, lambda layer, name: (0, 0)), spec, spec],
+        16,
+        in_specs=[pl.BlockSpec(total.shape, lambda layer: (0, 0)), spec, spec],
         out_specs=[spec, spec],
-        grid_spec=(0, (layers, names)),
+        grid_spec=(0, (layers,)),
     )
 
 

time: 491 us -> 489 us (level)
  no operation moved by 1% of the time
where the time goes in v5:
time: 489 us; the launch traced here: 481 us
  waiting for transfers between devices  235 us (48%)
  Pallas kernels  133 us (27%)
  starting transfers between devices  84.6 us (17%)
  local copies, waits for them, and re-layouts  23.1 us (5%)
    ppermute x41, waiting for transfers between devices, swap(): lax.ppermute(values, 'dp', [(source, source ^ stride) for source in range...  161 us
    pallas_call x127, Pallas kernels, __call__(): pl.pallas_call(wrapped, out_shape=[*outs, TOKEN], **places, input_output_...  133 us
    ppermute x17, waiting for transfers between devices, chip_swap(): return lax.ppermute(values_in, 'mp', [(0, 2), (2, 0), (1, 3), (3, 1)])  57.1 us
    ppermute x41, starting transfers between devices, swap(): lax.ppermute(values, 'dp', [(source, source ^ stride) for source in range...  53.4 us
    unnamed x189, local copies, waits for them, and re-layouts  21.4 us
    ppermute x65, starting transfers between devices, core_swap(): return lax.ppermute(values_in, 'mp', [(0, 1), (1, 0), (2, 3), (3, 2)])  16.3 us
    ppermute x65, waiting for transfers between devices, core_swap(): return lax.ppermute(values_in, 'mp', [(0, 1), (1, 0), (2, 3), (3, 2)])  16.1 us
    ppermute x17, starting transfers between devices, chip_swap(): return lax.ppermute(values_in, 'mp', [(0, 2), (2, 0), (1, 3), (3, 1)])  15 us
  transfers between devices with their start and end apart: 123, of which 61 were waited for; matrix products, arithmetic and copies ran while one was open for 0% of the time, Pallas kernels for 23%

profile of v5, /device:TPU:0, one launch (start us, length us, event | category | flops | bytes accessed | tf_op | source)
XLA Modules:
  0.0 480.8 jit_solution(12591226621512588591)
XLA Ops:
  3.1 4.0 collective-permute-start.2
  12.8 3.7 collective-permute-done.2.refs_1_.refs_3_
  19.9 7.9 %collective-permute-done.3.refs_1_ = bf16[256,768]{1,0:T(8,128)(2,1)S(1)} collective-permute-done((bf16[256,768]{1,0:T(8,128)(2,1)S(1)}, bf16[256,768]{1,0:T(8,128)(2,1)S(1)}, u32[]{:S(2)}, u32[]{:S(2)}) %collective-permute-start.3) | collective-permute-done | bytes 393248 | tf_op jit(solution)/shard_map/ppermute | solution.py:713
  29.8 3.3 collective-permute-start.8
  34.7 3.3 collective-permute-start.5
  42.3 5.8 %collective-permute-done.5.refs_1_.refs_3_ = bf16[128,256]{1,0:T(8,128)(2,1)S(1)} collective-permute-done((bf16[128,256]{1,0:T(8,128)(2,1)S(1)}, bf16[128,256]{1,0:T(8,128)(2,1)S(1)}, u32[]{:S(2)}, u32[]{:S(2)}) %collective-permute-start.5) | collective-permute-done | bytes 65568 | tf_op jit(solution)/shard_map/ppermute | solution.py:713
  51.8 2.9 collective-permute-done.7.refs_1_
  62.0 3.4 collective-permute-start.14
  67.9 2.9 attend.2
  73.7 2.5 collective-permute-done.14.refs_5_.refs_1_.refs_3_
  85.1 3.2 collective-permute-start.23
  88.5 10.4 %collective-permute-done.19.refs_3_ = bf16[320,1024]{1,0:T(8,128)(2,1)S(1)} collective-permute-done((bf16[320,1024]{1,0:T(8,128)(2,1)S(1)}, bf16[320,1024]{1,0:T(8,128)(2,1)S(1)}, u32[]{:S(2)}, u32[]{:S(2)}) %collective-permute-start.19) | collective-permute-done | bytes 655392 | tf_op jit(solution)/shard_map/ppermute | solution.py:830
  99.9 9.4 %collective-permute-done.24.refs_0_ = bf16[256,1024]{1,0:T(8,128)(2,1)S(1)} collective-permute-done((bf16[256,1024]{1,0:T(8,128)(2,1)S(1)}, bf16[256,1024]{1,0:T(8,128)(2,1)S(1)}, u32[]{:S(2)}, u32[]{:S(2)}) %collective-permute-start.24) | collective-permute-done | bytes 524320 | tf_op jit(solution)/shard_map/ppermute | solution.py:713
  111.6 3.0 collective-permute-start.30
  115.2 2.3 widen.4
  118.6 5.5 %collective-permute-done.26.refs_4_.refs_3_.refs_6_.refs_5_ = bf16[256,1024]{1,0:T(8,128)(2,1)S(1)} collective-permute-done((bf16[256,1024]{1,0:T(8,128)(2,1)S(1)}, bf16[256,1024]{1,0:T(8,128)(2,1)S(1)}, u32[]{:S(2)}, u32[]{:S(2)}) %collective-permute-start.26) | collective-permute-done | bytes 524320 | tf_op jit(solution)/shard_map/ppermute | solution.py:713
  124.1 3.9 collective-permute-done.30.refs_3_
  130.6 1.9 collective-permute-start.38
  133.0 2.3 widen.5
  141.9 13.9 %collective-permute-done.38.refs_5_.refs_1_ = bf16[256,2048]{1,0:T(8,128)(2,1)S(1)} collective-permute-done((bf16[256,2048]{1,0:T(8,128)(2,1)S(1)}, bf16[256,2048]{1,0:T(8,128)(2,1)S(1)}, u32[]{:S(2)}, u32[]{:S(2)}) %collective-permute-start.38) | collective-permute-done | bytes 1048608 | tf_op jit(solution)/shard_map/ppermute | solution.py:713
  162.6 11.2 %collective-permute-done.42.refs_0_ = bf16[320,1024]{1,0:T(8,128)(2,1)S(1)} collective-permute-done((bf16[320,1024]{1,0:T(8,128)(2,1)S(1)}, bf16[320,1024]{1,0:T(8,128)(2,1)S(1)}, u32[]{:S(2)}, u32[]{:S(2)}) %collective-permute-start.42) | collective-permute-done | bytes 655392 | tf_op jit(solution)/shard_map/ppermute | solution.py:830
  177.7 2.9 attend.3
  186.4 13.9 %collective-permute-done.49.refs_3_ = bf16[320,1024]{1,0:T(8,128)(2,1)S(1)} collective-permute-done((bf16[320,1024]{1,0:T(8,128)(2,1)S(1)}, bf16[320,1024]{1,0:T(8,128)(2,1)S(1)}, u32[]{:S(2)}, u32[]{:S(2)}) %collective-permute-start.49) | collective-permute-done | bytes 655392 | tf_op jit(solution)/shard_map/ppermute | solution.py:830
  202.1 3.2 collective-permute-done.52.refs_4_.refs_6_.refs_2_
  205.3 2.3 widen.6
  207.7 2.6 bend_back.4
  210.3 6.5 %collective-permute-done.53.refs_0_ = bf16[320,1024]{1,0:T(8,128)(2,1)S(1)} collective-permute-done((bf16[320,1024]{1,0:T(8,128)(2,1)S(1)}, bf16[320,1024]{1,0:T(8,128)(2,1)S(1)}, u32[]{:S(2)}, u32[]{:S(2)}) %collective-permute-start.53) | collective-permute-done | bytes 655392 | tf_op jit(solution)/shard_map/ppermute | solution.py:830
  219.1 2.3 widen.7
  230.4 4.0 weight_terms.6
  238.0 3.0 weight_terms.7
  241.0 4.6 collective-permute-done.64.refs_4_
  246.9 2.3 norm_back.4
  250.5 10.4 %collective-permute-done.67.refs_1_ = bf16[512,1024]{1,0:T(8,128)(2,1)} collective-permute-done((bf16[512,1024]{1,0:T(8,128)(2,1)}, bf16[512,1024]{1,0:T(8,128)(2,1)}, u32[]{:S(2)}, u32[]{:S(2)}) %collective-permute-start.67) | collective-permute-done | bytes 1048608 | tf_op jit(solution)/shard_map/ppermute | solution.py:713
  268.0 7.6 %attend_back.2 = (bf16[640,768]{1,0:T(8,128)(2,1)S(1)}, bf16[640,768]{1,0:T(8,128)(2,1)S(1)}, f32[8,128]{1,0:T(8,128)S(1)}) custom-call(s32[1]{0:T(128)} %bitcast.refs_0_, f32[1280,256]{1,0:T(8,128)S(1)} %fusion.refs_1_, bf16[640,768]{1,0:T(8,128)(2,1)S(1)} %get-tuple-element.491.refs_2_, bf16[640,768]{1,0:T(8,128)(2,1)S(1)} %get-tuple-element.497.refs_3_, ...), custom_call_target="tpu_custom_call" | custom-call | flops 1 | bytes 1 | tf_op jit(solution)/shard_map/attend_back/pallas_call | solution.py:87
  281.3 5.5 %collective-permute-done.77.refs_1_ = bf16[512,1024]{1,0:T(8,128)(2,1)S(1)} collective-permute-done((bf16[512,1024]{1,0:T(8,128)(2,1)S(1)}, bf16[512,1024]{1,0:T(8,128)(2,1)S(1)}, u32[]{:S(2)}, u32[]{:S(2)}) %collective-permute-start.77) | collective-permute-done | bytes 1048608 | tf_op jit(solution)/shard_map/ppermute | solution.py:713
  287.8 3.4 weight_terms.8
  292.5 4.7 collective-permute-done.76.refs_4_
  303.7 13.6 %collective-permute-done.83.refs_4_.refs_2_ = bf16[128,1024]{1,0:T(8,128)(2,1)S(1)} collective-permute-done((bf16[128,1024]{1,0:T(8,128)(2,1)S(1)}, bf16[128,1024]{1,0:T(8,128)(2,1)S(1)}, u32[]{:S(2)}, u32[]{:S(2)}) %collective-permute-start.83) | collective-permute-done | bytes 262176 | tf_op jit(solution)/shard_map/ppermute | solution.py:713
  329.2 2.9 weight_terms.9
  332.8 2.5 collective-permute-start.91
  336.9 10.6 %collective-permute-done.91.refs_6_.refs_2_ = bf16[128,1024]{1,0:T(8,128)(2,1)S(1)} collective-permute-done((bf16[128,1024]{1,0:T(8,128)(2,1)S(1)}, bf16[128,1024]{1,0:T(8,128)(2,1)S(1)}, u32[]{:S(2)}, u32[]{:S(2)}) %collective-permute-start.91) | collective-permute-done | bytes 262176 | tf_op jit(solution)/shard_map/ppermute | solution.py:713
  350.6 2.4 collective-permute-done.94.refs_1_
  353.2 1.8 collective-permute-start.97
  355.0 2.9 weight_terms.10
  362.8 4.0 collective-permute-done.97.refs_2_
  370.6 7.6 %attend_back.3 = (bf16[640,768]{1,0:T(8,128)(2,1)S(1)}, bf16[640,768]{1,0:T(8,128)(2,1)S(1)}, f32[8,128]{1,0:T(8,128)S(1)}) custom-call(s32[1]{0:T(128)} %bitcast.refs_0_, f32[1280,256]{1,0:T(8,128)S(1)} %fusion.refs_1_, bf16[640,768]{1,0:T(8,128)(2,1)S(1)} %copy-done.20, bf16[640,768]{1,0:T(8,128)(2,1)S(1)} %copy-done.23, ...), custom_call_target="tpu_custom_call" | custom-call | flops 1 | bytes 1 | tf_op jit(solution)/shard_map/attend_back/pallas_call | solution.py:87
  378.3 3.0 weight_terms.11
  384.9 1.9 collective-permute-start.108
  388.6 2.5 collective-permute-start.107
  391.2 2.0 moments.8
  393.2 12.2 %collective-permute-done.107.refs_6_.refs_2_ = bf16[128,1024]{1,0:T(8,128)(2,1)S(1)} collective-permute-done((bf16[128,1024]{1,0:T(8,128)(2,1)S(1)}, bf16[128,1024]{1,0:T(8,128)(2,1)S(1)}, u32[]{:S(2)}, u32[]{:S(2)}) %collective-permute-start.107) | collective-permute-done | bytes 262176 | tf_op jit(solution)/shard_map/ppermute | solution.py:713
  405.4 2.0 norm_back.7
  407.8 2.5 collective-permute-done.108.refs_1_
  416.6 1.8 narrow.31
  419.9 2.8 collective-permute-start.115
  422.8 12.8 %collective-permute-done.116.refs_1_ = bf16[256,1024]{1,0:T(8,128)(2,1)S(1)} collective-permute-done((bf16[256,1024]{1,0:T(8,128)(2,1)S(1)}, bf16[256,1024]{1,0:T(8,128)(2,1)S(1)}, u32[]{:S(2)}, u32[]{:S(2)}) %collective-permute-start.116) | collective-permute-done | bytes 524320 | tf_op jit(solution)/shard_map/ppermute | solution.py:713
  439.1 1.8 move_columns.11
  440.9 8.9 %collective-permute-done.117.refs_2_ = bf16[128,1024]{1,0:T(8,128)(2,1)S(1)} collective-permute-done((bf16[128,1024]{1,0:T(8,128)(2,1)S(1)}, bf16[128,1024]{1,0:T(8,128)(2,1)S(1)}, u32[]{:S(2)}, u32[]{:S(2)}) %collective-permute-start.117) | collective-permute-done | bytes 262176 | tf_op jit(solution)/shard_map/ppermute | solution.py:713
  449.8 2.0 moments.11
  455.0 3.5 collective-permute-done.119.refs_1_
  459.3 3.5 collective-permute-done.120.refs_1_
  462.9 4.3 collective-permute-done.121.refs_1_
  467.6 5.0 %collective-permute-done.122.refs_1_ = f32[16,1024]{1,0:T(8,128)S(1)} collective-permute-done((f32[16,1024]{1,0:T(8,128)S(1)}, f32[16,1024]{1,0:T(8,128)S(1)}, u32[]{:S(2)}, u32[]{:S(2)}) %collective-permute-start.122) | collective-permute-done | bytes 65568 | tf_op jit(solution)/shard_map/ppermute | solution.py:713
  476.4 2.0 apply.3
  (521 shorter events, 169.2 us)
Async XLA Ops:
  3.1 13.4 %collective-permute-start.2 = (bf16[128,768]{1,0:T(8,128)(2,1)}, bf16[128,768]{1,0:T(8,128)(2,1)S(1)}, u32[]{:S(2)}, u32[]{:S(2)}) collective-permute-start(bf16[128,768]{1,0:T(8,128)(2,1)} %get-tuple-element.396.refs_0_), channel_id=1, source_target_pairs={{0,16},{4,20},{8,24},{12,28},{16,0},{20,4},{24,8},{28,12},{1,17},{... | collective-permute-start | bytes 589832 | tf_op jit(solution)/shard_map/ppermute | solution.py:713
  17.5 10.4 %collective-permute-start.3 = (bf16[256,768]{1,0:T(8,128)(2,1)S(1)}, bf16[256,768]{1,0:T(8,128)(2,1)S(1)}, u32[]{:S(2)}, u32[]{:S(2)}) collective-permute-start(bf16[256,768]{1,0:T(8,128)(2,1)S(1)} %get-tuple-element.398.refs_0_), channel_id=1, source_target_pairs={{0,8},{4,12},{8,0},{12,4},{16,24},{20,28},{24,16},{28,20},{1,9},{5... | collective-permute-start | bytes 1179656 | tf_op jit(solution)/shard_map/ppermute | solution.py:713
  18.4 16.4 %collective-permute-start.6 = (bf16[320,1024]{1,0:T(8,128)(2,1)S(1)}, bf16[320,1024]{1,0:T(8,128)(2,1)S(1)}, u32[]{:S(2)}, u32[]{:S(2)}) collective-permute-start(bf16[320,1024]{1,0:T(8,128)(2,1)S(1)} %get-tuple-element.393.refs_0_), channel_id=1, source_target_pairs={{0,2},{2,0},{1,3},{3,1},{4,6},{6,4},{5,7},{7,5},{8,10},{10,8},{9,1... | collective-permute-start | bytes 1966088 | tf_op jit(solution)/shard_map/ppermute | solution.py:830
  27.9 28.4 %collective-permute-start.4 = (bf16[512,768]{1,0:T(8,128)(2,1)S(1)}, bf16[512,768]{1,0:T(8,128)(2,1)S(1)}, u32[]{:S(2)}, u32[]{:S(2)}) collective-permute-start(bf16[512,768]{1,0:T(8,128)(2,1)S(1)} %get-tuple-element.401.refs_3_.refs_1_), channel_id=1, source_target_pairs={{0,4},{4,0},{8,12},{12,8},{16,20},{20,16},{24,28},{28,24},{1,5},{5... | collective-permute-start | bytes 2359304 | tf_op jit(solution)/shard_map/ppermute | solution.py:713
  29.3 20.3 %collective-permute-start = (bf16[160,1024]{1,0:T(8,128)(2,1)S(1)}, bf16[160,1024]{1,0:T(8,128)(2,1)S(1)}, u32[]{:S(2)}, u32[]{:S(2)}) collective-permute-start(bf16[160,1024]{1,0:T(8,128)(2,1)S(1)} %get-tuple-element.394), channel_id=1, source_target_pairs={{0,1},{1,0},{2,3},{3,2},{4,5},{5,4},{6,7},{7,6},{8,9},{9,8},{10,11... | collective-permute-start | bytes 983048 | tf_op jit(solution)/shard_map/ppermute | solution.py:826
  29.3 21.1 %collective-permute-start.1 = (bf16[160,1024]{1,0:T(8,128)(2,1)S(1)}, bf16[160,1024]{1,0:T(8,128)(2,1)S(1)}, u32[]{:S(2)}, u32[]{:S(2)}) collective-permute-start(bf16[160,1024]{1,0:T(8,128)(2,1)S(1)} %get-tuple-element.395), channel_id=1, source_target_pairs={{0,1},{1,0},{2,3},{3,2},{4,5},{5,4},{6,7},{7,6},{8,9},{9,8},{10,11... | collective-permute-start | bytes 983048 | tf_op jit(solution)/shard_map/ppermute | solution.py:826
  29.8 20.6 %collective-permute-start.8 = (bf16[128,1024]{1,0:T(8,128)(2,1)S(1)}, bf16[128,1024]{1,0:T(8,128)(2,1)S(1)}, u32[]{:S(2)}, u32[]{:S(2)}) collective-permute-start(bf16[128,1024]{1,0:T(8,128)(2,1)S(1)} %get-tuple-element.410.refs_0_), channel_id=1, source_target_pairs={{0,16},{4,20},{8,24},{12,28},{16,0},{20,4},{24,8},{28,12},{1,17},{... | collective-permute-start | bytes 786440 | tf_op jit(solution)/shard_map/ppermute | solution.py:713
  34.7 13.3 %collective-permute-start.5 = (bf16[128,256]{1,0:T(8,128)(2,1)S(1)}, bf16[128,256]{1,0:T(8,128)(2,1)S(1)}, u32[]{:S(2)}, u32[]{:S(2)}) collective-permute-start(bf16[128,256]{1,0:T(8,128)(2,1)S(1)} %get-tuple-element.402.refs_0_), channel_id=1, source_target_pairs={{0,16},{4,20},{8,24},{12,28},{16,0},{20,4},{24,8},{28,12},{1,17},{... | collective-permute-start | bytes 196616 | tf_op jit(solution)/shard_map/ppermute | solution.py:713
  48.1 22.8 %collective-permute-start.13 = (bf16[320,1024]{1,0:T(8,128)(2,1)}, bf16[320,1024]{1,0:T(8,128)(2,1)}, u32[]{:S(2)}, u32[]{:S(2)}) collective-permute-start(bf16[320,1024]{1,0:T(8,128)(2,1)} %get-tuple-element.426.refs_0_), channel_id=1, source_target_pairs={{0,2},{2,0},{1,3},{3,1},{4,6},{6,4},{5,7},{7,5},{8,10},{10,8},{9,1... | collective-permute-start | bytes 1966088 | tf_op jit(solution)/shard_map/ppermute | solution.py:830
  49.6 5.0 %collective-permute-start.7 = (bf16[256,256]{1,0:T(8,128)(2,1)S(1)}, bf16[256,256]{1,0:T(8,128)(2,1)S(1)}, u32[]{:S(2)}, u32[]{:S(2)}) collective-permute-start(bf16[256,256]{1,0:T(8,128)(2,1)S(1)} %get-tuple-element.409.refs_0_), channel_id=1, source_target_pairs={{0,8},{4,12},{8,0},{12,4},{16,24},{20,28},{24,16},{28,20},{1,9},{5... | collective-permute-start | bytes 393224 | tf_op jit(solution)/shard_map/ppermute | solution.py:713
  50.4 8.6 %collective-permute-start.9 = (bf16[160,1024]{1,0:T(8,128)(2,1)S(1)}, bf16[160,1024]{1,0:T(8,128)(2,1)S(1)}, u32[]{:S(2)}, u32[]{:S(2)}) collective-permute-start(bf16[160,1024]{1,0:T(8,128)(2,1)S(1)} %get-tuple-element.416), channel_id=1, source_target_pairs={{0,1},{1,0},{2,3},{3,2},{4,5},{5,4},{6,7},{7,6},{8,9},{9,8},{10,11... | collective-permute-start | bytes 983048 | tf_op jit(solution)/shard_map/ppermute | solution.py:826
  50.4 8.6 %collective-permute-start.10 = (bf16[160,1024]{1,0:T(8,128)(2,1)S(1)}, bf16[160,1024]{1,0:T(8,128)(2,1)S(1)}, u32[]{:S(2)}, u32[]{:S(2)}) collective-permute-start(bf16[160,1024]{1,0:T(8,128)(2,1)S(1)} %get-tuple-element.417), channel_id=1, source_target_pairs={{0,1},{1,0},{2,3},{3,2},{4,5},{5,4},{6,7},{7,6},{8,9},{9,8},{10,11... | collective-permute-start | bytes 983048 | tf_op jit(solution)/shard_map/ppermute | solution.py:826
  54.7 17.8 %collective-permute-start.12 = (bf16[256,1024]{1,0:T(8,128)(2,1)}, bf16[256,1024]{1,0:T(8,128)(2,1)}, u32[]{:S(2)}, u32[]{:S(2)}) collective-permute-start(bf16[256,1024]{1,0:T(8,128)(2,1)} %get-tuple-element.425.refs_0_), channel_id=1, source_target_pairs={{0,8},{4,12},{8,0},{12,4},{16,24},{20,28},{24,16},{28,20},{1,9},{5... | collective-permute-start | bytes 1572872 | tf_op jit(solution)/shard_map/ppermute | solution.py:713
  56.3 17.4 %collective-permute-start.11 = (bf16[512,256]{1,0:T(8,128)(2,1)}, bf16[512,256]{1,0:T(8,128)(2,1)S(1)}, u32[]{:S(2)}, u32[]{:S(2)}) collective-permute-start(bf16[512,256]{1,0:T(8,128)(2,1)} %get-tuple-element.423.refs_1_.refs_3_), channel_id=1, source_target_pairs={{0,4},{4,0},{8,12},{12,8},{16,20},{20,16},{24,28},{28,24},{1,5},{5... | collective-permute-start | bytes 786440 | tf_op jit(solution)/shard_map/ppermute | solution.py:713
  62.0 14.2 %collective-permute-start.14 = (bf16[128,1024]{1,0:T(8,128)(2,1)}, bf16[128,1024]{1,0:T(8,128)(2,1)}, u32[]{:S(2)}, u32[]{:S(2)}) collective-permute-start(bf16[128,1024]{1,0:T(8,128)(2,1)} %get-tuple-element.430.refs_0_), channel_id=1, source_target_pairs={{0,16},{4,20},{8,24},{12,28},{16,0},{20,4},{24,8},{28,12},{1,17},{... | collective-permute-start | bytes 786440 | tf_op jit(solution)/shard_map/ppermute | solution.py:713
  78.3 33.3 %collective-permute-start.22 = (bf16[512,1024]{1,0:T(8,128)(2,1)S(1)}, bf16[512,1024]{1,0:T(8,128)(2,1)S(1)}, u32[]{:S(2)}, u32[]{:S(2)}) collective-permute-start(bf16[512,1024]{1,0:T(8,128)(2,1)S(1)} %get-tuple-element.450.refs_3_.refs_1_), channel_id=1, source_target_pairs={{0,4},{4,0},{8,12},{12,8},{16,20},{20,16},{24,28},{28,24},{1,5},{5... | collective-permute-start | bytes 3145736 | tf_op jit(solution)/shard_map/ppermute | solution.py:713
  82.0 16.8 %collective-permute-start.19 = (bf16[320,1024]{1,0:T(8,128)(2,1)S(1)}, bf16[320,1024]{1,0:T(8,128)(2,1)S(1)}, u32[]{:S(2)}, u32[]{:S(2)}) collective-permute-start(bf16[320,1024]{1,0:T(8,128)(2,1)S(1)} %get-tuple-element.441), channel_id=1, source_target_pairs={{0,2},{2,0},{1,3},{3,1},{4,6},{6,4},{5,7},{7,5},{8,10},{10,8},{9,1... | collective-permute-start | bytes 1966088 | tf_op jit(solution)/shard_map/ppermute | solution.py:830
  84.7 24.6 %collective-permute-start.24 = (bf16[256,1024]{1,0:T(8,128)(2,1)S(1)}, bf16[256,1024]{1,0:T(8,128)(2,1)S(1)}, u32[]{:S(2)}, u32[]{:S(2)}) collective-permute-start(bf16[256,1024]{1,0:T(8,128)(2,1)S(1)} %get-tuple-element.452.refs_1_.refs_3_), channel_id=1, source_target_pairs={{0,8},{4,12},{8,0},{12,4},{16,24},{20,28},{24,16},{28,20},{1,9},{5... | collective-permute-start | bytes 1572872 | tf_op jit(solution)/shard_map/ppermute | solution.py:713
  85.1 24.2 %collective-permute-start.23 = (bf16[128,1024]{1,0:T(8,128)(2,1)S(1)}, bf16[128,1024]{1,0:T(8,128)(2,1)S(1)}, u32[]{:S(2)}, u32[]{:S(2)}) collective-permute-start(bf16[128,1024]{1,0:T(8,128)(2,1)S(1)} %get-tuple-element.451.refs_0_), channel_id=1, source_target_pairs={{0,16},{4,20},{8,24},{12,28},{16,0},{20,4},{24,8},{28,12},{1,17},{... | collective-permute-start | bytes 786440 | tf_op jit(solution)/shard_map/ppermute | solution.py:713
  88.4 23.2 %collective-permute-start.25 = (bf16[128,1024]{1,0:T(8,128)(2,1)S(1)}, bf16[128,1024]{1,0:T(8,128)(2,1)S(1)}, u32[]{:S(2)}, u32[]{:S(2)}) collective-permute-start(bf16[128,1024]{1,0:T(8,128)(2,1)S(1)} %get-tuple-element.456.refs_0_), channel_id=1, source_target_pairs={{0,16},{4,20},{8,24},{12,28},{16,0},{20,4},{24,8},{28,12},{1,17},{... | collective-permute-start | bytes 786440 | tf_op jit(solution)/shard_map/ppermute | solution.py:713
  99.3 30.4 %collective-permute-start.28 = (bf16[320,1024]{1,0:T(8,128)(2,1)S(1)}, bf16[320,1024]{1,0:T(8,128)(2,1)S(1)}, u32[]{:S(2)}, u32[]{:S(2)}) collective-permute-start(bf16[320,1024]{1,0:T(8,128)(2,1)S(1)} %get-tuple-element.447.refs_0_), channel_id=1, source_target_pairs={{0,2},{2,0},{1,3},{3,1},{4,6},{6,4},{5,7},{7,5},{8,10},{10,8},{9,1... | collective-permute-start | bytes 1966088 | tf_op jit(solution)/shard_map/ppermute | solution.py:830
  109.4 14.8 %collective-permute-start.26 = (bf16[256,1024]{1,0:T(8,128)(2,1)S(1)}, bf16[256,1024]{1,0:T(8,128)(2,1)S(1)}, u32[]{:S(2)}, u32[]{:S(2)}) collective-permute-start(bf16[256,1024]{1,0:T(8,128)(2,1)S(1)} %get-tuple-element.452.refs_1_.refs_3_), channel_id=1, source_target_pairs={{0,4},{4,0},{8,12},{12,8},{16,20},{20,16},{24,28},{28,24},{1,5},{5... | collective-permute-start | bytes 1572872 | tf_op jit(solution)/shard_map/ppermute | solution.py:713
  111.6 18.2 %collective-permute-start.29 = (bf16[256,1024]{1,0:T(8,128)(2,1)S(1)}, bf16[256,1024]{1,0:T(8,128)(2,1)S(1)}, u32[]{:S(2)}, u32[]{:S(2)}) collective-permute-start(bf16[256,1024]{1,0:T(8,128)(2,1)S(1)} %get-tuple-element.461.refs_0_), channel_id=1, source_target_pairs={{0,8},{4,12},{8,0},{12,4},{16,24},{20,28},{24,16},{28,20},{1,9},{5... | collective-permute-start | bytes 1572872 | tf_op jit(solution)/shard_map/ppermute | solution.py:713
  111.6 16.4 %collective-permute-start.30 = (bf16[128,1024]{1,0:T(8,128)(2,1)S(1)}, bf16[128,1024]{1,0:T(8,128)(2,1)S(1)}, u32[]{:S(2)}, u32[]{:S(2)}) collective-permute-start(bf16[128,1024]{1,0:T(8,128)(2,1)S(1)} %get-tuple-element.462.refs_2_), channel_id=1, source_target_pairs={{0,16},{4,20},{8,24},{12,28},{16,0},{20,4},{24,8},{28,12},{1,17},{... | collective-permute-start | bytes 786440 | tf_op jit(solution)/shard_map/ppermute | solution.py:713
  114.7 20.7 %collective-permute-start.27 = (bf16[256,1024]{1,0:T(8,128)(2,1)S(1)}, bf16[256,1024]{1,0:T(8,128)(2,1)S(1)}, u32[]{:S(2)}, u32[]{:S(2)}) collective-permute-start(bf16[256,1024]{1,0:T(8,128)(2,1)S(1)} %get-tuple-element.459.refs_2_.refs_4_), channel_id=1, source_target_pairs={{0,4},{4,0},{8,12},{12,8},{16,20},{20,16},{24,28},{28,24},{1,5},{5... | collective-permute-start | bytes 1572872 | tf_op jit(solution)/shard_map/ppermute | solution.py:713
  130.6 25.3 %collective-permute-start.38 = (bf16[256,2048]{1,0:T(8,128)(2,1)S(1)}, bf16[256,2048]{1,0:T(8,128)(2,1)S(1)}, u32[]{:S(2)}, u32[]{:S(2)}) collective-permute-start(bf16[256,2048]{1,0:T(8,128)(2,1)S(1)} %get-tuple-element.483.refs_0_), channel_id=1, source_target_pairs={{0,8},{4,12},{8,0},{12,4},{16,24},{20,28},{24,16},{28,20},{1,9},{5... | collective-permute-start | bytes 3145736 | tf_op jit(solution)/shard_map/ppermute | solution.py:713
  132.4 25.0 %collective-permute-start.39 = (bf16[512,1024]{1,0:T(8,128)(2,1)S(1)}, bf16[512,1024]{1,0:T(8,128)(2,1)S(1)}, u32[]{:S(2)}, u32[]{:S(2)}) collective-permute-start(bf16[512,1024]{1,0:T(8,128)(2,1)S(1)} %get-tuple-element.484.refs_3_.refs_1_), channel_id=1, source_target_pairs={{0,4},{4,0},{8,12},{12,8},{16,20},{20,16},{24,28},{28,24},{1,5},{5... | collective-permute-start | bytes 3145736 | tf_op jit(solution)/shard_map/ppermute | solution.py:713
  139.3 18.2 %collective-permute-start.37 = (bf16[320,1024]{1,0:T(8,128)(2,1)S(1)}, bf16[320,1024]{1,0:T(8,128)(2,1)S(1)}, u32[]{:S(2)}, u32[]{:S(2)}) collective-permute-start(bf16[320,1024]{1,0:T(8,128)(2,1)S(1)} %get-tuple-element.481), channel_id=1, source_target_pairs={{0,2},{2,0},{1,3},{3,1},{4,6},{6,4},{5,7},{7,5},{8,10},{10,8},{9,1... | collective-permute-start | bytes 1966088 | tf_op jit(solution)/shard_map/ppermute | solution.py:830
  158.0 15.8 %collective-permute-start.42 = (bf16[320,1024]{1,0:T(8,128)(2,1)S(1)}, bf16[320,1024]{1,0:T(8,128)(2,1)S(1)}, u32[]{:S(2)}, u32[]{:S(2)}) collective-permute-start(bf16[320,1024]{1,0:T(8,128)(2,1)S(1)} %get-tuple-element.486.refs_0_), channel_id=1, source_target_pairs={{0,2},{2,0},{1,3},{3,1},{4,6},{6,4},{5,7},{7,5},{8,10},{10,8},{9,1... | collective-permute-start | bytes 1966088 | tf_op jit(solution)/shard_map/ppermute | solution.py:830
  158.7 46.6 %collective-permute-start.52 = (bf16[512,2048]{1,0:T(8,128)(2,1)S(1)}, bf16[512,2048]{1,0:T(8,128)(2,1)S(1)}, u32[]{:S(2)}, u32[]{:S(2)}) collective-permute-start(bf16[512,2048]{1,0:T(8,128)(2,1)S(1)} %get-tuple-element.518.refs_3_.refs_1_), channel_id=1, source_target_pairs={{0,4},{4,0},{8,12},{12,8},{16,20},{20,16},{24,28},{28,24},{1,5},{5... | collective-permute-start | bytes 6291464 | tf_op jit(solution)/shard_map/ppermute | solution.py:713
  183.5 16.8 %collective-permute-start.49 = (bf16[320,1024]{1,0:T(8,128)(2,1)S(1)}, bf16[320,1024]{1,0:T(8,128)(2,1)S(1)}, u32[]{:S(2)}, u32[]{:S(2)}) collective-permute-start(bf16[320,1024]{1,0:T(8,128)(2,1)S(1)} %get-tuple-element.512), channel_id=1, source_target_pairs={{0,2},{2,0},{1,3},{3,1},{4,6},{6,4},{5,7},{7,5},{8,10},{10,8},{9,1... | collective-permute-start | bytes 1966088 | tf_op jit(solution)/shard_map/ppermute | solution.py:830
  200.8 16.0 %collective-permute-start.53 = (bf16[320,1024]{1,0:T(8,128)(2,1)S(1)}, bf16[320,1024]{1,0:T(8,128)(2,1)S(1)}, u32[]{:S(2)}, u32[]{:S(2)}) collective-permute-start(bf16[320,1024]{1,0:T(8,128)(2,1)S(1)} %get-tuple-element.515.refs_0_), channel_id=1, source_target_pairs={{0,2},{2,0},{1,3},{3,1},{4,6},{6,4},{5,7},{7,5},{8,10},{10,8},{9,1... | collective-permute-start | bytes 1966088 | tf_op jit(solution)/shard_map/ppermute | solution.py:830
  202.1 5.6 %collective-permute-start.54 = (bf16[160,1024]{1,0:T(8,128)(2,1)S(1)}, bf16[160,1024]{1,0:T(8,128)(2,1)S(1)}, u32[]{:S(2)}, u32[]{:S(2)}) collective-permute-start(bf16[160,1024]{1,0:T(8,128)(2,1)S(1)} %copy-done.87), channel_id=1, source_target_pairs={{0,1},{1,0},{2,3},{3,2},{4,5},{5,4},{6,7},{7,6},{8,9},{9,8},{10,11... | collective-permute-start | bytes 983048 | tf_op jit(solution)/shard_map/ppermute | solution.py:826
  228.5 17.1 %collective-permute-start.64 = (bf16[320,1024]{1,0:T(8,128)(2,1)}, bf16[320,1024]{1,0:T(8,128)(2,1)}, u32[]{:S(2)}, u32[]{:S(2)}) collective-permute-start(bf16[320,1024]{1,0:T(8,128)(2,1)} %get-tuple-element.549), channel_id=1, source_target_pairs={{0,2},{2,0},{1,3},{3,1},{4,6},{6,4},{5,7},{7,5},{8,10},{10,8},{9,1... | collective-permute-start | bytes 1966088 | tf_op jit(solution)/shard_map/ppermute | solution.py:830
  235.4 25.4 %collective-permute-start.67 = (bf16[512,1024]{1,0:T(8,128)(2,1)}, bf16[512,1024]{1,0:T(8,128)(2,1)}, u32[]{:S(2)}, u32[]{:S(2)}) collective-permute-start(bf16[512,1024]{1,0:T(8,128)(2,1)} %get-tuple-element.558), channel_id=1, source_target_pairs={{0,4},{4,0},{8,12},{12,8},{16,20},{20,16},{24,28},{28,24},{1,5},{5... | collective-permute-start | bytes 3145736 | tf_op jit(solution)/shard_map/ppermute | solution.py:713
  249.2 16.0 %collective-permute-start.68 = (bf16[320,1024]{1,0:T(8,128)(2,1)S(1)}, bf16[320,1024]{1,0:T(8,128)(2,1)S(1)}, u32[]{:S(2)}, u32[]{:S(2)}) collective-permute-start(bf16[320,1024]{1,0:T(8,128)(2,1)S(1)} %get-tuple-element.554.refs_0_.refs_8_), channel_id=1, source_target_pairs={{0,2},{2,0},{1,3},{3,1},{4,6},{6,4},{5,7},{7,5},{8,10},{10,8},{9,1... | collective-permute-start | bytes 1966088 | tf_op jit(solution)/shard_map/ppermute | solution.py:830
  250.0 13.8 %collective-permute-start.65 = (bf16[160,1024]{1,0:T(8,128)(2,1)S(1)}, bf16[160,1024]{1,0:T(8,128)(2,1)S(1)}, u32[]{:S(2)}, u32[]{:S(2)}) collective-permute-start(bf16[160,1024]{1,0:T(8,128)(2,1)S(1)} %get-tuple-element.555), channel_id=1, source_target_pairs={{0,1},{1,0},{2,3},{3,2},{4,5},{5,4},{6,7},{7,6},{8,9},{9,8},{10,11... | collective-permute-start | bytes 983048 | tf_op jit(solution)/shard_map/ppermute | solution.py:826
  250.0 13.8 %collective-permute-start.66 = (bf16[160,1024]{1,0:T(8,128)(2,1)S(1)}, bf16[160,1024]{1,0:T(8,128)(2,1)S(1)}, u32[]{:S(2)}, u32[]{:S(2)}) collective-permute-start(bf16[160,1024]{1,0:T(8,128)(2,1)S(1)} %get-tuple-element.556), channel_id=1, source_target_pairs={{0,1},{1,0},{2,3},{3,2},{4,5},{5,4},{6,7},{7,6},{8,9},{9,8},{10,11... | collective-permute-start | bytes 983048 | tf_op jit(solution)/shard_map/ppermute | solution.py:826
  262.3 13.2 %collective-permute-start.71 = (bf16[256,1024]{1,0:T(8,128)(2,1)S(1)}, bf16[256,1024]{1,0:T(8,128)(2,1)S(1)}, u32[]{:S(2)}, u32[]{:S(2)}) collective-permute-start(bf16[256,1024]{1,0:T(8,128)(2,1)S(1)} %get-tuple-element.572), channel_id=1, source_target_pairs={{0,8},{4,12},{8,0},{12,4},{16,24},{20,28},{24,16},{28,20},{1,9},{5... | collective-permute-start | bytes 1572872 | tf_op jit(solution)/shard_map/ppermute | solution.py:713
  262.7 24.1 %collective-permute-start.77 = (bf16[512,1024]{1,0:T(8,128)(2,1)S(1)}, bf16[512,1024]{1,0:T(8,128)(2,1)S(1)}, u32[]{:S(2)}, u32[]{:S(2)}) collective-permute-start(bf16[512,1024]{1,0:T(8,128)(2,1)S(1)} %copy-done.81), channel_id=1, source_target_pairs={{0,4},{4,0},{8,12},{12,8},{16,20},{20,16},{24,28},{28,24},{1,5},{5... | collective-permute-start | bytes 3145736 | tf_op jit(solution)/shard_map/ppermute | solution.py:713
  280.2 17.0 %collective-permute-start.76 = (bf16[320,1024]{1,0:T(8,128)(2,1)}, bf16[320,1024]{1,0:T(8,128)(2,1)S(1)}, u32[]{:S(2)}, u32[]{:S(2)}) collective-permute-start(bf16[320,1024]{1,0:T(8,128)(2,1)} %get-tuple-element.583), channel_id=1, source_target_pairs={{0,2},{2,0},{1,3},{3,1},{4,6},{6,4},{5,7},{7,5},{8,10},{10,8},{9,1... | collective-permute-start | bytes 1966088 | tf_op jit(solution)/shard_map/ppermute | solution.py:830
  291.3 27.7 %collective-permute-start.81 = (bf16[512,1024]{1,0:T(8,128)(2,1)S(1)}, bf16[512,1024]{1,0:T(8,128)(2,1)S(1)}, u32[]{:S(2)}, u32[]{:S(2)}) collective-permute-start(bf16[512,1024]{1,0:T(8,128)(2,1)S(1)} %get-tuple-element.599), channel_id=1, source_target_pairs={{0,4},{4,0},{8,12},{12,8},{16,20},{20,16},{24,28},{28,24},{1,5},{5... | collective-permute-start | bytes 3145736 | tf_op jit(solution)/shard_map/ppermute | solution.py:713
  298.2 20.8 %collective-permute-start.80 = (bf16[320,1024]{1,0:T(8,128)(2,1)S(1)}, bf16[320,1024]{1,0:T(8,128)(2,1)S(1)}, u32[]{:S(2)}, u32[]{:S(2)}) collective-permute-start(bf16[320,1024]{1,0:T(8,128)(2,1)S(1)} %get-tuple-element.592.refs_0_), channel_id=1, source_target_pairs={{0,2},{2,0},{1,3},{3,1},{4,6},{6,4},{5,7},{7,5},{8,10},{10,8},{9,1... | collective-permute-start | bytes 1966088 | tf_op jit(solution)/shard_map/ppermute | solution.py:830
  299.0 20.0 %collective-permute-start.82 = (bf16[256,1024]{1,0:T(8,128)(2,1)S(1)}, bf16[256,1024]{1,0:T(8,128)(2,1)S(1)}, u32[]{:S(2)}, u32[]{:S(2)}) collective-permute-start(bf16[256,1024]{1,0:T(8,128)(2,1)S(1)} %copy-done.83), channel_id=1, source_target_pairs={{0,8},{4,12},{8,0},{12,4},{16,24},{20,28},{24,16},{28,20},{1,9},{5... | collective-permute-start | bytes 1572872 | tf_op jit(solution)/shard_map/ppermute | solution.py:713
  300.6 16.6 %collective-permute-start.83 = (bf16[128,1024]{1,0:T(8,128)(2,1)S(1)}, bf16[128,1024]{1,0:T(8,128)(2,1)S(1)}, u32[]{:S(2)}, u32[]{:S(2)}) collective-permute-start(bf16[128,1024]{1,0:T(8,128)(2,1)S(1)} %get-tuple-element.601), channel_id=1, source_target_pairs={{0,16},{4,20},{8,24},{12,28},{16,0},{20,4},{24,8},{28,12},{1,17},{... | collective-permute-start | bytes 786440 | tf_op jit(solution)/shard_map/ppermute | solution.py:713
  327.2 20.3 %collective-permute-start.90 = (bf16[320,1024]{1,0:T(8,128)(2,1)S(1)}, bf16[320,1024]{1,0:T(8,128)(2,1)S(1)}, u32[]{:S(2)}, u32[]{:S(2)}) collective-permute-start(bf16[320,1024]{1,0:T(8,128)(2,1)S(1)} %get-tuple-element.619), channel_id=1, source_target_pairs={{0,2},{2,0},{1,3},{3,1},{4,6},{6,4},{5,7},{7,5},{8,10},{10,8},{9,1... | collective-permute-start | bytes 1966088 | tf_op jit(solution)/shard_map/ppermute | solution.py:830
  332.2 28.4 %collective-permute-start.96 = (bf16[512,1024]{1,0:T(8,128)(2,1)S(1)}, bf16[512,1024]{1,0:T(8,128)(2,1)S(1)}, u32[]{:S(2)}, u32[]{:S(2)}) collective-permute-start(bf16[512,1024]{1,0:T(8,128)(2,1)S(1)} %get-tuple-element.640), channel_id=1, source_target_pairs={{0,4},{4,0},{8,12},{12,8},{16,20},{20,16},{24,28},{28,24},{1,5},{5... | collective-permute-start | bytes 3145736 | tf_op jit(solution)/shard_map/ppermute | solution.py:713
  332.8 14.7 %collective-permute-start.91 = (bf16[128,1024]{1,0:T(8,128)(2,1)S(1)}, bf16[128,1024]{1,0:T(8,128)(2,1)S(1)}, u32[]{:S(2)}, u32[]{:S(2)}) collective-permute-start(bf16[128,1024]{1,0:T(8,128)(2,1)S(1)} %get-tuple-element.628), channel_id=1, source_target_pairs={{0,16},{4,20},{8,24},{12,28},{16,0},{20,4},{24,8},{28,12},{1,17},{... | collective-permute-start | bytes 786440 | tf_op jit(solution)/shard_map/ppermute | solution.py:713
  335.4 17.7 %collective-permute-start.94 = (bf16[256,1024]{1,0:T(8,128)(2,1)S(1)}, bf16[256,1024]{1,0:T(8,128)(2,1)S(1)}, u32[]{:S(2)}, u32[]{:S(2)}) collective-permute-start(bf16[256,1024]{1,0:T(8,128)(2,1)S(1)} %get-tuple-element.634), channel_id=1, source_target_pairs={{0,8},{4,12},{8,0},{12,4},{16,24},{20,28},{24,16},{28,20},{1,9},{5... | collective-permute-start | bytes 1572872 | tf_op jit(solution)/shard_map/ppermute | solution.py:713
  348.8 18.0 %collective-permute-start.95 = (bf16[320,1024]{1,0:T(8,128)(2,1)S(1)}, bf16[320,1024]{1,0:T(8,128)(2,1)S(1)}, u32[]{:S(2)}, u32[]{:S(2)}) collective-permute-start(bf16[320,1024]{1,0:T(8,128)(2,1)S(1)} %get-tuple-element.630.refs_0_.refs_8_), channel_id=1, source_target_pairs={{0,2},{2,0},{1,3},{3,1},{4,6},{6,4},{5,7},{7,5},{8,10},{10,8},{9,1... | collective-permute-start | bytes 1966088 | tf_op jit(solution)/shard_map/ppermute | solution.py:830
  350.1 7.9 %collective-permute-start.92 = (bf16[160,1024]{1,0:T(8,128)(2,1)S(1)}, bf16[160,1024]{1,0:T(8,128)(2,1)S(1)}, u32[]{:S(2)}, u32[]{:S(2)}) collective-permute-start(bf16[160,1024]{1,0:T(8,128)(2,1)S(1)} %get-tuple-element.631), channel_id=1, source_target_pairs={{0,1},{1,0},{2,3},{3,2},{4,5},{5,4},{6,7},{7,6},{8,9},{9,8},{10,11... | collective-permute-start | bytes 983048 | tf_op jit(solution)/shard_map/ppermute | solution.py:826
  350.1 7.9 %collective-permute-start.93 = (bf16[160,1024]{1,0:T(8,128)(2,1)S(1)}, bf16[160,1024]{1,0:T(8,128)(2,1)S(1)}, u32[]{:S(2)}, u32[]{:S(2)}) collective-permute-start(bf16[160,1024]{1,0:T(8,128)(2,1)S(1)} %get-tuple-element.632), channel_id=1, source_target_pairs={{0,1},{1,0},{2,3},{3,2},{4,5},{5,4},{6,7},{7,6},{8,9},{9,8},{10,11... | collective-permute-start | bytes 983048 | tf_op jit(solution)/shard_map/ppermute | solution.py:826
  353.2 13.6 %collective-permute-start.97 = (bf16[128,1024]{1,0:T(8,128)(2,1)S(1)}, bf16[128,1024]{1,0:T(8,128)(2,1)S(1)}, u32[]{:S(2)}, u32[]{:S(2)}) collective-permute-start(bf16[128,1024]{1,0:T(8,128)(2,1)S(1)} %get-tuple-element.648), channel_id=1, source_target_pairs={{0,16},{4,20},{8,24},{12,28},{16,0},{20,4},{24,8},{28,12},{1,17},{... | collective-permute-start | bytes 786440 | tf_op jit(solution)/shard_map/ppermute | solution.py:713
  360.8 20.5 %collective-permute-start.100 = (bf16[256,1024]{1,0:T(8,128)(2,1)S(1)}, bf16[256,1024]{1,0:T(8,128)(2,1)S(1)}, u32[]{:S(2)}, u32[]{:S(2)}) collective-permute-start(bf16[256,1024]{1,0:T(8,128)(2,1)S(1)} %get-tuple-element.659), channel_id=1, source_target_pairs={{0,8},{4,12},{8,0},{12,4},{16,24},{20,28},{24,16},{28,20},{1,9},{5... | collective-permute-start | bytes 1572872 | tf_op jit(solution)/shard_map/ppermute | solution.py:713
  362.1 26.1 %collective-permute-start.106 = (bf16[512,1024]{1,0:T(8,128)(2,1)S(1)}, bf16[512,1024]{1,0:T(8,128)(2,1)S(1)}, u32[]{:S(2)}, u32[]{:S(2)}) collective-permute-start(bf16[512,1024]{1,0:T(8,128)(2,1)S(1)} %get-tuple-element.673), channel_id=1, source_target_pairs={{0,4},{4,0},{8,12},{12,8},{16,20},{20,16},{24,28},{28,24},{1,5},{5... | collective-permute-start | bytes 3145736 | tf_op jit(solution)/shard_map/ppermute | solution.py:713
  384.9 25.4 %collective-permute-start.108 = (bf16[512,1024]{1,0:T(8,128)(2,1)S(1)}, bf16[512,1024]{1,0:T(8,128)(2,1)S(1)}, u32[]{:S(2)}, u32[]{:S(2)}) collective-permute-start(bf16[512,1024]{1,0:T(8,128)(2,1)S(1)} %get-tuple-element.690), channel_id=1, source_target_pairs={{0,4},{4,0},{8,12},{12,8},{16,20},{20,16},{24,28},{28,24},{1,5},{5... | collective-permute-start | bytes 3145736 | tf_op jit(solution)/shard_map/ppermute | solution.py:713
  387.0 18.5 %collective-permute-start.105 = (bf16[320,1024]{1,0:T(8,128)(2,1)S(1)}, bf16[320,1024]{1,0:T(8,128)(2,1)S(1)}, u32[]{:S(2)}, u32[]{:S(2)}) collective-permute-start(bf16[320,1024]{1,0:T(8,128)(2,1)S(1)} %get-tuple-element.670), channel_id=1, source_target_pairs={{0,2},{2,0},{1,3},{3,1},{4,6},{6,4},{5,7},{7,5},{8,10},{10,8},{9,1... | collective-permute-start | bytes 1966088 | tf_op jit(solution)/shard_map/ppermute | solution.py:830
  388.5 19.1 %collective-permute-start.109 = (bf16[256,1024]{1,0:T(8,128)(2,1)S(1)}, bf16[256,1024]{1,0:T(8,128)(2,1)S(1)}, u32[]{:S(2)}, u32[]{:S(2)}) collective-permute-start(bf16[256,1024]{1,0:T(8,128)(2,1)S(1)} %get-tuple-element.692), channel_id=1, source_target_pairs={{0,8},{4,12},{8,0},{12,4},{16,24},{20,28},{24,16},{28,20},{1,9},{5... | collective-permute-start | bytes 1572872 | tf_op jit(solution)/shard_map/ppermute | solution.py:713
  388.6 16.8 %collective-permute-start.107 = (bf16[128,1024]{1,0:T(8,128)(2,1)S(1)}, bf16[128,1024]{1,0:T(8,128)(2,1)S(1)}, u32[]{:S(2)}, u32[]{:S(2)}) collective-permute-start(bf16[128,1024]{1,0:T(8,128)(2,1)S(1)} %get-tuple-element.679), channel_id=1, source_target_pairs={{0,16},{4,20},{8,24},{12,28},{16,0},{20,4},{24,8},{28,12},{1,17},{... | collective-permute-start | bytes 786440 | tf_op jit(solution)/shard_map/ppermute | solution.py:713
  416.1 19.5 %collective-permute-start.116 = (bf16[256,1024]{1,0:T(8,128)(2,1)S(1)}, bf16[256,1024]{1,0:T(8,128)(2,1)S(1)}, u32[]{:S(2)}, u32[]{:S(2)}) collective-permute-start(bf16[256,1024]{1,0:T(8,128)(2,1)S(1)} %get-tuple-element.716), channel_id=1, source_target_pairs={{0,8},{4,12},{8,0},{12,4},{16,24},{20,28},{24,16},{28,20},{1,9},{5... | collective-permute-start | bytes 1572872 | tf_op jit(solution)/shard_map/ppermute | solution.py:713
  418.6 19.2 %collective-permute-start.114 = (bf16[320,1024]{1,0:T(8,128)(2,1)S(1)}, bf16[320,1024]{1,0:T(8,128)(2,1)S(1)}, u32[]{:S(2)}, u32[]{:S(2)}) collective-permute-start(bf16[320,1024]{1,0:T(8,128)(2,1)S(1)} %get-tuple-element.709), channel_id=1, source_target_pairs={{0,2},{2,0},{1,3},{3,1},{4,6},{6,4},{5,7},{7,5},{8,10},{10,8},{9,1... | collective-permute-start | bytes 1966088 | tf_op jit(solution)/shard_map/ppermute | solution.py:830
  419.9 16.8 %collective-permute-start.115 = (bf16[128,1024]{1,0:T(8,128)(2,1)S(1)}, bf16[128,1024]{1,0:T(8,128)(2,1)S(1)}, u32[]{:S(2)}, u32[]{:S(2)}) collective-permute-start(bf16[128,1024]{1,0:T(8,128)(2,1)S(1)} %get-tuple-element.711), channel_id=1, source_target_pairs={{0,16},{4,20},{8,24},{12,28},{16,0},{20,4},{24,8},{28,12},{1,17},{... | collective-permute-start | bytes 786440 | tf_op jit(solution)/shard_map/ppermute | solution.py:713
  435.7 14.0 %collective-permute-start.117 = (bf16[128,1024]{1,0:T(8,128)(2,1)S(1)}, bf16[128,1024]{1,0:T(8,128)(2,1)S(1)}, u32[]{:S(2)}, u32[]{:S(2)}) collective-permute-start(bf16[128,1024]{1,0:T(8,128)(2,1)S(1)} %get-tuple-element.731), channel_id=1, source_target_pairs={{0,16},{4,20},{8,24},{12,28},{16,0},{20,4},{24,8},{28,12},{1,17},{... | collective-permute-start | bytes 786440 | tf_op jit(solution)/shard_map/ppermute | solution.py:713
  467.2 5.4 %collective-permute-start.122 = (f32[16,1024]{1,0:T(8,128)S(1)}, f32[16,1024]{1,0:T(8,128)S(1)}, u32[]{:S(2)}, u32[]{:S(2)}) collective-permute-start(f32[16,1024]{1,0:T(8,128)S(1)} %get-tuple-element.746.refs_0_), channel_id=1, source_target_pairs={{0,16},{4,20},{8,24},{12,28},{16,0},{20,4},{24,8},{28,12},{1,17},{... | collective-permute-start | bytes 196616 | tf_op jit(solution)/shard_map/ppermute | solution.py:713
  (152 other events, 676.8 us)
